TPU v7x, 32 devices: a whole 2x2x4 slice. The times are simulated.
32 devices in a mesh: dp: 4 (over y, x), mp: 8 (over z, core).
Axes of the slice: x: 2, y: 2, z: 4, core: 2. Of those that a mesh axis runs over, the one named last changes fastest.
Arguments:
- layer_input: bfloat16 [8192, 2048], P(('dp', 'mp')), may hold values from -6 to 6
- cotangent: bfloat16 [8192, 2048], P(('dp', 'mp')), may hold values from -6 to 6
- lengths: int32 [4], P('dp'), may hold values from 1024 to 2048, as said below
- offsets: int32 [4], P('dp'), may hold values from 0 to 1024, as said below
- step: int32 [1], replicated, may hold values from 2 to 20
- mix_weight: float32 [3, 2048, 2048], P(None, 'dp', 'mp'), may hold values from -0.125 to 0.125
- out_weight: float32 [2048, 2048], P('mp', 'dp'), may hold values from -2 to 2
- up_weight: float32 [2048, 8192], P('dp', 'mp'), may hold values from -0.125 to 0.125
- down_weight: float32 [8192, 2048], P('mp', 'dp'), may hold values from -0.0625 to 0.0625
- mix_first: float32 [3, 2048, 2048], P(None, 'dp', 'mp'), may hold values from -80 to 80
- out_first: float32 [2048, 2048], P('mp', 'dp'), may hold values from -5 to 5
- up_first: float32 [2048, 8192], P('dp', 'mp'), may hold values from -32 to 32
- down_first: float32 [8192, 2048], P('mp', 'dp'), may hold values from -32 to 32
- mix_second: float32 [3, 2048, 2048], P(None, 'dp', 'mp'), may hold values from 6.5536 to 106.496
- out_second: float32 [2048, 2048], P('mp', 'dp'), may hold values from 0.024 to 0.4
- up_second: float32 [2048, 8192], P('dp', 'mp'), may hold values from 1.024 to 16.384
- down_second: float32 [8192, 2048], P('mp', 'dp'), may hold values from 1.024 to 16.384
- mix_bias: float32 [2, 2048], P(None, 'mp'), may hold values from -1.75 to 1.75
- up_bias: float32 [8192], P('mp'), may hold values from -1.75 to 1.75
- norm_gains: float32 [2, 2048], replicated, may hold values from 0.5 to 1.5
- shifts: float32 [4, 2048], replicated, may hold values from -1.25 to 1.25
- mix_bias_first: float32 [2, 2048], P(None, 'mp'), may hold values from -80 to 80
- up_bias_first: float32 [8192], P('mp'), may hold values from -32 to 32
- gains_first: float32 [2, 2048], replicated, may hold values from -96 to 96
- shifts_first: float32 [4, 2048], replicated, may hold values from -96 to 96
- mix_bias_second: float32 [2, 2048], P(None, 'mp'), may hold values from 6.5536 to 106.496
- up_bias_second: float32 [8192], P('mp'), may hold values from 1.024 to 16.384
- gains_second: float32 [2, 2048], replicated, may hold values from 9.0112 to 147.456
- shifts_second: float32 [4, 2048], replicated, may hold values from 9.0112 to 147.456
Outputs:
- layer_output: bfloat16 [8192, 2048], P(('dp', 'mp'))
- input_grad: float32 [8192, 2048], P(('dp', 'mp'))
- mix_updated: float32 [3, 2048, 2048], P(None, 'dp', 'mp')
- mix_first_next: float32 [3, 2048, 2048], P(None, 'dp', 'mp')
- mix_second_next: float32 [3, 2048, 2048], P(None, 'dp', 'mp')
- out_updated: float32 [2048, 2048], P('mp', 'dp')
- out_first_next: float32 [2048, 2048], P('mp', 'dp')
- out_second_next: float32 [2048, 2048], P('mp', 'dp')
- up_updated: float32 [2048, 8192], P('dp', 'mp')
- up_first_next: float32 [2048, 8192], P('dp', 'mp')
- up_second_next: float32 [2048, 8192], P('dp', 'mp')
- down_updated: float32 [8192, 2048], P('mp', 'dp')
- down_first_next: float32 [8192, 2048], P('mp', 'dp')
- down_second_next: float32 [8192, 2048], P('mp', 'dp')
- mix_bias_updated: float32 [2, 2048], P(None, 'mp')
- mix_bias_first_next: float32 [2, 2048], P(None, 'mp')
- mix_bias_second_next: float32 [2, 2048], P(None, 'mp')
- up_bias_updated: float32 [8192], P('mp')
- up_bias_first_next: float32 [8192], P('mp')
- up_bias_second_next: float32 [8192], P('mp')
- gains_updated: float32 [2, 2048], replicated
- gains_first_next: float32 [2, 2048], replicated
- gains_second_next: float32 [2, 2048], replicated
- shifts_updated: float32 [4, 2048], replicated
- shifts_first_next: float32 [4, 2048], replicated
- shifts_second_next: float32 [4, 2048], replicated
- mix_grad: float32 [3, 2048, 2048], P(None, 'dp', 'mp')
- out_weight_grad: float32 [2048, 2048], P('mp', 'dp')
- up_grad: float32 [2048, 8192], P('dp', 'mp')
- down_grad: float32 [8192, 2048], P('mp', 'dp')
- mix_bias_grad: float32 [2, 2048], P(None, 'mp')
- up_bias_grad: float32 [8192], P('mp')
- gains_grad: float32 [2, 2048], replicated
- shifts_grad: float32 [4, 2048], replicated
- mix_copy: bfloat16 [3, 2048, 2048], P(None, 'dp', 'mp')
- out_copy: bfloat16 [2048, 2048], P('mp', 'dp')
- up_copy: bfloat16 [2048, 8192], P('dp', 'mp')
- down_copy: bfloat16 [8192, 2048], P('mp', 'dp')
Inputs may be any that keep to these rules, and one draw needn't show every extreme that they name: `lengths`: some slot holds a sequence of exactly 2048 tokens and another one of exactly 1024. offsets[s] + lengths[s] <= 2048 for every slot; the slot of 1024 tokens has its sequence at the slot's end.
All inputs are finite; a program needn't handle non-finite values.
Results may differ from a plain program's by a relative error of at most 0.009.
The roundings to bfloat16 on the way count: a program that leaves them out, or rounds other values in their place, can miss the bound.
Values may be sent and summed in bfloat16 or wider, within the bound.
A program may use at most 384 MiB of HBM per device.

v0:
```python
import jax
import jax.numpy as jnp
from jax import lax
from jax.sharding import PartitionSpec as P

D = 2048
HEAD_DIM = 128
FF = 8192
BLOCK = 512
OUT_FAN = 7


NORM_EPSILON = 1e-05
ADAM_EPSILON = 1e-08
BETA_FIRST = 0.9
BETA_SECOND = 0.999
MATRIX_DECAY = 0.1
SMALL_RATE = 0.2
MASK_FILL = -1e30


def layer_norm_parts(rows, gain, shift):
    center = rows - jnp.mean(rows, axis=-1, keepdims=True)
    inverse = lax.rsqrt(jnp.mean(center * center, axis=-1, keepdims=True) + NORM_EPSILON)
    normed = center * inverse
    return (normed * gain + shift, normed, inverse)


def layer_norm_back(grad_out, normed, inverse, gain):
    scaled = grad_out * gain
    return inverse * (
        scaled
        - jnp.mean(scaled, axis=-1, keepdims=True)
        - normed * jnp.mean(scaled * normed, axis=-1, keepdims=True)
    )


def tanh_gelu(values):
    return jax.nn.gelu(values, approximate=True)


def own_slice(whole, first_row, count):
    return lax.dynamic_slice_in_dim(whole, first_row, count, 0)


def gather_rows(rows):
    return lax.all_gather(rows, "mp", axis=0, tiled=True)


def scatter_rows(terms):
    return lax.psum_scatter(terms, "mp", scatter_dimension=0, tiled=True)


def sum_middle(terms):
    return lax.psum(terms, "mp")


def tile_scores(query_tile, keys, segment, row_block, col_block):
    key_tile = keys[col_block * BLOCK : (col_block + 1) * BLOCK]
    scale = query_tile.shape[2] ** (-0.5)
    scores = (
        jnp.einsum("qhe,khe->hqk", query_tile, key_tile, preferred_element_type=jnp.float32) * scale
    )
    row_place = row_block * BLOCK + jnp.arange(BLOCK)
    key_place = col_block * BLOCK + jnp.arange(BLOCK)
    row_segment = segment[row_block * BLOCK : (row_block + 1) * BLOCK]
    key_segment = segment[col_block * BLOCK : (col_block + 1) * BLOCK]
    allowed = (key_place[None, :] <= row_place[:, None]) & (
        row_segment[:, None] == key_segment[None, :]
    )
    return (jnp.where(allowed[None], scores, MASK_FILL), allowed)


def attention_forward(queries, keys, values, segment):
    count = queries.shape[0] // BLOCK
    heads = queries.shape[1]
    depth = queries.shape[2]
    outputs = []
    totals = []
    for row_block in range(count):
        query_tile = queries[row_block * BLOCK : (row_block + 1) * BLOCK]
        peak = jnp.full((heads, BLOCK), MASK_FILL, jnp.float32)
        mass = jnp.zeros((heads, BLOCK), jnp.float32)
        for col_block in range(row_block + 1):
            scores, allowed = tile_scores(query_tile, keys, segment, row_block, col_block)
            new_peak = jnp.maximum(peak, jnp.max(scores, axis=-1))
            weights = jnp.where(allowed[None], jnp.exp(scores - new_peak[:, :, None]), 0.0)
            mass = mass * jnp.exp(peak - new_peak) + jnp.sum(weights, axis=-1)
            peak = new_peak
        total = peak + jnp.log(mass)
        gathered = jnp.zeros((BLOCK, heads, depth), jnp.float32)
        for col_block in range(row_block + 1):
            scores, allowed = tile_scores(query_tile, keys, segment, row_block, col_block)
            probs = jnp.where(allowed[None], jnp.exp(scores - total[:, :, None]), 0.0).astype(
                jnp.bfloat16
            )
            value_tile = values[col_block * BLOCK : (col_block + 1) * BLOCK]
            gathered = gathered + jnp.einsum(
                "hqk,khe->qhe", probs, value_tile, preferred_element_type=jnp.float32
            )
        outputs.append(gathered.astype(jnp.bfloat16))
        totals.append(total)
    return (jnp.concatenate(outputs, axis=0), jnp.concatenate(totals, axis=1))


def attention_backward(queries, keys, values, segment, totals, grads):
    count = queries.shape[0] // BLOCK
    heads = queries.shape[1]
    depth = queries.shape[2]
    scale = depth ** (-0.5)
    key_grads = [jnp.zeros((BLOCK, heads, depth), jnp.float32) for index in range(count)]
    value_grads = [jnp.zeros((BLOCK, heads, depth), jnp.float32) for index in range(count)]
    query_grads = []
    for row_block in range(count):
        query_tile = queries[row_block * BLOCK : (row_block + 1) * BLOCK]
        grad_tile = grads[row_block * BLOCK : (row_block + 1) * BLOCK]
        total = totals[:, row_block * BLOCK : (row_block + 1) * BLOCK]
        flows = jnp.zeros((heads, BLOCK), jnp.float32)
        for col_block in range(row_block + 1):
            scores, allowed = tile_scores(query_tile, keys, segment, row_block, col_block)
            probs = jnp.where(allowed[None], jnp.exp(scores - total[:, :, None]), 0.0)
            value_tile = values[col_block * BLOCK : (col_block + 1) * BLOCK]
            prob_grad = jnp.einsum(
                "qhe,khe->hqk", grad_tile, value_tile, preferred_element_type=jnp.float32
            )
            flows = flows + jnp.sum(prob_grad * probs, axis=-1)
            value_grads[col_block] = value_grads[col_block] + jnp.einsum(
                "hqk,qhe->khe",
                probs.astype(jnp.bfloat16),
                grad_tile,
                preferred_element_type=jnp.float32,
            )
        query_sum = jnp.zeros((BLOCK, heads, depth), jnp.float32)
        for col_block in range(row_block + 1):
            scores, allowed = tile_scores(query_tile, keys, segment, row_block, col_block)
            probs = jnp.where(allowed[None], jnp.exp(scores - total[:, :, None]), 0.0)
            value_tile = values[col_block * BLOCK : (col_block + 1) * BLOCK]
            key_tile = keys[col_block * BLOCK : (col_block + 1) * BLOCK]
            prob_grad = jnp.einsum(
                "qhe,khe->hqk", grad_tile, value_tile, preferred_element_type=jnp.float32
            )
            score_grad = (probs * (prob_grad - flows[:, :, None])).astype(jnp.bfloat16)
            query_sum = query_sum + scale * jnp.einsum(
                "hqk,khe->qhe", score_grad, key_tile, preferred_element_type=jnp.float32
            )
            key_grads[col_block] = key_grads[col_block] + scale * jnp.einsum(
                "hqk,qhe->khe", score_grad, query_tile, preferred_element_type=jnp.float32
            )
        query_grads.append(query_sum)
    return (
        jnp.concatenate(query_grads, axis=0).astype(jnp.bfloat16),
        jnp.concatenate(key_grads, axis=0).astype(jnp.bfloat16),
        jnp.concatenate(value_grads, axis=0).astype(jnp.bfloat16),
    )


def adam_update(master, grad, first, second, rate, decay, first_fix, second_fix):
    first_next = BETA_FIRST * first + (1.0 - BETA_FIRST) * grad
    second_next = BETA_SECOND * second + (1.0 - BETA_SECOND) * grad * grad
    change = (
        first_next / first_fix / (jnp.sqrt(second_next / second_fix) + ADAM_EPSILON)
        + decay * master
    )
    return (master - rate * change, first_next, second_next)


def per_device(
    layer_input,
    cotangent,
    lengths,
    offsets,
    step,
    mix_weight,
    out_weight,
    up_weight,
    down_weight,
    mix_first,
    out_first,
    up_first,
    down_first,
    mix_second,
    out_second,
    up_second,
    down_second,
    mix_bias,
    up_bias,
    norm_gains,
    shifts,
    mix_bias_first,
    up_bias_first,
    gains_first,
    shifts_first,
    mix_bias_second,
    up_bias_second,
    gains_second,
    shifts_second,
):
    own_rows = layer_input.shape[0]
    parts = lax.axis_size("mp")
    group_rows = own_rows * parts
    slots_here = lengths.shape[0]
    slot_len = group_rows // slots_here
    local_width = mix_weight.shape[2]
    depth = HEAD_DIM
    heads_here = local_width // depth
    positions = jnp.arange(slot_len, dtype=jnp.int32)
    live = (positions[None, :] >= offsets[:, None]) & (
        positions[None, :] < (offsets + lengths)[:, None]
    )
    segment = live.astype(jnp.int32)
    first_row = lax.axis_index("mp") * own_rows
    own_live = own_slice(live.reshape(-1), first_row, own_rows)[:, None]
    mix_low = mix_weight.astype(jnp.bfloat16)
    out_low = out_weight.astype(jnp.bfloat16)
    up_low = up_weight.astype(jnp.bfloat16)
    down_low = down_weight.astype(jnp.bfloat16)
    mix_full, out_full, up_full, down_full = (
        lax.all_gather(mix_low, "dp", axis=1, tiled=True),
        lax.all_gather(out_low, "dp", axis=1, tiled=True),
        lax.all_gather(up_low, "dp", axis=0, tiled=True),
        lax.all_gather(down_low, "dp", axis=1, tiled=True),
    )
    full_rows = gather_rows(layer_input).astype(jnp.float32)
    normed_full, hat_full, inv_full = layer_norm_parts(full_rows, norm_gains[0], shifts[0])
    normed_one = normed_full.astype(jnp.bfloat16)
    hat_one = own_slice(hat_full, first_row, own_rows)
    inv_one = own_slice(inv_full, first_row, own_rows)
    mixed = jnp.einsum("td,cde->cte", normed_one, mix_full, preferred_element_type=jnp.float32)
    queries = (
        (mixed[0] + mix_bias[0])
        .astype(jnp.bfloat16)
        .reshape(slots_here, slot_len, heads_here, depth)
    )
    keys = mixed[1].astype(jnp.bfloat16).reshape(slots_here, slot_len, heads_here, depth)
    values = (
        (mixed[2] + mix_bias[1])
        .astype(jnp.bfloat16)
        .reshape(slots_here, slot_len, heads_here, depth)
    )

    def attend(item):
        return attention_forward(item[0], item[1], item[2], item[3])

    attended, totals = lax.map(attend, (queries, keys, values, segment))
    attended_flat = attended.reshape(group_rows, local_width)
    attn_part = jnp.dot(attended_flat, out_full, preferred_element_type=jnp.float32)
    resid_full = full_rows + sum_middle(attn_part) + shifts[1]
    normed_mid, hat_two, inv_two = layer_norm_parts(resid_full, norm_gains[1], shifts[2])
    normed_two = normed_mid.astype(jnp.bfloat16)
    resid_own = own_slice(resid_full, first_row, own_rows)
    hidden = jnp.dot(normed_two, up_full, preferred_element_type=jnp.float32) + up_bias
    active_value, gelu_pull = jax.vjp(tanh_gelu, hidden)
    active = active_value.astype(jnp.bfloat16)
    down_part = jnp.dot(active, down_full, preferred_element_type=jnp.float32)
    result_own = resid_own + scatter_rows(down_part) + shifts[3]
    layer_output = jnp.where(own_live, result_own, 0.0).astype(jnp.bfloat16)
    out_grad = jnp.where(own_live, cotangent.astype(jnp.float32), 0.0)
    bias_down_grad = jnp.sum(out_grad, axis=0)
    branch_grad = gather_rows(out_grad.astype(jnp.bfloat16))
    active_grad = jnp.einsum(
        "td,fd->tf", branch_grad, down_full, preferred_element_type=jnp.float32
    )
    down_grad = jnp.einsum("tf,td->fd", active, branch_grad, preferred_element_type=jnp.float32)
    hidden_grad = gelu_pull(active_grad)[0].astype(jnp.bfloat16)
    up_bias_grad = jnp.sum(hidden_grad, axis=0, dtype=jnp.float32)
    up_grad = jnp.einsum("td,tf->df", normed_two, hidden_grad, preferred_element_type=jnp.float32)
    two_part = jnp.einsum("tf,df->td", hidden_grad, up_full, preferred_element_type=jnp.float32)
    two_full = sum_middle(two_part)
    resid_grad_full = branch_grad.astype(jnp.float32) + layer_norm_back(
        two_full, hat_two, inv_two, norm_gains[1]
    )
    attn_branch = resid_grad_full.astype(jnp.bfloat16)
    two_grad = own_slice(two_full, first_row, own_rows)
    hat_two_own = own_slice(hat_two, first_row, own_rows)
    resid_grad = own_slice(resid_grad_full, first_row, own_rows)
    gain_two_grad = jnp.sum(two_grad * hat_two_own, axis=0)
    shift_two_grad = jnp.sum(two_grad, axis=0)
    bias_out_grad = jnp.sum(resid_grad, axis=0)
    attended_grad = jnp.einsum(
        "td,ed->te", attn_branch, out_full, preferred_element_type=jnp.float32
    ).astype(jnp.bfloat16)
    out_weight_grad = jnp.einsum(
        "te,td->ed", attended_flat, attn_branch, preferred_element_type=jnp.float32
    )

    def attend_back(item):
        return attention_backward(item[0], item[1], item[2], item[3], item[4], item[5])

    query_grad, key_grad, value_grad = lax.map(
        attend_back,
        (
            queries,
            keys,
            values,
            segment,
            totals,
            attended_grad.reshape(slots_here, slot_len, heads_here, depth),
        ),
    )
    stacked = jnp.stack(
        [
            query_grad.reshape(group_rows, local_width),
            key_grad.reshape(group_rows, local_width),
            value_grad.reshape(group_rows, local_width),
        ]
    )
    mix_grad = jnp.einsum("td,cte->cde", normed_one, stacked, preferred_element_type=jnp.float32)
    mix_bias_grad = jnp.stack(
        [
            jnp.sum(stacked[0], axis=0, dtype=jnp.float32),
            jnp.sum(stacked[2], axis=0, dtype=jnp.float32),
        ]
    )
    one_part = jnp.einsum("cte,cde->td", stacked, mix_full, preferred_element_type=jnp.float32)
    mix_owned, out_owned, up_owned, down_owned = (
        lax.psum_scatter(mix_grad, "dp", scatter_dimension=1, tiled=True),
        lax.psum_scatter(out_weight_grad, "dp", scatter_dimension=1, tiled=True),
        lax.psum_scatter(up_grad, "dp", scatter_dimension=0, tiled=True),
        lax.psum_scatter(down_grad, "dp", scatter_dimension=1, tiled=True),
    )
    one_grad = scatter_rows(one_part)
    input_grad = resid_grad + layer_norm_back(one_grad, hat_one, inv_one, norm_gains[0])
    gain_one_grad = jnp.sum(one_grad * hat_one, axis=0)
    shift_one_grad = jnp.sum(one_grad, axis=0)
    gain_grad = jnp.stack([gain_one_grad, gain_two_grad])
    shift_grad = jnp.stack([shift_one_grad, bias_out_grad, shift_two_grad, bias_down_grad])
    gain_group, shift_group = lax.psum((gain_grad, shift_grad), "mp")
    mix_bias_total, up_bias_total, gain_total, shift_total = lax.psum(
        (mix_bias_grad, up_bias_grad, gain_group, shift_group), "dp"
    )
    step_count = step[0].astype(jnp.float32)
    first_fix = 1.0 - BETA_FIRST**step_count
    second_fix = 1.0 - BETA_SECOND**step_count
    mix_new = adam_update(
        mix_weight,
        mix_owned,
        mix_first,
        mix_second,
        D ** (-0.5),
        MATRIX_DECAY,
        first_fix,
        second_fix,
    )
    out_new = adam_update(
        out_weight,
        out_owned,
        out_first,
        out_second,
        OUT_FAN ** (-0.5),
        MATRIX_DECAY,
        first_fix,
        second_fix,
    )
    up_new = adam_update(
        up_weight, up_owned, up_first, up_second, D ** (-0.5), MATRIX_DECAY, first_fix, second_fix
    )
    down_new = adam_update(
        down_weight,
        down_owned,
        down_first,
        down_second,
        FF ** (-0.5),
        MATRIX_DECAY,
        first_fix,
        second_fix,
    )
    mix_bias_new = adam_update(
        mix_bias,
        mix_bias_total,
        mix_bias_first,
        mix_bias_second,
        SMALL_RATE,
        0.0,
        first_fix,
        second_fix,
    )
    up_bias_new = adam_update(
        up_bias,
        up_bias_total,
        up_bias_first,
        up_bias_second,
        SMALL_RATE,
        0.0,
        first_fix,
        second_fix,
    )
    gains_new = adam_update(
        norm_gains, gain_total, gains_first, gains_second, SMALL_RATE, 0.0, first_fix, second_fix
    )
    shifts_new = adam_update(
        shifts, shift_total, shifts_first, shifts_second, SMALL_RATE, 0.0, first_fix, second_fix
    )
    return (
        layer_output,
        input_grad,
        mix_new[0],
        mix_new[1],
        mix_new[2],
        out_new[0],
        out_new[1],
        out_new[2],
        up_new[0],
        up_new[1],
        up_new[2],
        down_new[0],
        down_new[1],
        down_new[2],
        mix_bias_new[0],
        mix_bias_new[1],
        mix_bias_new[2],
        up_bias_new[0],
        up_bias_new[1],
        up_bias_new[2],
        gains_new[0],
        gains_new[1],
        gains_new[2],
        shifts_new[0],
        shifts_new[1],
        shifts_new[2],
        mix_owned,
        out_owned,
        up_owned,
        down_owned,
        mix_bias_total,
        up_bias_total,
        gain_total,
        shift_total,
        mix_new[0].astype(jnp.bfloat16),
        out_new[0].astype(jnp.bfloat16),
        up_new[0].astype(jnp.bfloat16),
        down_new[0].astype(jnp.bfloat16),
    )


def solution(mesh):
    placed = (
        P(("dp", "mp"), None),
        P(("dp", "mp"), None),
        P("dp"),
        P("dp"),
        P(),
        P(None, "dp", "mp"),
        P("mp", "dp"),
        P("dp", "mp"),
        P("mp", "dp"),
        P(None, "dp", "mp"),
        P("mp", "dp"),
        P("dp", "mp"),
        P("mp", "dp"),
        P(None, "dp", "mp"),
        P("mp", "dp"),
        P("dp", "mp"),
        P("mp", "dp"),
        P(None, "mp"),
        P("mp"),
        P(),
        P(),
        P(None, "mp"),
        P("mp"),
        P(),
        P(),
        P(None, "mp"),
        P("mp"),
        P(),
        P(),
    )
    return jax.shard_map(
        per_device,
        mesh=mesh,
        in_specs=placed,
        out_specs=(
            P(("dp", "mp"), None),
            P(("dp", "mp"), None),
            P(None, "dp", "mp"),
            P(None, "dp", "mp"),
            P(None, "dp", "mp"),
            P("mp", "dp"),
            P("mp", "dp"),
            P("mp", "dp"),
            P("dp", "mp"),
            P("dp", "mp"),
            P("dp", "mp"),
            P("mp", "dp"),
            P("mp", "dp"),
            P("mp", "dp"),
            P(None, "mp"),
            P(None, "mp"),
            P(None, "mp"),
            P("mp"),
            P("mp"),
            P("mp"),
            P(),
            P(),
            P(),
            P(),
            P(),
            P(),
            P(None, "dp", "mp"),
            P("mp", "dp"),
            P("dp", "mp"),
            P("mp", "dp"),
            P(None, "mp"),
            P("mp"),
            P(),
            P(),
            P(None, "dp", "mp"),
            P("mp", "dp"),
            P("dp", "mp"),
            P("mp", "dp"),
        ),
        check_vma=False,
    )
```

profile of v0, /device:TPU:0, one launch (start us, length us, event | category | flops | bytes accessed | tf_op | source)
XLA Modules:
  0.0 1818.8 jit_solution(7182103038282821882)
XLA Ops:
  14.2 2.5 compare_and_fusion.5
  16.8 77.7 %all-gather.7.cloned.1.call-done = bf16[2048,2048]{1,0:T(8,128)(2,1)} async-done(((bf16[256,2048]{1,0:T(8,128)(2,1)}), bf16[2048,2048]{1,0:T(8,128)(2,1)}) %all-gather.7.cloned.1.call-update) | async-done | bytes 8388624 | tf_op jit(solution)/shard_map/all_gather | solution.py:47
  94.4 4.7 convert_reduce_fusion
  103.1 36.1 %all-gather.9.cloned.1.call-done = bf16[3,2048,256]{1,2,0:T(8,128)(2,1)} async-done(((bf16[3,512,256]{1,2,0:T(8,128)(2,1)}), bf16[3,2048,256]{1,2,0:T(8,128)(2,1)}) %all-gather.9.cloned.1.call-update) | async-done | bytes 3145744 | tf_op jit(solution)/shard_map/all_gather | solution.py:218
  139.2 10.7 fusion.156
  169.1 9.8 fusion.167
  183.8 328.2 %all-reduce.5.cloned.1.call-done = f32[2048,2048]{1,0:T(8,128)} async-done(((f32[2048,2048]{1,0:T(8,128)}), f32[2048,2048]{1,0:T(8,128)}) %all-reduce.5.cloned.1.call-update) | async-done | bytes 16777232 | tf_op jit(solution)/shard_map/psum | solution.py:55
  512.0 21.6 %fusion.142 = (f32[2048]{0:T(1024)S(1)}, f32[2048,2048]{1,0:T(8,128)}, f32[2048,2048]{1,0:T(8,128)}) fusion(f32[2048]{0:T(1024)S(1)} %bitcast.355, f32[2048,2048]{1,0:T(8,128)} %all-reduce.5.cloned.1.call-done, bf16[2048,2048]{1,0:T(8,128)(2,1)} %all-gather.7.cloned.1.call-done, f32[2048]{0:T(1024)} %add_rsqrt_fusion.1, f32[2048]{0:T(1024)S(1)} %broadcast_multiply_fusion.3), kind=kLoop, calls=%fused_computation.277 | loop fusion | flops 25163776 | bytes 58753024 | tf_op jit(solution)/shard_map/reduce_sum | solution.py:23
  533.6 7.6 multiply_reduce_fusion.1
  541.1 12.5 subtract_multiply_fusion
  553.6 13.5 all-gather.13.cloned.1.call-done
  567.1 15.6 fusion.20
  582.7 68.5 %all-gather.17.cloned.1.call-done = bf16[2048,2048]{1,0:T(8,128)(2,1)} async-done(((bf16[256,2048]{1,0:T(8,128)(2,1)}), bf16[2048,2048]{1,0:T(8,128)(2,1)}) %all-gather.17.cloned.1.call-update) | async-done | bytes 8388624 | tf_op jit(solution)/shard_map/all_gather | solution.py:47
  651.2 18.7 %fusion.125 = f32[1024,2048]{1,0:T(8,128)} fusion(bf16[2048,2048]{1,0:T(8,128)(2,1)} %all-gather.17.cloned.1.call-done, f32[2048,1024]{1,0:T(8,128)} %fusion.20, f32[1024]{0:T(1024)S(1)} %copy-done.175), kind=kOutput, calls=%fused_computation.271 | convolution fusion | flops 8610906112 | bytes 25169920 | tf_op jit(solution)/shard_map/tf,td->fd/dot_general | solution.py:263
  670.9 84.2 %reduce-scatter.17.cloned.1.call-done = f32[1024,512]{1,0:T(8,128)} async-done(((f32[1024,2048]{1,0:T(8,128)}), f32[1024,512]{1,0:T(8,128)}) %reduce-scatter.17.cloned.1.call-update) | async-done | bytes 2097168 | tf_op jit(solution)/shard_map/reduce_scatter | solution.py:319
  755.0 7.5 fusion.129
  762.6 52.7 %all-gather.15.cloned.1.call-done = bf16[1024,2048]{1,0:T(8,128)(2,1)} async-done(((bf16[1024,512]{1,0:T(8,128)(2,1)}), bf16[1024,2048]{1,0:T(8,128)(2,1)}) %all-gather.15.cloned.1.call-update) | async-done | bytes 4194320 | tf_op jit(solution)/shard_map/all_gather | solution.py:221
  815.3 21.0 %convert_reduce_fusion.1 = (f32[1024]{0:T(1024)}, bf16[2048,1024]{1,0:T(8,128)(2,1)S(1)}) fusion(f32[2048,1024]{1,0:T(8,128)} %fusion.20, f32[1024]{0:T(1024)S(1)} %copy-done.175, bf16[2048,2048]{1,0:T(8,128)(2,1)} %all-gather.17.cloned.1.call-done, bf16[1024,2048]{1,0:T(8,128)(2,1)} %all-gather.15.cloned.1.call-done), kind=kOutput, calls=%fused_computation.25 | convolution fusion | flops 8638168064 | bytes 25174016 | tf_op jit(solution)/shard_map/td,fd->tf/dot_general | solution.py:260
  838.2 11.8 fusion.168
  850.0 332.9 %all-reduce.7.cloned.1.call-done = f32[2048,2048]{1,0:T(8,128)} async-done(((f32[2048,2048]{1,0:T(8,128)}), f32[2048,2048]{1,0:T(8,128)}) %all-reduce.7.cloned.1.call-update) | async-done | bytes 16777232 | tf_op jit(solution)/shard_map/psum | solution.py:55
  1182.9 12.3 multiply_reduce_fusion.2
  1195.3 14.9 multiply_add_fusion
  1210.2 5.8 copy-done
  1216.0 3.7 fusion.12
  1219.8 15.8 fusion.19
  1236.8 8.3 fusion.16
  1271.6 2.9 multiply_reduce_fusion.8
  1274.5 3.6 multiply_convert_fusion.4
  1283.6 3.0 multiply_reduce_fusion.11
  1286.6 3.2 multiply_convert_fusion.7
  1296.1 3.4 multiply_reduce_fusion.13
  1321.7 14.2 convolution_bitcast_fusion.1
  1336.6 16.8 fusion.126
  1354.9 16.1 convolution_bitcast_fusion
  1373.1 3.0 copy.161
  1377.0 2.7 dynamic-slice_reduce_fusion
  1380.2 3.0 fusion.133
  1383.2 8.2 fusion.131
  1391.4 27.2 %reduce-scatter.11.cloned.1.call-done = f32[3,512,256]{1,2,0:T(8,128)} async-done(((f32[3,2048,256]{1,2,0:T(8,128)}), f32[3,512,256]{1,2,0:T(8,128)}) %reduce-scatter.11.cloned.1.call-update) | async-done | bytes 1572880 | tf_op jit(solution)/shard_map/reduce_scatter | solution.py:316
  1418.6 5.2 fusion.135
  1423.8 3.1 copy.166
  1434.4 154.9 %reduce-scatter.7.cloned.1.call-done = f32[256,2048]{1,0:T(8,128)} async-done(((f32[2048,2048]{1,0:T(8,128)}), f32[256,2048]{1,0:T(8,128)}) %reduce-scatter.7.cloned.1.call-update) | async-done | bytes 2097168 | tf_op jit(solution)/shard_map/reduce_scatter | solution.py:51
  1589.3 3.5 select_convert_fusion
  1592.8 165.5 %reduce-scatter.9.cloned.1.call-done = f32[256,2048]{1,0:T(8,128)} async-done(((f32[2048,2048]{1,0:T(8,128)}), f32[256,2048]{1,0:T(8,128)}) %reduce-scatter.9.cloned.1.call-update) | async-done | bytes 2097168 | tf_op jit(solution)/shard_map/reduce_scatter | solution.py:51
  1758.3 3.1 multiply_reduce_fusion.4
  1761.6 4.2 dynamic-slice_reduce_fusion.1
  1765.9 26.4 %all-reduce = (f32[2,2048]{1,0:T(2,128)S(1)}, f32[4,2048]{1,0:T(4,128)S(1)}) all-reduce(f32[2,2048]{1,0:T(2,128)S(1)} %pad_maximum_fusion.2, f32[4,2048]{1,0:T(4,128)S(1)} %pad_maximum_fusion.1), channel_id=1, replica_groups=mesh['dp'=4,'mp'=8] {'mp'}, use_global_device_ids=true, to_apply=%region_53.54 | all-reduce | flops 12288 | bytes 98304 | tf_op jit(solution)/shard_map/psum | solution.py:327
  1792.3 17.0 all-reduce.1
  (535 shorter events, 111.6 us)
Async XLA Ops:
  7.2 87.2 %all-gather.7.cloned.1.call-start = ((), (), s32[]{:S(2)}) async-start(), calls=%async_computation.6 | async-start | bytes 9437184 | tf_op jit(solution)/shard_map/all_gather | solution.py:47
  8.0 131.3 %all-gather.9.cloned.1.call-start = ((), (), s32[]{:S(2)}) async-start(), calls=%async_computation.7 | async-start | bytes 3932160 | tf_op jit(solution)/shard_map/all_gather | solution.py:218
  10.9 158.2 %all-gather.11.cloned.1.call-start = ((), (), s32[]{:S(2)}) async-start(), calls=%async_computation.8 | async-start | bytes 1310720 | tf_op jit(solution)/shard_map/all_gather | solution.py:219
  12.1 499.9 %all-reduce.5.cloned.1.call-start = ((), (), s32[]{:S(2)}) async-start(), calls=%async_computation.9 | async-start | bytes 33554432 | tf_op jit(solution)/shard_map/psum | solution.py:55
  14.1 125.2 %copy-start.170 = (f32[1,2048]{1,0:T(1,128)}, f32[1,2048]{1,0:T(1,128)S(1)}, u32[]{:S(2)}) copy-start(f32[1,2048]{1,0:T(1,128)S(1)} %get-tuple-element.214) | copy-start | bytes 24580
  14.1 125.1 %copy-start.152 = (f32[1,2048]{1,0:T(1,128)}, f32[1,2048]{1,0:T(1,128)S(1)}, u32[]{:S(2)}) copy-start(f32[1,2048]{1,0:T(1,128)S(1)} %get-tuple-element.216) | copy-start | bytes 24580
  16.6 140.4 %copy-start.42 = (pred[512,512]{0,1:T(8,128)(4,1)}, pred[512,512]{0,1:T(8,128)(4,1)S(1)}, u32[]{:S(2)}) copy-start(pred[512,512]{0,1:T(8,128)(4,1)S(1)} %get-tuple-element.238) | copy-start | bytes 786436
  16.7 142.4 %copy-start.50 = (pred[512,512]{0,1:T(8,128)(4,1)}, pred[512,512]{0,1:T(8,128)(4,1)S(1)}, u32[]{:S(2)}) copy-start(pred[512,512]{0,1:T(8,128)(4,1)S(1)} %get-tuple-element.237) | copy-start | bytes 786436
  16.7 145.3 %copy-start.58 = (pred[512,512]{0,1:T(8,128)(4,1)}, pred[512,512]{0,1:T(8,128)(4,1)S(1)}, u32[]{:S(2)}) copy-start(pred[512,512]{0,1:T(8,128)(4,1)S(1)} %get-tuple-element.239) | copy-start | bytes 786436
  16.7 146.0 %copy-start.47 = (pred[512,512]{0,1:T(8,128)(4,1)}, pred[512,512]{0,1:T(8,128)(4,1)S(1)}, u32[]{:S(2)}) copy-start(pred[512,512]{0,1:T(8,128)(4,1)S(1)} %get-tuple-element.235) | copy-start | bytes 786436
  16.7 146.6 %copy-start.61 = (pred[512,512]{0,1:T(8,128)(4,1)}, pred[512,512]{0,1:T(8,128)(4,1)S(1)}, u32[]{:S(2)}) copy-start(pred[512,512]{0,1:T(8,128)(4,1)S(1)} %get-tuple-element.232) | copy-start | bytes 786436
  16.7 148.7 %copy-start.94 = (pred[512,512]{0,1:T(8,128)(4,1)}, pred[512,512]{0,1:T(8,128)(4,1)S(1)}, u32[]{:S(2)}) copy-start(pred[512,512]{0,1:T(8,128)(4,1)S(1)} %get-tuple-element.243) | copy-start | bytes 786436
  16.7 149.5 %copy-start.53 = (pred[512,512]{0,1:T(8,128)(4,1)}, pred[512,512]{0,1:T(8,128)(4,1)S(1)}, u32[]{:S(2)}) copy-start(pred[512,512]{0,1:T(8,128)(4,1)S(1)} %get-tuple-element.236) | copy-start | bytes 786436
  16.7 150.2 %copy-start.38 = (pred[512,512]{0,1:T(8,128)(4,1)}, pred[512,512]{0,1:T(8,128)(4,1)S(1)}, u32[]{:S(2)}) copy-start(pred[512,512]{0,1:T(8,128)(4,1)S(1)} %get-tuple-element.233) | copy-start | bytes 786436
  16.7 150.9 %copy-start.40 = (pred[512,512]{0,1:T(8,128)(4,1)}, pred[512,512]{0,1:T(8,128)(4,1)S(1)}, u32[]{:S(2)}) copy-start(pred[512,512]{0,1:T(8,128)(4,1)S(1)} %get-tuple-element.234) | copy-start | bytes 786436
  16.7 151.5 %copy-start.69 = (pred[512,512]{0,1:T(8,128)(4,1)}, pred[512,512]{0,1:T(8,128)(4,1)S(1)}, u32[]{:S(2)}) copy-start(pred[512,512]{0,1:T(8,128)(4,1)S(1)} %get-tuple-element.240) | copy-start | bytes 786436
  100.2 411.8 %copy-start.154 = (f32[2048]{0:T(1024)}, f32[2048]{0:T(1024)S(1)}, u32[]{:S(2)}) copy-start(f32[2048]{0:T(1024)S(1)} %broadcast_multiply_fusion.3) | copy-start | bytes 24580
  150.7 17.0 copy-start.98
  150.7 17.6 copy-start.114
  179.0 388.1 %all-gather.13.cloned.1.call-start = ((), (), s32[]{:S(2)}) async-start(), calls=%async_computation.10 | async-start | bytes 5242880 | tf_op jit(solution)/shard_map/all_gather | solution.py:220
  181.7 469.5 %all-gather.17.cloned.1.call-start = ((), (), s32[]{:S(2)}) async-start(), calls=%async_computation.13 | async-start | bytes 9437184 | tf_op jit(solution)/shard_map/all_gather | solution.py:47
  183.7 571.3 %reduce-scatter.17.cloned.1.call-start = ((), (), s32[]{:S(2)}) async-start(), calls=%async_computation.19 | async-start | bytes 10485760 | tf_op jit(solution)/shard_map/reduce_scatter | solution.py:319
  567.1 84.1 %copy-start.175 = (f32[1024]{0:T(1024)S(1)}, f32[1024]{0:T(1024)}, u32[]{:S(2)}) copy-start(f32[1024]{0:T(1024)} %param.47) | copy-start | bytes 12292
  669.9 85.1 %copy-start.126 = (f32[1024,512]{1,0:T(8,128)S(1)}, f32[1024,512]{1,0:T(8,128)}, u32[]{:S(2)}) copy-start(f32[1024,512]{1,0:T(8,128)} %param.37) | copy-start | bytes 6291460
  670.0 145.3 %all-gather.15.cloned.1.call-start = ((), (), s32[]{:S(2)}) async-start(), calls=%async_computation.11 | async-start | bytes 5242880 | tf_op jit(solution)/shard_map/all_gather | solution.py:221
  762.5 420.4 %all-reduce.7.cloned.1.call-start = ((), (), s32[]{:S(2)}) async-start(), calls=%async_computation.14 | async-start | bytes 33554432 | tf_op jit(solution)/shard_map/psum | solution.py:55
  815.3 22.9 %copy-start.183 = (bf16[2048,1024]{1,0:T(8,128)(2,1)S(1)}, bf16[2048,1024]{1,0:T(8,128)(2,1)}, u32[]{:S(2)}) copy-start(bf16[2048,1024]{1,0:T(8,128)(2,1)} %all-gather.13.cloned.1.call-done) | copy-start | bytes 12582916
  850.0 530.3 %reduce-scatter.13.cloned.1.call-start = ((), (), s32[]{:S(2)}) async-start(), calls=%async_computation.17 | async-start | bytes 2621440 | tf_op jit(solution)/shard_map/reduce_scatter | solution.py:317
  1195.3 20.8 %copy-start.73 = (bf16[2048,2,128]{0,2,1:T(8,128)(2,1)S(1)}, bf16[2048,2,128]{0,2,1:T(8,128)(2,1)}, u32[]{:S(2)}) copy-start(bf16[2048,2,128]{0,2,1:T(8,128)(2,1)} %copy-done.72) | copy-start | bytes 3145732
  1219.7 163.5 %reduce-scatter.15.cloned.1.call-start = ((), (), s32[]{:S(2)}) async-start(), calls=%async_computation.18 | async-start | bytes 10485760 | tf_op jit(solution)/shard_map/reduce_scatter | solution.py:318
  1235.6 183.0 %reduce-scatter.11.cloned.1.call-start = ((), (), s32[]{:S(2)}) async-start(), calls=%async_computation.16 | async-start | bytes 7864320 | tf_op jit(solution)/shard_map/reduce_scatter | solution.py:316
  1336.0 253.4 %reduce-scatter.7.cloned.1.call-start = ((), (), s32[]{:S(2)}) async-start(), calls=%async_computation.12 | async-start | bytes 18874368 | tf_op jit(solution)/shard_map/reduce_scatter | solution.py:51
  1353.5 404.8 %reduce-scatter.9.cloned.1.call-start = ((), (), s32[]{:S(2)}) async-start(), calls=%async_computation.15 | async-start | bytes 18874368 | tf_op jit(solution)/shard_map/reduce_scatter | solution.py:51
  1383.2 35.4 %copy-start.37 = (f32[3,512,256]{1,2,0:T(8,128)S(1)}, f32[3,512,256]{1,2,0:T(8,128)}, u32[]{:S(2)}) copy-start(f32[3,512,256]{1,2,0:T(8,128)} %copy-done.36) | copy-start | bytes 4718596
  1430.5 158.8 %copy-start.160 = (f32[1,2048]{1,0:T(1,128)S(1)}, f32[1,2048]{1,0:T(1,128)}, u32[]{:S(2)}) copy-start(f32[1,2048]{1,0:T(1,128)} %get-tuple-element.211) | copy-start | bytes 24580
  1430.5 158.8 %copy-start.173 = (pred[256]{0:T(512)(128)(4,1)S(1)}, pred[256]{0:T(512)(128)(4,1)}, u32[]{:S(2)}) copy-start(pred[256]{0:T(512)(128)(4,1)} %copy-done.172) | copy-start | bytes 772
  1761.5 30.8 %copy-start.174 = (f32[1024]{0:T(1024)S(1)}, f32[1024]{0:T(1024)}, u32[]{:S(2)}) copy-start(f32[1024]{0:T(1024)} %get-tuple-element.178) | copy-start | bytes 12292
  1761.5 47.9 %copy-start.169 = (f32[2,256]{1,0:T(2,128)S(1)}, f32[2,256]{1,0:T(2,128)}, u32[]{:S(2)}) copy-start(f32[2,256]{1,0:T(2,128)} %param.46) | copy-start | bytes 6148
  1761.5 47.9 %copy-start.180 = (f32[2,256]{1,0:T(2,128)S(1)}, f32[2,256]{1,0:T(2,128)}, u32[]{:S(2)}) copy-start(f32[2,256]{1,0:T(2,128)} %param.54) | copy-start | bytes 6148
  1761.5 47.9 %copy-start.181 = (f32[2,256]{1,0:T(2,128)S(1)}, f32[2,256]{1,0:T(2,128)}, u32[]{:S(2)}) copy-start(f32[2,256]{1,0:T(2,128)} %param.50) | copy-start | bytes 6148
  1761.5 48.5 %copy-start.177 = (f32[1024]{0:T(1024)S(1)}, f32[1024]{0:T(1024)}, u32[]{:S(2)}) copy-start(f32[1024]{0:T(1024)} %param.55) | copy-start | bytes 12292
  1761.5 48.5 %copy-start.178 = (f32[1024]{0:T(1024)S(1)}, f32[1024]{0:T(1024)}, u32[]{:S(2)}) copy-start(f32[1024]{0:T(1024)} %param.51) | copy-start | bytes 12292
  1761.5 49.1 %copy-start.157 = (f32[2,2048]{1,0:T(2,128)S(1)}, f32[2,2048]{1,0:T(2,128)}, u32[]{:S(2)}) copy-start(f32[2,2048]{1,0:T(2,128)} %param.48) | copy-start | bytes 49156
  1761.6 49.1 %copy-start.165 = (f32[2,2048]{1,0:T(2,128)S(1)}, f32[2,2048]{1,0:T(2,128)}, u32[]{:S(2)}) copy-start(f32[2,2048]{1,0:T(2,128)} %param.56) | copy-start | bytes 49156
  1761.6 49.1 %copy-start.166 = (f32[2,2048]{1,0:T(2,128)S(1)}, f32[2,2048]{1,0:T(2,128)}, u32[]{:S(2)}) copy-start(f32[2,2048]{1,0:T(2,128)} %param.52) | copy-start | bytes 49156
  1761.6 49.7 %copy-start.151 = (f32[4,2048]{1,0:T(4,128)S(1)}, f32[4,2048]{1,0:T(4,128)}, u32[]{:S(2)}) copy-start(f32[4,2048]{1,0:T(4,128)} %param.49) | copy-start | bytes 98308
  1761.6 49.7 %copy-start.162 = (f32[4,2048]{1,0:T(4,128)S(1)}, f32[4,2048]{1,0:T(4,128)}, u32[]{:S(2)}) copy-start(f32[4,2048]{1,0:T(4,128)} %param.57) | copy-start | bytes 98308
  1761.6 49.7 %copy-start.163 = (f32[4,2048]{1,0:T(4,128)S(1)}, f32[4,2048]{1,0:T(4,128)}, u32[]{:S(2)}) copy-start(f32[4,2048]{1,0:T(4,128)} %param.53) | copy-start | bytes 98308
  (151 other events, 553.0 us)
Sparse Core Ops, SparseCore 0:
  9.7 84.7 all-gather.6
  96.8 42.3 all-gather.8
  141.6 26.4 all-gather.10
  179.1 332.8 all-reduce.4
  514.2 52.8 all-gather.12
  569.1 82.0 all-gather.16
  670.1 84.9 reduce-scatter.16
  762.7 52.5 all-gather.14
  850.1 332.8 all-reduce.6
  1219.8 35.2 reduce-scatter.12
  1258.8 86.3 reduce-scatter.14
  1348.3 70.2 reduce-scatter.10
  1421.1 168.1 reduce-scatter.6
  1591.6 166.5 reduce-scatter.8
where the time goes:
time: 1830 us; the launch traced here: 1820 us
  waiting for transfers between devices  1340 us (73%)
  matrix products  213 us (12%)
  other arithmetic  139 us (8%)
  local copies, waits for them, and re-layouts  61.8 us (3%)
  blocking collectives  43.4 us (2%)
  between operations  18.8 us (1%)
    psum x2, waiting for transfers between devices, sum_middle(): return lax.psum(terms, 'mp')  661 us
    reduce_scatter x2, waiting for transfers between devices, scatter_rows(): return lax.psum_scatter(terms, 'mp', scatter_dimension=0, tiled=True)  320 us
    all_gather x2, waiting for transfers between devices, gather_rows(): return lax.all_gather(rows, 'mp', axis=0, tiled=True)  146 us
    reduce_scatter x1, waiting for transfers between devices, per_device(): lax.psum_scatter(down_grad, 'dp', scatter_dimension=1, tiled=True)  84.2 us
    all_gather x1, waiting for transfers between devices, per_device(): lax.all_gather(down_low, 'dp', axis=1, tiled=True)  52.7 us
    unnamed x378, local copies, waits for them, and re-layouts  44.6 us
  transfers between devices with their start and end apart: 14, of which 11 were waited for; matrix products, arithmetic and copies ran while one was open for 15% of the time, Pallas kernels for 0%

commit v1 on v0

--- a/solution.py
+++ b/solution.py
@@ -48,11 +48,53 @@
 
 
 def scatter_rows(terms):
-    return lax.psum_scatter(terms, "mp", scatter_dimension=0, tiled=True)
-
-
-def sum_middle(terms):
-    return lax.psum(terms, "mp")
+    low = terms.astype(jnp.bfloat16)
+    return lax.psum_scatter(low, "mp", scatter_dimension=0, tiled=True).astype(jnp.float32)
+
+
+def swap(value, mask):
+    size = lax.axis_size("dp")
+    return lax.ppermute(value, "dp", [(place, place ^ mask) for place in range(size)])
+
+
+def gather_shards(shard, axis):
+    if lax.axis_size("dp") != 4:
+        return lax.all_gather(shard, "dp", axis=axis, tiled=True)
+    count = shard.shape[axis]
+    me = lax.axis_index("dp")
+    from_x = swap(shard, 1)
+    from_y = swap(shard, 2)
+    half = count // 2
+    low = swap(lax.slice_in_dim(from_x, 0, half, axis=axis), 2)
+    high = swap(lax.slice_in_dim(from_y, half, count, axis=axis), 1)
+    shape = list(shard.shape)
+    shape[axis] = 4 * count
+    full = jnp.zeros(shape, shard.dtype)
+    full = lax.dynamic_update_slice_in_dim(full, shard, me * count, axis)
+    full = lax.dynamic_update_slice_in_dim(full, from_x, (me ^ 1) * count, axis)
+    full = lax.dynamic_update_slice_in_dim(full, from_y, (me ^ 2) * count, axis)
+    full = lax.dynamic_update_slice_in_dim(full, low, (me ^ 3) * count, axis)
+    return lax.dynamic_update_slice_in_dim(full, high, (me ^ 3) * count + half, axis)
+
+
+def scatter_shards(grad, axis):
+    if lax.axis_size("dp") != 4:
+        return lax.psum_scatter(grad, "dp", scatter_dimension=axis, tiled=True)
+    count = grad.shape[axis] // 4
+    half = count // 2
+    me = lax.axis_index("dp")
+
+    def piece(owner, upper):
+        return lax.dynamic_slice_in_dim(grad, owner * count + upper * half, half, axis)
+
+    def one_way(first, second, upper):
+        near = swap(piece(me ^ first, upper).astype(jnp.bfloat16), first)
+        far = swap(piece(me ^ 3, upper).astype(jnp.bfloat16), first)
+        onward = piece(me ^ second, upper) + far.astype(jnp.float32)
+        last = swap(onward.astype(jnp.bfloat16), second)
+        return piece(me, upper) + near.astype(jnp.float32) + last.astype(jnp.float32)
+
+    return lax.concatenate([one_way(1, 2, 0), one_way(2, 1, 1)], axis)
 
 
 def tile_scores(query_tile, keys, segment, row_block, col_block):
@@ -210,21 +252,16 @@
     segment = live.astype(jnp.int32)
     first_row = lax.axis_index("mp") * own_rows
     own_live = own_slice(live.reshape(-1), first_row, own_rows)[:, None]
-    mix_low = mix_weight.astype(jnp.bfloat16)
-    out_low = out_weight.astype(jnp.bfloat16)
-    up_low = up_weight.astype(jnp.bfloat16)
-    down_low = down_weight.astype(jnp.bfloat16)
-    mix_full, out_full, up_full, down_full = (
-        lax.all_gather(mix_low, "dp", axis=1, tiled=True),
-        lax.all_gather(out_low, "dp", axis=1, tiled=True),
-        lax.all_gather(up_low, "dp", axis=0, tiled=True),
-        lax.all_gather(down_low, "dp", axis=1, tiled=True),
-    )
-    full_rows = gather_rows(layer_input).astype(jnp.float32)
-    normed_full, hat_full, inv_full = layer_norm_parts(full_rows, norm_gains[0], shifts[0])
-    normed_one = normed_full.astype(jnp.bfloat16)
-    hat_one = own_slice(hat_full, first_row, own_rows)
-    inv_one = own_slice(inv_full, first_row, own_rows)
+    own_input = layer_input.astype(jnp.float32)
+    normed_own, hat_one, inv_one = layer_norm_parts(own_input, norm_gains[0], shifts[0])
+    normed_one = gather_rows(normed_own.astype(jnp.bfloat16))
+    mix_full = gather_shards(mix_weight.astype(jnp.bfloat16), 1)
+    out_full = gather_shards(out_weight.astype(jnp.bfloat16), 1)
+    up_full = gather_shards(up_weight.astype(jnp.bfloat16), 0)
+    down_full = gather_shards(down_weight.astype(jnp.bfloat16), 1)
+    out_grad = jnp.where(own_live, cotangent.astype(jnp.float32), 0.0)
+    bias_down_grad = jnp.sum(out_grad, axis=0)
+    branch_grad = gather_rows(out_grad.astype(jnp.bfloat16))
     mixed = jnp.einsum("td,cde->cte", normed_one, mix_full, preferred_element_type=jnp.float32)
     queries = (
         (mixed[0] + mix_bias[0])
@@ -244,36 +281,27 @@
     attended, totals = lax.map(attend, (queries, keys, values, segment))
     attended_flat = attended.reshape(group_rows, local_width)
     attn_part = jnp.dot(attended_flat, out_full, preferred_element_type=jnp.float32)
-    resid_full = full_rows + sum_middle(attn_part) + shifts[1]
-    normed_mid, hat_two, inv_two = layer_norm_parts(resid_full, norm_gains[1], shifts[2])
-    normed_two = normed_mid.astype(jnp.bfloat16)
-    resid_own = own_slice(resid_full, first_row, own_rows)
+    resid_own = own_input + scatter_rows(attn_part) + shifts[1]
+    normed_mid, hat_two, inv_two = layer_norm_parts(resid_own, norm_gains[1], shifts[2])
+    normed_two = gather_rows(normed_mid.astype(jnp.bfloat16))
     hidden = jnp.dot(normed_two, up_full, preferred_element_type=jnp.float32) + up_bias
     active_value, gelu_pull = jax.vjp(tanh_gelu, hidden)
     active = active_value.astype(jnp.bfloat16)
+    active_grad = jnp.einsum(
+        "td,fd->tf", branch_grad, down_full, preferred_element_type=jnp.float32
+    )
+    hidden_grad = gelu_pull(active_grad)[0].astype(jnp.bfloat16)
+    two_part = jnp.einsum("tf,df->td", hidden_grad, up_full, preferred_element_type=jnp.float32)
+    two_grad = scatter_rows(two_part)
     down_part = jnp.dot(active, down_full, preferred_element_type=jnp.float32)
+    down_grad = jnp.einsum("tf,td->fd", active, branch_grad, preferred_element_type=jnp.float32)
+    up_bias_grad = jnp.sum(hidden_grad, axis=0, dtype=jnp.float32)
+    up_grad = jnp.einsum("td,tf->df", normed_two, hidden_grad, preferred_element_type=jnp.float32)
+    resid_grad = out_grad + layer_norm_back(two_grad, hat_two, inv_two, norm_gains[1])
+    attn_branch = gather_rows(resid_grad.astype(jnp.bfloat16))
     result_own = resid_own + scatter_rows(down_part) + shifts[3]
     layer_output = jnp.where(own_live, result_own, 0.0).astype(jnp.bfloat16)
-    out_grad = jnp.where(own_live, cotangent.astype(jnp.float32), 0.0)
-    bias_down_grad = jnp.sum(out_grad, axis=0)
-    branch_grad = gather_rows(out_grad.astype(jnp.bfloat16))
-    active_grad = jnp.einsum(
-        "td,fd->tf", branch_grad, down_full, preferred_element_type=jnp.float32
-    )
-    down_grad = jnp.einsum("tf,td->fd", active, branch_grad, preferred_element_type=jnp.float32)
-    hidden_grad = gelu_pull(active_grad)[0].astype(jnp.bfloat16)
-    up_bias_grad = jnp.sum(hidden_grad, axis=0, dtype=jnp.float32)
-    up_grad = jnp.einsum("td,tf->df", normed_two, hidden_grad, preferred_element_type=jnp.float32)
-    two_part = jnp.einsum("tf,df->td", hidden_grad, up_full, preferred_element_type=jnp.float32)
-    two_full = sum_middle(two_part)
-    resid_grad_full = branch_grad.astype(jnp.float32) + layer_norm_back(
-        two_full, hat_two, inv_two, norm_gains[1]
-    )
-    attn_branch = resid_grad_full.astype(jnp.bfloat16)
-    two_grad = own_slice(two_full, first_row, own_rows)
-    hat_two_own = own_slice(hat_two, first_row, own_rows)
-    resid_grad = own_slice(resid_grad_full, first_row, own_rows)
-    gain_two_grad = jnp.sum(two_grad * hat_two_own, axis=0)
+    gain_two_grad = jnp.sum(two_grad * hat_two, axis=0)
     shift_two_grad = jnp.sum(two_grad, axis=0)
     bias_out_grad = jnp.sum(resid_grad, axis=0)
     attended_grad = jnp.einsum(
@@ -304,6 +332,8 @@
             value_grad.reshape(group_rows, local_width),
         ]
     )
+    one_part = jnp.einsum("cte,cde->td", stacked, mix_full, preferred_element_type=jnp.float32)
+    one_grad = scatter_rows(one_part)
     mix_grad = jnp.einsum("td,cte->cde", normed_one, stacked, preferred_element_type=jnp.float32)
     mix_bias_grad = jnp.stack(
         [
@@ -311,23 +341,17 @@
             jnp.sum(stacked[2], axis=0, dtype=jnp.float32),
         ]
     )
-    one_part = jnp.einsum("cte,cde->td", stacked, mix_full, preferred_element_type=jnp.float32)
-    mix_owned, out_owned, up_owned, down_owned = (
-        lax.psum_scatter(mix_grad, "dp", scatter_dimension=1, tiled=True),
-        lax.psum_scatter(out_weight_grad, "dp", scatter_dimension=1, tiled=True),
-        lax.psum_scatter(up_grad, "dp", scatter_dimension=0, tiled=True),
-        lax.psum_scatter(down_grad, "dp", scatter_dimension=1, tiled=True),
-    )
-    one_grad = scatter_rows(one_part)
+    mix_owned = scatter_shards(mix_grad, 1)
+    out_owned = scatter_shards(out_weight_grad, 1)
+    up_owned = scatter_shards(up_grad, 0)
+    down_owned = scatter_shards(down_grad, 1)
     input_grad = resid_grad + layer_norm_back(one_grad, hat_one, inv_one, norm_gains[0])
     gain_one_grad = jnp.sum(one_grad * hat_one, axis=0)
     shift_one_grad = jnp.sum(one_grad, axis=0)
     gain_grad = jnp.stack([gain_one_grad, gain_two_grad])
     shift_grad = jnp.stack([shift_one_grad, bias_out_grad, shift_two_grad, bias_down_grad])
-    gain_group, shift_group = lax.psum((gain_grad, shift_grad), "mp")
-    mix_bias_total, up_bias_total, gain_total, shift_total = lax.psum(
-        (mix_bias_grad, up_bias_grad, gain_group, shift_group), "dp"
-    )
+    mix_bias_total, up_bias_total = lax.psum((mix_bias_grad, up_bias_grad), "dp")
+    gain_total, shift_total = lax.psum((gain_grad, shift_grad), ("dp", "mp"))
     step_count = step[0].astype(jnp.float32)
     first_fix = 1.0 - BETA_FIRST**step_count
     second_fix = 1.0 - BETA_SECOND**step_count

time: 1830 us -> 1080 us (0.59)
  waiting for transfers between devices: 1340 us -> 563 us
  other arithmetic: 139 us -> 83.8 us
  starting transfers between devices: 1.04 us -> 46.6 us
  local copies, waits for them, and re-layouts: 61.8 us -> 83.1 us
    psum x2 -> x0, waiting for transfers between devices: 661 us -> none  [sum_middle(): return lax.psum(terms, 'mp')]
    reduce_scatter x6 -> x4, waiting for transfers between devices: 432 us -> 248 us  [scatter_rows(): lax.psum_scatter(low, 'mp', scatter_dimension=0, tiled=True)]
    ppermute x0 -> x40, waiting for transfers between devices: none -> 121 us  [swap(): lax.ppermute(value, 'dp', [(place, place ^ mask) for place in range(size)])]
    all_gather x4 -> x0, waiting for transfers between devices: 102 us -> none  [the longest x1 52.7 us: per_device(): lax.all_gather(down_low, 'dp', axis=1, tiled=True)]
    all_gather x2 -> x4, waiting for transfers between devices: 146 us -> 193 us  [gather_rows(): return lax.all_gather(rows, 'mp', axis=0, tiled=True)]
    ppermute x0 -> x40, starting transfers between devices: none -> 46.1 us  [swap(): lax.ppermute(value, 'dp', [(place, place ^ mask) for place in range(size)])]
    reduce_sum x2, other arithmetic: 26.3 us -> 3.26 us  [layer_norm_parts(): center = rows - jnp.mean(rows, axis=-1, keepdims=True)]
    unnamed x378 -> x394, local copies, waits for them, and re-layouts: 44.6 us -> 36.6 us
  transfers between devices with their start and end apart: 14 -> 48, of which waited for: 11 -> 27; matrix products, arithmetic and copies ran while one was open for 15% -> 16% of each run, Pallas kernels for 0% -> 0%
where the time goes in v1:
time: 1080 us; the launch traced here: 1070 us
  waiting for transfers between devices  563 us (52%)
  matrix products  219 us (20%)
  other arithmetic  83.8 us (8%)
  local copies, waits for them, and re-layouts  83.1 us (8%)
  blocking collectives  57.8 us (5%)
  starting transfers between devices  46.6 us (4%)
  between operations  19.1 us (2%)
    reduce_scatter x4, waiting for transfers between devices, scatter_rows(): lax.psum_scatter(low, 'mp', scatter_dimension=0, tiled=True)  248 us
    all_gather x4, waiting for transfers between devices, gather_rows(): return lax.all_gather(rows, 'mp', axis=0, tiled=True)  193 us
    ppermute x40, waiting for transfers between devices, swap(): lax.ppermute(value, 'dp', [(place, place ^ mask) for place in range(size)])  121 us
    ppermute x40, starting transfers between devices, swap(): lax.ppermute(value, 'dp', [(place, place ^ mask) for place in range(size)])  46.1 us
    psum x1, blocking collectives, per_device(): gain_total, shift_total = lax.psum((gain_grad, shift_grad), ('dp', 'mp'))  38.3 us
    unnamed x394, local copies, waits for them, and re-layouts  36.6 us
    dot_general x10, matrix products, attention_backward(): jnp.einsum('qhe,khe->hqk', grad_tile, value_tile, preferred_element_type=...  28.4 us
  transfers between devices with their start and end apart: 48, of which 27 were waited for; matrix products, arithmetic and copies ran while one was open for 16% of the time, Pallas kernels for 0%

profile of v1, /device:TPU:0, one launch (start us, length us, event | category | flops | bytes accessed | tf_op | source)
XLA Modules:
  0.0 1072.3 jit_solution(12138211189298562550)
XLA Ops:
  23.3 3.1 compare_and_fusion.5
  34.0 7.8 collective-permute-done
  56.2 41.4 %all-gather.5.cloned.1.call-done = bf16[2048,2048]{1,0:T(8,128)(2,1)} async-done(((bf16[256,2048]{1,0:T(8,128)(2,1)}), bf16[2048,2048]{1,0:T(8,128)(2,1)}) %all-gather.5.cloned.1.call-update) | async-done | bytes 8388624 | tf_op jit(solution)/shard_map/all_gather | solution.py:47
  97.6 10.6 fusion.178
  130.3 5.7 convolution_convert_fusion.2
  136.1 88.3 %reduce-scatter.5.cloned.1.call-done = bf16[256,2048]{1,0:T(8,128)(2,1)} async-done(((bf16[2048,2048]{1,0:T(8,128)(2,1)}), bf16[256,2048]{1,0:T(8,128)(2,1)}) %reduce-scatter.5.cloned.1.call-update) | async-done | bytes 1048592 | tf_op jit(solution)/shard_map/reduce_scatter | solution.py:52
  242.6 18.3 %collective-permute-done.12 = bf16[1024,512]{1,0:T(8,128)(2,1)S(1)} collective-permute-done((bf16[1024,512]{1,0:T(8,128)(2,1)S(1)}, bf16[1024,512]{1,0:T(8,128)(2,1)S(1)}, u32[]{:S(2)}, u32[]{:S(2)}) %collective-permute-start.12) | collective-permute-done | bytes 1048608 | tf_op jit(solution)/shard_map/ppermute | solution.py:57
  263.9 19.4 %collective-permute-done.8 = bf16[512,1024]{1,0:T(8,128)(2,1)S(1)} collective-permute-done((bf16[512,1024]{1,0:T(8,128)(2,1)S(1)}, bf16[512,1024]{1,0:T(8,128)(2,1)S(1)}, u32[]{:S(2)}, u32[]{:S(2)}) %collective-permute-start.8) | collective-permute-done | bytes 1048608 | tf_op jit(solution)/shard_map/ppermute | solution.py:57
  290.7 5.3 collective-permute-done.14
  297.7 5.9 collective-permute-done.10
  305.3 3.6 all-gather.7.cloned.1.call-done
  308.9 14.6 %fusion.189 = f32[2048,1024]{1,0:T(8,128)} fusion(bf16[2048,2048]{1,0:T(8,128)(2,1)} %all-gather.7.cloned.1.call-done, bf16[2048,1024]{1,0:T(8,128)(2,1)} %constant_dynamic-update-slice_fusion.5), kind=kOutput, calls=%fused_computation.378 | convolution fusion | flops 8589934592 | bytes 20971520 | tf_op jit(solution)/shard_map/dot_general | solution.py:287
  323.5 68.0 %all-gather.9.cloned.1.call-done = bf16[2048,2048]{1,0:T(8,128)(2,1)} async-done(((bf16[256,2048]{1,0:T(8,128)(2,1)}), bf16[2048,2048]{1,0:T(8,128)(2,1)}) %all-gather.9.cloned.1.call-update) | async-done | bytes 8388624 | tf_op jit(solution)/shard_map/all_gather | solution.py:47
  391.6 20.7 %convert_reduce_fusion = (f32[1024]{0:T(1024)}, bf16[2048,1024]{1,0:T(8,128)(2,1)S(1)}) fusion(f32[2048,1024]{1,0:T(8,128)} %fusion.189, f32[1024]{0:T(1024)S(1)} %copy-done.186, bf16[2048,2048]{1,0:T(8,128)(2,1)} %all-gather.9.cloned.1.call-done, bf16[1024,2048]{1,0:T(8,128)(2,1)} %constant_dynamic-update-slice_fusion), kind=kOutput, calls=%fused_computation.14 | convolution fusion | flops 8638168064 | bytes 25174016 | tf_op jit(solution)/shard_map/td,fd->tf/dot_general | solution.py:290
  414.2 13.5 %convolution_convert_fusion = bf16[2048,2048]{1,0:T(8,128)(2,1)} fusion(bf16[2048,1024]{1,0:T(8,128)(2,1)S(1)} %get-tuple-element.182, bf16[2048,1024]{1,0:T(8,128)(2,1)} %constant_dynamic-update-slice_fusion.5), kind=kOutput, calls=%fused_computation.16 | convolution fusion | flops 8594128896 | bytes 16777216 | tf_op jit(solution)/shard_map/tf,df->td/dot_general | solution.py:294
  427.7 15.4 %convolution_convert_fusion.1 = bf16[2048,2048]{1,0:T(8,128)(2,1)} fusion(bf16[1024,2048]{1,0:T(8,128)(2,1)} %constant_dynamic-update-slice_fusion, f32[2048,1024]{1,0:T(8,128)} %fusion.189, f32[1024]{0:T(1024)S(1)} %copy-done.186), kind=kOutput, calls=%fused_computation.17 | convolution fusion | flops 8615100416 | bytes 20975616 | tf_op jit(solution)/shard_map/dot_general | solution.py:296
  443.2 72.8 %reduce-scatter.9.cloned.1.call-done = bf16[256,2048]{1,0:T(8,128)(2,1)} async-done(((bf16[2048,2048]{1,0:T(8,128)(2,1)}), bf16[256,2048]{1,0:T(8,128)(2,1)}) %reduce-scatter.9.cloned.1.call-update) | async-done | bytes 1048592 | tf_op jit(solution)/shard_map/reduce_scatter | solution.py:52
  516.0 3.4 fusion.36
  519.4 86.7 %reduce-scatter.7.cloned.1.call-done = bf16[256,2048]{1,0:T(8,128)(2,1)} async-done(((bf16[2048,2048]{1,0:T(8,128)(2,1)}), bf16[256,2048]{1,0:T(8,128)(2,1)}) %reduce-scatter.7.cloned.1.call-update) | async-done | bytes 1048592 | tf_op jit(solution)/shard_map/reduce_scatter | solution.py:52
  606.1 5.2 fusion.161
  614.0 80.3 %all-gather.11.cloned.1.call-done = bf16[2048,2048]{1,0:T(8,128)(2,1)} async-done(((bf16[256,2048]{1,0:T(8,128)(2,1)}), bf16[2048,2048]{1,0:T(8,128)(2,1)}) %all-gather.11.cloned.1.call-update) | async-done | bytes 8388624 | tf_op jit(solution)/shard_map/all_gather | solution.py:47
  694.4 6.0 convolution_convert_fusion.3
  742.4 7.2 multiply_reduce_fusion.2
  750.8 3.6 multiply_convert_fusion.4
  762.4 3.8 multiply_reduce_fusion.7
  774.1 5.7 multiply_reduce_fusion.5
  788.9 15.4 %bitcast_convert_fusion = bf16[2048,2048]{1,0:T(8,128)(2,1)} fusion(bf16[3,2048,256]{2,1,0:T(8,128)(2,1)} %constant_dynamic-update-slice_fusion.15, bf16[1,512,256]{2,1,0:T(8,128)(2,1)S(1)} %copy-done.138, bf16[1,512,256]{2,1,0:T(8,128)(2,1)S(1)} %copy-done.142, bf16[1,512,256]{2,1,0:T(8,128)(2,1)S(1)} %copy-done.144, ...), kind=kOutput, calls=%fused_computation | convolution fusion | flops 6484393984 | bytes 14680064 | tf_op jit(solution)/shard_map/cte,cde->td/dot_general | solution.py:335
  804.3 12.7 %fusion.203 = f32[2048,1024]{1,0:T(8,128)S(1)} fusion(bf16[2048,2048]{1,0:T(8,128)(2,1)} %all-gather.7.cloned.1.call-done, bf16[2048,1024]{1,0:T(8,128)(2,1)} %copy-done.192), kind=kOutput, calls=%fused_computation.392 | convolution fusion | flops 8589934592 | bytes 20971520 | tf_op jit(solution)/shard_map/td,tf->df/dot_general | solution.py:299
  819.9 17.3 %fusion.150 = f32[1024,2048]{1,0:T(8,128)S(1)} fusion(bf16[2048,2048]{1,0:T(8,128)(2,1)} %all-gather.9.cloned.1.call-done, f32[2048,1024]{1,0:T(8,128)} %fusion.189, f32[1024]{0:T(1024)S(1)} %copy-done.186), kind=kOutput, calls=%fused_computation.351 | convolution fusion | flops 8610906112 | bytes 25169920 | tf_op jit(solution)/shard_map/tf,td->fd/dot_general | solution.py:297
  844.6 8.9 collective-permute-done.35
  855.2 9.7 collective-permute-done.28
  868.5 3.6 convert_add_fusion.4
  872.1 3.2 collective-permute-done.34
  878.2 11.2 %collective-permute-done.36 = bf16[1024,256]{1,0:T(8,128)(2,1)} collective-permute-done((bf16[1024,256]{1,0:T(8,128)(2,1)S(1)}, bf16[1024,256]{1,0:T(8,128)(2,1)}, u32[]{:S(2)}, u32[]{:S(2)}) %collective-permute-start.36) | collective-permute-done | bytes 524320 | tf_op jit(solution)/shard_map/ppermute | solution.py:57
  889.4 3.2 convert_add_fusion.2
  903.3 7.2 collective-permute-done.37
  912.1 6.3 fusion.151
  918.4 4.4 fusion.153
  922.9 5.9 fusion.202
  933.4 10.6 fusion.7
  950.5 19.6 %all-reduce.1 = (f32[2,256]{1,0:T(2,128)S(1)}, f32[1024]{0:T(1024)S(1)}) all-reduce(f32[2,256]{1,0:T(2,128)S(1)} %pad_maximum_fusion.7, f32[1024]{0:T(1024)S(1)} %copy-done.185), channel_id=1, replica_groups=mesh['dp'=4,'mp'=8] {'dp'}, use_global_device_ids=true, to_apply=%region_44.45 | all-reduce | flops 1536 | bytes 12288 | tf_op jit(solution)/shard_map/psum | solution.py:353
  978.7 7.8 collective-permute-done.24
  988.7 6.2 collective-permute-done.18
  1001.1 3.3 collective-permute-done.21
  1005.7 3.3 fusion.157
  1014.7 3.1 copy.166
  1022.2 38.3 %all-reduce = (f32[2,2048]{1,0:T(2,128)S(1)}, f32[4,2048]{1,0:T(4,128)S(1)}) all-reduce(f32[2,2048]{1,0:T(2,128)S(1)} %pad_maximum_fusion.6, f32[4,2048]{1,0:T(4,128)S(1)} %pad_maximum_fusion.5), channel_id=1, replica_groups=mesh['dp'=4,'mp'=8] {'dp','mp'}, use_global_device_ids=true, to_apply=%region_49.50 | all-reduce | flops 12288 | bytes 98304 | tf_op jit(solution)/shard_map/psum | solution.py:354
  1061.9 3.3 fusion.28
  (657 shorter events, 232.6 us)
Async XLA Ops:
  7.3 90.3 %all-gather.5.cloned.1.call-start = ((), (), s32[]{:S(2)}) async-start(), calls=%async_computation.4 | async-start | bytes 9437184 | tf_op jit(solution)/shard_map/all_gather | solution.py:47
  12.7 211.7 %reduce-scatter.5.cloned.1.call-start = ((), (), s32[]{:S(2)}) async-start(), calls=%async_computation.5 | async-start | bytes 9437184 | tf_op jit(solution)/shard_map/reduce_scatter | solution.py:52
  13.6 12.8 %collective-permute-start.4 = (bf16[256,512]{1,0:T(8,128)(2,1)}, bf16[256,512]{1,0:T(8,128)(2,1)}, u32[]{:S(2)}, u32[]{:S(2)}) collective-permute-start(bf16[256,512]{1,0:T(8,128)(2,1)} %get-tuple-element.186), channel_id=1, source_target_pairs={{0,8},{8,0},{16,24},{24,16},{1,9},{9,1},{17,25},{25,17},{2,10},{10... | collective-permute-start | bytes 786440 | tf_op jit(solution)/shard_map/ppermute | solution.py:57
  16.6 13.0 %collective-permute-start.5 = (bf16[256,512]{1,0:T(8,128)(2,1)}, bf16[256,512]{1,0:T(8,128)(2,1)}, u32[]{:S(2)}, u32[]{:S(2)}) collective-permute-start(bf16[256,512]{1,0:T(8,128)(2,1)} %get-tuple-element.186), channel_id=1, source_target_pairs={{0,16},{8,24},{16,0},{24,8},{1,17},{9,25},{17,1},{25,9},{2,18},{10... | collective-permute-start | bytes 786440 | tf_op jit(solution)/shard_map/ppermute | solution.py:57
  21.3 20.4 %collective-permute-start = (bf16[3,512,256]{2,1,0:T(8,128)(2,1)}, bf16[3,512,256]{2,1,0:T(8,128)(2,1)}, u32[]{:S(2)}, u32[]{:S(2)}) collective-permute-start(bf16[3,512,256]{2,1,0:T(8,128)(2,1)} %get-tuple-element.193), channel_id=1, source_target_pairs={{0,8},{8,0},{16,24},{24,16},{1,9},{9,1},{17,25},{25,17},{2,10},{10... | collective-permute-start | bytes 2359304 | tf_op jit(solution)/shard_map/ppermute | solution.py:57
  21.9 23.4 %collective-permute-start.1 = (bf16[3,512,256]{2,1,0:T(8,128)(2,1)}, bf16[3,512,256]{2,1,0:T(8,128)(2,1)}, u32[]{:S(2)}, u32[]{:S(2)}) collective-permute-start(bf16[3,512,256]{2,1,0:T(8,128)(2,1)} %get-tuple-element.193), channel_id=1, source_target_pairs={{0,16},{8,24},{16,0},{24,8},{1,17},{9,25},{17,1},{25,9},{2,18},{10... | collective-permute-start | bytes 2359304 | tf_op jit(solution)/shard_map/ppermute | solution.py:57
  27.5 17.8 %collective-permute-start.6 = (bf16[256,256]{1,0:T(8,128)(2,1)S(1)}, bf16[256,256]{1,0:T(8,128)(2,1)S(1)}, u32[]{:S(2)}, u32[]{:S(2)}) collective-permute-start(bf16[256,256]{1,0:T(8,128)(2,1)S(1)} %slice.448), channel_id=1, source_target_pairs={{0,16},{8,24},{16,0},{24,8},{1,17},{9,25},{17,1},{25,9},{2,18},{10... | collective-permute-start | bytes 393224 | tf_op jit(solution)/shard_map/ppermute | solution.py:57
  30.5 16.2 %collective-permute-start.7 = (bf16[256,256]{1,0:T(8,128)(2,1)S(1)}, bf16[256,256]{1,0:T(8,128)(2,1)S(1)}, u32[]{:S(2)}, u32[]{:S(2)}) collective-permute-start(bf16[256,256]{1,0:T(8,128)(2,1)S(1)} %slice.449), channel_id=1, source_target_pairs={{0,8},{8,0},{16,24},{24,16},{1,9},{9,1},{17,25},{25,17},{2,10},{10... | collective-permute-start | bytes 393224 | tf_op jit(solution)/shard_map/ppermute | solution.py:57
  42.8 9.9 collective-permute-start.2
  46.3 9.0 collective-permute-start.3
  136.0 172.9 %all-gather.7.cloned.1.call-start = ((), (), s32[]{:S(2)}) async-start(), calls=%async_computation.6 | async-start | bytes 9437184 | tf_op jit(solution)/shard_map/all_gather | solution.py:47
  228.4 163.2 %all-gather.9.cloned.1.call-start = ((), (), s32[]{:S(2)}) async-start(), calls=%async_computation.8 | async-start | bytes 9437184 | tf_op jit(solution)/shard_map/all_gather | solution.py:47
  230.9 285.0 %reduce-scatter.9.cloned.1.call-start = ((), (), s32[]{:S(2)}) async-start(), calls=%async_computation.9 | async-start | bytes 9437184 | tf_op jit(solution)/shard_map/reduce_scatter | solution.py:52
  234.7 26.1 %collective-permute-start.12 = (bf16[1024,512]{1,0:T(8,128)(2,1)S(1)}, bf16[1024,512]{1,0:T(8,128)(2,1)S(1)}, u32[]{:S(2)}, u32[]{:S(2)}) collective-permute-start(bf16[1024,512]{1,0:T(8,128)(2,1)S(1)} %get-tuple-element.195), channel_id=1, source_target_pairs={{0,8},{8,0},{16,24},{24,16},{1,9},{9,1},{17,25},{25,17},{2,10},{10... | collective-permute-start | bytes 3145736 | tf_op jit(solution)/shard_map/ppermute | solution.py:57
  236.2 26.2 %collective-permute-start.13 = (bf16[1024,512]{1,0:T(8,128)(2,1)S(1)}, bf16[1024,512]{1,0:T(8,128)(2,1)S(1)}, u32[]{:S(2)}, u32[]{:S(2)}) collective-permute-start(bf16[1024,512]{1,0:T(8,128)(2,1)S(1)} %get-tuple-element.195), channel_id=1, source_target_pairs={{0,16},{8,24},{16,0},{24,8},{1,17},{9,25},{17,1},{25,9},{2,18},{10... | collective-permute-start | bytes 3145736 | tf_op jit(solution)/shard_map/ppermute | solution.py:57
  241.4 41.9 %collective-permute-start.8 = (bf16[512,1024]{1,0:T(8,128)(2,1)S(1)}, bf16[512,1024]{1,0:T(8,128)(2,1)S(1)}, u32[]{:S(2)}, u32[]{:S(2)}) collective-permute-start(bf16[512,1024]{1,0:T(8,128)(2,1)S(1)} %get-tuple-element.184), channel_id=1, source_target_pairs={{0,8},{8,0},{16,24},{24,16},{1,9},{9,1},{17,25},{25,17},{2,10},{10... | collective-permute-start | bytes 3145736 | tf_op jit(solution)/shard_map/ppermute | solution.py:57
  242.0 42.9 %collective-permute-start.9 = (bf16[512,1024]{1,0:T(8,128)(2,1)S(1)}, bf16[512,1024]{1,0:T(8,128)(2,1)S(1)}, u32[]{:S(2)}, u32[]{:S(2)}) collective-permute-start(bf16[512,1024]{1,0:T(8,128)(2,1)S(1)} %get-tuple-element.184), channel_id=1, source_target_pairs={{0,16},{8,24},{16,0},{24,8},{1,17},{9,25},{17,1},{25,9},{2,18},{10... | collective-permute-start | bytes 3145736 | tf_op jit(solution)/shard_map/ppermute | solution.py:57
  260.9 35.1 %collective-permute-start.14 = (bf16[1024,256]{1,0:T(8,128)(2,1)S(1)}, bf16[1024,256]{1,0:T(8,128)(2,1)S(1)}, u32[]{:S(2)}, u32[]{:S(2)}) collective-permute-start(bf16[1024,256]{1,0:T(8,128)(2,1)S(1)} %slice.452), channel_id=1, source_target_pairs={{0,16},{8,24},{16,0},{24,8},{1,17},{9,25},{17,1},{25,9},{2,18},{10... | collective-permute-start | bytes 1572872 | tf_op jit(solution)/shard_map/ppermute | solution.py:57
  262.4 34.4 %collective-permute-start.15 = (bf16[1024,256]{1,0:T(8,128)(2,1)S(1)}, bf16[1024,256]{1,0:T(8,128)(2,1)S(1)}, u32[]{:S(2)}, u32[]{:S(2)}) collective-permute-start(bf16[1024,256]{1,0:T(8,128)(2,1)S(1)} %slice.453), channel_id=1, source_target_pairs={{0,8},{8,0},{16,24},{24,16},{1,9},{9,1},{17,25},{25,17},{2,10},{10... | collective-permute-start | bytes 1572872 | tf_op jit(solution)/shard_map/ppermute | solution.py:57
  283.3 20.2 %collective-permute-start.10 = (bf16[256,1024]{1,0:T(8,128)(2,1)S(1)}, bf16[256,1024]{1,0:T(8,128)(2,1)S(1)}, u32[]{:S(2)}, u32[]{:S(2)}) collective-permute-start(bf16[256,1024]{1,0:T(8,128)(2,1)S(1)} %slice.450), channel_id=1, source_target_pairs={{0,16},{8,24},{16,0},{24,8},{1,17},{9,25},{17,1},{25,9},{2,18},{10... | collective-permute-start | bytes 1572872 | tf_op jit(solution)/shard_map/ppermute | solution.py:57
  284.9 19.5 %collective-permute-start.11 = (bf16[256,1024]{1,0:T(8,128)(2,1)S(1)}, bf16[256,1024]{1,0:T(8,128)(2,1)S(1)}, u32[]{:S(2)}, u32[]{:S(2)}) collective-permute-start(bf16[256,1024]{1,0:T(8,128)(2,1)S(1)} %slice.451), channel_id=1, source_target_pairs={{0,8},{8,0},{16,24},{24,16},{1,9},{9,1},{17,25},{25,17},{2,10},{10... | collective-permute-start | bytes 1572872 | tf_op jit(solution)/shard_map/ppermute | solution.py:57
  427.7 178.4 %reduce-scatter.7.cloned.1.call-start = ((), (), s32[]{:S(2)}) async-start(), calls=%async_computation.7 | async-start | bytes 9437184 | tf_op jit(solution)/shard_map/reduce_scatter | solution.py:52
  443.1 251.2 %all-gather.11.cloned.1.call-start = ((), (), s32[]{:S(2)}) async-start(), calls=%async_computation.10 | async-start | bytes 9437184 | tf_op jit(solution)/shard_map/all_gather | solution.py:47
  613.8 405.9 %reduce-scatter.11.cloned.1.call-start = ((), (), s32[]{:S(2)}) async-start(), calls=%async_computation.11 | async-start | bytes 9437184 | tf_op jit(solution)/shard_map/reduce_scatter | solution.py:52
  818.4 23.9 %collective-permute-start.29 = (bf16[256,1024]{1,0:T(8,128)(2,1)S(1)}, bf16[256,1024]{1,0:T(8,128)(2,1)S(1)}, u32[]{:S(2)}, u32[]{:S(2)}) collective-permute-start(bf16[256,1024]{1,0:T(8,128)(2,1)S(1)} %get-tuple-element.207), channel_id=1, source_target_pairs={{0,8},{8,0},{16,24},{24,16},{1,9},{9,1},{17,25},{25,17},{2,10},{10... | collective-permute-start | bytes 1572872 | tf_op jit(solution)/shard_map/ppermute | solution.py:57
  838.8 14.8 %collective-permute-start.35 = (bf16[1024,256]{1,0:T(8,128)(2,1)S(1)}, bf16[1024,256]{1,0:T(8,128)(2,1)S(1)}, u32[]{:S(2)}, u32[]{:S(2)}) collective-permute-start(bf16[1024,256]{1,0:T(8,128)(2,1)S(1)} %get-tuple-element.201), channel_id=1, source_target_pairs={{0,8},{8,0},{16,24},{24,16},{1,9},{9,1},{17,25},{25,17},{2,10},{10... | collective-permute-start | bytes 1572872 | tf_op jit(solution)/shard_map/ppermute | solution.py:57
  840.3 24.6 %collective-permute-start.28 = (bf16[256,1024]{1,0:T(8,128)(2,1)S(1)}, bf16[256,1024]{1,0:T(8,128)(2,1)}, u32[]{:S(2)}, u32[]{:S(2)}) collective-permute-start(bf16[256,1024]{1,0:T(8,128)(2,1)S(1)} %get-tuple-element.204), channel_id=1, source_target_pairs={{0,8},{8,0},{16,24},{24,16},{1,9},{9,1},{17,25},{25,17},{2,10},{10... | collective-permute-start | bytes 1572872 | tf_op jit(solution)/shard_map/ppermute | solution.py:57
  840.8 25.6 %collective-permute-start.32 = (bf16[256,1024]{1,0:T(8,128)(2,1)S(1)}, bf16[256,1024]{1,0:T(8,128)(2,1)S(1)}, u32[]{:S(2)}, u32[]{:S(2)}) collective-permute-start(bf16[256,1024]{1,0:T(8,128)(2,1)S(1)} %get-tuple-element.205), channel_id=1, source_target_pairs={{0,16},{8,24},{16,0},{24,8},{1,17},{9,25},{17,1},{25,9},{2,18},{10... | collective-permute-start | bytes 1572872 | tf_op jit(solution)/shard_map/ppermute | solution.py:57
  842.4 24.5 %collective-permute-start.30 = (bf16[256,1024]{1,0:T(8,128)(2,1)S(1)}, bf16[256,1024]{1,0:T(8,128)(2,1)}, u32[]{:S(2)}, u32[]{:S(2)}) collective-permute-start(bf16[256,1024]{1,0:T(8,128)(2,1)S(1)} %add_convert_fusion.4), channel_id=1, source_target_pairs={{0,16},{8,24},{16,0},{24,8},{1,17},{9,25},{17,1},{25,9},{2,18},{10... | collective-permute-start | bytes 1572872 | tf_op jit(solution)/shard_map/ppermute | solution.py:57
  843.0 32.2 %collective-permute-start.34 = (bf16[1024,256]{1,0:T(8,128)(2,1)S(1)}, bf16[1024,256]{1,0:T(8,128)(2,1)S(1)}, u32[]{:S(2)}, u32[]{:S(2)}) collective-permute-start(bf16[1024,256]{1,0:T(8,128)(2,1)S(1)} %get-tuple-element.198), channel_id=1, source_target_pairs={{0,8},{8,0},{16,24},{24,16},{1,9},{9,1},{17,25},{25,17},{2,10},{10... | collective-permute-start | bytes 1572872 | tf_op jit(solution)/shard_map/ppermute | solution.py:57
  853.5 24.7 %collective-permute-start.38 = (bf16[1024,256]{1,0:T(8,128)(2,1)}, bf16[1024,256]{1,0:T(8,128)(2,1)}, u32[]{:S(2)}, u32[]{:S(2)}) collective-permute-start(bf16[1024,256]{1,0:T(8,128)(2,1)} %get-tuple-element.199), channel_id=1, source_target_pairs={{0,16},{8,24},{16,0},{24,8},{1,17},{9,25},{17,1},{25,9},{2,18},{10... | collective-permute-start | bytes 1572872 | tf_op jit(solution)/shard_map/ppermute | solution.py:57
  864.9 24.6 %collective-permute-start.36 = (bf16[1024,256]{1,0:T(8,128)(2,1)S(1)}, bf16[1024,256]{1,0:T(8,128)(2,1)}, u32[]{:S(2)}, u32[]{:S(2)}) collective-permute-start(bf16[1024,256]{1,0:T(8,128)(2,1)S(1)} %add_convert_fusion.2), channel_id=1, source_target_pairs={{0,16},{8,24},{16,0},{24,8},{1,17},{9,25},{17,1},{25,9},{2,18},{10... | collective-permute-start | bytes 1572872 | tf_op jit(solution)/shard_map/ppermute | solution.py:57
  866.4 35.1 %collective-permute-start.31 = (bf16[256,1024]{1,0:T(8,128)(2,1)}, bf16[256,1024]{1,0:T(8,128)(2,1)}, u32[]{:S(2)}, u32[]{:S(2)}) collective-permute-start(bf16[256,1024]{1,0:T(8,128)(2,1)} %get-tuple-element.206), channel_id=1, source_target_pairs={{0,16},{8,24},{16,0},{24,8},{1,17},{9,25},{17,1},{25,9},{2,18},{10... | collective-permute-start | bytes 1572872 | tf_op jit(solution)/shard_map/ppermute | solution.py:57
  867.1 43.3 %collective-permute-start.37 = (bf16[1024,256]{1,0:T(8,128)(2,1)}, bf16[1024,256]{1,0:T(8,128)(2,1)S(1)}, u32[]{:S(2)}, u32[]{:S(2)}) collective-permute-start(bf16[1024,256]{1,0:T(8,128)(2,1)} %get-tuple-element.200), channel_id=1, source_target_pairs={{0,16},{8,24},{16,0},{24,8},{1,17},{9,25},{17,1},{25,9},{2,18},{10... | collective-permute-start | bytes 1572872 | tf_op jit(solution)/shard_map/ppermute | solution.py:57
  876.1 25.4 %collective-permute-start.33 = (bf16[256,1024]{1,0:T(8,128)(2,1)}, bf16[256,1024]{1,0:T(8,128)(2,1)S(1)}, u32[]{:S(2)}, u32[]{:S(2)}) collective-permute-start(bf16[256,1024]{1,0:T(8,128)(2,1)} %get-tuple-element.203), channel_id=1, source_target_pairs={{0,8},{8,0},{16,24},{24,16},{1,9},{9,1},{17,25},{25,17},{2,10},{10... | collective-permute-start | bytes 1572872 | tf_op jit(solution)/shard_map/ppermute | solution.py:57
  892.7 17.8 %collective-permute-start.39 = (bf16[1024,256]{1,0:T(8,128)(2,1)S(1)}, bf16[1024,256]{1,0:T(8,128)(2,1)}, u32[]{:S(2)}, u32[]{:S(2)}) collective-permute-start(bf16[1024,256]{1,0:T(8,128)(2,1)S(1)} %get-tuple-element.197), channel_id=1, source_target_pairs={{0,8},{8,0},{16,24},{24,16},{1,9},{9,1},{17,25},{25,17},{2,10},{10... | collective-permute-start | bytes 1572872 | tf_op jit(solution)/shard_map/ppermute | solution.py:57
  929.7 46.2 %collective-permute-start.22 = (bf16[256,256]{1,0:T(8,128)(2,1)}, bf16[256,256]{1,0:T(8,128)(2,1)S(1)}, u32[]{:S(2)}, u32[]{:S(2)}) collective-permute-start(bf16[256,256]{1,0:T(8,128)(2,1)} %get-tuple-element.223), channel_id=1, source_target_pairs={{0,8},{8,0},{16,24},{24,16},{1,9},{9,1},{17,25},{25,17},{2,10},{10... | collective-permute-start | bytes 393224 | tf_op jit(solution)/shard_map/ppermute | solution.py:57
  931.2 45.9 %collective-permute-start.26 = (bf16[256,256]{1,0:T(8,128)(2,1)}, bf16[256,256]{1,0:T(8,128)(2,1)S(1)}, u32[]{:S(2)}, u32[]{:S(2)}) collective-permute-start(bf16[256,256]{1,0:T(8,128)(2,1)} %get-tuple-element.224), channel_id=1, source_target_pairs={{0,16},{8,24},{16,0},{24,8},{1,17},{9,25},{17,1},{25,9},{2,18},{10... | collective-permute-start | bytes 393224 | tf_op jit(solution)/shard_map/ppermute | solution.py:57
  932.7 38.7 %collective-permute-start.23 = (bf16[256,256]{1,0:T(8,128)(2,1)}, bf16[256,256]{1,0:T(8,128)(2,1)}, u32[]{:S(2)}, u32[]{:S(2)}) collective-permute-start(bf16[256,256]{1,0:T(8,128)(2,1)} %get-tuple-element.226), channel_id=1, source_target_pairs={{0,8},{8,0},{16,24},{24,16},{1,9},{9,1},{17,25},{25,17},{2,10},{10... | collective-permute-start | bytes 393224 | tf_op jit(solution)/shard_map/ppermute | solution.py:57
  947.9 40.2 %collective-permute-start.16 = (bf16[3,256,256]{1,2,0:T(8,128)(2,1)}, bf16[3,256,256]{1,2,0:T(8,128)(2,1)S(1)}, u32[]{:S(2)}, u32[]{:S(2)}) collective-permute-start(bf16[3,256,256]{1,2,0:T(8,128)(2,1)} %get-tuple-element.210), channel_id=1, source_target_pairs={{0,8},{8,0},{16,24},{24,16},{1,9},{9,1},{17,25},{25,17},{2,10},{10... | collective-permute-start | bytes 1179656 | tf_op jit(solution)/shard_map/ppermute | solution.py:57
  949.4 23.6 %collective-permute-start.17 = (bf16[3,256,256]{1,2,0:T(8,128)(2,1)}, bf16[3,256,256]{1,2,0:T(8,128)(2,1)}, u32[]{:S(2)}, u32[]{:S(2)}) collective-permute-start(bf16[3,256,256]{1,2,0:T(8,128)(2,1)} %get-tuple-element.213), channel_id=1, source_target_pairs={{0,8},{8,0},{16,24},{24,16},{1,9},{9,1},{17,25},{25,17},{2,10},{10... | collective-permute-start | bytes 1179656 | tf_op jit(solution)/shard_map/ppermute | solution.py:57
  971.4 17.3 %collective-permute-start.20 = (bf16[3,256,256]{1,2,0:T(8,128)(2,1)}, bf16[3,256,256]{1,2,0:T(8,128)(2,1)S(1)}, u32[]{:S(2)}, u32[]{:S(2)}) collective-permute-start(bf16[3,256,256]{1,2,0:T(8,128)(2,1)} %get-tuple-element.211), channel_id=1, source_target_pairs={{0,16},{8,24},{16,0},{24,8},{1,17},{9,25},{17,1},{25,9},{2,18},{10... | collective-permute-start | bytes 1179656 | tf_op jit(solution)/shard_map/ppermute | solution.py:57
  973.0 13.5 %collective-permute-start.24 = (bf16[256,256]{1,0:T(8,128)(2,1)S(1)}, bf16[256,256]{1,0:T(8,128)(2,1)S(1)}, u32[]{:S(2)}, u32[]{:S(2)}) collective-permute-start(bf16[256,256]{1,0:T(8,128)(2,1)S(1)} %add_convert_fusion.6), channel_id=1, source_target_pairs={{0,16},{8,24},{16,0},{24,8},{1,17},{9,25},{17,1},{25,9},{2,18},{10... | collective-permute-start | bytes 393224 | tf_op jit(solution)/shard_map/ppermute | solution.py:57
  975.9 19.0 %collective-permute-start.18 = (bf16[3,256,256]{1,2,0:T(8,128)(2,1)S(1)}, bf16[3,256,256]{1,2,0:T(8,128)(2,1)S(1)}, u32[]{:S(2)}, u32[]{:S(2)}) collective-permute-start(bf16[3,256,256]{1,2,0:T(8,128)(2,1)S(1)} %fusion.87), channel_id=1, source_target_pairs={{0,16},{8,24},{16,0},{24,8},{1,17},{9,25},{17,1},{25,9},{2,18},{10... | collective-permute-start | bytes 1179656 | tf_op jit(solution)/shard_map/ppermute | solution.py:57
  977.1 19.7 %collective-permute-start.25 = (bf16[256,256]{1,0:T(8,128)(2,1)}, bf16[256,256]{1,0:T(8,128)(2,1)S(1)}, u32[]{:S(2)}, u32[]{:S(2)}) collective-permute-start(bf16[256,256]{1,0:T(8,128)(2,1)} %get-tuple-element.225), channel_id=1, source_target_pairs={{0,16},{8,24},{16,0},{24,8},{1,17},{9,25},{17,1},{25,9},{2,18},{10... | collective-permute-start | bytes 393224 | tf_op jit(solution)/shard_map/ppermute | solution.py:57
  986.5 14.6 %collective-permute-start.19 = (bf16[3,256,256]{1,2,0:T(8,128)(2,1)}, bf16[3,256,256]{1,2,0:T(8,128)(2,1)S(1)}, u32[]{:S(2)}, u32[]{:S(2)}) collective-permute-start(bf16[3,256,256]{1,2,0:T(8,128)(2,1)} %get-tuple-element.212), channel_id=1, source_target_pairs={{0,16},{8,24},{16,0},{24,8},{1,17},{9,25},{17,1},{25,9},{2,18},{10... | collective-permute-start | bytes 1179656 | tf_op jit(solution)/shard_map/ppermute | solution.py:57
  988.1 8.7 collective-permute-start.27
  996.5 7.8 collective-permute-start.21
  (193 other events, 2641.6 us)
Sparse Core Ops, SparseCore 0:
  12.8 84.7 all-gather.4
  136.1 88.1 reduce-scatter.4
  228.5 80.3 all-gather.6
  310.9 80.5 all-gather.8
  427.8 88.1 reduce-scatter.8
  518.1 87.9 reduce-scatter.6
  613.9 80.4 all-gather.10
  804.5 88.1 reduce-scatter.10

commit v2 on v1

--- a/solution.py
+++ b/solution.py
@@ -1,6 +1,10 @@
+import functools
+
 import jax
 import jax.numpy as jnp
 from jax import lax
+from jax.experimental import pallas as pl
+from jax.experimental.pallas import tpu as pltpu
 from jax.sharding import PartitionSpec as P
 
 D = 2048
@@ -95,6 +99,674 @@
         return piece(me, upper) + near.astype(jnp.float32) + last.astype(jnp.float32)
 
     return lax.concatenate([one_way(1, 2, 0), one_way(2, 1, 1)], axis)
+
+
+MESH = pl.DeviceIdType.MESH
+VMEM_LIMIT = 60 * 1024 * 1024
+
+
+class Place:
+    def __init__(self, chips):
+        self.chips = chips
+        self.dp = lax.axis_index("dp")
+        self.me = lax.axis_index("mp")
+        self.chip = self.me // 2
+        self.core = self.me % 2
+        self.has_up = self.chip < chips - 1
+        self.has_down = self.chip > 0
+        self.up = (self.dp, jnp.minimum(self.me + 2, 2 * chips - 1))
+        self.down = (self.dp, jnp.maximum(self.me - 2, 0))
+        self.side = (self.dp, self.me + 1 - 2 * self.core)
+        self.x_peer = self.dp + 1 - 2 * (self.dp % 2)
+        self.y_peer = (self.dp + 2) % 4
+        self.across = 3 - self.dp
+        self.x_way = (self.x_peer, self.me)
+        self.y_way = (self.y_peer, self.me)
+
+    def greet(self, square):
+        barrier = pltpu.get_barrier_semaphore()
+
+        def signal(device):
+            pl.semaphore_signal(barrier, inc=1, device_id=device, device_id_type=MESH)
+
+        signal(self.side)
+        pl.when(self.has_up)(lambda: signal(self.up))
+        pl.when(self.has_down)(lambda: signal(self.down))
+        count = 1 + self.has_up.astype(jnp.int32) + self.has_down.astype(jnp.int32)
+        if square:
+            signal(self.x_way)
+            signal(self.y_way)
+            count = count + 2
+        pl.semaphore_wait(barrier, count)
+
+
+def remote(source, target, send, recv, device):
+    return pltpu.make_async_remote_copy(
+        src_ref=source,
+        dst_ref=target,
+        send_sem=send,
+        recv_sem=recv,
+        device_id=device,
+        device_id_type=MESH,
+    )
+
+
+class LineGather:
+    def __init__(self, place, blocks, send, recv):
+        self.place, self.blocks, self.send, self.recv = place, blocks, send, recv
+
+    def copy(self, way, chip):
+        place = self.place
+        block = 2 * chip + place.core
+        device = (place.up, place.down, place.side)[way]
+        return remote(
+            self.blocks.at[block],
+            self.blocks.at[block],
+            self.send.at[way, chip],
+            self.recv.at[block],
+            device,
+        )
+
+    def arrive(self, chip, core):
+        place = self.place
+        block = 2 * chip + core
+        remote(
+            self.blocks.at[block],
+            self.blocks.at[block],
+            self.send.at[2, chip],
+            self.recv.at[block],
+            place.side,
+        ).wait_recv()
+
+    def begin(self):
+        place = self.place
+        pl.when(place.has_up)(lambda: self.copy(0, place.chip).start())
+        pl.when(place.has_down)(lambda: self.copy(1, place.chip).start())
+        self.copy(2, place.chip).start()
+
+    def step(self, distance):
+        place = self.place
+        low = place.chip - distance
+        high = place.chip + distance
+
+        @pl.when(low >= 0)
+        def _():
+            self.arrive(low, place.core)
+            pl.when(place.has_up)(lambda: self.copy(0, low).start())
+            self.copy(2, low).start()
+
+        @pl.when(high < place.chips)
+        def _():
+            self.arrive(high, place.core)
+            pl.when(place.has_down)(lambda: self.copy(1, high).start())
+            self.copy(2, high).start()
+
+    def finish(self):
+        place = self.place
+
+        def drain(chip, carry):
+            pl.when(place.has_up & (chip <= place.chip))(lambda: self.copy(0, chip).wait_send())
+            pl.when(place.has_down & (chip >= place.chip))(lambda: self.copy(1, chip).wait_send())
+            self.copy(2, chip).wait_send()
+            return carry
+
+        lax.fori_loop(0, place.chips, drain, 0)
+
+
+class SquareGather:
+    def __init__(self, place, shard, view, half, send, recv):
+        self.place, self.shard, self.view, self.half = place, shard, view, half
+        self.send, self.recv = send, recv
+
+    def first(self, way):
+        place = self.place
+        device = (place.x_way, place.y_way)[way]
+        return remote(
+            self.shard, self.view(place.dp), self.send.at[way], self.recv.at[way], device
+        )
+
+    def first_landed(self, way):
+        place = self.place
+        owner = (place.x_peer, place.y_peer)[way]
+        device = (place.x_way, place.y_way)[way]
+        remote(
+            self.view(owner), self.view(owner), self.send.at[way], self.recv.at[way], device
+        ).wait_recv()
+
+    def second(self, way):
+        place = self.place
+        owner = (place.y_peer, place.x_peer)[way]
+        device = (place.x_way, place.y_way)[way]
+        part = self.half(owner, 1 - way)
+        return remote(part, part, self.send.at[2 + way], self.recv.at[2 + way], device)
+
+    def second_landed(self, way):
+        place = self.place
+        device = (place.x_way, place.y_way)[way]
+        part = self.half(place.across, 1 - way)
+        remote(part, part, self.send.at[2 + way], self.recv.at[2 + way], device).wait_recv()
+
+    def begin(self):
+        self.first(0).start()
+        self.first(1).start()
+
+    def middle(self):
+        self.first_landed(0)
+        self.second(1).start()
+        self.first_landed(1)
+        self.second(0).start()
+
+    def end(self):
+        self.second_landed(0)
+        self.second_landed(1)
+
+    def finish(self):
+        self.first(0).wait_send()
+        self.first(1).wait_send()
+        self.second(0).wait_send()
+        self.second(1).wait_send()
+
+
+def norm_rows(rows, gain, shift):
+    normed, hat, inverse = layer_norm_parts(rows, gain, shift)
+    return normed
+
+
+def project_kernel(
+    chips,
+    rows_ref,
+    gain_ref,
+    shift_ref,
+    mix_ref,
+    out_ref,
+    bias_ref,
+    normed_ref,
+    mixed_ref,
+    mix_whole,
+    out_whole,
+    blocks,
+    line_send,
+    line_recv,
+    mix_send,
+    mix_recv,
+    out_send,
+    out_recv,
+    own_sem,
+    keep_sem,
+):
+    place = Place(chips)
+    count = rows_ref.shape[0]
+    place.greet(True)
+    mix = SquareGather(
+        place,
+        mix_ref,
+        lambda owner: mix_whole.at[:, owner],
+        lambda owner, which: mix_whole.at[:, owner, pl.ds(which * 256, 256)],
+        mix_send,
+        mix_recv,
+    )
+    out = SquareGather(
+        place,
+        out_ref,
+        lambda owner: out_whole.at[owner],
+        lambda owner, which: out_whole.at[owner, pl.ds(which * 128, 128)],
+        out_send,
+        out_recv,
+    )
+    mix.begin()
+    own_mix = pltpu.make_async_copy(mix_ref, mix_whole.at[:, place.dp], own_sem.at[0])
+    own_out = pltpu.make_async_copy(out_ref, out_whole.at[place.dp], own_sem.at[1])
+    own_mix.start()
+    own_out.start()
+    tile = 64
+
+    def norm(index, carry):
+        span = pl.ds(pl.multiple_of(index * tile, tile), tile)
+        rows = rows_ref[span, :].astype(jnp.float32)
+        normed = norm_rows(rows, gain_ref[...], shift_ref[...])
+        blocks[place.me, span, :] = normed.astype(jnp.bfloat16)
+        return carry
+
+    lax.fori_loop(0, count // tile, norm, 0)
+    line = LineGather(place, blocks, line_send, line_recv)
+    line.begin()
+    mix.middle()
+    out.begin()
+
+    def keep(block):
+        span = pl.ds(pl.multiple_of(block * count, count), count)
+        return pltpu.make_async_copy(blocks.at[block], normed_ref.at[span], keep_sem.at[block])
+
+    def project(block):
+        keep(block).start()
+        span = pl.ds(pl.multiple_of(block * count, count), count)
+        rows = blocks[block]
+        for part in range(3):
+            weight = mix_whole[part].reshape(-1, mix_whole.shape[3])
+            result = jnp.dot(rows, weight, preferred_element_type=jnp.float32)
+            if part == 0:
+                result = result + bias_ref[0:1, :]
+            if part == 2:
+                result = result + bias_ref[1:2, :]
+            mixed_ref[part, span, :] = result.astype(jnp.bfloat16)
+
+    def step(distance, carry):
+        @pl.when((distance > 0) & (distance < chips))
+        def _():
+            line.step(distance)
+
+        @pl.when(distance == 1)
+        def _():
+            mix.end()
+            own_mix.wait()
+            out.middle()
+
+        def one(index, inner):
+            near = distance - 1
+            side = index % 2
+            core = (place.core + index // 2) % 2
+            chip = place.chip + near * (2 * side - 1)
+
+            @pl.when((chip >= 0) & (chip < chips) & ((near > 0) | (side == 0)))
+            def _():
+                pl.when(index >= 2)(lambda: line.arrive(chip, core))
+                project(2 * chip + core)
+
+            return inner
+
+        @pl.when(distance > 0)
+        def _():
+            lax.fori_loop(0, 4, one, 0)
+
+        return carry
+
+    lax.fori_loop(0, chips + 1, step, 0)
+    out.end()
+    own_out.wait()
+    line.finish()
+    mix.finish()
+    out.finish()
+
+    def kept(block, carry):
+        keep(block).wait()
+        return carry
+
+    lax.fori_loop(0, 2 * chips, kept, 0)
+
+
+def project_call(rows, gain, shift, mix_shard, out_shard, bias, chips):
+    count, width = rows.shape
+    total = 2 * chips * count
+    local = mix_shard.shape[2]
+    vmem = pl.BlockSpec(memory_space=pltpu.VMEM)
+    dma = pltpu.SemaphoreType.DMA
+    flops = 2 * total * width * 3 * local
+    return pl.pallas_call(
+        functools.partial(project_kernel, chips),
+        out_shape=(
+            jax.ShapeDtypeStruct((total, width), jnp.bfloat16),
+            jax.ShapeDtypeStruct((3, total, local), jnp.bfloat16),
+            jax.ShapeDtypeStruct((3, 4, mix_shard.shape[1], local), jnp.bfloat16),
+            jax.ShapeDtypeStruct((4,) + out_shard.shape, jnp.bfloat16),
+        ),
+        in_specs=[vmem] * 6,
+        out_specs=(pl.BlockSpec(memory_space=pl.ANY), vmem, vmem, vmem),
+        scratch_shapes=[
+            pltpu.VMEM((2 * chips, count, width), jnp.bfloat16),
+            dma((3, chips)),
+            dma((2 * chips,)),
+            dma((4,)),
+            dma((4,)),
+            dma((4,)),
+            dma((4,)),
+            dma((2,)),
+            dma((2 * chips,)),
+        ],
+        compiler_params=pltpu.CompilerParams(
+            collective_id=0, has_side_effects=True, vmem_limit_bytes=VMEM_LIMIT
+        ),
+        cost_estimate=pl.CostEstimate(flops=flops * 7, bytes_accessed=0, transcendentals=0),
+        name="project",
+    )(rows, gain, shift, mix_shard, out_shard, bias)
+
+
+class LineScatter:
+    def __init__(self, place, term, tiles, bufs, sems):
+        self.place, self.term, self.tiles = place, term, tiles
+        self.total, self.side_out, self.side_in, self.line_out, self.line_in = bufs
+        self.side_send, self.side_recv, self.line_send, self.line_recv = sems
+
+    def side_copy(self, chip):
+        return remote(
+            self.side_out.at[chip],
+            self.side_in.at[chip],
+            self.side_send.at[chip],
+            self.side_recv.at[chip],
+            self.place.side,
+        )
+
+    def line_copy(self, way, chip):
+        return remote(
+            self.line_out.at[chip],
+            self.line_in.at[way, chip],
+            self.line_send.at[chip],
+            self.line_recv.at[way, chip],
+            (self.place.up, self.place.down)[way],
+        )
+
+    def each(self, distance, action):
+        place = self.place
+
+        def one(index, carry):
+            chip = place.chip + distance * (1 - 2 * index)
+            valid = (chip >= 0) & (chip < place.chips) & ((distance > 0) | (index == 0))
+            pl.when(valid)(lambda: action(chip))
+            return carry
+
+        lax.fori_loop(0, 2, one, 0)
+
+    def hand_over(self, chip):
+        block = 2 * chip + 1 - self.place.core
+        width = self.total.shape[1] // self.tiles
+        for tile in range(self.tiles):
+            span = slice(tile * width, (tile + 1) * width)
+            self.side_out[chip, :, span] = self.term(block, tile).astype(jnp.bfloat16)
+        self.side_copy(chip).start()
+
+    def sum_up(self, chip):
+        place = self.place
+        block = 2 * chip + place.core
+        width = self.total.shape[1] // self.tiles
+        self.side_copy(chip).wait_recv()
+        for tile in range(self.tiles):
+            span = slice(tile * width, (tile + 1) * width)
+            self.total[:, span] = self.term(block, tile) + self.side_in[chip, :, span].astype(
+                jnp.float32
+            )
+        for way in range(2):
+            behind = (place.has_down, place.has_up)[way]
+            goes = (chip >= place.chip) if way == 0 else (chip <= place.chip)
+
+            @pl.when(behind & goes)
+            def _():
+                self.line_copy(way, chip).wait_recv()
+                self.total[...] += self.line_in[way, chip].astype(jnp.float32)
+
+        @pl.when(chip != place.chip)
+        def _():
+            self.line_out[chip] = self.total[...].astype(jnp.bfloat16)
+            pl.when(chip > place.chip)(lambda: self.line_copy(0, chip).start())
+            pl.when(chip < place.chip)(lambda: self.line_copy(1, chip).start())
+
+    def begin(self):
+        self.each(self.place.chips - 1, self.hand_over)
+
+    def step(self, index):
+        distance = self.place.chips - 1 - index
+        pl.when(distance > 0)(lambda: self.each(distance - 1, self.hand_over))
+        self.each(distance, self.sum_up)
+
+    def finish(self):
+        place = self.place
+
+        def drain(chip, carry):
+            self.side_copy(chip).wait_send()
+            pl.when(chip != place.chip)(lambda: self.line_copy(0, chip).wait_send())
+            return carry
+
+        lax.fori_loop(0, place.chips, drain, 0)
+
+
+def scatter_scratch(chips, count, width):
+    low = jnp.bfloat16
+    dma = pltpu.SemaphoreType.DMA
+    return [
+        pltpu.VMEM((count, width), jnp.float32),
+        pltpu.VMEM((chips, count, width), low),
+        pltpu.VMEM((chips, count, width), low),
+        pltpu.VMEM((chips, count, width), low),
+        pltpu.VMEM((2, chips, count, width), low),
+        dma((chips,)),
+        dma((chips,)),
+        dma((chips,)),
+        dma((2, chips)),
+    ]
+
+
+def by_rows(count, tile, action):
+    def one(index, carry):
+        action(pl.ds(pl.multiple_of(index * tile, tile), tile))
+        return carry
+
+    lax.fori_loop(0, count // tile, one, 0)
+
+
+def attend_out_kernel(
+    chips,
+    attended_ref,
+    out_ref,
+    rows_ref,
+    branch_ref,
+    gain_ref,
+    shift_ref,
+    bias_ref,
+    up_ref,
+    down_ref,
+    resid_ref,
+    normed_ref,
+    branch_whole,
+    up_whole,
+    down_whole,
+    blocks,
+    line_send,
+    line_recv,
+    up_send,
+    up_recv,
+    down_send,
+    down_recv,
+    own_sem,
+    keep_sem,
+    *scatter,
+):
+    place = Place(chips)
+    count = rows_ref.shape[0]
+    place.greet(True)
+
+    def square(shard, whole, send, recv):
+        half = shard.shape[0] // 2
+        return SquareGather(
+            place,
+            shard,
+            lambda owner: whole.at[owner],
+            lambda owner, which: whole.at[owner, pl.ds(which * half, half)],
+            send,
+            recv,
+        )
+
+    up = square(up_ref, up_whole, up_send, up_recv)
+    down = square(down_ref, down_whole, down_send, down_recv)
+    up.begin()
+    own = [
+        pltpu.make_async_copy(up_ref, up_whole.at[place.dp], own_sem.at[0]),
+        pltpu.make_async_copy(down_ref, down_whole.at[place.dp], own_sem.at[1]),
+    ]
+    own[0].start()
+    own[1].start()
+
+    def term(block, tile):
+        span = pl.ds(pl.multiple_of(block * count, count), count)
+        return jnp.dot(attended_ref[span, :], out_ref[tile], preferred_element_type=jnp.float32)
+
+    sums = LineScatter(place, term, 4, scatter[:5], scatter[5:])
+    sums.begin()
+
+    def copy_in(span):
+        blocks[place.me, span, :] = branch_ref[span, :]
+
+    by_rows(count, 64, copy_in)
+    line = LineGather(place, blocks, line_send, line_recv)
+    line.begin()
+
+    def keep(block):
+        span = pl.ds(pl.multiple_of(block * count, count), count)
+        return pltpu.make_async_copy(blocks.at[block], branch_whole.at[span], keep_sem.at[block])
+
+    def step(index, carry):
+        sums.step(index)
+        pl.when(index < chips - 1)(lambda: line.step(index + 1))
+
+        @pl.when(index == 1)
+        def _():
+            up.middle()
+            down.begin()
+
+        pl.when(index == 2)(down.middle)
+        return carry
+
+    lax.fori_loop(0, chips, step, 0)
+    total = scatter[0]
+
+    def norm(span):
+        resid = rows_ref[span, :].astype(jnp.float32) + total[span, :] + bias_ref[...]
+        resid_ref[span, :] = resid
+        normed_ref[span, :] = norm_rows(resid, gain_ref[...], shift_ref[...]).astype(jnp.bfloat16)
+
+    by_rows(count, 64, norm)
+
+    def store(block, carry):
+        pl.when((block % 2 != place.core))(lambda: line.arrive(block // 2, block % 2))
+        keep(block).start()
+        return carry
+
+    lax.fori_loop(0, 2 * chips, store, 0)
+    sums.finish()
+    line.finish()
+    up.end()
+    down.end()
+    up.finish()
+    down.finish()
+    own[0].wait()
+    own[1].wait()
+
+    def kept(block, carry):
+        keep(block).wait()
+        return carry
+
+    lax.fori_loop(0, 2 * chips, kept, 0)
+
+
+def attend_out_call(attended, out_whole, rows, branch, gain, shift, bias, up, down, chips):
+    count, width = rows.shape
+    total = 2 * chips * count
+    low = jnp.bfloat16
+    vmem = pl.BlockSpec(memory_space=pltpu.VMEM)
+    hbm = pl.BlockSpec(memory_space=pl.ANY)
+    dma = pltpu.SemaphoreType.DMA
+    return pl.pallas_call(
+        functools.partial(attend_out_kernel, chips),
+        out_shape=(
+            jax.ShapeDtypeStruct((count, width), jnp.float32),
+            jax.ShapeDtypeStruct((count, width), low),
+            jax.ShapeDtypeStruct((total, width), low),
+            jax.ShapeDtypeStruct((4,) + up.shape, low),
+            jax.ShapeDtypeStruct((4,) + down.shape, low),
+        ),
+        in_specs=[vmem] * 9,
+        out_specs=(vmem, vmem, hbm, vmem, vmem),
+        scratch_shapes=[
+            pltpu.VMEM((2 * chips, count, width), low),
+            dma((3, chips)),
+            dma((2 * chips,)),
+            dma((4,)),
+            dma((4,)),
+            dma((4,)),
+            dma((4,)),
+            dma((2,)),
+            dma((2 * chips,)),
+        ]
+        + scatter_scratch(chips, count, width),
+        compiler_params=pltpu.CompilerParams(
+            collective_id=1, has_side_effects=True, vmem_limit_bytes=VMEM_LIMIT
+        ),
+        cost_estimate=pl.CostEstimate(flops=10**11, bytes_accessed=0, transcendentals=0),
+        name="attend_out",
+    )(attended, out_whole, rows, branch, gain, shift, bias, up, down)
+
+
+def input_back_kernel(
+    chips,
+    stacked_ref,
+    mix_ref,
+    rows_ref,
+    resid_grad_ref,
+    gain_ref,
+    grad_ref,
+    gain_grad_ref,
+    shift_grad_ref,
+    *scatter,
+):
+    place = Place(chips)
+    count = rows_ref.shape[0]
+    place.greet(False)
+
+    def term(block, tile):
+        span = pl.ds(pl.multiple_of(block * count, count), count)
+        result = None
+        for part in range(3):
+            product = lax.dot_general(
+                stacked_ref[part, span, :],
+                mix_ref[part, tile],
+                (((1,), (1,)), ((), ())),
+                preferred_element_type=jnp.float32,
+            )
+            result = product if result is None else result + product
+        return result
+
+    sums = LineScatter(place, term, 4, scatter[:5], scatter[5:])
+    sums.begin()
+
+    def step(index, carry):
+        sums.step(index)
+        return carry
+
+    lax.fori_loop(0, chips, step, 0)
+    total = scatter[0]
+    gain_grad_ref[...] = jnp.zeros_like(gain_grad_ref)
+    shift_grad_ref[...] = jnp.zeros_like(shift_grad_ref)
+
+    def back(span):
+        rows = rows_ref[span, :].astype(jnp.float32)
+        one_grad = total[span, :]
+        _, hat, inverse = layer_norm_parts(rows, gain_ref[...], 0.0)
+        grad_ref[span, :] = resid_grad_ref[span, :] + layer_norm_back(
+            one_grad, hat, inverse, gain_ref[...]
+        )
+        gain_grad_ref[...] += jnp.sum(one_grad * hat, axis=0, keepdims=True)
+        shift_grad_ref[...] += jnp.sum(one_grad, axis=0, keepdims=True)
+
+    by_rows(count, 64, back)
+    sums.finish()
+
+
+def input_back_call(stacked, mix_whole, rows, resid_grad, gain, chips):
+    count, width = rows.shape
+    vmem = pl.BlockSpec(memory_space=pltpu.VMEM)
+    return pl.pallas_call(
+        functools.partial(input_back_kernel, chips),
+        out_shape=(
+            jax.ShapeDtypeStruct((count, width), jnp.float32),
+            jax.ShapeDtypeStruct((1, width), jnp.float32),
+            jax.ShapeDtypeStruct((1, width), jnp.float32),
+        ),
+        in_specs=[vmem] * 5,
+        out_specs=(vmem,) * 3,
+        scratch_shapes=scatter_scratch(chips, count, width),
+        compiler_params=pltpu.CompilerParams(
+            collective_id=2, has_side_effects=True, vmem_limit_bytes=VMEM_LIMIT
+        ),
+        cost_estimate=pl.CostEstimate(flops=10**11, bytes_accessed=0, transcendentals=0),
+        name="input_back",
+    )(stacked, mix_whole, rows, resid_grad, gain)
 
 
 def tile_scores(query_tile, keys, segment, row_block, col_block):
@@ -252,38 +924,44 @@
     segment = live.astype(jnp.int32)
     first_row = lax.axis_index("mp") * own_rows
     own_live = own_slice(live.reshape(-1), first_row, own_rows)[:, None]
-    own_input = layer_input.astype(jnp.float32)
-    normed_own, hat_one, inv_one = layer_norm_parts(own_input, norm_gains[0], shifts[0])
-    normed_one = gather_rows(normed_own.astype(jnp.bfloat16))
-    mix_full = gather_shards(mix_weight.astype(jnp.bfloat16), 1)
-    out_full = gather_shards(out_weight.astype(jnp.bfloat16), 1)
-    up_full = gather_shards(up_weight.astype(jnp.bfloat16), 0)
-    down_full = gather_shards(down_weight.astype(jnp.bfloat16), 1)
+    low = jnp.bfloat16
+    normed_one, mixed, mix_whole, out_whole = project_call(
+        layer_input,
+        norm_gains[0:1],
+        shifts[0:1],
+        mix_weight.astype(low),
+        out_weight.astype(low),
+        mix_bias,
+        parts // 2,
+    )
+    out_full = out_whole.transpose(1, 0, 2).reshape(local_width, -1)
     out_grad = jnp.where(own_live, cotangent.astype(jnp.float32), 0.0)
     bias_down_grad = jnp.sum(out_grad, axis=0)
-    branch_grad = gather_rows(out_grad.astype(jnp.bfloat16))
-    mixed = jnp.einsum("td,cde->cte", normed_one, mix_full, preferred_element_type=jnp.float32)
-    queries = (
-        (mixed[0] + mix_bias[0])
-        .astype(jnp.bfloat16)
-        .reshape(slots_here, slot_len, heads_here, depth)
-    )
-    keys = mixed[1].astype(jnp.bfloat16).reshape(slots_here, slot_len, heads_here, depth)
-    values = (
-        (mixed[2] + mix_bias[1])
-        .astype(jnp.bfloat16)
-        .reshape(slots_here, slot_len, heads_here, depth)
-    )
+    queries = mixed[0].reshape(slots_here, slot_len, heads_here, depth)
+    keys = mixed[1].reshape(slots_here, slot_len, heads_here, depth)
+    values = mixed[2].reshape(slots_here, slot_len, heads_here, depth)
 
     def attend(item):
         return attention_forward(item[0], item[1], item[2], item[3])
 
     attended, totals = lax.map(attend, (queries, keys, values, segment))
     attended_flat = attended.reshape(group_rows, local_width)
-    attn_part = jnp.dot(attended_flat, out_full, preferred_element_type=jnp.float32)
-    resid_own = own_input + scatter_rows(attn_part) + shifts[1]
-    normed_mid, hat_two, inv_two = layer_norm_parts(resid_own, norm_gains[1], shifts[2])
-    normed_two = gather_rows(normed_mid.astype(jnp.bfloat16))
+    resid_own, normed_mid, branch_grad, up_whole, down_whole = attend_out_call(
+        attended_flat,
+        out_whole,
+        layer_input,
+        out_grad.astype(low),
+        norm_gains[1:2],
+        shifts[2:3],
+        shifts[1:2],
+        up_weight.astype(low),
+        down_weight.astype(low),
+        parts // 2,
+    )
+    _, hat_two, inv_two = layer_norm_parts(resid_own, norm_gains[1], shifts[2])
+    normed_two = gather_rows(normed_mid)
+    up_full = up_whole.reshape(-1, up_whole.shape[2])
+    down_full = down_whole.transpose(1, 0, 2).reshape(down_whole.shape[1], -1)
     hidden = jnp.dot(normed_two, up_full, preferred_element_type=jnp.float32) + up_bias
     active_value, gelu_pull = jax.vjp(tanh_gelu, hidden)
     active = active_value.astype(jnp.bfloat16)
@@ -332,8 +1010,10 @@
             value_grad.reshape(group_rows, local_width),
         ]
     )
-    one_part = jnp.einsum("cte,cde->td", stacked, mix_full, preferred_element_type=jnp.float32)
-    one_grad = scatter_rows(one_part)
+    input_grad, gain_one_grad, shift_one_grad = input_back_call(
+        stacked, mix_whole, layer_input, resid_grad, norm_gains[0:1], parts // 2
+    )
+    gain_one_grad, shift_one_grad = gain_one_grad[0], shift_one_grad[0]
     mix_grad = jnp.einsum("td,cte->cde", normed_one, stacked, preferred_element_type=jnp.float32)
     mix_bias_grad = jnp.stack(
         [
@@ -345,9 +1025,6 @@
     out_owned = scatter_shards(out_weight_grad, 1)
     up_owned = scatter_shards(up_grad, 0)
     down_owned = scatter_shards(down_grad, 1)
-    input_grad = resid_grad + layer_norm_back(one_grad, hat_one, inv_one, norm_gains[0])
-    gain_one_grad = jnp.sum(one_grad * hat_one, axis=0)
-    shift_one_grad = jnp.sum(one_grad, axis=0)
     gain_grad = jnp.stack([gain_one_grad, gain_two_grad])
     shift_grad = jnp.stack([shift_one_grad, bias_out_grad, shift_two_grad, bias_down_grad])
     mix_bias_total, up_bias_total = lax.psum((mix_bias_grad, up_bias_grad), "dp")
@@ -456,6 +1133,256 @@
     )
 
 
+def per_device_any(
+    layer_input,
+    cotangent,
+    lengths,
+    offsets,
+    step,
+    mix_weight,
+    out_weight,
+    up_weight,
+    down_weight,
+    mix_first,
+    out_first,
+    up_first,
+    down_first,
+    mix_second,
+    out_second,
+    up_second,
+    down_second,
+    mix_bias,
+    up_bias,
+    norm_gains,
+    shifts,
+    mix_bias_first,
+    up_bias_first,
+    gains_first,
+    shifts_first,
+    mix_bias_second,
+    up_bias_second,
+    gains_second,
+    shifts_second,
+):
+    own_rows = layer_input.shape[0]
+    parts = lax.axis_size("mp")
+    group_rows = own_rows * parts
+    slots_here = lengths.shape[0]
+    slot_len = group_rows // slots_here
+    local_width = mix_weight.shape[2]
+    depth = HEAD_DIM
+    heads_here = local_width // depth
+    positions = jnp.arange(slot_len, dtype=jnp.int32)
+    live = (positions[None, :] >= offsets[:, None]) & (
+        positions[None, :] < (offsets + lengths)[:, None]
+    )
+    segment = live.astype(jnp.int32)
+    first_row = lax.axis_index("mp") * own_rows
+    own_live = own_slice(live.reshape(-1), first_row, own_rows)[:, None]
+    own_input = layer_input.astype(jnp.float32)
+    normed_own, hat_one, inv_one = layer_norm_parts(own_input, norm_gains[0], shifts[0])
+    normed_one = gather_rows(normed_own.astype(jnp.bfloat16))
+    mix_full = gather_shards(mix_weight.astype(jnp.bfloat16), 1)
+    out_full = gather_shards(out_weight.astype(jnp.bfloat16), 1)
+    up_full = gather_shards(up_weight.astype(jnp.bfloat16), 0)
+    down_full = gather_shards(down_weight.astype(jnp.bfloat16), 1)
+    out_grad = jnp.where(own_live, cotangent.astype(jnp.float32), 0.0)
+    bias_down_grad = jnp.sum(out_grad, axis=0)
+    branch_grad = gather_rows(out_grad.astype(jnp.bfloat16))
+    mixed = jnp.einsum("td,cde->cte", normed_one, mix_full, preferred_element_type=jnp.float32)
+    queries = (
+        (mixed[0] + mix_bias[0])
+        .astype(jnp.bfloat16)
+        .reshape(slots_here, slot_len, heads_here, depth)
+    )
+    keys = mixed[1].astype(jnp.bfloat16).reshape(slots_here, slot_len, heads_here, depth)
+    values = (
+        (mixed[2] + mix_bias[1])
+        .astype(jnp.bfloat16)
+        .reshape(slots_here, slot_len, heads_here, depth)
+    )
+
+    def attend(item):
+        return attention_forward(item[0], item[1], item[2], item[3])
+
+    attended, totals = lax.map(attend, (queries, keys, values, segment))
+    attended_flat = attended.reshape(group_rows, local_width)
+    attn_part = jnp.dot(attended_flat, out_full, preferred_element_type=jnp.float32)
+    resid_own = own_input + scatter_rows(attn_part) + shifts[1]
+    normed_mid, hat_two, inv_two = layer_norm_parts(resid_own, norm_gains[1], shifts[2])
+    normed_two = gather_rows(normed_mid.astype(jnp.bfloat16))
+    hidden = jnp.dot(normed_two, up_full, preferred_element_type=jnp.float32) + up_bias
+    active_value, gelu_pull = jax.vjp(tanh_gelu, hidden)
+    active = active_value.astype(jnp.bfloat16)
+    active_grad = jnp.einsum(
+        "td,fd->tf", branch_grad, down_full, preferred_element_type=jnp.float32
+    )
+    hidden_grad = gelu_pull(active_grad)[0].astype(jnp.bfloat16)
+    two_part = jnp.einsum("tf,df->td", hidden_grad, up_full, preferred_element_type=jnp.float32)
+    two_grad = scatter_rows(two_part)
+    down_part = jnp.dot(active, down_full, preferred_element_type=jnp.float32)
+    down_grad = jnp.einsum("tf,td->fd", active, branch_grad, preferred_element_type=jnp.float32)
+    up_bias_grad = jnp.sum(hidden_grad, axis=0, dtype=jnp.float32)
+    up_grad = jnp.einsum("td,tf->df", normed_two, hidden_grad, preferred_element_type=jnp.float32)
+    resid_grad = out_grad + layer_norm_back(two_grad, hat_two, inv_two, norm_gains[1])
+    attn_branch = gather_rows(resid_grad.astype(jnp.bfloat16))
+    result_own = resid_own + scatter_rows(down_part) + shifts[3]
+    layer_output = jnp.where(own_live, result_own, 0.0).astype(jnp.bfloat16)
+    gain_two_grad = jnp.sum(two_grad * hat_two, axis=0)
+    shift_two_grad = jnp.sum(two_grad, axis=0)
+    bias_out_grad = jnp.sum(resid_grad, axis=0)
+    attended_grad = jnp.einsum(
+        "td,ed->te", attn_branch, out_full, preferred_element_type=jnp.float32
+    ).astype(jnp.bfloat16)
+    out_weight_grad = jnp.einsum(
+        "te,td->ed", attended_flat, attn_branch, preferred_element_type=jnp.float32
+    )
+
+    def attend_back(item):
+        return attention_backward(item[0], item[1], item[2], item[3], item[4], item[5])
+
+    query_grad, key_grad, value_grad = lax.map(
+        attend_back,
+        (
+            queries,
+            keys,
+            values,
+            segment,
+            totals,
+            attended_grad.reshape(slots_here, slot_len, heads_here, depth),
+        ),
+    )
+    stacked = jnp.stack(
+        [
+            query_grad.reshape(group_rows, local_width),
+            key_grad.reshape(group_rows, local_width),
+            value_grad.reshape(group_rows, local_width),
+        ]
+    )
+    one_part = jnp.einsum("cte,cde->td", stacked, mix_full, preferred_element_type=jnp.float32)
+    one_grad = scatter_rows(one_part)
+    mix_grad = jnp.einsum("td,cte->cde", normed_one, stacked, preferred_element_type=jnp.float32)
+    mix_bias_grad = jnp.stack(
+        [
+            jnp.sum(stacked[0], axis=0, dtype=jnp.float32),
+            jnp.sum(stacked[2], axis=0, dtype=jnp.float32),
+        ]
+    )
+    mix_owned = scatter_shards(mix_grad, 1)
+    out_owned = scatter_shards(out_weight_grad, 1)
+    up_owned = scatter_shards(up_grad, 0)
+    down_owned = scatter_shards(down_grad, 1)
+    input_grad = resid_grad + layer_norm_back(one_grad, hat_one, inv_one, norm_gains[0])
+    gain_one_grad = jnp.sum(one_grad * hat_one, axis=0)
+    shift_one_grad = jnp.sum(one_grad, axis=0)
+    gain_grad = jnp.stack([gain_one_grad, gain_two_grad])
+    shift_grad = jnp.stack([shift_one_grad, bias_out_grad, shift_two_grad, bias_down_grad])
+    mix_bias_total, up_bias_total = lax.psum((mix_bias_grad, up_bias_grad), "dp")
+    gain_total, shift_total = lax.psum((gain_grad, shift_grad), ("dp", "mp"))
+    step_count = step[0].astype(jnp.float32)
+    first_fix = 1.0 - BETA_FIRST**step_count
+    second_fix = 1.0 - BETA_SECOND**step_count
+    mix_new = adam_update(
+        mix_weight,
+        mix_owned,
+        mix_first,
+        mix_second,
+        D ** (-0.5),
+        MATRIX_DECAY,
+        first_fix,
+        second_fix,
+    )
+    out_new = adam_update(
+        out_weight,
+        out_owned,
+        out_first,
+        out_second,
+        OUT_FAN ** (-0.5),
+        MATRIX_DECAY,
+        first_fix,
+        second_fix,
+    )
+    up_new = adam_update(
+        up_weight, up_owned, up_first, up_second, D ** (-0.5), MATRIX_DECAY, first_fix, second_fix
+    )
+    down_new = adam_update(
+        down_weight,
+        down_owned,
+        down_first,
+        down_second,
+        FF ** (-0.5),
+        MATRIX_DECAY,
+        first_fix,
+        second_fix,
+    )
+    mix_bias_new = adam_update(
+        mix_bias,
+        mix_bias_total,
+        mix_bias_first,
+        mix_bias_second,
+        SMALL_RATE,
+        0.0,
+        first_fix,
+        second_fix,
+    )
+    up_bias_new = adam_update(
+        up_bias,
+        up_bias_total,
+        up_bias_first,
+        up_bias_second,
+        SMALL_RATE,
+        0.0,
+        first_fix,
+        second_fix,
+    )
+    gains_new = adam_update(
+        norm_gains, gain_total, gains_first, gains_second, SMALL_RATE, 0.0, first_fix, second_fix
+    )
+    shifts_new = adam_update(
+        shifts, shift_total, shifts_first, shifts_second, SMALL_RATE, 0.0, first_fix, second_fix
+    )
+    return (
+        layer_output,
+        input_grad,
+        mix_new[0],
+        mix_new[1],
+        mix_new[2],
+        out_new[0],
+        out_new[1],
+        out_new[2],
+        up_new[0],
+        up_new[1],
+        up_new[2],
+        down_new[0],
+        down_new[1],
+        down_new[2],
+        mix_bias_new[0],
+        mix_bias_new[1],
+        mix_bias_new[2],
+        up_bias_new[0],
+        up_bias_new[1],
+        up_bias_new[2],
+        gains_new[0],
+        gains_new[1],
+        gains_new[2],
+        shifts_new[0],
+        shifts_new[1],
+        shifts_new[2],
+        mix_owned,
+        out_owned,
+        up_owned,
+        down_owned,
+        mix_bias_total,
+        up_bias_total,
+        gain_total,
+        shift_total,
+        mix_new[0].astype(jnp.bfloat16),
+        out_new[0].astype(jnp.bfloat16),
+        up_new[0].astype(jnp.bfloat16),
+        down_new[0].astype(jnp.bfloat16),
+    )
+
+
 def solution(mesh):
     placed = (
         P(("dp", "mp"), None),
@@ -488,8 +1415,9 @@
         P(),
         P(),
     )
+    fits = mesh.shape["dp"] == 4 and mesh.shape["mp"] == 8
     return jax.shard_map(
-        per_device,
+        per_device if fits else per_device_any,
         mesh=mesh,
         in_specs=placed,
         out_specs=(

time: 1080 us -> 1020 us (0.944)
  Pallas kernels: 0 us -> 279 us
  waiting for transfers between devices: 563 us -> 286 us
  matrix products: 219 us -> 184 us
  starting transfers between devices: 46.6 us -> 27.2 us
    pallas_call x0 -> x3, Pallas kernels: none -> 279 us  [the longest x1 107 us: attend_out_call(): pl.pallas_call(functools.partial(attend_out_kernel, chips), out_shape=(ja...]
    all_gather x4 -> x2, waiting for transfers between devices: 193 us -> 77.2 us  [gather_rows(): return lax.all_gather(rows, 'mp', axis=0, tiled=True)]
    reduce_scatter x4 -> x2, waiting for transfers between devices: 248 us -> 156 us  [scatter_rows(): lax.psum_scatter(low, 'mp', scatter_dimension=0, tiled=True)]
    ppermute x40 -> x24, waiting for transfers between devices: 121 us -> 53.3 us  [swap(): lax.ppermute(value, 'dp', [(place, place ^ mask) for place in range(size)])]
    dot_general x3 -> x0, matrix products: 31.7 us -> none  [the longest x1 15.4 us: per_device(): jnp.einsum('cte,cde->td', stacked, mix_full, preferred_element_type=jnp.f...]
    ppermute x40 -> x24, starting transfers between devices: 46.1 us -> 27 us  [swap(): lax.ppermute(value, 'dp', [(place, place ^ mask) for place in range(size)])]
    dynamic_update_slice x16 -> x0, local copies, waits for them, and re-layouts: 15.9 us -> none  [the longest x4 5.61 us: gather_shards(): full = lax.dynamic_update_slice_in_dim(full, from_x, (me ^ 1) * count, axis)]
    unnamed x394 -> x341, local copies, waits for them, and re-layouts: 36.6 us -> 46.7 us
  transfers between devices with their start and end apart: 48 -> 28, of which waited for: 27 -> 14; matrix products, arithmetic and copies ran while one was open for 16% -> 17% of each run, Pallas kernels for 0% -> 8%
where the time goes in v2:
time: 1020 us
  waiting for transfers between devices  286 us (28%)
  Pallas kernels  279 us (27%)
  matrix products  184 us (18%)
  other arithmetic  82 us (8%)
  local copies, waits for them, and re-layouts  81 us (8%)
  blocking collectives  60.8 us (6%)
  starting transfers between devices  27.2 us (3%)
  between operations  19 us (2%)
    reduce_scatter x2, waiting for transfers between devices, scatter_rows(): lax.psum_scatter(low, 'mp', scatter_dimension=0, tiled=True)  156 us
    pallas_call x1, Pallas kernels, attend_out_call(): pl.pallas_call(functools.partial(attend_out_kernel, chips), out_shape=(ja...  107 us
    pallas_call x1, Pallas kernels, input_back_call(): pl.pallas_call(functools.partial(input_back_kernel, chips), out_shape=(ja...  86.6 us
    pallas_call x1, Pallas kernels, project_call(): pl.pallas_call(functools.partial(project_kernel, chips), out_shape=(jax.S...  84.9 us
    all_gather x2, waiting for transfers between devices, gather_rows(): return lax.all_gather(rows, 'mp', axis=0, tiled=True)  77.2 us
    ppermute x24, waiting for transfers between devices, swap(): lax.ppermute(value, 'dp', [(place, place ^ mask) for place in range(size)])  53.3 us
    unnamed x341, local copies, waits for them, and re-layouts  46.7 us
    psum x1, blocking collectives, per_device(): gain_total, shift_total = lax.psum((gain_grad, shift_grad), ('dp', 'mp'))  40.2 us
  transfers between devices with their start and end apart: 28, of which 14 were waited for; matrix products, arithmetic and copies ran while one was open for 17% of the time, Pallas kernels for 8%

profile of v2, /device:TPU:0, one launch (start us, length us, event | category | flops | bytes accessed | tf_op | source)
XLA Modules:
  0.0 1019.2 jit_solution(12525522223533297448)
XLA Ops:
  16.6 84.9 %project.1 = (bf16[2048,2048]{1,0:T(8,128)(2,1)}, bf16[3,2048,256]{2,1,0:T(8,128)(2,1)}, bf16[3,4,512,256]{3,2,1,0:T(8,128)(2,1)}, bf16[4,256,512]{2,1,0:T(8,128)(2,1)}) custom-call(bf16[256,2048]{1,0:T(8,128)(2,1)} %rows_ref.5, f32[1,2048]{1,0:T(1,128)} %get-tuple-element.347.gain_ref, f32[1,2048]{1,0:T(1,128)} %get-tuple-element.292.shift_ref, ...), custom_call_target="tpu_custom_call" | custom-call | flops 45097156608 | tf_op jit(solution)/shard_map/project/pallas_call | solution.py:404
  105.2 2.7 compare_and_fusion.5
  129.3 107.2 %attend_out.1 = (f32[256,2048]{1,0:T(8,128)}, bf16[256,2048]{1,0:T(8,128)(2,1)}, bf16[2048,2048]{1,0:T(8,128)(2,1)}, bf16[4,512,1024]{2,1,0:T(8,128)(2,1)}, bf16[4,1024,512]{2,1,0:T(8,128)(2,1)}) custom-call(bf16[2048,256]{1,0:T(8,128)(2,1)} %copy.386.attended_ref, bf16[4,256,512]{2,1,0:T(8,128)(2,1)} %get-tuple-element.102.out_ref, ...), custom_call_target="tpu_custom_call" | custom-call | flops 99999997952 | tf_op jit(solution)/shard_map/attend_out/pallas_call | solution.py:665
  236.5 6.3 copy.241
  242.9 77.2 %all-gather.3.cloned.1.call-done = bf16[2048,2048]{1,0:T(8,128)(2,1)} async-done(((bf16[256,2048]{1,0:T(8,128)(2,1)}), bf16[2048,2048]{1,0:T(8,128)(2,1)}) %all-gather.3.cloned.1.call-update) | async-done | bytes 8388624 | tf_op jit(solution)/shard_map/all_gather | solution.py:51
  320.1 12.6 %fusion.189 = f32[2048,1024]{1,0:T(8,128)S(1)} fusion(bf16[2048,2048]{1,0:T(8,128)(2,1)} %all-gather.3.cloned.1.call-done, bf16[2048,1024]{1,0:T(8,128)(2,1)} %bitcast.316), kind=kOutput, calls=%fused_computation.345 | convolution fusion | flops 8589934592 | bytes 20971520 | tf_op jit(solution)/shard_map/dot_general | solution.py:965
  332.7 19.7 %convert_reduce_fusion = (f32[1024]{0:T(1024)}, bf16[2048,1024]{1,0:T(8,128)(2,1)S(1)}) fusion(f32[2048,1024]{1,0:T(8,128)S(1)} %fusion.189, f32[1024]{0:T(1024)S(1)} %copy-done.160, bf16[2048,2048]{1,0:T(8,128)(2,1)} %get-tuple-element.107, bf16[1024,2048]{0,1:T(8,128)(2,1)S(1)} %bitcast.272), kind=kOutput, calls=%fused_computation.11 | convolution fusion | flops 8638168064 | bytes 25174016 | tf_op jit(solution)/shard_map/td,fd->tf/dot_general | solution.py:968
  354.3 10.9 %convolution_convert_fusion = bf16[2048,2048]{1,0:T(8,128)(2,1)} fusion(bf16[2048,1024]{1,0:T(8,128)(2,1)S(1)} %get-tuple-element.240, bf16[2048,1024]{1,0:T(8,128)(2,1)S(1)} %bitcast.317), kind=kOutput, calls=%fused_computation.13 | convolution fusion | flops 8594128896 | bytes 16777216 | tf_op jit(solution)/shard_map/tf,df->td/dot_general | solution.py:972
  365.3 17.8 %convolution_convert_fusion.1 = bf16[2048,2048]{1,0:T(8,128)(2,1)} fusion(bf16[1024,2048]{0,1:T(8,128)(2,1)} %bitcast.271, f32[2048,1024]{1,0:T(8,128)} %copy-done.164, f32[1024]{0:T(1024)S(1)} %copy-done.160), kind=kOutput, calls=%fused_computation.14 | convolution fusion | flops 8615100416 | bytes 20975616 | tf_op jit(solution)/shard_map/dot_general | solution.py:974
  385.3 68.2 %reduce-scatter.5.cloned.1.call-done = bf16[256,2048]{1,0:T(8,128)(2,1)} async-done(((bf16[2048,2048]{1,0:T(8,128)(2,1)}), bf16[256,2048]{1,0:T(8,128)(2,1)}) %reduce-scatter.5.cloned.1.call-update) | async-done | bytes 1048592 | tf_op jit(solution)/shard_map/reduce_scatter | solution.py:56
  453.6 2.8 fusion.16
  456.4 87.5 %reduce-scatter.3.cloned.1.call-done = bf16[256,2048]{1,0:T(8,128)(2,1)} async-done(((bf16[2048,2048]{1,0:T(8,128)(2,1)}), bf16[256,2048]{1,0:T(8,128)(2,1)}) %reduce-scatter.3.cloned.1.call-update) | async-done | bytes 1048592 | tf_op jit(solution)/shard_map/reduce_scatter | solution.py:56
  543.9 4.9 fusion.165
  551.2 13.0 %fusion.197 = f32[2048,1024]{1,0:T(8,128)S(1)} fusion(bf16[2048,2048]{1,0:T(8,128)(2,1)} %all-gather.3.cloned.1.call-done, bf16[2048,1024]{1,0:T(8,128)(2,1)} %copy-done.165), kind=kOutput, calls=%fused_computation.353 | convolution fusion | flops 8589934592 | bytes 20971520 | tf_op jit(solution)/shard_map/td,tf->df/dot_general | solution.py:977
  564.2 3.2 copy-done.99
  570.2 16.8 %fusion.154 = f32[1024,2048]{1,0:T(8,128)S(1)} fusion(bf16[2048,2048]{1,0:T(8,128)(2,1)} %get-tuple-element.107, f32[2048,1024]{1,0:T(8,128)} %copy-done.164, f32[1024]{0:T(1024)S(1)} %copy-done.160), kind=kOutput, calls=%fused_computation.322 | convolution fusion | flops 8610906112 | bytes 25169920 | tf_op jit(solution)/shard_map/tf,td->fd/dot_general | solution.py:975
  587.0 3.3 copy-done.100
  597.7 8.7 collective-permute-done.19
  609.2 8.4 collective-permute-done.12
  621.3 3.2 convert_add_fusion.3
  626.7 4.3 collective-permute-done.22
  631.0 11.2 %collective-permute-done.20 = bf16[1024,256]{1,0:T(8,128)(2,1)} collective-permute-done((bf16[1024,256]{1,0:T(8,128)(2,1)S(1)}, bf16[1024,256]{1,0:T(8,128)(2,1)}, u32[]{:S(2)}, u32[]{:S(2)}) %collective-permute-start.20) | collective-permute-done | bytes 524320 | tf_op jit(solution)/shard_map/ppermute | solution.py:61
  642.3 3.4 convert_add_fusion.1
  648.7 3.0 copy.325
  657.2 3.4 collective-permute-done.21
  662.3 6.3 fusion.155
  668.6 4.4 fusion.157
  673.0 5.8 convolution_convert_fusion.2
  703.4 2.4 convolution_add_fusion.5
  709.0 2.4 fusion.45
  718.0 6.1 fusion.196
  731.6 6.2 multiply_reduce_fusion.2
  740.1 3.8 multiply_convert_fusion.4
  751.9 3.8 multiply_reduce_fusion.7
  763.5 5.7 multiply_reduce_fusion.5
  781.1 7.9 maximum_maximum_fusion.stacked_ref
  788.9 12.0 %fusion.7 = f32[3,256,2048]{2,1,0:T(8,128)} fusion(bf16[2048,2048]{1,0:T(8,128)(2,1)} %get-tuple-element.110, bf16[1,512,256]{2,1,0:T(8,128)(2,1)S(1)} %copy-done.131, bf16[1,512,256]{2,1,0:T(8,128)(2,1)S(1)} %copy-done.133, bf16[1,512,256]{2,1,0:T(8,128)(2,1)S(1)} %copy-done.134, bf16[1,512,256]{2,1,0:T(8,128)(2,1)S(1)} %copy-done.132, ...), kind=kOutput, calls=%fused_computation.9 | convolution fusion | flops 6480199680 | bytes 17825792 | tf_op jit(solution)/shard_map/td,cte->cde/dot_general | solution.py:1017
  800.9 86.6 %input_back.1 = (f32[256,2048]{1,0:T(8,128)}, f32[1,2048]{1,0:T(1,128)}, f32[1,2048]{1,0:T(1,128)}) custom-call(bf16[3,2048,256]{2,1,0:T(8,128)(2,1)} %maximum_maximum_fusion.stacked_ref, bf16[3,4,512,256]{3,2,1,0:T(8,128)(2,1)} %get-tuple-element.108.mix_ref, bf16[256,2048]{1,0:T(8,128)(2,1)} %rows_ref.5, f32[256,2048]{1,0:T(8,128)} %copy-done.84, ...), custom_call_target="tpu_custom_call" | custom-call | flops 99999997952 | tf_op jit(solution)/shard_map/input_back/pallas_call | solution.py:754
  887.6 3.0 fusion.65
  893.2 20.6 %all-reduce.1 = (f32[2,256]{1,0:T(2,128)S(1)}, f32[1024]{0:T(1024)S(1)}) all-reduce(f32[2,256]{1,0:T(2,128)S(1)} %pad_maximum_fusion.7, f32[1024]{0:T(1024)} %get-tuple-element.239), channel_id=1, replica_groups=mesh['dp'=4,'mp'=8] {'dp'}, use_global_device_ids=true, to_apply=%region_38.39 | all-reduce | flops 1536 | bytes 12288 | tf_op jit(solution)/shard_map/psum | solution.py:1030
  915.4 40.2 %all-reduce = (f32[2,2048]{1,0:T(2,128)S(1)}, f32[4,2048]{1,0:T(4,128)S(1)}) all-reduce(f32[2,2048]{1,0:T(2,128)S(1)} %pad_maximum_fusion.6, f32[4,2048]{1,0:T(4,128)S(1)} %pad_maximum_fusion.5), channel_id=1, replica_groups=mesh['dp'=4,'mp'=8] {'dp','mp'}, use_global_device_ids=true, to_apply=%region_42.43 | all-reduce | flops 12288 | bytes 98304 | tf_op jit(solution)/shard_map/psum | solution.py:1031
  967.8 7.4 collective-permute-done.8
  979.0 4.6 collective-permute-done.2
  988.9 3.7 collective-permute-done.3
  994.4 3.2 fusion.161
  999.8 3.0 copy.330
  1002.8 3.0 copy.332
  1009.1 3.1 copy.459
  (533 shorter events, 170.5 us)
Async XLA Ops:
  7.2 312.8 %all-gather.3.cloned.1.call-start = ((), (), s32[]{:S(2)}) async-start(), calls=%async_computation.2 | async-start | bytes 9437184 | tf_op jit(solution)/shard_map/all_gather | solution.py:51
  103.9 19.2 %copy-start.85 = (bf16[512,2,128]{2,1,0:T(2,128)(2,1)}, bf16[512,2,128]{2,1,0:T(2,128)(2,1)S(1)}, u32[]{:S(2)}) copy-start(bf16[512,2,128]{2,1,0:T(2,128)(2,1)S(1)} %slice.233) | copy-start | bytes 786436
  103.9 19.8 %copy-start.41 = (bf16[512,2,128]{2,1,0:T(2,128)(2,1)}, bf16[512,2,128]{2,1,0:T(2,128)(2,1)S(1)}, u32[]{:S(2)}) copy-start(bf16[512,2,128]{2,1,0:T(2,128)(2,1)S(1)} %slice.245) | copy-start | bytes 786436
  104.0 21.1 %copy-start.87 = (bf16[512,2,128]{2,1,0:T(2,128)(2,1)}, bf16[512,2,128]{2,1,0:T(2,128)(2,1)S(1)}, u32[]{:S(2)}) copy-start(bf16[512,2,128]{2,1,0:T(2,128)(2,1)S(1)} %slice.252) | copy-start | bytes 786436
  104.1 21.7 %copy-start.109 = (bf16[512,2,128]{2,1,0:T(2,128)(2,1)}, bf16[512,2,128]{2,1,0:T(2,128)(2,1)S(1)}, u32[]{:S(2)}) copy-start(bf16[512,2,128]{2,1,0:T(2,128)(2,1)S(1)} %slice.259) | copy-start | bytes 786436
  128.0 108.4 %copy-start.158 = (pred[256]{0:T(512)(128)(4,1)}, pred[256]{0:T(512)(128)(4,1)S(1)}, u32[]{:S(2)}) copy-start(pred[256]{0:T(512)(128)(4,1)S(1)} %fusion.128) | copy-start | bytes 772
  236.5 217.1 %reduce-scatter.5.cloned.1.call-start = ((), (), s32[]{:S(2)}) async-start(), calls=%async_computation.4 | async-start | bytes 9437184 | tf_op jit(solution)/shard_map/reduce_scatter | solution.py:56
  332.7 19.7 %copy-start.164 = (f32[2048,1024]{1,0:T(8,128)}, f32[2048,1024]{1,0:T(8,128)S(1)}, u32[]{:S(2)}) copy-start(f32[2048,1024]{1,0:T(8,128)S(1)} %fusion.189) | copy-start | bytes 25165828
  332.7 21.6 %copy-start.163 = (bf16[4,512,1024]{2,1,0:T(8,128)(2,1)S(1)}, bf16[4,512,1024]{2,1,0:T(8,128)(2,1)}, u32[]{:S(2)}) copy-start(bf16[4,512,1024]{2,1,0:T(8,128)(2,1)} %get-tuple-element.105) | copy-start | bytes 12582916
  365.3 178.6 %reduce-scatter.3.cloned.1.call-start = ((), (), s32[]{:S(2)}) async-start(), calls=%async_computation.3 | async-start | bytes 9437184 | tf_op jit(solution)/shard_map/reduce_scatter | solution.py:56
  383.2 289.8 %all-gather.5.cloned.1.call-start = ((), (), s32[]{:S(2)}) async-start(), calls=%async_computation.5 | async-start | bytes 9437184 | tf_op jit(solution)/shard_map/all_gather | solution.py:51
  384.7 68.8 %copy-start.150 = (f32[1,2048]{1,0:T(1,128)S(1)}, f32[1,2048]{1,0:T(1,128)}, u32[]{:S(2)}) copy-start(f32[1,2048]{1,0:T(1,128)} %get-tuple-element.348.gain_ref) | copy-start | bytes 24580
  385.3 158.6 %copy-start.105 = (bf16[256,2048]{1,0:T(8,128)(2,1)S(1)}, bf16[256,2048]{1,0:T(8,128)(2,1)}, u32[]{:S(2)}) copy-start(bf16[256,2048]{1,0:T(8,128)(2,1)} %param.30) | copy-start | bytes 3145732
  385.3 158.6 %copy-start.156 = (f32[1,2048]{1,0:T(1,128)S(1)}, f32[1,2048]{1,0:T(1,128)}, u32[]{:S(2)}) copy-start(f32[1,2048]{1,0:T(1,128)} %get-tuple-element.289) | copy-start | bytes 24580
  385.3 158.6 %copy-start.159 = (pred[256]{0:T(512)(128)(4,1)S(1)}, pred[256]{0:T(512)(128)(4,1)}, u32[]{:S(2)}) copy-start(pred[256]{0:T(512)(128)(4,1)} %copy-done.158) | copy-start | bytes 772
  568.7 26.4 %collective-permute-start.13 = (bf16[256,1024]{1,0:T(8,128)(2,1)S(1)}, bf16[256,1024]{1,0:T(8,128)(2,1)S(1)}, u32[]{:S(2)}, u32[]{:S(2)}) collective-permute-start(bf16[256,1024]{1,0:T(8,128)(2,1)S(1)} %get-tuple-element.257), channel_id=1, source_target_pairs={{0,8},{8,0},{16,24},{24,16},{1,9},{9,1},{17,25},{25,17},{2,10},{10... | collective-permute-start | bytes 1572872 | tf_op jit(solution)/shard_map/ppermute | solution.py:61
  591.6 14.9 %collective-permute-start.19 = (bf16[1024,256]{1,0:T(8,128)(2,1)S(1)}, bf16[1024,256]{1,0:T(8,128)(2,1)S(1)}, u32[]{:S(2)}, u32[]{:S(2)}) collective-permute-start(bf16[1024,256]{1,0:T(8,128)(2,1)S(1)} %get-tuple-element.251), channel_id=1, source_target_pairs={{0,8},{8,0},{16,24},{24,16},{1,9},{9,1},{17,25},{25,17},{2,10},{10... | collective-permute-start | bytes 1572872 | tf_op jit(solution)/shard_map/ppermute | solution.py:61
  592.2 25.5 %collective-permute-start.12 = (bf16[256,1024]{1,0:T(8,128)(2,1)}, bf16[256,1024]{1,0:T(8,128)(2,1)S(1)}, u32[]{:S(2)}, u32[]{:S(2)}) collective-permute-start(bf16[256,1024]{1,0:T(8,128)(2,1)} %get-tuple-element.254), channel_id=1, source_target_pairs={{0,8},{8,0},{16,24},{24,16},{1,9},{9,1},{17,25},{25,17},{2,10},{10... | collective-permute-start | bytes 1572872 | tf_op jit(solution)/shard_map/ppermute | solution.py:61
  593.6 25.6 %collective-permute-start.16 = (bf16[256,1024]{1,0:T(8,128)(2,1)S(1)}, bf16[256,1024]{1,0:T(8,128)(2,1)}, u32[]{:S(2)}, u32[]{:S(2)}) collective-permute-start(bf16[256,1024]{1,0:T(8,128)(2,1)S(1)} %get-tuple-element.255), channel_id=1, source_target_pairs={{0,16},{8,24},{16,0},{24,8},{1,17},{9,25},{17,1},{25,9},{2,18},{10... | collective-permute-start | bytes 1572872 | tf_op jit(solution)/shard_map/ppermute | solution.py:61
  596.4 23.3 %collective-permute-start.14 = (bf16[256,1024]{1,0:T(8,128)(2,1)S(1)}, bf16[256,1024]{1,0:T(8,128)(2,1)}, u32[]{:S(2)}, u32[]{:S(2)}) collective-permute-start(bf16[256,1024]{1,0:T(8,128)(2,1)S(1)} %add_convert_fusion.3), channel_id=1, source_target_pairs={{0,16},{8,24},{16,0},{24,8},{1,17},{9,25},{17,1},{25,9},{2,18},{10... | collective-permute-start | bytes 1572872 | tf_op jit(solution)/shard_map/ppermute | solution.py:61
  597.0 28.3 %collective-permute-start.18 = (bf16[1024,256]{1,0:T(8,128)(2,1)}, bf16[1024,256]{1,0:T(8,128)(2,1)S(1)}, u32[]{:S(2)}, u32[]{:S(2)}) collective-permute-start(bf16[1024,256]{1,0:T(8,128)(2,1)} %get-tuple-element.248), channel_id=1, source_target_pairs={{0,8},{8,0},{16,24},{24,16},{1,9},{9,1},{17,25},{25,17},{2,10},{10... | collective-permute-start | bytes 1572872 | tf_op jit(solution)/shard_map/ppermute | solution.py:61
  606.4 24.6 %collective-permute-start.22 = (bf16[1024,256]{1,0:T(8,128)(2,1)}, bf16[1024,256]{1,0:T(8,128)(2,1)}, u32[]{:S(2)}, u32[]{:S(2)}) collective-permute-start(bf16[1024,256]{1,0:T(8,128)(2,1)} %get-tuple-element.249), channel_id=1, source_target_pairs={{0,16},{8,24},{16,0},{24,8},{1,17},{9,25},{17,1},{25,9},{2,18},{10... | collective-permute-start | bytes 1572872 | tf_op jit(solution)/shard_map/ppermute | solution.py:61
  617.7 24.6 %collective-permute-start.20 = (bf16[1024,256]{1,0:T(8,128)(2,1)S(1)}, bf16[1024,256]{1,0:T(8,128)(2,1)}, u32[]{:S(2)}, u32[]{:S(2)}) collective-permute-start(bf16[1024,256]{1,0:T(8,128)(2,1)S(1)} %add_convert_fusion.1), channel_id=1, source_target_pairs={{0,16},{8,24},{16,0},{24,8},{1,17},{9,25},{17,1},{25,9},{2,18},{10... | collective-permute-start | bytes 1572872 | tf_op jit(solution)/shard_map/ppermute | solution.py:61
  619.1 36.1 %collective-permute-start.15 = (bf16[256,1024]{1,0:T(8,128)(2,1)}, bf16[256,1024]{1,0:T(8,128)(2,1)}, u32[]{:S(2)}, u32[]{:S(2)}) collective-permute-start(bf16[256,1024]{1,0:T(8,128)(2,1)} %get-tuple-element.256), channel_id=1, source_target_pairs={{0,16},{8,24},{16,0},{24,8},{1,17},{9,25},{17,1},{25,9},{2,18},{10... | collective-permute-start | bytes 1572872 | tf_op jit(solution)/shard_map/ppermute | solution.py:61
  619.8 40.9 %collective-permute-start.21 = (bf16[1024,256]{1,0:T(8,128)(2,1)}, bf16[1024,256]{1,0:T(8,128)(2,1)}, u32[]{:S(2)}, u32[]{:S(2)}) collective-permute-start(bf16[1024,256]{1,0:T(8,128)(2,1)} %get-tuple-element.250), channel_id=1, source_target_pairs={{0,16},{8,24},{16,0},{24,8},{1,17},{9,25},{17,1},{25,9},{2,18},{10... | collective-permute-start | bytes 1572872 | tf_op jit(solution)/shard_map/ppermute | solution.py:61
  626.2 20.1 %copy-start.95 = (f32[3,512,256]{2,1,0:T(8,128)S(1)}, f32[3,512,256]{2,1,0:T(8,128)}, u32[]{:S(2)}) copy-start(f32[3,512,256]{2,1,0:T(8,128)} %param.34) | copy-start | bytes 4718596
  626.2 29.1 %collective-permute-start.17 = (bf16[256,1024]{1,0:T(8,128)(2,1)}, bf16[256,1024]{1,0:T(8,128)(2,1)}, u32[]{:S(2)}, u32[]{:S(2)}) collective-permute-start(bf16[256,1024]{1,0:T(8,128)(2,1)} %get-tuple-element.253), channel_id=1, source_target_pairs={{0,8},{8,0},{16,24},{24,16},{1,9},{9,1},{17,25},{25,17},{2,10},{10... | collective-permute-start | bytes 1572872 | tf_op jit(solution)/shard_map/ppermute | solution.py:61
  645.6 15.0 %collective-permute-start.23 = (bf16[1024,256]{1,0:T(8,128)(2,1)}, bf16[1024,256]{1,0:T(8,128)(2,1)S(1)}, u32[]{:S(2)}, u32[]{:S(2)}) collective-permute-start(bf16[1024,256]{1,0:T(8,128)(2,1)} %get-tuple-element.247), channel_id=1, source_target_pairs={{0,8},{8,0},{16,24},{24,16},{1,9},{9,1},{17,25},{25,17},{2,10},{10... | collective-permute-start | bytes 1572872 | tf_op jit(solution)/shard_map/ppermute | solution.py:61
  678.9 20.8 %copy-start.89 = (bf16[512,256]{0,1:T(8,128)(2,1)}, bf16[512,256]{0,1:T(8,128)(2,1)S(1)}, u32[]{:S(2)}) copy-start(bf16[512,256]{0,1:T(8,128)(2,1)S(1)} %get-tuple-element.288) | copy-start | bytes 786436
  678.9 26.9 %copy-start.49 = (bf16[512,256]{0,1:T(8,128)(2,1)}, bf16[512,256]{0,1:T(8,128)(2,1)S(1)}, u32[]{:S(2)}) copy-start(bf16[512,256]{0,1:T(8,128)(2,1)S(1)} %get-tuple-element.287) | copy-start | bytes 786436
  726.3 238.1 %collective-permute-start.6 = (bf16[256,256]{1,0:T(8,128)(2,1)}, bf16[256,256]{1,0:T(8,128)(2,1)}, u32[]{:S(2)}, u32[]{:S(2)}) collective-permute-start(bf16[256,256]{1,0:T(8,128)(2,1)} %get-tuple-element.279), channel_id=1, source_target_pairs={{0,8},{8,0},{16,24},{24,16},{1,9},{9,1},{17,25},{25,17},{2,10},{10... | collective-permute-start | bytes 393224 | tf_op jit(solution)/shard_map/ppermute | solution.py:61
  726.8 241.0 %collective-permute-start.10 = (bf16[256,256]{1,0:T(8,128)(2,1)}, bf16[256,256]{1,0:T(8,128)(2,1)}, u32[]{:S(2)}, u32[]{:S(2)}) collective-permute-start(bf16[256,256]{1,0:T(8,128)(2,1)} %get-tuple-element.280), channel_id=1, source_target_pairs={{0,16},{8,24},{16,0},{24,8},{1,17},{9,25},{17,1},{25,9},{2,18},{10... | collective-permute-start | bytes 393224 | tf_op jit(solution)/shard_map/ppermute | solution.py:61
  728.3 231.5 %collective-permute-start.7 = (bf16[256,256]{1,0:T(8,128)(2,1)}, bf16[256,256]{1,0:T(8,128)(2,1)}, u32[]{:S(2)}, u32[]{:S(2)}) collective-permute-start(bf16[256,256]{1,0:T(8,128)(2,1)} %get-tuple-element.282), channel_id=1, source_target_pairs={{0,8},{8,0},{16,24},{24,16},{1,9},{9,1},{17,25},{25,17},{2,10},{10... | collective-permute-start | bytes 393224 | tf_op jit(solution)/shard_map/ppermute | solution.py:61
  887.6 67.9 %copy-start.152 = (f32[2,2048]{1,0:T(2,128)S(1)}, f32[2,2048]{1,0:T(2,128)}, u32[]{:S(2)}) copy-start(f32[2,2048]{1,0:T(2,128)} %param.48) | copy-start | bytes 49156
  890.7 71.4 %copy-start.129 = (f32[256,2048]{1,0:T(8,128)S(1)}, f32[256,2048]{1,0:T(8,128)}, u32[]{:S(2)}) copy-start(f32[256,2048]{1,0:T(8,128)} %copy-done.128) | copy-start | bytes 6291460
  890.7 87.5 %collective-permute-start = (bf16[3,256,256]{1,2,0:T(8,128)(2,1)}, bf16[3,256,256]{1,2,0:T(8,128)(2,1)S(1)}, u32[]{:S(2)}, u32[]{:S(2)}) collective-permute-start(bf16[3,256,256]{1,2,0:T(8,128)(2,1)} %get-tuple-element.260), channel_id=1, source_target_pairs={{0,8},{8,0},{16,24},{24,16},{1,9},{9,1},{17,25},{25,17},{2,10},{10... | collective-permute-start | bytes 1179656 | tf_op jit(solution)/shard_map/ppermute | solution.py:61
  891.1 72.0 %collective-permute-start.1 = (bf16[3,256,256]{1,2,0:T(8,128)(2,1)}, bf16[3,256,256]{1,2,0:T(8,128)(2,1)S(1)}, u32[]{:S(2)}, u32[]{:S(2)}) collective-permute-start(bf16[3,256,256]{1,2,0:T(8,128)(2,1)} %get-tuple-element.263), channel_id=1, source_target_pairs={{0,8},{8,0},{16,24},{24,16},{1,9},{9,1},{17,25},{25,17},{2,10},{10... | collective-permute-start | bytes 1179656 | tf_op jit(solution)/shard_map/ppermute | solution.py:61
  913.8 71.4 %copy-start.161 = (f32[1024]{0:T(1024)}, f32[1024]{0:T(1024)S(1)}, u32[]{:S(2)}) copy-start(f32[1024]{0:T(1024)S(1)} %get-tuple-element.422) | copy-start | bytes 12292
  913.8 71.4 %copy-start.162 = (f32[2,256]{1,0:T(2,128)}, f32[2,256]{1,0:T(2,128)S(1)}, u32[]{:S(2)}) copy-start(f32[2,256]{1,0:T(2,128)S(1)} %get-tuple-element.421) | copy-start | bytes 6148
  955.5 29.6 %copy-start.155 = (f32[4,2048]{1,0:T(4,128)}, f32[4,2048]{1,0:T(4,128)S(1)}, u32[]{:S(2)}) copy-start(f32[4,2048]{1,0:T(4,128)S(1)} %get-tuple-element.424) | copy-start | bytes 98308
  955.6 29.6 %copy-start.157 = (f32[2,2048]{1,0:T(2,128)}, f32[2,2048]{1,0:T(2,128)S(1)}, u32[]{:S(2)}) copy-start(f32[2,2048]{1,0:T(2,128)S(1)} %get-tuple-element.423) | copy-start | bytes 49156
  959.8 19.2 %collective-permute-start.4 = (bf16[3,256,256]{1,2,0:T(8,128)(2,1)}, bf16[3,256,256]{1,2,0:T(8,128)(2,1)S(1)}, u32[]{:S(2)}, u32[]{:S(2)}) collective-permute-start(bf16[3,256,256]{1,2,0:T(8,128)(2,1)} %get-tuple-element.261), channel_id=1, source_target_pairs={{0,16},{8,24},{16,0},{24,8},{1,17},{9,25},{17,1},{25,9},{2,18},{10... | collective-permute-start | bytes 1179656 | tf_op jit(solution)/shard_map/ppermute | solution.py:61
  963.0 12.1 %collective-permute-start.8 = (bf16[256,256]{1,0:T(8,128)(2,1)S(1)}, bf16[256,256]{1,0:T(8,128)(2,1)S(1)}, u32[]{:S(2)}, u32[]{:S(2)}) collective-permute-start(bf16[256,256]{1,0:T(8,128)(2,1)S(1)} %add_convert_fusion.5), channel_id=1, source_target_pairs={{0,16},{8,24},{16,0},{24,8},{1,17},{9,25},{17,1},{25,9},{2,18},{10... | collective-permute-start | bytes 393224 | tf_op jit(solution)/shard_map/ppermute | solution.py:61
  964.4 19.2 %collective-permute-start.2 = (bf16[3,256,256]{1,2,0:T(8,128)(2,1)S(1)}, bf16[3,256,256]{1,2,0:T(8,128)(2,1)S(1)}, u32[]{:S(2)}, u32[]{:S(2)}) collective-permute-start(bf16[3,256,256]{1,2,0:T(8,128)(2,1)S(1)} %fusion.62), channel_id=1, source_target_pairs={{0,16},{8,24},{16,0},{24,8},{1,17},{9,25},{17,1},{25,9},{2,18},{10... | collective-permute-start | bytes 1179656 | tf_op jit(solution)/shard_map/ppermute | solution.py:61
  967.7 19.5 %collective-permute-start.9 = (bf16[256,256]{1,0:T(8,128)(2,1)}, bf16[256,256]{1,0:T(8,128)(2,1)S(1)}, u32[]{:S(2)}, u32[]{:S(2)}) collective-permute-start(bf16[256,256]{1,0:T(8,128)(2,1)} %get-tuple-element.281), channel_id=1, source_target_pairs={{0,16},{8,24},{16,0},{24,8},{1,17},{9,25},{17,1},{25,9},{2,18},{10... | collective-permute-start | bytes 393224 | tf_op jit(solution)/shard_map/ppermute | solution.py:61
  975.1 17.4 %collective-permute-start.3 = (bf16[3,256,256]{1,2,0:T(8,128)(2,1)S(1)}, bf16[3,256,256]{1,2,0:T(8,128)(2,1)S(1)}, u32[]{:S(2)}, u32[]{:S(2)}) collective-permute-start(bf16[3,256,256]{1,2,0:T(8,128)(2,1)S(1)} %get-tuple-element.262), channel_id=1, source_target_pairs={{0,16},{8,24},{16,0},{24,8},{1,17},{9,25},{17,1},{25,9},{2,18},{10... | collective-permute-start | bytes 1179656 | tf_op jit(solution)/shard_map/ppermute | solution.py:61
  978.3 9.0 collective-permute-start.11
  985.2 7.8 collective-permute-start.5
  (146 other events, 743.0 us)
Sparse Core Ops, SparseCore 0:
  236.6 83.4 all-gather.2
  365.4 88.1 reduce-scatter.4
  455.9 87.9 reduce-scatter.2
  551.3 80.3 all-gather.4

commit v3 on v2

--- a/solution.py
+++ b/solution.py
@@ -103,6 +103,8 @@
 
 MESH = pl.DeviceIdType.MESH
 VMEM_LIMIT = 60 * 1024 * 1024
+TURNED = (((1,), (1,)), ((), ()))
+CROSSED = (((0,), (0,)), ((), ()))
 
 
 class Place:
@@ -123,7 +125,7 @@
         self.x_way = (self.x_peer, self.me)
         self.y_way = (self.y_peer, self.me)
 
-    def greet(self, square):
+    def greet(self, square, everyone=False):
         barrier = pltpu.get_barrier_semaphore()
 
         def signal(device):
@@ -137,6 +139,18 @@
             signal(self.x_way)
             signal(self.y_way)
             count = count + 2
+        if everyone:
+            signal((self.across, self.me))
+            count = count + 1
+
+            def beyond(chip, carry):
+                far = (chip > self.chip + 1) | (chip < self.chip - 1)
+                pl.when(far)(lambda: signal((self.dp, 2 * chip + self.core)))
+                return carry
+
+            lax.fori_loop(0, self.chips, beyond, 0)
+            near = self.has_up.astype(jnp.int32) + self.has_down.astype(jnp.int32)
+            count = count + (self.chips - 1) - near
         pl.semaphore_wait(barrier, count)
 
 
@@ -152,62 +166,70 @@
 
 
 class LineGather:
-    def __init__(self, place, blocks, send, recv):
+    def __init__(self, place, blocks, send, recv, parts=1):
         self.place, self.blocks, self.send, self.recv = place, blocks, send, recv
-
-    def copy(self, way, chip):
+        self.parts = parts
+
+    def copy(self, way, chip, part=0):
         place = self.place
-        block = 2 * chip + place.core
+        piece = chip * self.parts + part
+        block = 2 * piece + place.core
         device = (place.up, place.down, place.side)[way]
         return remote(
             self.blocks.at[block],
             self.blocks.at[block],
-            self.send.at[way, chip],
+            self.send.at[way, piece],
             self.recv.at[block],
             device,
         )
 
-    def arrive(self, chip, core):
-        place = self.place
-        block = 2 * chip + core
+    def arrive(self, chip, core, part=0):
+        piece = chip * self.parts + part
+        block = 2 * piece + core
         remote(
             self.blocks.at[block],
             self.blocks.at[block],
-            self.send.at[2, chip],
+            self.send.at[2, piece],
             self.recv.at[block],
-            place.side,
+            self.place.side,
         ).wait_recv()
 
     def begin(self):
         place = self.place
-        pl.when(place.has_up)(lambda: self.copy(0, place.chip).start())
-        pl.when(place.has_down)(lambda: self.copy(1, place.chip).start())
-        self.copy(2, place.chip).start()
-
-    def step(self, distance):
+        for part in range(self.parts):
+            pl.when(place.has_up)(lambda: self.copy(0, place.chip, part).start())
+            pl.when(place.has_down)(lambda: self.copy(1, place.chip, part).start())
+            self.copy(2, place.chip, part).start()
+
+    def step(self, distance, part=0):
         place = self.place
         low = place.chip - distance
         high = place.chip + distance
 
         @pl.when(low >= 0)
         def _():
-            self.arrive(low, place.core)
-            pl.when(place.has_up)(lambda: self.copy(0, low).start())
-            self.copy(2, low).start()
+            self.arrive(low, place.core, part)
+            pl.when(place.has_up)(lambda: self.copy(0, low, part).start())
+            self.copy(2, low, part).start()
 
         @pl.when(high < place.chips)
         def _():
-            self.arrive(high, place.core)
-            pl.when(place.has_down)(lambda: self.copy(1, high).start())
-            self.copy(2, high).start()
+            self.arrive(high, place.core, part)
+            pl.when(place.has_down)(lambda: self.copy(1, high, part).start())
+            self.copy(2, high, part).start()
 
     def finish(self):
         place = self.place
 
         def drain(chip, carry):
-            pl.when(place.has_up & (chip <= place.chip))(lambda: self.copy(0, chip).wait_send())
-            pl.when(place.has_down & (chip >= place.chip))(lambda: self.copy(1, chip).wait_send())
-            self.copy(2, chip).wait_send()
+            for part in range(self.parts):
+                pl.when(place.has_up & (chip <= place.chip))(
+                    lambda: self.copy(0, chip, part).wait_send()
+                )
+                pl.when(place.has_down & (chip >= place.chip))(
+                    lambda: self.copy(1, chip, part).wait_send()
+                )
+                self.copy(2, chip, part).wait_send()
             return carry
 
         lax.fori_loop(0, place.chips, drain, 0)
@@ -433,7 +455,7 @@
 class LineScatter:
     def __init__(self, place, term, tiles, bufs, sems):
         self.place, self.term, self.tiles = place, term, tiles
-        self.total, self.side_out, self.side_in, self.line_out, self.line_in = bufs
+        self.total, self.side_out, self.side_in, self.line_in = bufs
         self.side_send, self.side_recv, self.line_send, self.line_recv = sems
 
     def side_copy(self, chip):
@@ -446,13 +468,28 @@
         )
 
     def line_copy(self, way, chip):
+        place = self.place
+        next_chip = place.chip + 1 - 2 * way
+        slot = jnp.where((way == 1) & (chip == next_chip), place.chips, chip)
         return remote(
-            self.line_out.at[chip],
-            self.line_in.at[way, chip],
+            self.line_in.at[chip],
+            self.line_in.at[slot],
             self.line_send.at[chip],
-            self.line_recv.at[way, chip],
-            (self.place.up, self.place.down)[way],
+            self.line_recv.at[slot],
+            (place.up, place.down)[way],
         )
+
+    def landed(self, way, chip):
+        place = self.place
+        slot = jnp.where((way == 1) & (chip == place.chip), place.chips, chip)
+        remote(
+            self.line_in.at[slot],
+            self.line_in.at[slot],
+            self.line_send.at[chip],
+            self.line_recv.at[slot],
+            (place.up, place.down)[way],
+        ).wait_recv()
+        return slot
 
     def each(self, distance, action):
         place = self.place
@@ -489,12 +526,12 @@
 
             @pl.when(behind & goes)
             def _():
-                self.line_copy(way, chip).wait_recv()
-                self.total[...] += self.line_in[way, chip].astype(jnp.float32)
+                slot = self.landed(way, chip)
+                self.total[...] += self.line_in[slot].astype(jnp.float32)
 
         @pl.when(chip != place.chip)
         def _():
-            self.line_out[chip] = self.total[...].astype(jnp.bfloat16)
+            self.line_in[chip] = self.total[...].astype(jnp.bfloat16)
             pl.when(chip > place.chip)(lambda: self.line_copy(0, chip).start())
             pl.when(chip < place.chip)(lambda: self.line_copy(1, chip).start())
 
@@ -515,6 +552,182 @@
             return carry
 
         lax.fori_loop(0, place.chips, drain, 0)
+
+
+class SquareScatter:
+    def __init__(self, place, piece, owned, bufs, sems):
+        self.place, self.piece, self.owned = place, piece, owned
+        self.out, self.arrived = bufs
+        self.send, self.recv = sems
+
+    def copy(self, kind, way):
+        place = self.place
+        turn = way if kind < 2 else 1 - way
+        peer = place.x_peer + turn * (place.y_peer - place.x_peer)
+        return remote(
+            self.out.at[kind, way],
+            self.arrived.at[kind, way],
+            self.send.at[kind, way],
+            self.recv.at[kind, way],
+            (peer, place.me),
+        )
+
+    def stage(self, kind):
+        place = self.place
+
+        def one(way, carry):
+            near = place.x_peer + way * (place.y_peer - place.x_peer)
+            other = place.y_peer + way * (place.x_peer - place.y_peer)
+            owner = (place.across, near, other, place.dp)[kind]
+            value = self.piece(owner, way)
+            if kind == 2:
+                self.copy(0, way).wait_recv()
+                value = value + self.arrived[0, way].astype(jnp.float32)
+            if kind < 3:
+                self.out[kind, way] = value.astype(jnp.bfloat16)
+                self.copy(kind, way).start()
+            else:
+                self.owned[way] = value
+            return carry
+
+        lax.fori_loop(0, 2, one, 0)
+
+    def end(self):
+        def one(way, carry):
+            self.copy(1, way).wait_recv()
+            self.copy(2, way).wait_recv()
+            self.owned[way] = (
+                self.owned[way]
+                + self.arrived[1, way].astype(jnp.float32)
+                + self.arrived[2, way].astype(jnp.float32)
+            )
+            for kind in range(3):
+                self.copy(kind, way).wait_send()
+            return carry
+
+        lax.fori_loop(0, 2, one, 0)
+
+
+def square_scratch(half):
+    dma = pltpu.SemaphoreType.DMA
+    return [
+        pltpu.VMEM((3, 2) + half, jnp.bfloat16),
+        pltpu.VMEM((3, 2) + half, jnp.bfloat16),
+        dma((3, 2)),
+        dma((3, 2)),
+    ]
+
+
+class SmallSum:
+    def __init__(self, place, rows, alone, bufs, sems):
+        self.place, self.rows, self.alone = place, rows, alone
+        self.side_buf, self.line_buf, self.square_buf = bufs
+        self.send, self.recv = sems
+
+    def side_copy(self):
+        place = self.place
+        return remote(
+            self.rows,
+            self.side_buf,
+            self.send.at[0],
+            self.recv.at[0],
+            place.side,
+        )
+
+    def line_copy(self, hop):
+        place = self.place
+        chip = (place.chip + hop) % place.chips
+        return remote(
+            self.rows,
+            self.line_buf.at[place.chip],
+            self.send.at[hop],
+            self.recv.at[hop],
+            (place.dp, 2 * chip + place.core),
+        )
+
+    def line_landed(self, hop):
+        place = self.place
+        chip = (place.chip + place.chips - hop) % place.chips
+        remote(
+            self.rows,
+            self.line_buf.at[chip],
+            self.send.at[hop],
+            self.recv.at[hop],
+            (place.dp, 2 * chip + place.core),
+        ).wait_recv()
+
+    def square_copy(self, hop):
+        place = self.place
+        target = (place.dp + hop) % 4
+        at = place.chips + hop
+        return remote(
+            self.rows,
+            self.square_buf.at[place.dp],
+            self.send.at[at],
+            self.recv.at[at],
+            (target, place.me),
+        )
+
+    def square_landed(self, hop):
+        place = self.place
+        source = (place.dp + 4 - hop) % 4
+        at = place.chips + hop
+        remote(
+            self.rows,
+            self.square_buf.at[source],
+            self.send.at[at],
+            self.recv.at[at],
+            (source, place.me),
+        ).wait_recv()
+
+    def put(self, value):
+        if self.alone < self.rows.shape[0]:
+            index = lax.broadcasted_iota(jnp.int32, value.shape, 0)
+            value = jnp.where(index < self.alone, value, self.rows[...])
+        self.rows[...] = value
+
+    def begin(self):
+        self.side_copy().start()
+
+    def middle(self):
+        self.side_copy().wait()
+        self.put(self.rows[...] + self.side_buf[...])
+        self.line_buf[self.place.chip] = self.rows[...]
+        for hop in range(1, self.place.chips):
+            self.line_copy(hop).start()
+
+    def late(self):
+        place = self.place
+        for hop in range(1, place.chips):
+            self.line_copy(hop).wait_send()
+            self.line_landed(hop)
+        value = self.line_buf[0]
+        for chip in range(1, place.chips):
+            value = value + self.line_buf[chip]
+        self.put(value)
+        self.square_buf[place.dp] = self.rows[...]
+        for hop in range(1, 4):
+            self.square_copy(hop).start()
+
+    def end(self):
+        for hop in range(1, 4):
+            self.square_copy(hop).wait_send()
+            self.square_landed(hop)
+        value = self.square_buf[0]
+        for device in range(1, 4):
+            value = value + self.square_buf[device]
+        self.rows[...] = value
+
+
+def small_scratch(chips, rows, width):
+    dma = pltpu.SemaphoreType.DMA
+    return [
+        pltpu.VMEM((rows, width), jnp.float32),
+        pltpu.VMEM((chips, rows, width), jnp.float32),
+        pltpu.VMEM((4, rows, width), jnp.float32),
+        dma((chips + 4,)),
+        dma((chips + 4,)),
+    ]
 
 
 def scatter_scratch(chips, count, width):
@@ -524,12 +737,11 @@
         pltpu.VMEM((count, width), jnp.float32),
         pltpu.VMEM((chips, count, width), low),
         pltpu.VMEM((chips, count, width), low),
-        pltpu.VMEM((chips, count, width), low),
-        pltpu.VMEM((2, chips, count, width), low),
+        pltpu.VMEM((chips + 1, count, width), low),
         dma((chips,)),
         dma((chips,)),
         dma((chips,)),
-        dma((2, chips)),
+        dma((chips + 1,)),
     ]
 
 
@@ -597,7 +809,7 @@
         span = pl.ds(pl.multiple_of(block * count, count), count)
         return jnp.dot(attended_ref[span, :], out_ref[tile], preferred_element_type=jnp.float32)
 
-    sums = LineScatter(place, term, 4, scatter[:5], scatter[5:])
+    sums = LineScatter(place, term, 4, scatter[:4], scatter[4:8])
     sums.begin()
 
     def copy_in(span):
@@ -607,9 +819,12 @@
     line = LineGather(place, blocks, line_send, line_recv)
     line.begin()
 
-    def keep(block):
-        span = pl.ds(pl.multiple_of(block * count, count), count)
-        return pltpu.make_async_copy(blocks.at[block], branch_whole.at[span], keep_sem.at[block])
+    def keep(block, part):
+        half = count // 2
+        place_of = ((block // 2 * 2 + part) * 2 + block % 2) * half
+        span = pl.ds(pl.multiple_of(place_of, half), half)
+        source = blocks.at[block, pl.ds(part * half, half)]
+        return pltpu.make_async_copy(source, branch_whole.at[span], keep_sem.at[block, part])
 
     def step(index, carry):
         sums.step(index)
@@ -635,7 +850,8 @@
 
     def store(block, carry):
         pl.when((block % 2 != place.core))(lambda: line.arrive(block // 2, block % 2))
-        keep(block).start()
+        keep(block, 0).start()
+        keep(block, 1).start()
         return carry
 
     lax.fori_loop(0, 2 * chips, store, 0)
@@ -649,7 +865,8 @@
     own[1].wait()
 
     def kept(block, carry):
-        keep(block).wait()
+        keep(block, 0).wait()
+        keep(block, 1).wait()
         return carry
 
     lax.fori_loop(0, 2 * chips, kept, 0)
@@ -682,7 +899,7 @@
             dma((4,)),
             dma((4,)),
             dma((2,)),
-            dma((2 * chips,)),
+            dma((2 * chips, 2)),
         ]
         + scatter_scratch(chips, count, width),
         compiler_params=pltpu.CompilerParams(
@@ -700,14 +917,25 @@
     rows_ref,
     resid_grad_ref,
     gain_ref,
+    early_ref,
+    hidden_ref,
+    normed_one_ref,
+    normed_two_ref,
     grad_ref,
-    gain_grad_ref,
-    shift_grad_ref,
+    late_out_ref,
+    early_out_ref,
+    mix_grad_ref,
+    up_grad_ref,
+    columns_buf,
+    columns_sem,
     *scatter,
 ):
     place = Place(chips)
     count = rows_ref.shape[0]
-    place.greet(False)
+    place.greet(True, True)
+    early_out_ref[...] = early_ref[...]
+    early = SmallSum(place, early_out_ref, 4, scatter[16:19], scatter[19:21])
+    late = SmallSum(place, late_out_ref, late_out_ref.shape[0], scatter[21:24], scatter[24:26])
 
     def term(block, tile):
         span = pl.ds(pl.multiple_of(block * count, count), count)
@@ -716,23 +944,66 @@
             product = lax.dot_general(
                 stacked_ref[part, span, :],
                 mix_ref[part, tile],
-                (((1,), (1,)), ((), ())),
+                TURNED,
                 preferred_element_type=jnp.float32,
             )
             result = product if result is None else result + product
         return result
 
-    sums = LineScatter(place, term, 4, scatter[:5], scatter[5:])
+    sums = LineScatter(place, term, 4, scatter[:4], scatter[4:8])
     sums.begin()
+    early.begin()
+    half_columns = columns_buf.shape[1]
+
+    def load(source, owner, half):
+        start = pl.multiple_of((2 * owner + half) * half_columns, half_columns)
+        copy = pltpu.make_async_copy(
+            source.at[:, pl.ds(start, half_columns)], columns_buf, columns_sem
+        )
+        copy.start()
+        copy.wait()
+
+    def mix_piece(owner, half):
+        load(normed_one_ref, owner, half)
+        return jnp.stack(
+            [
+                lax.dot_general(
+                    columns_buf[...],
+                    stacked_ref[part],
+                    CROSSED,
+                    preferred_element_type=jnp.float32,
+                )
+                for part in range(3)
+            ]
+        )
+
+    def up_piece(owner, half):
+        load(normed_two_ref, owner, half)
+        return lax.dot_general(
+            columns_buf[...], hidden_ref[...], CROSSED, preferred_element_type=jnp.float32
+        )
+
+    mix = SquareScatter(place, mix_piece, mix_grad_ref, scatter[8:10], scatter[10:12])
+    up = SquareScatter(place, up_piece, up_grad_ref, scatter[12:14], scatter[14:16])
 
     def step(index, carry):
         sums.step(index)
+        for kind in range(4):
+
+            @pl.when(index == kind)
+            def _():
+                up.stage(kind)
+                mix.stage(kind)
+                if kind == 1:
+                    early.middle()
+                if kind == 2:
+                    early.late()
+
         return carry
 
     lax.fori_loop(0, chips, step, 0)
     total = scatter[0]
-    gain_grad_ref[...] = jnp.zeros_like(gain_grad_ref)
-    shift_grad_ref[...] = jnp.zeros_like(shift_grad_ref)
+    late_out_ref[...] = jnp.zeros_like(late_out_ref)
 
     def back(span):
         rows = rows_ref[span, :].astype(jnp.float32)
@@ -741,32 +1012,747 @@
         grad_ref[span, :] = resid_grad_ref[span, :] + layer_norm_back(
             one_grad, hat, inverse, gain_ref[...]
         )
-        gain_grad_ref[...] += jnp.sum(one_grad * hat, axis=0, keepdims=True)
-        shift_grad_ref[...] += jnp.sum(one_grad, axis=0, keepdims=True)
+        late_out_ref[0:1, :] += jnp.sum(one_grad * hat, axis=0, keepdims=True)
+        late_out_ref[1:2, :] += jnp.sum(one_grad, axis=0, keepdims=True)
 
     by_rows(count, 64, back)
+    late.begin()
+    early.end()
+    up.end()
+    late.middle()
+    mix.end()
+    late.late()
     sums.finish()
-
-
-def input_back_call(stacked, mix_whole, rows, resid_grad, gain, chips):
+    late.end()
+
+
+def input_back_call(
+    stacked, mix_whole, rows, resid_grad, gain, early, hidden, normed_one, normed_two, chips
+):
     count, width = rows.shape
+    total, units = hidden.shape
+    local = stacked.shape[2]
+    half = width // 8
     vmem = pl.BlockSpec(memory_space=pltpu.VMEM)
+    hbm = pl.BlockSpec(memory_space=pl.ANY)
     return pl.pallas_call(
         functools.partial(input_back_kernel, chips),
         out_shape=(
             jax.ShapeDtypeStruct((count, width), jnp.float32),
-            jax.ShapeDtypeStruct((1, width), jnp.float32),
-            jax.ShapeDtypeStruct((1, width), jnp.float32),
+            jax.ShapeDtypeStruct((2, width), jnp.float32),
+            jax.ShapeDtypeStruct(early.shape, jnp.float32),
+            jax.ShapeDtypeStruct((2, 3, half, local), jnp.float32),
+            jax.ShapeDtypeStruct((2, half, units), jnp.float32),
         ),
-        in_specs=[vmem] * 5,
-        out_specs=(vmem,) * 3,
-        scratch_shapes=scatter_scratch(chips, count, width),
+        in_specs=[vmem] * 7 + [hbm] * 2,
+        out_specs=(vmem,) * 5,
+        scratch_shapes=[
+            pltpu.VMEM((total, half), jnp.bfloat16),
+            pltpu.SemaphoreType.DMA,
+        ]
+        + scatter_scratch(chips, count, width)
+        + square_scratch((3, half, local))
+        + square_scratch((half, units))
+        + small_scratch(chips, early.shape[0], width)
+        + small_scratch(chips, 2, width),
         compiler_params=pltpu.CompilerParams(
             collective_id=2, has_side_effects=True, vmem_limit_bytes=VMEM_LIMIT
         ),
         cost_estimate=pl.CostEstimate(flops=10**11, bytes_accessed=0, transcendentals=0),
         name="input_back",
-    )(stacked, mix_whole, rows, resid_grad, gain)
+    )(stacked, mix_whole, rows, resid_grad, gain, early, hidden, normed_one, normed_two)
+
+
+GELU_SLOPE = 0.7978845608028654
+GELU_CUBE = 0.044715
+
+
+def gelu_parts(hidden):
+    square = hidden * hidden
+    bend = jnp.tanh(GELU_SLOPE * hidden * (1.0 + GELU_CUBE * square))
+    lift = 0.5 * (1.0 + bend)
+    slope = lift + 0.5 * hidden * (1.0 - bend * bend) * (
+        GELU_SLOPE * (1.0 + 3.0 * GELU_CUBE * square)
+    )
+    return hidden * lift, slope
+
+
+def feed_kernel(
+    chips,
+    parts,
+    normed_ref,
+    branch_ref,
+    up_ref,
+    down_ref,
+    bias_ref,
+    resid_ref,
+    own_branch_ref,
+    gain_ref,
+    normed_whole,
+    active_ref,
+    hidden_ref,
+    grad_ref,
+    grad_low_ref,
+    sums_ref,
+    bias_grad_ref,
+    blocks,
+    branch_buf,
+    work,
+    hold,
+    side_out,
+    side_in,
+    line_in,
+    line_send,
+    line_recv,
+    keep_sem,
+    load_sem,
+    side_send,
+    side_recv,
+    out_send,
+    out_recv,
+):
+    place = Place(chips)
+    count = normed_ref.shape[0]
+    rows = count // parts
+    pair = 2 * rows
+    last = chips - 1
+    place.greet(False)
+
+    def fill(part, carry):
+        block = 2 * (place.chip * parts + part) + place.core
+        blocks[block] = normed_ref[pl.ds(pl.multiple_of(part * rows, rows), rows), :]
+        return carry
+
+    lax.fori_loop(0, parts, fill, 0)
+    line = LineGather(place, blocks, line_send, line_recv, parts)
+    line.begin()
+    bias_grad_ref[...] = jnp.zeros_like(bias_grad_ref)
+
+    def piece_span(piece):
+        return pl.ds(pl.multiple_of(piece * pair, pair), pair)
+
+    def load(piece, slot):
+        return pltpu.make_async_copy(
+            branch_ref.at[piece_span(piece)], branch_buf.at[slot], load_sem.at[slot]
+        )
+
+    def keep(piece, core):
+        span = pl.ds(pl.multiple_of(piece * pair + core * rows, rows), rows)
+        return pltpu.make_async_copy(
+            blocks.at[2 * piece + core], normed_whole.at[span], keep_sem.at[piece, core]
+        )
+
+    def side_copy(piece):
+        return remote(
+            side_out.at[piece],
+            side_in.at[piece],
+            side_send.at[piece],
+            side_recv.at[piece],
+            place.side,
+        )
+
+    def line_copy(way, chip, part):
+        piece = chip * parts + part
+        next_chip = place.chip + 1 - 2 * way
+        slot = jnp.where((way == 1) & (chip == next_chip), chips * parts + part, piece)
+        return remote(
+            line_in.at[piece],
+            line_in.at[slot],
+            out_send.at[piece],
+            out_recv.at[slot],
+            (place.up, place.down)[way],
+        )
+
+    def line_landed(way, chip, part):
+        piece = chip * parts + part
+        slot = jnp.where((way == 1) & (chip == place.chip), chips * parts + part, piece)
+        remote(
+            line_in.at[slot],
+            line_in.at[slot],
+            out_send.at[piece],
+            out_recv.at[slot],
+            (place.up, place.down)[way],
+        ).wait_recv()
+        return slot
+
+    width = 256
+    tiles = up_ref.shape[2] // width
+
+    def compute(chip, part):
+        piece = chip * parts + part
+        load(piece, 0).start()
+        keep(piece, 0).start()
+        keep(piece, 1).start()
+        span = piece_span(piece)
+        own_rows = blocks[pl.ds(2 * piece, 2)].reshape(pair, -1)
+        load(piece, 0).wait()
+
+        def tile(index, carry):
+            units = pl.ds(pl.multiple_of(index * width, width), width)
+            hidden = jnp.dot(
+                own_rows,
+                up_ref[:, :, units].reshape(-1, width),
+                preferred_element_type=jnp.float32,
+            )
+            active, slope = gelu_parts(hidden + bias_ref[:, units])
+            active_ref[span, units] = active.astype(jnp.bfloat16)
+            grad = None
+            for owner in range(4):
+                columns = down_ref.shape[2]
+                product = lax.dot_general(
+                    branch_buf[0, :, owner * columns : (owner + 1) * columns],
+                    down_ref[owner, units, :],
+                    TURNED,
+                    preferred_element_type=jnp.float32,
+                )
+                grad = product if grad is None else grad + product
+            low = (grad * slope).astype(jnp.bfloat16)
+            hidden_ref[span, units] = low
+            bias_grad_ref[:, units] += jnp.sum(low.astype(jnp.float32), axis=0, keepdims=True)
+            return carry
+
+        lax.fori_loop(0, tiles, tile, 0)
+        low = hidden_ref[span, :]
+        depth = up_ref.shape[1]
+        for owner in range(4):
+            columns = slice(owner * depth, (owner + 1) * depth)
+            product = lax.dot_general(
+                low, up_ref[owner], TURNED, preferred_element_type=jnp.float32
+            )
+            work[:, :, columns] = product.reshape(2, rows, depth)
+        side_out[piece] = work[1 - place.core].astype(jnp.bfloat16)
+        side_copy(piece).start()
+        hold[piece] = work[place.core]
+
+    def pass_on(way, chip, part):
+        piece = chip * parts + part
+        side_copy(piece).wait_recv()
+        total = hold[piece] + side_in[piece].astype(jnp.float32)
+        behind = (place.has_down, place.has_up)[way]
+
+        @pl.when(behind)
+        def _():
+            slot = line_landed(way, chip, part)
+            line_in[piece] = (total + line_in[slot].astype(jnp.float32)).astype(jnp.bfloat16)
+
+        @pl.when(jnp.logical_not(behind))
+        def _():
+            line_in[piece] = total.astype(jnp.bfloat16)
+
+        line_copy(way, chip, part).start()
+
+    def turn(index, carry):
+        distance = index // parts
+        part = index % parts
+
+        @pl.when(distance < chips)
+        def _():
+            pl.when(distance > 0)(lambda: line.step(distance, part))
+
+            def one(side, inner):
+                chip = place.chip + distance * (2 * side - 1)
+
+                @pl.when((chip >= 0) & (chip < chips) & ((distance > 0) | (side == 0)))
+                def _():
+                    line.arrive(chip, 1 - place.core, part)
+                    compute(chip, part)
+
+                return inner
+
+            lax.fori_loop(0, 2, one, 0)
+
+        upward = index - place.chip
+
+        @pl.when((upward >= 0) & (upward // parts > place.chip) & (upward // parts < chips))
+        def _():
+            pass_on(0, upward // parts, upward % parts)
+
+        downward = index - (last - place.chip)
+        target = last - downward // parts
+
+        @pl.when((downward >= 0) & (target >= 0) & (target < place.chip))
+        def _():
+            pass_on(1, target, downward % parts)
+
+        return carry
+
+    lax.fori_loop(0, parts * chips + last, turn, 0)
+    sums_ref[...] = jnp.zeros_like(sums_ref)
+
+    def own_part(part, carry):
+        piece = place.chip * parts + part
+        side_copy(piece).wait_recv()
+        hold[piece] += side_in[piece].astype(jnp.float32)
+
+        @pl.when(place.has_down)
+        def _():
+            slot = line_landed(0, place.chip, part)
+            hold[piece] += line_in[slot].astype(jnp.float32)
+
+        @pl.when(place.has_up)
+        def _():
+            slot = line_landed(1, place.chip, part)
+            hold[piece] += line_in[slot].astype(jnp.float32)
+
+        tile = 64
+
+        def back(index, inner):
+            here = pl.ds(pl.multiple_of(index * tile, tile), tile)
+            span = pl.ds(pl.multiple_of(part * rows + index * tile, tile), tile)
+            two_grad = hold[piece, here, :]
+            _, hat, inverse = layer_norm_parts(resid_ref[span, :], gain_ref[...], 0.0)
+            grad = own_branch_ref[span, :].astype(jnp.float32) + layer_norm_back(
+                two_grad, hat, inverse, gain_ref[...]
+            )
+            grad_ref[span, :] = grad
+            grad_low_ref[span, :] = grad.astype(jnp.bfloat16)
+            sums_ref[0:1, :] += jnp.sum(two_grad * hat, axis=0, keepdims=True)
+            sums_ref[1:2, :] += jnp.sum(two_grad, axis=0, keepdims=True)
+            sums_ref[2:3, :] += jnp.sum(grad, axis=0, keepdims=True)
+            return inner
+
+        lax.fori_loop(0, rows // tile, back, 0)
+        return carry
+
+    lax.fori_loop(0, parts, own_part, 0)
+    line.finish()
+
+    def drain(piece, carry):
+        side_copy(piece).wait_send()
+        keep(piece, 0).wait()
+        keep(piece, 1).wait()
+        pl.when(piece // parts != place.chip)(
+            lambda: line_copy(0, piece // parts, piece % parts).wait_send()
+        )
+        return carry
+
+    lax.fori_loop(0, chips * parts, drain, 0)
+
+
+def feed_call(normed, branch, up_whole, down_whole, bias, resid, own_branch, gain, chips):
+    count, width = normed.shape
+    total = 2 * chips * count
+    units = up_whole.shape[2]
+    parts = 2
+    rows = count // parts
+    low = jnp.bfloat16
+    vmem = pl.BlockSpec(memory_space=pltpu.VMEM)
+    hbm = pl.BlockSpec(memory_space=pl.ANY)
+    dma = pltpu.SemaphoreType.DMA
+    pieces = chips * parts
+    return pl.pallas_call(
+        functools.partial(feed_kernel, chips, parts),
+        out_shape=(
+            jax.ShapeDtypeStruct((total, width), low),
+            jax.ShapeDtypeStruct((total, units), low),
+            jax.ShapeDtypeStruct((total, units), low),
+            jax.ShapeDtypeStruct((count, width), jnp.float32),
+            jax.ShapeDtypeStruct((count, width), low),
+            jax.ShapeDtypeStruct((3, width), jnp.float32),
+            jax.ShapeDtypeStruct((1, units), jnp.float32),
+        ),
+        in_specs=[vmem, hbm] + [vmem] * 6,
+        out_specs=(hbm,) + (vmem,) * 6,
+        scratch_shapes=[
+            pltpu.VMEM((2 * pieces, rows, width), low),
+            pltpu.VMEM((1, 2 * rows, width), low),
+            pltpu.VMEM((2, rows, width), jnp.float32),
+            pltpu.VMEM((pieces, rows, width), jnp.float32),
+            pltpu.VMEM((pieces, rows, width), low),
+            pltpu.VMEM((pieces, rows, width), low),
+            pltpu.VMEM((pieces + parts, rows, width), low),
+            dma((3, pieces)),
+            dma((2 * pieces,)),
+            dma((pieces, 2)),
+            dma((1,)),
+            dma((pieces,)),
+            dma((pieces,)),
+            dma((pieces,)),
+            dma((pieces + parts,)),
+        ],
+        compiler_params=pltpu.CompilerParams(
+            collective_id=3, has_side_effects=True, vmem_limit_bytes=VMEM_LIMIT
+        ),
+        cost_estimate=pl.CostEstimate(flops=10**11, bytes_accessed=0, transcendentals=0),
+        name="feed",
+    )(normed, branch, up_whole, down_whole, bias, resid, own_branch, gain)
+
+
+def branch_back_kernel(
+    chips,
+    parts,
+    branch_ref,
+    active_ref,
+    down_ref,
+    attended_ref,
+    out_ref,
+    resid_ref,
+    shift_ref,
+    live_ref,
+    cotangent_ref,
+    attended_grad_ref,
+    down_grad_ref,
+    out_owned_ref,
+    output_ref,
+    blocks,
+    out_grad_ref,
+    columns_buf,
+    line_send,
+    line_recv,
+    columns_sem,
+    *scatter,
+):
+    place = Place(chips)
+    count = branch_ref.shape[0]
+    rows = count // parts
+    place.greet(True)
+
+    def copy_in(span):
+        blocks[place.me, span, :] = branch_ref[span, :]
+
+    by_rows(count, 64, copy_in)
+    line = LineGather(place, blocks, line_send, line_recv)
+    line.begin()
+
+    def term(block, tile):
+        chip, core = block // 2, block % 2
+        taken = []
+        for part in range(parts):
+            start = ((chip * parts + part) * 2 + core) * rows
+            taken.append(active_ref[pl.ds(pl.multiple_of(start, rows), rows), :])
+        return jnp.dot(
+            jnp.concatenate(taken, axis=0), down_ref[tile], preferred_element_type=jnp.float32
+        )
+
+    sums = LineScatter(place, term, 4, scatter[:4], scatter[4:8])
+    sums.begin()
+    out_grad_ref[...] = jnp.zeros_like(out_grad_ref)
+    down_units = down_ref.shape[1] // 2
+    down_columns = down_ref.shape[2]
+
+    def down_piece(owner, half):
+        load = pltpu.make_async_copy(
+            cotangent_ref.at[:, pl.ds(pl.multiple_of(owner * down_columns, 128), down_columns)],
+            columns_buf,
+            columns_sem,
+        )
+        load.start()
+        load.wait()
+        units = pl.ds(pl.multiple_of(half * down_units, down_units), down_units)
+        return lax.dot_general(
+            active_ref[:, units], columns_buf[...], CROSSED, preferred_element_type=jnp.float32
+        )
+
+    down = SquareScatter(place, down_piece, down_grad_ref, scatter[8:10], scatter[10:12])
+    out_units = out_ref.shape[1] // 2
+
+    def out_piece(owner, half):
+        units = pl.ds(pl.multiple_of(half * out_units, out_units), out_units)
+        columns = pl.ds(pl.multiple_of(owner * down_columns, 128), down_columns)
+        return out_grad_ref[units, columns]
+
+    out = SquareScatter(place, out_piece, out_owned_ref, scatter[12:14], scatter[14:16])
+
+    def take(block):
+        span = pl.ds(pl.multiple_of(block * count, count), count)
+        columns = out_ref.shape[2]
+        result = None
+        for owner in range(4):
+            here = blocks[block, :, owner * columns : (owner + 1) * columns]
+            product = lax.dot_general(
+                here, out_ref[owner], TURNED, preferred_element_type=jnp.float32
+            )
+            result = product if result is None else result + product
+            out_grad_ref[:, owner * columns : (owner + 1) * columns] += lax.dot_general(
+                attended_ref[span, :],
+                here,
+                (((0,), (0,)), ((), ())),
+                preferred_element_type=jnp.float32,
+            )
+        attended_grad_ref[span, :] = result.astype(jnp.bfloat16)
+
+    def step(index, carry):
+        def one(side, inner):
+            chip = place.chip + index * (2 * (side % 2) - 1)
+            core = (place.core + side // 2) % 2
+
+            @pl.when((chip >= 0) & (chip < chips) & ((index > 0) | (side % 2 == 0)))
+            def _():
+                pl.when(side >= 2)(lambda: line.arrive(chip, core))
+                take(2 * chip + core)
+
+            return inner
+
+        lax.fori_loop(0, 4, one, 0)
+        sums.step(index)
+        pl.when(index < chips - 1)(lambda: line.step(index + 1))
+        for kind in range(4):
+            pl.when(index == kind)(lambda: down.stage(kind))
+        return carry
+
+    lax.fori_loop(0, chips, step, 0)
+    out.stage(0)
+    out.stage(1)
+    total = scatter[0]
+
+    def emit(span):
+        result = resid_ref[span, :] + total[span, :] + shift_ref[...]
+        output_ref[span, :] = jnp.where(live_ref[span, :] > 0, result, 0.0).astype(jnp.bfloat16)
+
+    by_rows(count, 64, emit)
+    down.end()
+    out.stage(2)
+    out.stage(3)
+    sums.finish()
+    line.finish()
+    out.end()
+
+
+def branch_back_call(
+    branch, active, down_whole, attended, out_whole, resid, shift, live, cotangent, chips
+):
+    count, width = branch.shape
+    total, local = attended.shape
+    _, units, columns = down_whole.shape
+    low = jnp.bfloat16
+    vmem = pl.BlockSpec(memory_space=pltpu.VMEM)
+    hbm = pl.BlockSpec(memory_space=pl.ANY)
+    dma = pltpu.SemaphoreType.DMA
+    return pl.pallas_call(
+        functools.partial(branch_back_kernel, chips, 2),
+        out_shape=(
+            jax.ShapeDtypeStruct((total, local), low),
+            jax.ShapeDtypeStruct((2, units // 2, columns), jnp.float32),
+            jax.ShapeDtypeStruct((2, local // 2, columns), jnp.float32),
+            jax.ShapeDtypeStruct((count, width), low),
+        ),
+        in_specs=[vmem] * 8 + [hbm],
+        out_specs=(vmem,) * 4,
+        scratch_shapes=[
+            pltpu.VMEM((2 * chips, count, width), low),
+            pltpu.VMEM((local, width), jnp.float32),
+            pltpu.VMEM((total, columns), low),
+            dma((3, chips)),
+            dma((2 * chips,)),
+            dma,
+        ]
+        + scatter_scratch(chips, count, width)
+        + square_scratch((units // 2, columns))
+        + square_scratch((local // 2, columns)),
+        compiler_params=pltpu.CompilerParams(
+            collective_id=4, has_side_effects=True, vmem_limit_bytes=VMEM_LIMIT
+        ),
+        cost_estimate=pl.CostEstimate(flops=10**11, bytes_accessed=0, transcendentals=0),
+        name="branch_back",
+    )(branch, active, down_whole, attended, out_whole, resid, shift, live, cotangent)
+
+
+ATTEND_ROWS = 256
+ATTEND_KEYS = 512
+
+
+def tile_mask(row_block, key_block, seg_col_ref, seg_row_ref):
+    rows = lax.broadcasted_iota(jnp.int32, (ATTEND_ROWS, ATTEND_KEYS), 0)
+    keys = lax.broadcasted_iota(jnp.int32, (ATTEND_ROWS, ATTEND_KEYS), 1)
+    causal = keys - rows <= row_block * ATTEND_ROWS - key_block * ATTEND_KEYS
+    row_span = pl.ds(pl.multiple_of(row_block * ATTEND_ROWS, ATTEND_ROWS), ATTEND_ROWS)
+    key_span = pl.ds(pl.multiple_of(key_block * ATTEND_KEYS, ATTEND_KEYS), ATTEND_KEYS)
+    return causal & (seg_col_ref[row_span, :] == seg_row_ref[:, key_span])
+
+
+def attention_kernel(mixed_ref, seg_col_ref, seg_row_ref, attended_ref, lse_ref, score_ref):
+    length = mixed_ref.shape[1]
+    heads = mixed_ref.shape[2] // HEAD_DIM
+    row_blocks = length // ATTEND_ROWS
+    scale = HEAD_DIM ** (-0.5)
+
+    def one(index, carry):
+        head = index // row_blocks
+        row_block = index % row_blocks
+        lanes = pl.ds(pl.multiple_of(head * HEAD_DIM, HEAD_DIM), HEAD_DIM)
+        row_span = pl.ds(pl.multiple_of(row_block * ATTEND_ROWS, ATTEND_ROWS), ATTEND_ROWS)
+        count = (row_block * ATTEND_ROWS) // ATTEND_KEYS + 1
+        query = mixed_ref[0, row_span, lanes]
+
+        def score(key_block, peak):
+            key_span = pl.ds(pl.multiple_of(key_block * ATTEND_KEYS, ATTEND_KEYS), ATTEND_KEYS)
+            scores = lax.dot_general(
+                query, mixed_ref[1, key_span, lanes], TURNED, preferred_element_type=jnp.float32
+            )
+            mask = tile_mask(row_block, key_block, seg_col_ref, seg_row_ref)
+            scores = jnp.where(mask, scores * scale, MASK_FILL)
+            score_ref[:, key_span] = scores
+            for part in range(ATTEND_KEYS // 128):
+                peak = jnp.maximum(peak, scores[:, part * 128 : (part + 1) * 128])
+            return peak
+
+        peak = lax.fori_loop(
+            0, count, score, jnp.full((ATTEND_ROWS, 128), MASK_FILL, jnp.float32)
+        )
+        peak = jnp.max(peak, axis=1, keepdims=True)
+
+        def weigh(key_block, mass):
+            key_span = pl.ds(pl.multiple_of(key_block * ATTEND_KEYS, ATTEND_KEYS), ATTEND_KEYS)
+            weights = jnp.exp(score_ref[:, key_span] - peak)
+            score_ref[:, key_span] = weights
+            for part in range(ATTEND_KEYS // 128):
+                mass = mass + weights[:, part * 128 : (part + 1) * 128]
+            return mass
+
+        mass = lax.fori_loop(0, count, weigh, jnp.zeros((ATTEND_ROWS, 128), jnp.float32))
+        mass = jnp.sum(mass, axis=1, keepdims=True)
+        inverse = 1.0 / mass
+        lse_ref[head, row_span, :] = peak + jnp.log(mass)
+
+        def gather(key_block, total):
+            key_span = pl.ds(pl.multiple_of(key_block * ATTEND_KEYS, ATTEND_KEYS), ATTEND_KEYS)
+            probs = (score_ref[:, key_span] * inverse).astype(jnp.bfloat16)
+            return total + jnp.dot(
+                probs, mixed_ref[2, key_span, lanes], preferred_element_type=jnp.float32
+            )
+
+        total = lax.fori_loop(
+            0, count, gather, jnp.zeros((ATTEND_ROWS, HEAD_DIM), jnp.float32)
+        )
+        attended_ref[row_span, lanes] = total.astype(jnp.bfloat16)
+        return carry
+
+    lax.fori_loop(0, heads * row_blocks, one, 0)
+
+
+def attention_call(mixed, seg_col, seg_row):
+    _, length, width = mixed.shape
+    heads = width // HEAD_DIM
+    vmem = pl.BlockSpec(memory_space=pltpu.VMEM)
+    return pl.pallas_call(
+        attention_kernel,
+        out_shape=(
+            jax.ShapeDtypeStruct((length, width), jnp.bfloat16),
+            jax.ShapeDtypeStruct((heads, length, 1), jnp.float32),
+        ),
+        in_specs=[vmem] * 3,
+        out_specs=(vmem,) * 2,
+        scratch_shapes=[pltpu.VMEM((ATTEND_ROWS, length), jnp.float32)],
+        compiler_params=pltpu.CompilerParams(vmem_limit_bytes=VMEM_LIMIT),
+        cost_estimate=pl.CostEstimate(flops=10**10, bytes_accessed=0, transcendentals=0),
+        name="attention",
+    )(mixed, seg_col, seg_row)
+
+
+def attention_back_kernel(
+    mixed_ref,
+    seg_col_ref,
+    seg_row_ref,
+    lse_ref,
+    grad_ref,
+    stacked_ref,
+    bias_grad_ref,
+    probs_ref,
+    flow_ref,
+    key_sum,
+    value_sum,
+):
+    length = mixed_ref.shape[1]
+    heads = mixed_ref.shape[2] // HEAD_DIM
+    row_blocks = length // ATTEND_ROWS
+    scale = HEAD_DIM ** (-0.5)
+
+    def one_head(head, carry):
+        lanes = pl.ds(pl.multiple_of(head * HEAD_DIM, HEAD_DIM), HEAD_DIM)
+        key_sum[...] = jnp.zeros_like(key_sum)
+        value_sum[...] = jnp.zeros_like(value_sum)
+
+        def one(row_block, bias_sum):
+            row_span = pl.ds(pl.multiple_of(row_block * ATTEND_ROWS, ATTEND_ROWS), ATTEND_ROWS)
+            count = (row_block * ATTEND_ROWS) // ATTEND_KEYS + 1
+            query = mixed_ref[0, row_span, lanes]
+            grad = grad_ref[row_span, lanes]
+            lse = lse_ref[head, row_span, :]
+
+            def first(key_block, delta):
+                key_span = pl.ds(pl.multiple_of(key_block * ATTEND_KEYS, ATTEND_KEYS), ATTEND_KEYS)
+                scores = lax.dot_general(
+                    query,
+                    mixed_ref[1, key_span, lanes],
+                    TURNED,
+                    preferred_element_type=jnp.float32,
+                )
+                flow = lax.dot_general(
+                    grad,
+                    mixed_ref[2, key_span, lanes],
+                    TURNED,
+                    preferred_element_type=jnp.float32,
+                )
+                mask = tile_mask(row_block, key_block, seg_col_ref, seg_row_ref)
+                probs = jnp.exp(jnp.where(mask, scores * scale, MASK_FILL) - lse)
+                probs_ref[:, key_span] = probs
+                flow_ref[:, key_span] = flow
+                product = probs * flow
+                for part in range(ATTEND_KEYS // 128):
+                    delta = delta + product[:, part * 128 : (part + 1) * 128]
+                value_sum[key_span, :] += lax.dot_general(
+                    probs.astype(jnp.bfloat16), grad, CROSSED, preferred_element_type=jnp.float32
+                )
+                return delta
+
+            delta = lax.fori_loop(
+                0, count, first, jnp.zeros((ATTEND_ROWS, 128), jnp.float32)
+            )
+            delta = jnp.sum(delta, axis=1, keepdims=True)
+
+            def second(key_block, total):
+                key_span = pl.ds(pl.multiple_of(key_block * ATTEND_KEYS, ATTEND_KEYS), ATTEND_KEYS)
+                low = (probs_ref[:, key_span] * (flow_ref[:, key_span] - delta)).astype(
+                    jnp.bfloat16
+                )
+                key_sum[key_span, :] += lax.dot_general(
+                    low, query, CROSSED, preferred_element_type=jnp.float32
+                )
+                return total + jnp.dot(
+                    low, mixed_ref[1, key_span, lanes], preferred_element_type=jnp.float32
+                )
+
+            total = lax.fori_loop(
+                0, count, second, jnp.zeros((ATTEND_ROWS, HEAD_DIM), jnp.float32)
+            )
+            query_grad = (total * scale).astype(jnp.bfloat16)
+            stacked_ref[0, row_span, lanes] = query_grad
+            return bias_sum + jnp.sum(query_grad.astype(jnp.float32), axis=0, keepdims=True)
+
+        bias_sum = lax.fori_loop(0, row_blocks, one, jnp.zeros((1, HEAD_DIM), jnp.float32))
+        bias_grad_ref[0:1, lanes] = bias_sum
+        stacked_ref[1, :, lanes] = (key_sum[...] * scale).astype(jnp.bfloat16)
+        value_grad = value_sum[...].astype(jnp.bfloat16)
+        stacked_ref[2, :, lanes] = value_grad
+        bias_grad_ref[1:2, lanes] = jnp.sum(
+            value_grad.astype(jnp.float32), axis=0, keepdims=True
+        )
+        return carry
+
+    lax.fori_loop(0, heads, one_head, 0)
+
+
+def attention_back_call(mixed, seg_col, seg_row, lse, grad):
+    _, length, width = mixed.shape
+    vmem = pl.BlockSpec(memory_space=pltpu.VMEM)
+    return pl.pallas_call(
+        attention_back_kernel,
+        out_shape=(
+            jax.ShapeDtypeStruct((3, length, width), jnp.bfloat16),
+            jax.ShapeDtypeStruct((2, width), jnp.float32),
+        ),
+        in_specs=[vmem] * 5,
+        out_specs=(vmem,) * 2,
+        scratch_shapes=[
+            pltpu.VMEM((ATTEND_ROWS, length), jnp.float32),
+            pltpu.VMEM((ATTEND_ROWS, length), jnp.float32),
+            pltpu.VMEM((length, HEAD_DIM), jnp.float32),
+            pltpu.VMEM((length, HEAD_DIM), jnp.float32),
+        ],
+        compiler_params=pltpu.CompilerParams(vmem_limit_bytes=VMEM_LIMIT),
+        cost_estimate=pl.CostEstimate(flops=3 * 10**10, bytes_accessed=0, transcendentals=0),
+        name="attention_back",
+    )(mixed, seg_col, seg_row, lse, grad)
 
 
 def tile_scores(query_tile, keys, segment, row_block, col_block):
@@ -915,13 +1901,10 @@
     slots_here = lengths.shape[0]
     slot_len = group_rows // slots_here
     local_width = mix_weight.shape[2]
-    depth = HEAD_DIM
-    heads_here = local_width // depth
     positions = jnp.arange(slot_len, dtype=jnp.int32)
     live = (positions[None, :] >= offsets[:, None]) & (
         positions[None, :] < (offsets + lengths)[:, None]
     )
-    segment = live.astype(jnp.int32)
     first_row = lax.axis_index("mp") * own_rows
     own_live = own_slice(live.reshape(-1), first_row, own_rows)[:, None]
     low = jnp.bfloat16
@@ -934,18 +1917,11 @@
         mix_bias,
         parts // 2,
     )
-    out_full = out_whole.transpose(1, 0, 2).reshape(local_width, -1)
     out_grad = jnp.where(own_live, cotangent.astype(jnp.float32), 0.0)
     bias_down_grad = jnp.sum(out_grad, axis=0)
-    queries = mixed[0].reshape(slots_here, slot_len, heads_here, depth)
-    keys = mixed[1].reshape(slots_here, slot_len, heads_here, depth)
-    values = mixed[2].reshape(slots_here, slot_len, heads_here, depth)
-
-    def attend(item):
-        return attention_forward(item[0], item[1], item[2], item[3])
-
-    attended, totals = lax.map(attend, (queries, keys, values, segment))
-    attended_flat = attended.reshape(group_rows, local_width)
+    seg_col = live.reshape(-1, 1).astype(jnp.float32)
+    seg_row = live.reshape(1, -1).astype(jnp.float32)
+    attended_flat, lse = attention_call(mixed, seg_col, seg_row)
     resid_own, normed_mid, branch_grad, up_whole, down_whole = attend_out_call(
         attended_flat,
         out_whole,
@@ -958,77 +1934,63 @@
         down_weight.astype(low),
         parts // 2,
     )
-    _, hat_two, inv_two = layer_norm_parts(resid_own, norm_gains[1], shifts[2])
-    normed_two = gather_rows(normed_mid)
-    up_full = up_whole.reshape(-1, up_whole.shape[2])
-    down_full = down_whole.transpose(1, 0, 2).reshape(down_whole.shape[1], -1)
-    hidden = jnp.dot(normed_two, up_full, preferred_element_type=jnp.float32) + up_bias
-    active_value, gelu_pull = jax.vjp(tanh_gelu, hidden)
-    active = active_value.astype(jnp.bfloat16)
-    active_grad = jnp.einsum(
-        "td,fd->tf", branch_grad, down_full, preferred_element_type=jnp.float32
-    )
-    hidden_grad = gelu_pull(active_grad)[0].astype(jnp.bfloat16)
-    two_part = jnp.einsum("tf,df->td", hidden_grad, up_full, preferred_element_type=jnp.float32)
-    two_grad = scatter_rows(two_part)
-    down_part = jnp.dot(active, down_full, preferred_element_type=jnp.float32)
-    down_grad = jnp.einsum("tf,td->fd", active, branch_grad, preferred_element_type=jnp.float32)
-    up_bias_grad = jnp.sum(hidden_grad, axis=0, dtype=jnp.float32)
-    up_grad = jnp.einsum("td,tf->df", normed_two, hidden_grad, preferred_element_type=jnp.float32)
-    resid_grad = out_grad + layer_norm_back(two_grad, hat_two, inv_two, norm_gains[1])
-    attn_branch = gather_rows(resid_grad.astype(jnp.bfloat16))
-    result_own = resid_own + scatter_rows(down_part) + shifts[3]
-    layer_output = jnp.where(own_live, result_own, 0.0).astype(jnp.bfloat16)
-    gain_two_grad = jnp.sum(two_grad * hat_two, axis=0)
-    shift_two_grad = jnp.sum(two_grad, axis=0)
-    bias_out_grad = jnp.sum(resid_grad, axis=0)
-    attended_grad = jnp.einsum(
-        "td,ed->te", attn_branch, out_full, preferred_element_type=jnp.float32
-    ).astype(jnp.bfloat16)
-    out_weight_grad = jnp.einsum(
-        "te,td->ed", attended_flat, attn_branch, preferred_element_type=jnp.float32
-    )
-
-    def attend_back(item):
-        return attention_backward(item[0], item[1], item[2], item[3], item[4], item[5])
-
-    query_grad, key_grad, value_grad = lax.map(
-        attend_back,
-        (
-            queries,
-            keys,
-            values,
-            segment,
-            totals,
-            attended_grad.reshape(slots_here, slot_len, heads_here, depth),
-        ),
-    )
-    stacked = jnp.stack(
+    own_branch = out_grad.astype(low)
+    normed_two, active, hidden_grad, resid_grad, resid_low, row_sums, up_bias_grad = feed_call(
+        normed_mid,
+        branch_grad,
+        up_whole,
+        down_whole,
+        up_bias[None],
+        resid_own,
+        own_branch,
+        norm_gains[1:2],
+        parts // 2,
+    )
+    up_bias_grad = up_bias_grad[0]
+    attended_grad, down_pieces, out_pieces, layer_output = branch_back_call(
+        resid_low,
+        active,
+        down_whole,
+        attended_flat,
+        out_whole,
+        resid_own,
+        shifts[3:4],
+        own_live.astype(jnp.float32),
+        branch_grad,
+        parts // 2,
+    )
+    stacked, mix_bias_grad = attention_back_call(mixed, seg_col, seg_row, lse, attended_grad)
+    early = jnp.concatenate(
         [
-            query_grad.reshape(group_rows, local_width),
-            key_grad.reshape(group_rows, local_width),
-            value_grad.reshape(group_rows, local_width),
-        ]
-    )
-    input_grad, gain_one_grad, shift_one_grad = input_back_call(
-        stacked, mix_whole, layer_input, resid_grad, norm_gains[0:1], parts // 2
-    )
-    gain_one_grad, shift_one_grad = gain_one_grad[0], shift_one_grad[0]
-    mix_grad = jnp.einsum("td,cte->cde", normed_one, stacked, preferred_element_type=jnp.float32)
-    mix_bias_grad = jnp.stack(
-        [
-            jnp.sum(stacked[0], axis=0, dtype=jnp.float32),
-            jnp.sum(stacked[2], axis=0, dtype=jnp.float32),
-        ]
-    )
-    mix_owned = scatter_shards(mix_grad, 1)
-    out_owned = scatter_shards(out_weight_grad, 1)
-    up_owned = scatter_shards(up_grad, 0)
-    down_owned = scatter_shards(down_grad, 1)
-    gain_grad = jnp.stack([gain_one_grad, gain_two_grad])
-    shift_grad = jnp.stack([shift_one_grad, bias_out_grad, shift_two_grad, bias_down_grad])
-    mix_bias_total, up_bias_total = lax.psum((mix_bias_grad, up_bias_grad), "dp")
-    gain_total, shift_total = lax.psum((gain_grad, shift_grad), ("dp", "mp"))
+            row_sums,
+            bias_down_grad[None],
+            jnp.pad(
+                jnp.concatenate([mix_bias_grad.reshape(-1), up_bias_grad]),
+                (0, row_sums.shape[1] - 2 * local_width - up_bias_grad.shape[0]),
+            )[None]
+        ],
+        axis=0,
+    )
+    input_grad, late, early, mix_pieces, up_pieces = input_back_call(
+        stacked,
+        mix_whole,
+        layer_input,
+        resid_grad,
+        norm_gains[0:1],
+        early,
+        hidden_grad,
+        normed_one,
+        normed_two,
+        parts // 2,
+    )
+    mix_owned = mix_pieces.transpose(1, 0, 2, 3).reshape(mix_weight.shape)
+    up_owned = up_pieces.reshape(up_weight.shape)
+    down_owned = down_pieces.reshape(down_weight.shape)
+    out_owned = out_pieces.reshape(out_weight.shape)
+    mix_bias_total = early[4, : 2 * local_width].reshape(2, local_width)
+    up_bias_total = early[4, 2 * local_width : 2 * local_width + up_bias.shape[0]]
+    gain_total = jnp.stack([late[0], early[0]])
+    shift_total = jnp.stack([late[1], early[2], early[1], early[3]])
     step_count = step[0].astype(jnp.float32)
     first_fix = 1.0 - BETA_FIRST**step_count
     second_fix = 1.0 - BETA_SECOND**step_count

time: 1020 us -> 701 us (0.69)
  Pallas kernels: 279 us -> 641 us
  waiting for transfers between devices: 286 us -> 0 us
  matrix products: 184 us -> 0 us
  local copies, waits for them, and re-layouts: 81 us -> 16.5 us
  blocking collectives: 60.8 us -> 0 us
  other arithmetic: 82 us -> 32.2 us
  starting transfers between devices: 27.2 us -> 0 us
  between operations: 19 us -> 3.51 us
    pallas_call x0 -> x4, Pallas kernels: none -> 339 us  [the longest x1 136 us: feed_call(): pl.pallas_call(functools.partial(feed_kernel, chips, parts), out_shape=(j...]
    dot_general x69 -> x0, matrix products: 184 us -> none  [the longest x10 27.1 us: attention_backward(): jnp.einsum('qhe,khe->hqk', grad_tile, value_tile, preferred_element_type=...]
    reduce_scatter x2 -> x0, waiting for transfers between devices: 156 us -> none  [scatter_rows(): lax.psum_scatter(low, 'mp', scatter_dimension=0, tiled=True)]
    all_gather x2 -> x0, waiting for transfers between devices: 77.2 us -> none  [gather_rows(): return lax.all_gather(rows, 'mp', axis=0, tiled=True)]
    psum x2 -> x0, blocking collectives: 60.8 us -> none  [the longest x1 40.2 us: per_device(): gain_total, shift_total = lax.psum((gain_grad, shift_grad), ('dp', 'mp'))]
    ppermute x24 -> x0, waiting for transfers between devices: 53.3 us -> none  [swap(): lax.ppermute(value, 'dp', [(place, place ^ mask) for place in range(size)])]
    unnamed x341 -> x80, local copies, waits for them, and re-layouts: 46.7 us -> 10.6 us
    ppermute x24 -> x0, starting transfers between devices: 27 us -> none  [swap(): lax.ppermute(value, 'dp', [(place, place ^ mask) for place in range(size)])]
  transfers between devices with their start and end apart: 28 -> 0, of which waited for: 14 -> 0; matrix products, arithmetic and copies ran while one was open for 17% -> 0% of each run, Pallas kernels for 8% -> 0%
where the time goes in v3:
time: 701 us; the launch traced here: 693 us
  Pallas kernels  641 us (91%)
  other arithmetic  32.2 us (5%)
  local copies, waits for them, and re-layouts  16.5 us (2%)
    pallas_call x1, Pallas kernels, feed_call(): pl.pallas_call(functools.partial(feed_kernel, chips, parts), out_shape=(j...  136 us
    pallas_call x1, Pallas kernels, branch_back_call(): pl.pallas_call(functools.partial(branch_back_kernel, chips, 2), out_shape...  123 us
    pallas_call x1, Pallas kernels, input_back_call(): pl.pallas_call(functools.partial(input_back_kernel, chips), out_shape=(ja...  110 us
    pallas_call x1, Pallas kernels, attend_out_call(): pl.pallas_call(functools.partial(attend_out_kernel, chips), out_shape=(ja...  107 us
    pallas_call x1, Pallas kernels, project_call(): pl.pallas_call(functools.partial(project_kernel, chips), out_shape=(jax.S...  84.9 us
    pallas_call x1, Pallas kernels, attention_back_call(): pl.pallas_call(attention_back_kernel, out_shape=(jax.ShapeDtypeStruct((3,...  48 us
    pallas_call x1, Pallas kernels, attention_call(): pl.pallas_call(attention_kernel, out_shape=(jax.ShapeDtypeStruct((length,...  31.7 us

profile of v3, /device:TPU:0, one launch (start us, length us, event | category | flops | bytes accessed | tf_op | source)
XLA Modules:
  0.0 692.9 jit_solution(4794889125790978000)
XLA Ops:
  0.7 1.6 fusion.27
  2.3 2.4 convert_element_type.48.mix_ref
  4.6 0.7 convert_element_type.49.out_ref
  5.4 84.9 %project.1 = (bf16[2048,2048]{1,0:T(8,128)(2,1)}, bf16[3,2048,256]{2,1,0:T(8,128)(2,1)}, bf16[3,4,512,256]{3,2,1,0:T(8,128)(2,1)}, bf16[4,256,512]{2,1,0:T(8,128)(2,1)}) custom-call(bf16[256,2048]{1,0:T(8,128)(2,1)} %rows_ref.5, f32[1,2048]{1,0:T(1,128)} %get-tuple-element.142.gain_ref, f32[1,2048]{1,0:T(1,128)} %get-tuple-element.135.shift_ref, ...), custom_call_target="tpu_custom_call" | custom-call | flops 45097156608 | tf_op jit(solution)/shard_map/project/pallas_call | solution.py:426
  91.6 0.6 compare_and_fusion
  92.2 1.1 fusion.6.seg_col_ref
  93.4 31.7 %attention.1 = (bf16[2048,256]{1,0:T(8,128)(2,1)}, f32[2,2048,1]{2,1,0:T(8,128)}) custom-call(bf16[3,2048,256]{2,1,0:T(8,128)(2,1)} %get-tuple-element.67.mixed_ref, f32[2048,1]{1,0:T(8,128)} %fusion.6.seg_col_ref, f32[1,2048]{1,0:T(1,128)} %get-tuple-element.145.seg_row_ref), custom_call_target="tpu_custom_call" | custom-call | flops 10000000000 | tf_op jit(solution)/shard_map/attention/pallas_call | solution.py:1627
  125.1 0.6 fusion.12
  125.7 1.9 fusion.2
  127.5 1.1 convert_element_type.54.up_ref
  128.7 0.8 copy-done.2
  129.5 1.1 convert_element_type.55.down_ref
  130.6 107.0 %attend_out.1 = (f32[256,2048]{1,0:T(8,128)}, bf16[256,2048]{1,0:T(8,128)(2,1)}, bf16[2048,2048]{1,0:T(8,128)(2,1)}, bf16[4,512,1024]{2,1,0:T(8,128)(2,1)}, bf16[4,1024,512]{2,1,0:T(8,128)(2,1)}) custom-call(bf16[2048,256]{1,0:T(8,128)(2,1)} %get-tuple-element.68.attended_ref, bf16[4,256,512]{2,1,0:T(8,128)(2,1)} %get-tuple-element.69.out_ref, ...), custom_call_target="tpu_custom_call" | custom-call | flops 99999997952 | tf_op jit(solution)/shard_map/attend_out/pallas_call | solution.py:882
  237.6 0.0 copy-start.29
  237.7 136.4 %feed.1 = (bf16[2048,2048]{1,0:T(8,128)(2,1)}, bf16[2048,1024]{1,0:T(8,128)(2,1)}, bf16[2048,1024]{1,0:T(8,128)(2,1)}, f32[256,2048]{1,0:T(8,128)}, bf16[256,204...) custom-call(bf16[256,2048]{1,0:T(8,128)(2,1)} %get-tuple-element.70.normed_ref, ...), custom_call_target="tpu_custom_call" | custom-call | flops 99999997952 | tf_op jit(solution)/shard_map/feed/pallas_call | solution.py:1343
  374.1 0.8 copy.67.live_ref
  374.9 122.6 %branch_back.1 = (bf16[2048,256]{1,0:T(8,128)(2,1)}, f32[2,512,512]{2,1,0:T(8,128)}, f32[2,128,512]{2,1,0:T(8,128)}, bf16[256,2048]{1,0:T(8,128)(2,1)}) custom-call(bf16[256,2048]{1,0:T(8,128)(2,1)} %get-tuple-element.75.branch_ref, bf16[2048,1024]{1,0:T(8,128)(2,1)} %get-tuple-element.76.active_ref, bf16[4,1024,512]{2,1,0:T(8,128)(2,1)} %get-tuple-element.73.down_ref, ...), custom_call_target="tpu_custom_call" | custom-call | flops 99999997952 | tf_op jit(solution)/shard_map/branch_back/pallas_call | solution.py:1521
  497.5 0.0 copy-start.21
  497.6 48.0 %attention_back.1 = (bf16[3,2048,256]{2,1,0:T(8,128)(2,1)}, f32[2,256]{1,0:T(2,128)}) custom-call(bf16[3,2048,256]{2,1,0:T(8,128)(2,1)} %get-tuple-element.67.mixed_ref, f32[2048,1]{1,0:T(8,128)} %fusion.6.seg_col_ref, f32[1,2048]{1,0:T(1,128)} %get-tuple-element.145.seg_row_ref, f32[2,2048,1]{2,1,0:T(8,128)} %get-tuple-element.78.lse_ref, ...), custom_call_target="tpu_custom_call" | custom-call | flops 30000001024 | tf_op jit(solution)/shard_map/attention_back/pallas_call | solution.py:1738
  545.6 0.7 copy.69
  546.3 0.7 pad_maximum_fusion.early_ref
  547.0 0.0 copy-start.27
  547.0 0.0 copy-start.1
  547.0 110.0 %input_back.1 = (f32[256,2048]{1,0:T(8,128)}, f32[2,2048]{1,0:T(2,128)}, f32[5,2048]{1,0:T(8,128)}, f32[2,3,256,256]{3,2,1,0:T(8,128)}, f32[2,256,1024]{2,1,0:T(8,128)}) custom-call(bf16[3,2048,256]{2,1,0:T(8,128)(2,1)} %get-tuple-element.80.stacked_ref, bf16[3,4,512,256]{3,2,1,0:T(8,128)(2,1)} %get-tuple-element.81.mix_ref, bf16[256,2048]{1,0:T(8,128)(2,1)} %rows_ref.5, ...), custom_call_target="tpu_custom_call" | custom-call | flops 99999997952 | tf_op jit(solution)/shard_map/input_back/pallas_call | solution.py:1038
  657.0 1.0 fusion.26
  658.0 0.8 fusion.28
  659.6 0.7 multiply_subtract_fusion.4
  660.3 0.7 multiply_subtract_fusion.5
  661.0 7.5 %fusion.16 = (bf16[512,1024]{1,0:T(8,128)(2,1)}, f32[512,1024]{1,0:T(8,128)}, f32[512,1024]{1,0:T(8,128)}, f32[512,1024]{1,0:T(8,128)}) fusion(f32[512,1024]{1,0:T(8,128)S(1)} %copy-done.1, f32[]{:T(128)} %bitcast.10, f32[]{:T(128)} %bitcast.9, f32[512,1024]{1,0:T(8,128)} %param.44, f32[512,1024]{1,0:T(8,128)} %param.40, f32[2,256,1024]{2,1,0:T(8,128)} %get-tuple-element.92), kind=kLoop, calls=%fused_computation.51 | loop fusion | flops 8388608 | bytes 15728648 | tf_op jit(solution)/shard_map/convert_element_type | solution.py:2093
  668.5 0.2 copy.68
  668.7 1.2 copy-done.6
  669.9 0.5 copy-done.12
  670.4 0.0 copy-start.34
  670.5 3.2 fusion.20
  673.7 0.8 slice.51
  674.5 0.6 multiply_subtract_fusion.6
  675.1 0.7 slice_reduce_fusion
  675.9 0.6 multiply_subtract_fusion.7
  676.5 7.1 %fusion.14 = (bf16[1024,512]{1,0:T(8,128)(2,1)}, f32[1024,512]{1,0:T(8,128)}, f32[1024,512]{1,0:T(8,128)}, f32[1024,512]{1,0:T(8,128)}) fusion(f32[1024,512]{1,0:T(8,128)S(1)} %copy-done.3, f32[]{:T(128)} %bitcast.10, f32[]{:T(128)} %bitcast.9, f32[1024,512]{1,0:T(8,128)} %param.45, f32[1024,512]{1,0:T(8,128)} %param.41, f32[2,512,512]{2,1,0:T(8,128)} %get-tuple-element.93), kind=kLoop, calls=%fused_computation.50 | loop fusion | flops 8388608 | bytes 15728648 | tf_op jit(solution)/shard_map/convert_element_type | solution.py:2094
  683.7 1.5 fusion.18
  685.2 1.0 copy.78
  686.2 0.2 copy-done.11
  686.4 1.3 copy.79
  687.7 0.8 copy.80
  688.5 0.4 copy-done.5
  688.8 1.3 copy.81
  690.1 1.0 copy-done.4
  691.2 1.3 copy.82
  (65 shorter events, 0.2 us)
Async XLA Ops:
  0.7 3.9 copy-start.8
  93.4 32.3 %copy-start.15 = (bf16[256,2048]{1,0:T(8,128)(2,1)S(1)}, bf16[256,2048]{1,0:T(8,128)(2,1)}, u32[]{:S(2)}) copy-start(bf16[256,2048]{1,0:T(8,128)(2,1)} %param.30) | copy-start | bytes 3145732
  125.1 2.5 copy-start
  127.5 2.0 copy-start.2
  237.6 136.4 %copy-start.29 = (f32[256,1]{0,1:T(1,128)S(1)}, f32[256,1]{0,1:T(1,128)}, u32[]{:S(2)}) copy-start(f32[256,1]{0,1:T(1,128)} %get-tuple-element.140) | copy-start | bytes 3076
  497.5 48.8 %copy-start.30 = (f32[1,1024]{1,0:T(1,128)S(1)}, f32[1,1024]{1,0:T(1,128)}, u32[]{:S(2)}) copy-start(f32[1,1024]{1,0:T(1,128)} %get-tuple-element.85) | copy-start | bytes 12292
  497.5 48.8 %copy-start.21 = (f32[2048]{0:T(1024)S(1)}, f32[2048]{0:T(1024)}, u32[]{:S(2)}) copy-start(f32[2048]{0:T(1024)} %get-tuple-element.126) | copy-start | bytes 24580
  497.6 48.8 %copy-start.22 = (f32[3,2048]{1,0:T(4,128)S(1)}, f32[3,2048]{1,0:T(4,128)}, u32[]{:S(2)}) copy-start(f32[3,2048]{1,0:T(4,128)} %get-tuple-element.83) | copy-start | bytes 73732
  547.0 112.6 %copy-start.19 = (f32[4,2048]{1,0:T(4,128)S(1)}, f32[4,2048]{1,0:T(4,128)}, u32[]{:S(2)}) copy-start(f32[4,2048]{1,0:T(4,128)} %param.49) | copy-start | bytes 98308
  547.0 112.6 %copy-start.23 = (f32[4,2048]{1,0:T(4,128)S(1)}, f32[4,2048]{1,0:T(4,128)}, u32[]{:S(2)}) copy-start(f32[4,2048]{1,0:T(4,128)} %param.57) | copy-start | bytes 98308
  547.0 112.6 %copy-start.24 = (f32[4,2048]{1,0:T(4,128)S(1)}, f32[4,2048]{1,0:T(4,128)}, u32[]{:S(2)}) copy-start(f32[4,2048]{1,0:T(4,128)} %param.53) | copy-start | bytes 98308
  547.0 113.3 %copy-start.20 = (f32[2,2048]{1,0:T(2,128)S(1)}, f32[2,2048]{1,0:T(2,128)}, u32[]{:S(2)}) copy-start(f32[2,2048]{1,0:T(2,128)} %param.48) | copy-start | bytes 49156
  547.0 113.3 %copy-start.26 = (f32[2,2048]{1,0:T(2,128)S(1)}, f32[2,2048]{1,0:T(2,128)}, u32[]{:S(2)}) copy-start(f32[2,2048]{1,0:T(2,128)} %param.56) | copy-start | bytes 49156
  547.0 113.3 %copy-start.27 = (f32[2,2048]{1,0:T(2,128)S(1)}, f32[2,2048]{1,0:T(2,128)}, u32[]{:S(2)}) copy-start(f32[2,2048]{1,0:T(2,128)} %param.52) | copy-start | bytes 49156
  547.0 114.0 %copy-start.1 = (f32[512,1024]{1,0:T(8,128)S(1)}, f32[512,1024]{1,0:T(8,128)}, u32[]{:S(2)}) copy-start(f32[512,1024]{1,0:T(8,128)} %param.36) | copy-start | bytes 6291460
  661.0 7.5 %copy-start.14 = (f32[2,3,256,256]{3,2,1,0:T(8,128)S(1)}, f32[2,3,256,256]{3,2,1,0:T(8,128)}, u32[]{:S(2)}) copy-start(f32[2,3,256,256]{3,2,1,0:T(8,128)} %get-tuple-element.90) | copy-start | bytes 4718596
  661.0 7.7 %copy-start.13 = (f32[3,512,256]{2,1,0:T(8,128)S(1)}, f32[3,512,256]{2,1,0:T(8,128)}, u32[]{:S(2)}) copy-start(f32[3,512,256]{2,1,0:T(8,128)} %param.38) | copy-start | bytes 4718596
  668.5 1.4 copy-start.6
  668.5 1.9 copy-start.12
  670.4 3.2 copy-start.7
  670.4 4.0 copy-start.31
  670.4 4.0 copy-start.32
  670.4 4.0 copy-start.33
  670.4 5.4 copy-start.34
  670.5 5.4 copy-start.35
  670.5 5.4 copy-start.36
  670.5 6.0 copy-start.3
  674.4 9.2 %copy-start.25 = (f32[1,1024]{1,0:T(1,128)}, f32[1,1024]{1,0:T(1,128)S(1)}, u32[]{:S(2)}) copy-start(f32[1,1024]{1,0:T(1,128)S(1)} %slice.51) | copy-start | bytes 12292
  675.9 7.8 %copy-start.28 = (f32[2,256]{1,0:T(2,128)}, f32[2,256]{1,0:T(2,128)S(1)}, u32[]{:S(2)}) copy-start(f32[2,256]{1,0:T(2,128)S(1)} %reshape_squeeze.3) | copy-start | bytes 6148
  676.5 7.2 %copy-start.9 = (f32[256,512]{1,0:T(8,128)S(1)}, f32[256,512]{1,0:T(8,128)}, u32[]{:S(2)}) copy-start(f32[256,512]{1,0:T(8,128)} %param.35) | copy-start | bytes 1572868
  676.5 7.2 %copy-start.10 = (f32[2,128,512]{2,1,0:T(8,128)S(1)}, f32[2,128,512]{2,1,0:T(8,128)}, u32[]{:S(2)}) copy-start(f32[2,128,512]{2,1,0:T(8,128)} %get-tuple-element.91) | copy-start | bytes 1572868
  676.5 7.2 %copy-start.17 = (f32[256,512]{1,0:T(8,128)S(1)}, f32[256,512]{1,0:T(8,128)}, u32[]{:S(2)}) copy-start(f32[256,512]{1,0:T(8,128)} %param.43) | copy-start | bytes 1572868
  676.5 7.2 %copy-start.18 = (f32[256,512]{1,0:T(8,128)S(1)}, f32[256,512]{1,0:T(8,128)}, u32[]{:S(2)}) copy-start(f32[256,512]{1,0:T(8,128)} %param.39) | copy-start | bytes 1572868
  683.7 1.6 copy-start.16
  683.7 2.6 copy-start.11
  686.4 2.5 copy-start.5
  688.8 2.3 copy-start.4

commit v4 on v3

--- a/solution.py
+++ b/solution.py
@@ -102,7 +102,7 @@
 
 
 MESH = pl.DeviceIdType.MESH
-VMEM_LIMIT = 60 * 1024 * 1024
+VMEM_LIMIT = 62 * 1024 * 1024
 TURNED = (((1,), (1,)), ((), ()))
 CROSSED = (((0,), (0,)), ((), ()))
 
@@ -165,18 +165,28 @@
     )
 
 
+def fetch(pairs, sems):
+    copies = [
+        pltpu.make_async_copy(source, target, sems.at[index])
+        for index, (source, target) in enumerate(pairs)
+    ]
+    for copy in copies:
+        copy.start()
+    return copies
+
+
 class LineGather:
-    def __init__(self, place, blocks, send, recv, parts=1):
+    def __init__(self, place, blocks, send, recv, parts=1, own=None):
         self.place, self.blocks, self.send, self.recv = place, blocks, send, recv
-        self.parts = parts
-
-    def copy(self, way, chip, part=0):
+        self.parts, self.own = parts, own
+
+    def copy(self, way, chip, part=0, own=None):
         place = self.place
         piece = chip * self.parts + part
         block = 2 * piece + place.core
         device = (place.up, place.down, place.side)[way]
         return remote(
-            self.blocks.at[block],
+            self.blocks.at[block] if own is None else own,
             self.blocks.at[block],
             self.send.at[way, piece],
             self.recv.at[block],
@@ -197,9 +207,9 @@
     def begin(self):
         place = self.place
         for part in range(self.parts):
-            pl.when(place.has_up)(lambda: self.copy(0, place.chip, part).start())
-            pl.when(place.has_down)(lambda: self.copy(1, place.chip, part).start())
-            self.copy(2, place.chip, part).start()
+            pl.when(place.has_up)(lambda: self.copy(0, place.chip, part, self.own).start())
+            pl.when(place.has_down)(lambda: self.copy(1, place.chip, part, self.own).start())
+            self.copy(2, place.chip, part, self.own).start()
 
     def step(self, distance, part=0):
         place = self.place
@@ -299,13 +309,26 @@
     rows_ref,
     gain_ref,
     shift_ref,
+    mix_weight_ref,
+    out_weight_ref,
+    bias_ref,
+    up_weight_ref,
+    down_weight_ref,
+    cotangent_ref,
+    bounds_ref,
+    normed_ref,
+    mixed_hbm,
+    mix_hbm,
+    out_whole,
+    up_ref,
+    down_ref,
+    branch_ref,
+    branch_sum_ref,
     mix_ref,
     out_ref,
-    bias_ref,
-    normed_ref,
     mixed_ref,
     mix_whole,
-    out_whole,
+    emit_sem,
     blocks,
     line_send,
     line_recv,
@@ -335,6 +358,16 @@
         out_send,
         out_recv,
     )
+
+    def lower(source, target):
+        def one(span):
+            target[span, :] = source[span, :].astype(jnp.bfloat16)
+
+        by_rows(source.shape[0], 64, one)
+
+    for part in range(3):
+        lower(mix_weight_ref.at[part], mix_ref.at[part])
+    lower(out_weight_ref, out_ref)
     mix.begin()
     own_mix = pltpu.make_async_copy(mix_ref, mix_whole.at[:, place.dp], own_sem.at[0])
     own_out = pltpu.make_async_copy(out_ref, out_whole.at[place.dp], own_sem.at[1])
@@ -352,12 +385,31 @@
     lax.fori_loop(0, count // tile, norm, 0)
     line = LineGather(place, blocks, line_send, line_recv)
     line.begin()
+    branch_sum_ref[...] = jnp.zeros_like(branch_sum_ref)
+
+    def branch(span):
+        live = alive((64, 1), 0, place.me * count + span.start, bounds_ref)
+        grad = jnp.where(live > 0, cotangent_ref[span, :].astype(jnp.float32), 0.0)
+        branch_ref[span, :] = grad.astype(jnp.bfloat16)
+        branch_sum_ref[...] += jnp.sum(grad, axis=0, keepdims=True)
+
+    by_rows(count, 64, branch)
+    lower(up_weight_ref, up_ref)
+    lower(down_weight_ref, down_ref)
     mix.middle()
     out.begin()
 
     def keep(block):
         span = pl.ds(pl.multiple_of(block * count, count), count)
         return pltpu.make_async_copy(blocks.at[block], normed_ref.at[span], keep_sem.at[block])
+
+    def emit(block):
+        span = pl.ds(pl.multiple_of(block * count, count), count)
+        return pltpu.make_async_copy(
+            mixed_ref.at[:, span], mixed_hbm.at[:, span], emit_sem.at[block]
+        )
+
+    keep_mix = pltpu.make_async_copy(mix_whole, mix_hbm, emit_sem.at[2 * chips])
 
     def project(block):
         keep(block).start()
@@ -371,6 +423,7 @@
             if part == 2:
                 result = result + bias_ref[1:2, :]
             mixed_ref[part, span, :] = result.astype(jnp.bfloat16)
+        emit(block).start()
 
     def step(distance, carry):
         @pl.when((distance > 0) & (distance < chips))
@@ -381,6 +434,7 @@
         def _():
             mix.end()
             own_mix.wait()
+            keep_mix.start()
             out.middle()
 
         def one(index, inner):
@@ -411,12 +465,16 @@
 
     def kept(block, carry):
         keep(block).wait()
+        emit(block).wait()
         return carry
 
     lax.fori_loop(0, 2 * chips, kept, 0)
-
-
-def project_call(rows, gain, shift, mix_shard, out_shard, bias, chips):
+    keep_mix.wait()
+
+
+def project_call(
+    rows, gain, shift, mix_shard, out_shard, bias, up, down, cotangent, bounds, chips
+):
     count, width = rows.shape
     total = 2 * chips * count
     local = mix_shard.shape[2]
@@ -430,10 +488,19 @@
             jax.ShapeDtypeStruct((3, total, local), jnp.bfloat16),
             jax.ShapeDtypeStruct((3, 4, mix_shard.shape[1], local), jnp.bfloat16),
             jax.ShapeDtypeStruct((4,) + out_shard.shape, jnp.bfloat16),
+            jax.ShapeDtypeStruct(up.shape, jnp.bfloat16),
+            jax.ShapeDtypeStruct(down.shape, jnp.bfloat16),
+            jax.ShapeDtypeStruct((count, width), jnp.bfloat16),
+            jax.ShapeDtypeStruct((1, width), jnp.float32),
         ),
-        in_specs=[vmem] * 6,
-        out_specs=(pl.BlockSpec(memory_space=pl.ANY), vmem, vmem, vmem),
+        in_specs=[vmem] * 9 + [pl.BlockSpec(memory_space=pltpu.SMEM)],
+        out_specs=(pl.BlockSpec(memory_space=pl.ANY),) * 4 + (vmem,) * 4,
         scratch_shapes=[
+            pltpu.VMEM(mix_shard.shape, jnp.bfloat16),
+            pltpu.VMEM(out_shard.shape, jnp.bfloat16),
+            pltpu.VMEM((3, total, local), jnp.bfloat16),
+            pltpu.VMEM((3, 4, mix_shard.shape[1], local), jnp.bfloat16),
+            dma((2 * chips + 1,)),
             pltpu.VMEM((2 * chips, count, width), jnp.bfloat16),
             dma((3, chips)),
             dma((2 * chips,)),
@@ -449,12 +516,12 @@
         ),
         cost_estimate=pl.CostEstimate(flops=flops * 7, bytes_accessed=0, transcendentals=0),
         name="project",
-    )(rows, gain, shift, mix_shard, out_shard, bias)
+    )(rows, gain, shift, mix_shard, out_shard, bias, up, down, cotangent, bounds)
 
 
 class LineScatter:
-    def __init__(self, place, term, tiles, bufs, sems):
-        self.place, self.term, self.tiles = place, term, tiles
+    def __init__(self, place, term, tiles, bufs, sems, prepare=lambda chip: None):
+        self.place, self.term, self.tiles, self.prepare = place, term, tiles, prepare
         self.total, self.side_out, self.side_in, self.line_in = bufs
         self.side_send, self.side_recv, self.line_send, self.line_recv = sems
 
@@ -467,26 +534,30 @@
             self.place.side,
         )
 
-    def line_copy(self, way, chip):
+    def span(self, tile):
+        width = self.total.shape[1] // self.tiles
+        return slice(tile * width, (tile + 1) * width)
+
+    def line_copy(self, way, chip, tile):
         place = self.place
         next_chip = place.chip + 1 - 2 * way
         slot = jnp.where((way == 1) & (chip == next_chip), place.chips, chip)
         return remote(
-            self.line_in.at[chip],
-            self.line_in.at[slot],
-            self.line_send.at[chip],
-            self.line_recv.at[slot],
+            self.line_in.at[chip, :, self.span(tile)],
+            self.line_in.at[slot, :, self.span(tile)],
+            self.line_send.at[chip, tile],
+            self.line_recv.at[slot, tile],
             (place.up, place.down)[way],
         )
 
-    def landed(self, way, chip):
+    def landed(self, way, chip, tile):
         place = self.place
         slot = jnp.where((way == 1) & (chip == place.chip), place.chips, chip)
         remote(
-            self.line_in.at[slot],
-            self.line_in.at[slot],
-            self.line_send.at[chip],
-            self.line_recv.at[slot],
+            self.line_in.at[slot, :, self.span(tile)],
+            self.line_in.at[slot, :, self.span(tile)],
+            self.line_send.at[chip, tile],
+            self.line_recv.at[slot, tile],
             (place.up, place.down)[way],
         ).wait_recv()
         return slot
@@ -503,37 +574,35 @@
         lax.fori_loop(0, 2, one, 0)
 
     def hand_over(self, chip):
+        self.prepare(chip)
         block = 2 * chip + 1 - self.place.core
-        width = self.total.shape[1] // self.tiles
         for tile in range(self.tiles):
-            span = slice(tile * width, (tile + 1) * width)
-            self.side_out[chip, :, span] = self.term(block, tile).astype(jnp.bfloat16)
+            self.side_out[chip, :, self.span(tile)] = self.term(block, tile).astype(jnp.bfloat16)
         self.side_copy(chip).start()
 
     def sum_up(self, chip):
         place = self.place
         block = 2 * chip + place.core
-        width = self.total.shape[1] // self.tiles
         self.side_copy(chip).wait_recv()
         for tile in range(self.tiles):
-            span = slice(tile * width, (tile + 1) * width)
+            span = self.span(tile)
             self.total[:, span] = self.term(block, tile) + self.side_in[chip, :, span].astype(
                 jnp.float32
             )
-        for way in range(2):
-            behind = (place.has_down, place.has_up)[way]
-            goes = (chip >= place.chip) if way == 0 else (chip <= place.chip)
-
-            @pl.when(behind & goes)
+            for way in range(2):
+                behind = (place.has_down, place.has_up)[way]
+                goes = (chip >= place.chip) if way == 0 else (chip <= place.chip)
+
+                @pl.when(behind & goes)
+                def _():
+                    slot = self.landed(way, chip, tile)
+                    self.total[:, span] += self.line_in[slot, :, span].astype(jnp.float32)
+
+            @pl.when(chip != place.chip)
             def _():
-                slot = self.landed(way, chip)
-                self.total[...] += self.line_in[slot].astype(jnp.float32)
-
-        @pl.when(chip != place.chip)
-        def _():
-            self.line_in[chip] = self.total[...].astype(jnp.bfloat16)
-            pl.when(chip > place.chip)(lambda: self.line_copy(0, chip).start())
-            pl.when(chip < place.chip)(lambda: self.line_copy(1, chip).start())
+                self.line_in[chip, :, span] = self.total[:, span].astype(jnp.bfloat16)
+                pl.when(chip > place.chip)(lambda: self.line_copy(0, chip, tile).start())
+                pl.when(chip < place.chip)(lambda: self.line_copy(1, chip, tile).start())
 
     def begin(self):
         self.each(self.place.chips - 1, self.hand_over)
@@ -548,7 +617,8 @@
 
         def drain(chip, carry):
             self.side_copy(chip).wait_send()
-            pl.when(chip != place.chip)(lambda: self.line_copy(0, chip).wait_send())
+            for tile in range(self.tiles):
+                pl.when(chip != place.chip)(lambda: self.line_copy(0, chip, tile).wait_send())
             return carry
 
         lax.fori_loop(0, place.chips, drain, 0)
@@ -572,22 +642,30 @@
             (peer, place.me),
         )
 
+    def owner(self, kind, way):
+        place = self.place
+        near = place.x_peer + way * (place.y_peer - place.x_peer)
+        other = place.y_peer + way * (place.x_peer - place.y_peer)
+        return (place.across, near, other, place.dp)[kind]
+
+    def following(self, kind, way):
+        after = self.owner(kind, 1) if kind == 3 else self.owner(kind + 1, 0)
+        return jnp.where(way == 0, self.owner(kind, 1), after), 1 - way
+
+    def one(self, kind, way):
+        value = self.piece(self.owner(kind, way), way)
+        if kind == 2:
+            self.copy(0, way).wait_recv()
+            value = value + self.arrived[0, way].astype(jnp.float32)
+        if kind < 3:
+            self.out[kind, way] = value.astype(jnp.bfloat16)
+            self.copy(kind, way).start()
+        else:
+            self.owned[way] = value
+
     def stage(self, kind):
-        place = self.place
-
         def one(way, carry):
-            near = place.x_peer + way * (place.y_peer - place.x_peer)
-            other = place.y_peer + way * (place.x_peer - place.y_peer)
-            owner = (place.across, near, other, place.dp)[kind]
-            value = self.piece(owner, way)
-            if kind == 2:
-                self.copy(0, way).wait_recv()
-                value = value + self.arrived[0, way].astype(jnp.float32)
-            if kind < 3:
-                self.out[kind, way] = value.astype(jnp.bfloat16)
-                self.copy(kind, way).start()
-            else:
-                self.owned[way] = value
+            self.one(kind, way)
             return carry
 
         lax.fori_loop(0, 2, one, 0)
@@ -740,9 +818,14 @@
         pltpu.VMEM((chips + 1, count, width), low),
         dma((chips,)),
         dma((chips,)),
-        dma((chips,)),
-        dma((chips + 1,)),
+        dma((chips, 4)),
+        dma((chips + 1, 4)),
     ]
+
+
+def alive(shape, axis, start, bounds_ref):
+    place = lax.broadcasted_iota(jnp.int32, shape, axis) + start
+    return jnp.where((place >= bounds_ref[0]) & (place < bounds_ref[1]), 1.0, 0.0)
 
 
 def by_rows(count, tile, action):
@@ -755,20 +838,30 @@
 
 def attend_out_kernel(
     chips,
-    attended_ref,
-    out_ref,
-    rows_ref,
+    mixed_hbm,
+    bounds_ref,
+    out_hbm,
+    rows_hbm,
     branch_ref,
     gain_ref,
     shift_ref,
     bias_ref,
     up_ref,
     down_ref,
+    attended_ref,
+    lse_ref,
     resid_ref,
     normed_ref,
     branch_whole,
     up_whole,
     down_whole,
+    mixed_ref,
+    out_ref,
+    rows_ref,
+    fetch_sem,
+    seg_col_ref,
+    seg_row_ref,
+    score_ref,
     blocks,
     line_send,
     line_recv,
@@ -782,6 +875,9 @@
 ):
     place = Place(chips)
     count = rows_ref.shape[0]
+    fetched = fetch(
+        [(mixed_hbm, mixed_ref), (out_hbm, out_ref), (rows_hbm, rows_ref)], fetch_sem
+    )
     place.greet(True)
 
     def square(shard, whole, send, recv):
@@ -809,8 +905,22 @@
         span = pl.ds(pl.multiple_of(block * count, count), count)
         return jnp.dot(attended_ref[span, :], out_ref[tile], preferred_element_type=jnp.float32)
 
-    sums = LineScatter(place, term, 4, scatter[:4], scatter[4:8])
-    sums.begin()
+    def prepare(chip):
+        def one(index, carry):
+            for head in range(mixed_ref.shape[2] // HEAD_DIM):
+                attend_rows(
+                    head,
+                    chip * (2 * count // ATTEND_ROWS) + index,
+                    mixed_ref,
+                    seg_col_ref,
+                    seg_row_ref,
+                    attended_ref,
+                    lse_ref,
+                    score_ref,
+                )
+            return carry
+
+        lax.fori_loop(0, 2 * count // ATTEND_ROWS, one, 0)
 
     def copy_in(span):
         blocks[place.me, span, :] = branch_ref[span, :]
@@ -818,6 +928,16 @@
     by_rows(count, 64, copy_in)
     line = LineGather(place, blocks, line_send, line_recv)
     line.begin()
+    seg_row_ref[...] = alive(seg_row_ref.shape, 1, 0, bounds_ref)
+
+    def column(span):
+        seg_col_ref[span, :] = alive((64, 1), 0, span.start, bounds_ref)
+
+    by_rows(seg_col_ref.shape[0], 64, column)
+    for copy in fetched:
+        copy.wait()
+    sums = LineScatter(place, term, 4, scatter[:4], scatter[4:8], prepare)
+    sums.begin()
 
     def keep(block, part):
         half = count // 2
@@ -872,8 +992,11 @@
     lax.fori_loop(0, 2 * chips, kept, 0)
 
 
-def attend_out_call(attended, out_whole, rows, branch, gain, shift, bias, up, down, chips):
+def attend_out_call(
+    mixed, bounds, out_whole, rows, branch, gain, shift, bias, up, down, chips
+):
     count, width = rows.shape
+    local = mixed.shape[2]
     total = 2 * chips * count
     low = jnp.bfloat16
     vmem = pl.BlockSpec(memory_space=pltpu.VMEM)
@@ -882,15 +1005,24 @@
     return pl.pallas_call(
         functools.partial(attend_out_kernel, chips),
         out_shape=(
+            jax.ShapeDtypeStruct((total, local), low),
+            jax.ShapeDtypeStruct((total, 1 + local // HEAD_DIM), jnp.float32),
             jax.ShapeDtypeStruct((count, width), jnp.float32),
             jax.ShapeDtypeStruct((count, width), low),
             jax.ShapeDtypeStruct((total, width), low),
             jax.ShapeDtypeStruct((4,) + up.shape, low),
             jax.ShapeDtypeStruct((4,) + down.shape, low),
         ),
-        in_specs=[vmem] * 9,
-        out_specs=(vmem, vmem, hbm, vmem, vmem),
+        in_specs=[hbm, pl.BlockSpec(memory_space=pltpu.SMEM), hbm, hbm] + [vmem] * 6,
+        out_specs=(vmem, vmem, vmem, vmem, hbm, hbm, hbm),
         scratch_shapes=[
+            pltpu.VMEM(mixed.shape, low),
+            pltpu.VMEM(out_whole.shape, low),
+            pltpu.VMEM(rows.shape, low),
+            dma((3,)),
+            pltpu.VMEM((total, 1), jnp.float32),
+            pltpu.VMEM((1, total), jnp.float32),
+            pltpu.VMEM((ATTEND_ROWS, total), jnp.float32),
             pltpu.VMEM((2 * chips, count, width), low),
             dma((3, chips)),
             dma((2 * chips,)),
@@ -907,18 +1039,19 @@
         ),
         cost_estimate=pl.CostEstimate(flops=10**11, bytes_accessed=0, transcendentals=0),
         name="attend_out",
-    )(attended, out_whole, rows, branch, gain, shift, bias, up, down)
+    )(mixed, bounds, out_whole, rows, branch, gain, shift, bias, up, down)
 
 
 def input_back_kernel(
     chips,
-    stacked_ref,
-    mix_ref,
-    rows_ref,
-    resid_grad_ref,
+    stacked_hbm,
+    mix_hbm,
+    rows_hbm,
+    resid_grad_hbm,
     gain_ref,
     early_ref,
-    hidden_ref,
+    hidden_hbm,
+    out_grad_hbm,
     normed_one_ref,
     normed_two_ref,
     grad_ref,
@@ -926,13 +1059,34 @@
     early_out_ref,
     mix_grad_ref,
     up_grad_ref,
+    out_owned_ref,
+    stacked_ref,
+    mix_ref,
+    rows_ref,
+    resid_grad_ref,
+    hidden_ref,
+    out_grad_ref,
+    fetch_sem,
     columns_buf,
     columns_sem,
     *scatter,
 ):
     place = Place(chips)
     count = rows_ref.shape[0]
+    fetched = fetch(
+        [
+            (stacked_hbm, stacked_ref),
+            (mix_hbm, mix_ref),
+            (hidden_hbm, hidden_ref),
+            (out_grad_hbm, out_grad_ref),
+            (rows_hbm, rows_ref),
+            (resid_grad_hbm, resid_grad_ref),
+        ],
+        fetch_sem,
+    )
     place.greet(True, True)
+    fetched[0].wait()
+    fetched[1].wait()
     early_out_ref[...] = early_ref[...]
     early = SmallSum(place, early_out_ref, 4, scatter[16:19], scatter[19:21])
     late = SmallSum(place, late_out_ref, late_out_ref.shape[0], scatter[21:24], scatter[24:26])
@@ -953,22 +1107,21 @@
     sums = LineScatter(place, term, 4, scatter[:4], scatter[4:8])
     sums.begin()
     early.begin()
-    half_columns = columns_buf.shape[1]
-
-    def load(source, owner, half):
+    half_columns = columns_buf.shape[2]
+
+    def load(which, owner, half):
         start = pl.multiple_of((2 * owner + half) * half_columns, half_columns)
-        copy = pltpu.make_async_copy(
-            source.at[:, pl.ds(start, half_columns)], columns_buf, columns_sem
-        )
-        copy.start()
-        copy.wait()
+        source = (normed_one_ref, normed_two_ref)[which]
+        return pltpu.make_async_copy(
+            source.at[:, pl.ds(start, half_columns)], columns_buf.at[which], columns_sem.at[which]
+        )
 
     def mix_piece(owner, half):
-        load(normed_one_ref, owner, half)
+        load(0, owner, half).wait()
         return jnp.stack(
             [
                 lax.dot_general(
-                    columns_buf[...],
+                    columns_buf[0],
                     stacked_ref[part],
                     CROSSED,
                     preferred_element_type=jnp.float32,
@@ -978,22 +1131,49 @@
         )
 
     def up_piece(owner, half):
-        load(normed_two_ref, owner, half)
+        load(1, owner, half).wait()
         return lax.dot_general(
-            columns_buf[...], hidden_ref[...], CROSSED, preferred_element_type=jnp.float32
-        )
-
+            columns_buf[1], hidden_ref[...], CROSSED, preferred_element_type=jnp.float32
+        )
+
+    out_units = out_grad_ref.shape[0] // 2
+    out_columns = out_grad_ref.shape[1] // 4
+
+    def out_piece(owner, half):
+        units = pl.ds(pl.multiple_of(half * out_units, out_units), out_units)
+        columns = pl.ds(pl.multiple_of(owner * out_columns, 128), out_columns)
+        return out_grad_ref[units, columns]
+
+    out = SquareScatter(place, out_piece, out_owned_ref, scatter[26:28], scatter[28:30])
     mix = SquareScatter(place, mix_piece, mix_grad_ref, scatter[8:10], scatter[10:12])
     up = SquareScatter(place, up_piece, up_grad_ref, scatter[12:14], scatter[14:16])
 
+    load(1, place.across, 0).start()
+    load(0, place.across, 0).start()
+
+    def stage(kind):
+        def one(way, carry):
+            for which, matrix in ((1, up), (0, mix)):
+                matrix.one(kind, way)
+                owner, half = matrix.following(kind, way)
+                more = (way == 0) | (kind < 3)
+                pl.when(more)(lambda: load(which, owner, half).start())
+            out.one(kind, way)
+            return carry
+
+        lax.fori_loop(0, 2, one, 0)
+
+    for copy in fetched[2:]:
+        copy.wait()
+
     def step(index, carry):
+        pl.when(index == 3)(lambda: stage(3))
         sums.step(index)
-        for kind in range(4):
+        for kind in range(3):
 
             @pl.when(index == kind)
             def _():
-                up.stage(kind)
-                mix.stage(kind)
+                stage(kind)
                 if kind == 1:
                     early.middle()
                 if kind == 2:
@@ -1005,29 +1185,34 @@
     total = scatter[0]
     late_out_ref[...] = jnp.zeros_like(late_out_ref)
 
+    def columns(span):
+        one_grad = total[span, :]
+        _, hat, _ = layer_norm_parts(rows_ref[span, :].astype(jnp.float32), gain_ref[...], 0.0)
+        late_out_ref[0:1, :] += jnp.sum(one_grad * hat, axis=0, keepdims=True)
+        late_out_ref[1:2, :] += jnp.sum(one_grad, axis=0, keepdims=True)
+
     def back(span):
         rows = rows_ref[span, :].astype(jnp.float32)
-        one_grad = total[span, :]
         _, hat, inverse = layer_norm_parts(rows, gain_ref[...], 0.0)
         grad_ref[span, :] = resid_grad_ref[span, :] + layer_norm_back(
-            one_grad, hat, inverse, gain_ref[...]
-        )
-        late_out_ref[0:1, :] += jnp.sum(one_grad * hat, axis=0, keepdims=True)
-        late_out_ref[1:2, :] += jnp.sum(one_grad, axis=0, keepdims=True)
-
-    by_rows(count, 64, back)
+            total[span, :], hat, inverse, gain_ref[...]
+        )
+
+    by_rows(count, 64, columns)
     late.begin()
-    early.end()
     up.end()
     late.middle()
+    by_rows(count, 64, back)
+    late.late()
+    early.end()
     mix.end()
-    late.late()
+    out.end()
     sums.finish()
     late.end()
 
 
 def input_back_call(
-    stacked, mix_whole, rows, resid_grad, gain, early, hidden, normed_one, normed_two, chips
+    stacked, mix_whole, rows, resid_grad, gain, early, hidden, out_grad, normed_one, normed_two, chips
 ):
     count, width = rows.shape
     total, units = hidden.shape
@@ -1043,24 +1228,33 @@
             jax.ShapeDtypeStruct(early.shape, jnp.float32),
             jax.ShapeDtypeStruct((2, 3, half, local), jnp.float32),
             jax.ShapeDtypeStruct((2, half, units), jnp.float32),
+            jax.ShapeDtypeStruct((2, local // 2, width // 4), jnp.float32),
         ),
-        in_specs=[vmem] * 7 + [hbm] * 2,
-        out_specs=(vmem,) * 5,
+        in_specs=[hbm] * 4 + [vmem] * 2 + [hbm] * 4,
+        out_specs=(vmem,) * 6,
         scratch_shapes=[
-            pltpu.VMEM((total, half), jnp.bfloat16),
-            pltpu.SemaphoreType.DMA,
+            pltpu.VMEM(stacked.shape, jnp.bfloat16),
+            pltpu.VMEM(mix_whole.shape, jnp.bfloat16),
+            pltpu.VMEM(rows.shape, jnp.bfloat16),
+            pltpu.VMEM(resid_grad.shape, jnp.float32),
+            pltpu.VMEM(hidden.shape, jnp.bfloat16),
+            pltpu.VMEM(out_grad.shape, jnp.float32),
+            pltpu.SemaphoreType.DMA((6,)),
+            pltpu.VMEM((2, total, half), jnp.bfloat16),
+            pltpu.SemaphoreType.DMA((2,)),
         ]
         + scatter_scratch(chips, count, width)
         + square_scratch((3, half, local))
         + square_scratch((half, units))
         + small_scratch(chips, early.shape[0], width)
-        + small_scratch(chips, 2, width),
+        + small_scratch(chips, 2, width)
+        + square_scratch((local // 2, width // 4)),
         compiler_params=pltpu.CompilerParams(
             collective_id=2, has_side_effects=True, vmem_limit_bytes=VMEM_LIMIT
         ),
         cost_estimate=pl.CostEstimate(flops=10**11, bytes_accessed=0, transcendentals=0),
         name="input_back",
-    )(stacked, mix_whole, rows, resid_grad, gain, early, hidden, normed_one, normed_two)
+    )(stacked, mix_whole, rows, resid_grad, gain, early, hidden, out_grad, normed_one, normed_two)
 
 
 GELU_SLOPE = 0.7978845608028654
@@ -1082,19 +1276,27 @@
     parts,
     normed_ref,
     branch_ref,
-    up_ref,
-    down_ref,
+    up_hbm,
+    down_hbm,
     bias_ref,
-    resid_ref,
-    own_branch_ref,
+    resid_hbm,
+    own_branch_hbm,
     gain_ref,
     normed_whole,
-    active_ref,
-    hidden_ref,
+    active_hbm,
+    hidden_hbm,
     grad_ref,
     grad_low_ref,
     sums_ref,
     bias_grad_ref,
+    up_ref,
+    down_ref,
+    resid_ref,
+    own_branch_ref,
+    active_ref,
+    hidden_ref,
+    fetch_sem,
+    emit_sem,
     blocks,
     branch_buf,
     work,
@@ -1116,6 +1318,15 @@
     rows = count // parts
     pair = 2 * rows
     last = chips - 1
+    fetched = fetch(
+        [
+            (up_hbm, up_ref),
+            (down_hbm, down_ref),
+            (resid_hbm, resid_ref),
+            (own_branch_hbm, own_branch_ref),
+        ],
+        fetch_sem,
+    )
     place.greet(False)
 
     def fill(part, carry):
@@ -1151,31 +1362,42 @@
             place.side,
         )
 
-    def line_copy(way, chip, part):
+    chunk = normed_ref.shape[1] // 4
+
+    def line_copy(way, chip, part, tile):
         piece = chip * parts + part
         next_chip = place.chip + 1 - 2 * way
         slot = jnp.where((way == 1) & (chip == next_chip), chips * parts + part, piece)
+        span = slice(tile * chunk, (tile + 1) * chunk)
         return remote(
-            line_in.at[piece],
-            line_in.at[slot],
-            out_send.at[piece],
-            out_recv.at[slot],
+            line_in.at[piece, :, span],
+            line_in.at[slot, :, span],
+            out_send.at[piece, tile],
+            out_recv.at[slot, tile],
             (place.up, place.down)[way],
         )
 
-    def line_landed(way, chip, part):
+    def line_landed(way, chip, part, tile):
         piece = chip * parts + part
         slot = jnp.where((way == 1) & (chip == place.chip), chips * parts + part, piece)
+        span = slice(tile * chunk, (tile + 1) * chunk)
         remote(
-            line_in.at[slot],
-            line_in.at[slot],
-            out_send.at[piece],
-            out_recv.at[slot],
+            line_in.at[slot, :, span],
+            line_in.at[slot, :, span],
+            out_send.at[piece, tile],
+            out_recv.at[slot, tile],
             (place.up, place.down)[way],
         ).wait_recv()
         return slot
 
-    width = 256
+    def emit(piece):
+        span = piece_span(piece)
+        return [
+            pltpu.make_async_copy(active_ref.at[span], active_hbm.at[span], emit_sem.at[piece, 0]),
+            pltpu.make_async_copy(hidden_ref.at[span], hidden_hbm.at[span], emit_sem.at[piece, 1]),
+        ]
+
+    width = 512
     tiles = up_ref.shape[2] // width
 
     def compute(chip, part):
@@ -1223,23 +1445,29 @@
         side_out[piece] = work[1 - place.core].astype(jnp.bfloat16)
         side_copy(piece).start()
         hold[piece] = work[place.core]
+        for copy in emit(piece):
+            copy.start()
 
     def pass_on(way, chip, part):
         piece = chip * parts + part
         side_copy(piece).wait_recv()
-        total = hold[piece] + side_in[piece].astype(jnp.float32)
         behind = (place.has_down, place.has_up)[way]
-
-        @pl.when(behind)
-        def _():
-            slot = line_landed(way, chip, part)
-            line_in[piece] = (total + line_in[slot].astype(jnp.float32)).astype(jnp.bfloat16)
-
-        @pl.when(jnp.logical_not(behind))
-        def _():
-            line_in[piece] = total.astype(jnp.bfloat16)
-
-        line_copy(way, chip, part).start()
+        for tile in range(4):
+            span = slice(tile * chunk, (tile + 1) * chunk)
+            total = hold[piece, :, span] + side_in[piece, :, span].astype(jnp.float32)
+
+            @pl.when(behind)
+            def _():
+                slot = line_landed(way, chip, part, tile)
+                line_in[piece, :, span] = (
+                    total + line_in[slot, :, span].astype(jnp.float32)
+                ).astype(jnp.bfloat16)
+
+            @pl.when(jnp.logical_not(behind))
+            def _():
+                line_in[piece, :, span] = total.astype(jnp.bfloat16)
+
+            line_copy(way, chip, part, tile).start()
 
     def turn(index, carry):
         distance = index // parts
@@ -1276,23 +1504,37 @@
 
         return carry
 
+    fetched[0].wait()
+    fetched[1].wait()
     lax.fori_loop(0, parts * chips + last, turn, 0)
     sums_ref[...] = jnp.zeros_like(sums_ref)
+    fetched[2].wait()
+    fetched[3].wait()
 
     def own_part(part, carry):
         piece = place.chip * parts + part
         side_copy(piece).wait_recv()
         hold[piece] += side_in[piece].astype(jnp.float32)
 
+        for tile in range(4):
+
+            @pl.when(place.has_down)
+            def _():
+                line_landed(0, place.chip, part, tile)
+
+            @pl.when(place.has_up)
+            def _():
+                line_landed(1, place.chip, part, tile)
+
+        pieces_end = chips * parts
+
         @pl.when(place.has_down)
         def _():
-            slot = line_landed(0, place.chip, part)
-            hold[piece] += line_in[slot].astype(jnp.float32)
+            hold[piece] += line_in[piece].astype(jnp.float32)
 
         @pl.when(place.has_up)
         def _():
-            slot = line_landed(1, place.chip, part)
-            hold[piece] += line_in[slot].astype(jnp.float32)
+            hold[piece] += line_in[pieces_end + part].astype(jnp.float32)
 
         tile = 64
 
@@ -1321,9 +1563,12 @@
         side_copy(piece).wait_send()
         keep(piece, 0).wait()
         keep(piece, 1).wait()
-        pl.when(piece // parts != place.chip)(
-            lambda: line_copy(0, piece // parts, piece % parts).wait_send()
-        )
+        for copy in emit(piece):
+            copy.wait()
+        for tile in range(4):
+            pl.when(piece // parts != place.chip)(
+                lambda: line_copy(0, piece // parts, piece % parts, tile).wait_send()
+            )
         return carry
 
     lax.fori_loop(0, chips * parts, drain, 0)
@@ -1351,9 +1596,17 @@
             jax.ShapeDtypeStruct((3, width), jnp.float32),
             jax.ShapeDtypeStruct((1, units), jnp.float32),
         ),
-        in_specs=[vmem, hbm] + [vmem] * 6,
-        out_specs=(hbm,) + (vmem,) * 6,
+        in_specs=[vmem, hbm, hbm, hbm, vmem, hbm, hbm, vmem],
+        out_specs=(hbm,) * 3 + (vmem,) * 4,
         scratch_shapes=[
+            pltpu.VMEM(up_whole.shape, low),
+            pltpu.VMEM(down_whole.shape, low),
+            pltpu.VMEM(resid.shape, jnp.float32),
+            pltpu.VMEM(own_branch.shape, low),
+            pltpu.VMEM((total, units), low),
+            pltpu.VMEM((total, units), low),
+            dma((4,)),
+            dma((pieces, 2)),
             pltpu.VMEM((2 * pieces, rows, width), low),
             pltpu.VMEM((1, 2 * rows, width), low),
             pltpu.VMEM((2, rows, width), jnp.float32),
@@ -1367,8 +1620,8 @@
             dma((1,)),
             dma((pieces,)),
             dma((pieces,)),
-            dma((pieces,)),
-            dma((pieces + parts,)),
+            dma((pieces, 4)),
+            dma((pieces + parts, 4)),
         ],
         compiler_params=pltpu.CompilerParams(
             collective_id=3, has_side_effects=True, vmem_limit_bytes=VMEM_LIMIT
@@ -1382,36 +1635,58 @@
     chips,
     parts,
     branch_ref,
+    active_hbm,
+    down_hbm,
+    attended_hbm,
+    out_hbm,
+    shift_ref,
+    bounds_ref,
+    mixed_hbm,
+    aux_hbm,
+    resid_ref,
+    cotangent_ref,
+    stacked_ref,
+    bias_sum_ref,
+    down_grad_ref,
+    out_grad_ref,
+    output_ref,
+    blocks,
     active_ref,
     down_ref,
     attended_ref,
     out_ref,
-    resid_ref,
-    shift_ref,
-    live_ref,
-    cotangent_ref,
-    attended_grad_ref,
-    down_grad_ref,
-    out_owned_ref,
-    output_ref,
-    blocks,
-    out_grad_ref,
+    mixed_ref,
+    aux_ref,
+    fetch_sem,
+    seg_row_ref,
+    block_buf,
     columns_buf,
+    probs_ref,
+    flow_ref,
+    key_sum,
+    value_sum,
     line_send,
     line_recv,
     columns_sem,
+    block_sem,
     *scatter,
 ):
     place = Place(chips)
     count = branch_ref.shape[0]
     rows = count // parts
+    fetched = fetch(
+        [
+            (active_hbm, active_ref),
+            (down_hbm, down_ref),
+            (attended_hbm, attended_ref),
+            (out_hbm, out_ref),
+            (mixed_hbm, mixed_ref),
+            (aux_hbm, aux_ref),
+        ],
+        fetch_sem,
+    )
     place.greet(True)
-
-    def copy_in(span):
-        blocks[place.me, span, :] = branch_ref[span, :]
-
-    by_rows(count, 64, copy_in)
-    line = LineGather(place, blocks, line_send, line_recv)
+    line = LineGather(place, blocks, line_send, line_recv, 1, branch_ref)
     line.begin()
 
     def term(block, tile):
@@ -1424,52 +1699,99 @@
             jnp.concatenate(taken, axis=0), down_ref[tile], preferred_element_type=jnp.float32
         )
 
+    fetched[0].wait()
+    fetched[1].wait()
     sums = LineScatter(place, term, 4, scatter[:4], scatter[4:8])
     sums.begin()
+    seg_row_ref[...] = alive(seg_row_ref.shape, 1, 0, bounds_ref)
     out_grad_ref[...] = jnp.zeros_like(out_grad_ref)
+    key_sum[...] = jnp.zeros_like(key_sum)
+    value_sum[...] = jnp.zeros_like(value_sum)
+    bias_sum_ref[...] = jnp.zeros_like(bias_sum_ref)
     down_units = down_ref.shape[1] // 2
     down_columns = down_ref.shape[2]
 
-    def down_piece(owner, half):
-        load = pltpu.make_async_copy(
+    def load_columns(owner):
+        return pltpu.make_async_copy(
             cotangent_ref.at[:, pl.ds(pl.multiple_of(owner * down_columns, 128), down_columns)],
             columns_buf,
             columns_sem,
         )
-        load.start()
-        load.wait()
+
+    load_columns(place.across).start()
+
+    def down_piece(owner, half):
         units = pl.ds(pl.multiple_of(half * down_units, down_units), down_units)
         return lax.dot_general(
             active_ref[:, units], columns_buf[...], CROSSED, preferred_element_type=jnp.float32
         )
 
     down = SquareScatter(place, down_piece, down_grad_ref, scatter[8:10], scatter[10:12])
-    out_units = out_ref.shape[1] // 2
-
-    def out_piece(owner, half):
-        units = pl.ds(pl.multiple_of(half * out_units, out_units), out_units)
-        columns = pl.ds(pl.multiple_of(owner * down_columns, 128), down_columns)
-        return out_grad_ref[units, columns]
-
-    out = SquareScatter(place, out_piece, out_owned_ref, scatter[12:14], scatter[14:16])
+    def down_stage(kind):
+        def one(way, carry):
+            fresh = (way == 0) if kind in (0, 3) else ((way >= 0) if kind == 1 else (way == 1))
+            pl.when(fresh)(lambda: load_columns(place.dp).wait())
+            down.one(kind, way)
+            owner, _ = down.following(kind, way)
+            more = (way == 1) if kind == 0 else ((way == 0) if kind == 1 else (way >= 0))
+            if kind < 3:
+                pl.when(more)(lambda: load_columns(owner).start())
+            return carry
+
+        lax.fori_loop(0, 2, one, 0)
+
+    def load_part(source, owner):
+        columns = out_ref.shape[2]
+        span = slice(owner * columns, (owner + 1) * columns)
+        return pltpu.make_async_copy(source.at[:, span], block_buf.at[:, span], block_sem.at[owner])
+
+    def load_block(block):
+        mine = block == place.me
+
+        @pl.when(mine)
+        def _():
+            for owner in range(4):
+                load_part(branch_ref, owner).start()
+
+        @pl.when(jnp.logical_not(mine))
+        def _():
+            for owner in range(4):
+                load_part(blocks.at[block], owner).start()
 
     def take(block):
         span = pl.ds(pl.multiple_of(block * count, count), count)
         columns = out_ref.shape[2]
+        load_block(block)
         result = None
         for owner in range(4):
-            here = blocks[block, :, owner * columns : (owner + 1) * columns]
+            load_part(branch_ref, owner).wait()
+            here = block_buf[:, owner * columns : (owner + 1) * columns]
             product = lax.dot_general(
                 here, out_ref[owner], TURNED, preferred_element_type=jnp.float32
             )
             result = product if result is None else result + product
             out_grad_ref[:, owner * columns : (owner + 1) * columns] += lax.dot_general(
-                attended_ref[span, :],
-                here,
-                (((0,), (0,)), ((), ())),
-                preferred_element_type=jnp.float32,
+                attended_ref[span, :], here, CROSSED, preferred_element_type=jnp.float32
             )
-        attended_grad_ref[span, :] = result.astype(jnp.bfloat16)
+        grad = result.astype(jnp.bfloat16)
+        for head in range(mixed_ref.shape[2] // HEAD_DIM):
+            attend_back_rows(
+                head,
+                block,
+                grad[:, head * HEAD_DIM : (head + 1) * HEAD_DIM],
+                mixed_ref,
+                aux_ref,
+                seg_row_ref,
+                stacked_ref,
+                probs_ref,
+                flow_ref,
+                key_sum,
+                value_sum,
+                bias_sum_ref,
+            )
+
+    for copy in fetched[2:]:
+        copy.wait()
 
     def step(index, carry):
         def one(side, inner):
@@ -1484,32 +1806,46 @@
             return inner
 
         lax.fori_loop(0, 4, one, 0)
+        for kind in range(4):
+            pl.when(index == kind)(lambda: down_stage(kind))
+        pl.when(index < chips - 1)(lambda: line.step(index + 1))
         sums.step(index)
-        pl.when(index < chips - 1)(lambda: line.step(index + 1))
-        for kind in range(4):
-            pl.when(index == kind)(lambda: down.stage(kind))
         return carry
 
     lax.fori_loop(0, chips, step, 0)
-    out.stage(0)
-    out.stage(1)
+    resid = pltpu.make_async_copy(resid_ref, probs_ref, columns_sem)
+    resid.start()
+    stacked_ref[1] = (key_sum[...] * HEAD_DIM ** (-0.5)).astype(jnp.bfloat16)
+    value_grad = value_sum[...].astype(jnp.bfloat16)
+    stacked_ref[2] = value_grad
+    bias_sum_ref[1:2, :] = jnp.sum(value_grad.astype(jnp.float32), axis=0, keepdims=True)
+    down.end()
     total = scatter[0]
+    resid.wait()
 
     def emit(span):
-        result = resid_ref[span, :] + total[span, :] + shift_ref[...]
-        output_ref[span, :] = jnp.where(live_ref[span, :] > 0, result, 0.0).astype(jnp.bfloat16)
+        result = probs_ref[span, :] + total[span, :] + shift_ref[...]
+        live = alive((64, 1), 0, place.me * count + span.start, bounds_ref)
+        output_ref[span, :] = jnp.where(live > 0, result, 0.0).astype(jnp.bfloat16)
 
     by_rows(count, 64, emit)
-    down.end()
-    out.stage(2)
-    out.stage(3)
     sums.finish()
     line.finish()
-    out.end()
 
 
 def branch_back_call(
-    branch, active, down_whole, attended, out_whole, resid, shift, live, cotangent, chips
+    branch,
+    active,
+    down_whole,
+    attended,
+    out_whole,
+    shift,
+    bounds,
+    mixed,
+    aux,
+    resid,
+    cotangent,
+    chips,
 ):
     count, width = branch.shape
     total, local = attended.shape
@@ -1521,30 +1857,55 @@
     return pl.pallas_call(
         functools.partial(branch_back_kernel, chips, 2),
         out_shape=(
-            jax.ShapeDtypeStruct((total, local), low),
+            jax.ShapeDtypeStruct((3, total, local), low),
+            jax.ShapeDtypeStruct((2, local), jnp.float32),
             jax.ShapeDtypeStruct((2, units // 2, columns), jnp.float32),
-            jax.ShapeDtypeStruct((2, local // 2, columns), jnp.float32),
+            jax.ShapeDtypeStruct((local, width), jnp.float32),
             jax.ShapeDtypeStruct((count, width), low),
+            jax.ShapeDtypeStruct((2 * chips, count, width), low),
         ),
-        in_specs=[vmem] * 8 + [hbm],
-        out_specs=(vmem,) * 4,
+        in_specs=[hbm] * 5 + [vmem, pl.BlockSpec(memory_space=pltpu.SMEM)] + [hbm] * 4,
+        out_specs=(vmem,) * 5 + (hbm,),
         scratch_shapes=[
-            pltpu.VMEM((2 * chips, count, width), low),
-            pltpu.VMEM((local, width), jnp.float32),
+            pltpu.VMEM(active.shape, low),
+            pltpu.VMEM(down_whole.shape, low),
+            pltpu.VMEM(attended.shape, low),
+            pltpu.VMEM(out_whole.shape, low),
+            pltpu.VMEM(mixed.shape, low),
+            pltpu.VMEM(aux.shape, jnp.float32),
+            dma((6,)),
+            pltpu.VMEM((1, total), jnp.float32),
+            pltpu.VMEM((count, width), low),
             pltpu.VMEM((total, columns), low),
+            pltpu.VMEM((ATTEND_ROWS, total), jnp.float32),
+            pltpu.VMEM((ATTEND_ROWS, total), jnp.float32),
+            pltpu.VMEM((total, local), jnp.float32),
+            pltpu.VMEM((total, local), jnp.float32),
             dma((3, chips)),
             dma((2 * chips,)),
             dma,
+            dma((4,)),
         ]
         + scatter_scratch(chips, count, width)
-        + square_scratch((units // 2, columns))
-        + square_scratch((local // 2, columns)),
+        + square_scratch((units // 2, columns)),
         compiler_params=pltpu.CompilerParams(
             collective_id=4, has_side_effects=True, vmem_limit_bytes=VMEM_LIMIT
         ),
         cost_estimate=pl.CostEstimate(flops=10**11, bytes_accessed=0, transcendentals=0),
         name="branch_back",
-    )(branch, active, down_whole, attended, out_whole, resid, shift, live, cotangent)
+    )(
+        branch,
+        active,
+        down_whole,
+        attended,
+        out_whole,
+        shift,
+        bounds,
+        mixed,
+        aux,
+        resid,
+        cotangent,
+    )
 
 
 ATTEND_ROWS = 256
@@ -1557,202 +1918,115 @@
     causal = keys - rows <= row_block * ATTEND_ROWS - key_block * ATTEND_KEYS
     row_span = pl.ds(pl.multiple_of(row_block * ATTEND_ROWS, ATTEND_ROWS), ATTEND_ROWS)
     key_span = pl.ds(pl.multiple_of(key_block * ATTEND_KEYS, ATTEND_KEYS), ATTEND_KEYS)
-    return causal & (seg_col_ref[row_span, :] == seg_row_ref[:, key_span])
-
-
-def attention_kernel(mixed_ref, seg_col_ref, seg_row_ref, attended_ref, lse_ref, score_ref):
-    length = mixed_ref.shape[1]
-    heads = mixed_ref.shape[2] // HEAD_DIM
-    row_blocks = length // ATTEND_ROWS
+    return causal & (seg_col_ref[row_span, 0:1] == seg_row_ref[:, key_span])
+
+
+def attend_rows(head, row_block, mixed_ref, seg_col_ref, seg_row_ref, attended_ref, lse_ref, score_ref):
     scale = HEAD_DIM ** (-0.5)
-
-    def one(index, carry):
-        head = index // row_blocks
-        row_block = index % row_blocks
-        lanes = pl.ds(pl.multiple_of(head * HEAD_DIM, HEAD_DIM), HEAD_DIM)
-        row_span = pl.ds(pl.multiple_of(row_block * ATTEND_ROWS, ATTEND_ROWS), ATTEND_ROWS)
-        count = (row_block * ATTEND_ROWS) // ATTEND_KEYS + 1
-        query = mixed_ref[0, row_span, lanes]
-
-        def score(key_block, peak):
-            key_span = pl.ds(pl.multiple_of(key_block * ATTEND_KEYS, ATTEND_KEYS), ATTEND_KEYS)
-            scores = lax.dot_general(
-                query, mixed_ref[1, key_span, lanes], TURNED, preferred_element_type=jnp.float32
-            )
-            mask = tile_mask(row_block, key_block, seg_col_ref, seg_row_ref)
-            scores = jnp.where(mask, scores * scale, MASK_FILL)
-            score_ref[:, key_span] = scores
-            for part in range(ATTEND_KEYS // 128):
-                peak = jnp.maximum(peak, scores[:, part * 128 : (part + 1) * 128])
-            return peak
-
-        peak = lax.fori_loop(
-            0, count, score, jnp.full((ATTEND_ROWS, 128), MASK_FILL, jnp.float32)
-        )
-        peak = jnp.max(peak, axis=1, keepdims=True)
-
-        def weigh(key_block, mass):
-            key_span = pl.ds(pl.multiple_of(key_block * ATTEND_KEYS, ATTEND_KEYS), ATTEND_KEYS)
-            weights = jnp.exp(score_ref[:, key_span] - peak)
-            score_ref[:, key_span] = weights
-            for part in range(ATTEND_KEYS // 128):
-                mass = mass + weights[:, part * 128 : (part + 1) * 128]
-            return mass
-
-        mass = lax.fori_loop(0, count, weigh, jnp.zeros((ATTEND_ROWS, 128), jnp.float32))
-        mass = jnp.sum(mass, axis=1, keepdims=True)
-        inverse = 1.0 / mass
-        lse_ref[head, row_span, :] = peak + jnp.log(mass)
-
-        def gather(key_block, total):
-            key_span = pl.ds(pl.multiple_of(key_block * ATTEND_KEYS, ATTEND_KEYS), ATTEND_KEYS)
-            probs = (score_ref[:, key_span] * inverse).astype(jnp.bfloat16)
-            return total + jnp.dot(
-                probs, mixed_ref[2, key_span, lanes], preferred_element_type=jnp.float32
-            )
-
-        total = lax.fori_loop(
-            0, count, gather, jnp.zeros((ATTEND_ROWS, HEAD_DIM), jnp.float32)
-        )
-        attended_ref[row_span, lanes] = total.astype(jnp.bfloat16)
-        return carry
-
-    lax.fori_loop(0, heads * row_blocks, one, 0)
-
-
-def attention_call(mixed, seg_col, seg_row):
-    _, length, width = mixed.shape
-    heads = width // HEAD_DIM
-    vmem = pl.BlockSpec(memory_space=pltpu.VMEM)
-    return pl.pallas_call(
-        attention_kernel,
-        out_shape=(
-            jax.ShapeDtypeStruct((length, width), jnp.bfloat16),
-            jax.ShapeDtypeStruct((heads, length, 1), jnp.float32),
-        ),
-        in_specs=[vmem] * 3,
-        out_specs=(vmem,) * 2,
-        scratch_shapes=[pltpu.VMEM((ATTEND_ROWS, length), jnp.float32)],
-        compiler_params=pltpu.CompilerParams(vmem_limit_bytes=VMEM_LIMIT),
-        cost_estimate=pl.CostEstimate(flops=10**10, bytes_accessed=0, transcendentals=0),
-        name="attention",
-    )(mixed, seg_col, seg_row)
-
-
-def attention_back_kernel(
+    lanes = slice(head * HEAD_DIM, (head + 1) * HEAD_DIM)
+    row_span = pl.ds(pl.multiple_of(row_block * ATTEND_ROWS, ATTEND_ROWS), ATTEND_ROWS)
+    count = (row_block * ATTEND_ROWS) // ATTEND_KEYS + 1
+    query = mixed_ref[0, row_span, lanes]
+
+    def score(key_block, peak):
+        key_span = pl.ds(pl.multiple_of(key_block * ATTEND_KEYS, ATTEND_KEYS), ATTEND_KEYS)
+        scores = lax.dot_general(
+            query, mixed_ref[1, key_span, lanes], TURNED, preferred_element_type=jnp.float32
+        )
+        mask = tile_mask(row_block, key_block, seg_col_ref, seg_row_ref)
+        scores = jnp.where(mask, scores * scale, MASK_FILL)
+        score_ref[:, key_span] = scores
+        for part in range(ATTEND_KEYS // 128):
+            peak = jnp.maximum(peak, scores[:, part * 128 : (part + 1) * 128])
+        return peak
+
+    peak = lax.fori_loop(0, count, score, jnp.full((ATTEND_ROWS, 128), MASK_FILL, jnp.float32))
+    peak = jnp.max(peak, axis=1, keepdims=True)
+
+    def weigh(key_block, mass):
+        key_span = pl.ds(pl.multiple_of(key_block * ATTEND_KEYS, ATTEND_KEYS), ATTEND_KEYS)
+        weights = jnp.exp(score_ref[:, key_span] - peak)
+        score_ref[:, key_span] = weights
+        for part in range(ATTEND_KEYS // 128):
+            mass = mass + weights[:, part * 128 : (part + 1) * 128]
+        return mass
+
+    mass = lax.fori_loop(0, count, weigh, jnp.zeros((ATTEND_ROWS, 128), jnp.float32))
+    mass = jnp.sum(mass, axis=1, keepdims=True)
+    inverse = 1.0 / mass
+    lse_ref[row_span, head + 1 : head + 2] = peak + jnp.log(mass)
+    if head == 0:
+        lse_ref[row_span, 0:1] = seg_col_ref[row_span, :]
+
+    def gather(key_block, total):
+        key_span = pl.ds(pl.multiple_of(key_block * ATTEND_KEYS, ATTEND_KEYS), ATTEND_KEYS)
+        probs = (score_ref[:, key_span] * inverse).astype(jnp.bfloat16)
+        return total + jnp.dot(
+            probs, mixed_ref[2, key_span, lanes], preferred_element_type=jnp.float32
+        )
+
+    total = lax.fori_loop(0, count, gather, jnp.zeros((ATTEND_ROWS, HEAD_DIM), jnp.float32))
+    attended_ref[row_span, lanes] = total.astype(jnp.bfloat16)
+
+
+def attend_back_rows(
+    head,
+    row_block,
+    grad,
     mixed_ref,
-    seg_col_ref,
+    aux_ref,
     seg_row_ref,
-    lse_ref,
-    grad_ref,
     stacked_ref,
-    bias_grad_ref,
     probs_ref,
     flow_ref,
     key_sum,
     value_sum,
+    bias_sum,
 ):
-    length = mixed_ref.shape[1]
-    heads = mixed_ref.shape[2] // HEAD_DIM
-    row_blocks = length // ATTEND_ROWS
     scale = HEAD_DIM ** (-0.5)
-
-    def one_head(head, carry):
-        lanes = pl.ds(pl.multiple_of(head * HEAD_DIM, HEAD_DIM), HEAD_DIM)
-        key_sum[...] = jnp.zeros_like(key_sum)
-        value_sum[...] = jnp.zeros_like(value_sum)
-
-        def one(row_block, bias_sum):
-            row_span = pl.ds(pl.multiple_of(row_block * ATTEND_ROWS, ATTEND_ROWS), ATTEND_ROWS)
-            count = (row_block * ATTEND_ROWS) // ATTEND_KEYS + 1
-            query = mixed_ref[0, row_span, lanes]
-            grad = grad_ref[row_span, lanes]
-            lse = lse_ref[head, row_span, :]
-
-            def first(key_block, delta):
-                key_span = pl.ds(pl.multiple_of(key_block * ATTEND_KEYS, ATTEND_KEYS), ATTEND_KEYS)
-                scores = lax.dot_general(
-                    query,
-                    mixed_ref[1, key_span, lanes],
-                    TURNED,
-                    preferred_element_type=jnp.float32,
-                )
-                flow = lax.dot_general(
-                    grad,
-                    mixed_ref[2, key_span, lanes],
-                    TURNED,
-                    preferred_element_type=jnp.float32,
-                )
-                mask = tile_mask(row_block, key_block, seg_col_ref, seg_row_ref)
-                probs = jnp.exp(jnp.where(mask, scores * scale, MASK_FILL) - lse)
-                probs_ref[:, key_span] = probs
-                flow_ref[:, key_span] = flow
-                product = probs * flow
-                for part in range(ATTEND_KEYS // 128):
-                    delta = delta + product[:, part * 128 : (part + 1) * 128]
-                value_sum[key_span, :] += lax.dot_general(
-                    probs.astype(jnp.bfloat16), grad, CROSSED, preferred_element_type=jnp.float32
-                )
-                return delta
-
-            delta = lax.fori_loop(
-                0, count, first, jnp.zeros((ATTEND_ROWS, 128), jnp.float32)
-            )
-            delta = jnp.sum(delta, axis=1, keepdims=True)
-
-            def second(key_block, total):
-                key_span = pl.ds(pl.multiple_of(key_block * ATTEND_KEYS, ATTEND_KEYS), ATTEND_KEYS)
-                low = (probs_ref[:, key_span] * (flow_ref[:, key_span] - delta)).astype(
-                    jnp.bfloat16
-                )
-                key_sum[key_span, :] += lax.dot_general(
-                    low, query, CROSSED, preferred_element_type=jnp.float32
-                )
-                return total + jnp.dot(
-                    low, mixed_ref[1, key_span, lanes], preferred_element_type=jnp.float32
-                )
-
-            total = lax.fori_loop(
-                0, count, second, jnp.zeros((ATTEND_ROWS, HEAD_DIM), jnp.float32)
-            )
-            query_grad = (total * scale).astype(jnp.bfloat16)
-            stacked_ref[0, row_span, lanes] = query_grad
-            return bias_sum + jnp.sum(query_grad.astype(jnp.float32), axis=0, keepdims=True)
-
-        bias_sum = lax.fori_loop(0, row_blocks, one, jnp.zeros((1, HEAD_DIM), jnp.float32))
-        bias_grad_ref[0:1, lanes] = bias_sum
-        stacked_ref[1, :, lanes] = (key_sum[...] * scale).astype(jnp.bfloat16)
-        value_grad = value_sum[...].astype(jnp.bfloat16)
-        stacked_ref[2, :, lanes] = value_grad
-        bias_grad_ref[1:2, lanes] = jnp.sum(
-            value_grad.astype(jnp.float32), axis=0, keepdims=True
-        )
-        return carry
-
-    lax.fori_loop(0, heads, one_head, 0)
-
-
-def attention_back_call(mixed, seg_col, seg_row, lse, grad):
-    _, length, width = mixed.shape
-    vmem = pl.BlockSpec(memory_space=pltpu.VMEM)
-    return pl.pallas_call(
-        attention_back_kernel,
-        out_shape=(
-            jax.ShapeDtypeStruct((3, length, width), jnp.bfloat16),
-            jax.ShapeDtypeStruct((2, width), jnp.float32),
-        ),
-        in_specs=[vmem] * 5,
-        out_specs=(vmem,) * 2,
-        scratch_shapes=[
-            pltpu.VMEM((ATTEND_ROWS, length), jnp.float32),
-            pltpu.VMEM((ATTEND_ROWS, length), jnp.float32),
-            pltpu.VMEM((length, HEAD_DIM), jnp.float32),
-            pltpu.VMEM((length, HEAD_DIM), jnp.float32),
-        ],
-        compiler_params=pltpu.CompilerParams(vmem_limit_bytes=VMEM_LIMIT),
-        cost_estimate=pl.CostEstimate(flops=3 * 10**10, bytes_accessed=0, transcendentals=0),
-        name="attention_back",
-    )(mixed, seg_col, seg_row, lse, grad)
+    lanes = slice(head * HEAD_DIM, (head + 1) * HEAD_DIM)
+    row_span = pl.ds(pl.multiple_of(row_block * ATTEND_ROWS, ATTEND_ROWS), ATTEND_ROWS)
+    count = (row_block * ATTEND_ROWS) // ATTEND_KEYS + 1
+    query = mixed_ref[0, row_span, lanes]
+    lse = aux_ref[row_span, head + 1 : head + 2]
+
+    def first(key_block, delta):
+        key_span = pl.ds(pl.multiple_of(key_block * ATTEND_KEYS, ATTEND_KEYS), ATTEND_KEYS)
+        scores = lax.dot_general(
+            query, mixed_ref[1, key_span, lanes], TURNED, preferred_element_type=jnp.float32
+        )
+        flow = lax.dot_general(
+            grad, mixed_ref[2, key_span, lanes], TURNED, preferred_element_type=jnp.float32
+        )
+        mask = tile_mask(row_block, key_block, aux_ref, seg_row_ref)
+        probs = jnp.exp(jnp.where(mask, scores * scale, MASK_FILL) - lse)
+        probs_ref[:, key_span] = probs
+        flow_ref[:, key_span] = flow
+        product = probs * flow
+        for part in range(ATTEND_KEYS // 128):
+            delta = delta + product[:, part * 128 : (part + 1) * 128]
+        value_sum[key_span, lanes] += lax.dot_general(
+            probs.astype(jnp.bfloat16), grad, CROSSED, preferred_element_type=jnp.float32
+        )
+        return delta
+
+    delta = lax.fori_loop(0, count, first, jnp.zeros((ATTEND_ROWS, 128), jnp.float32))
+    delta = jnp.sum(delta, axis=1, keepdims=True)
+
+    def second(key_block, total):
+        key_span = pl.ds(pl.multiple_of(key_block * ATTEND_KEYS, ATTEND_KEYS), ATTEND_KEYS)
+        low = (probs_ref[:, key_span] * (flow_ref[:, key_span] - delta)).astype(jnp.bfloat16)
+        key_sum[key_span, lanes] += lax.dot_general(
+            low, query, CROSSED, preferred_element_type=jnp.float32
+        )
+        return total + jnp.dot(
+            low, mixed_ref[1, key_span, lanes], preferred_element_type=jnp.float32
+        )
+
+    total = lax.fori_loop(0, count, second, jnp.zeros((ATTEND_ROWS, HEAD_DIM), jnp.float32))
+    query_grad = (total * scale).astype(jnp.bfloat16)
+    stacked_ref[0, row_span, lanes] = query_grad
+    bias_sum[0:1, lanes] += jnp.sum(query_grad.astype(jnp.float32), axis=0, keepdims=True)
 
 
 def tile_scores(query_tile, keys, segment, row_block, col_block):
@@ -1864,6 +2138,96 @@
     return (master - rate * change, first_next, second_next)
 
 
+def adam_step(master, grad, first, second, rate, decay, fixes):
+    first_next = BETA_FIRST * first + (1.0 - BETA_FIRST) * grad
+    second_next = BETA_SECOND * second + (1.0 - BETA_SECOND) * grad * grad
+    change = (
+        first_next / fixes[0] / (jnp.sqrt(second_next / fixes[1]) + ADAM_EPSILON)
+        + decay * master
+    )
+    return master - rate * change, first_next, second_next
+
+
+def adam_kernel(rates, fix_ref, late_ref, early_ref, *refs):
+    fixes = (fix_ref[0], fix_ref[1])
+    smalls = 4
+    matrix_inputs, small_inputs = refs[: 4 * len(rates)], refs[4 * len(rates) :][: 3 * smalls]
+    outputs = refs[4 * len(rates) + 3 * smalls :]
+    for index, rate in enumerate(rates):
+        master, grad, first, second = matrix_inputs[4 * index : 4 * index + 4]
+        updated, first_out, second_out, grad_out, low_out = outputs[5 * index : 5 * index + 5]
+        value = grad[...].reshape(master.shape)
+        fresh = adam_step(
+            master[...], value, first[...], second[...], rate, MATRIX_DECAY, fixes
+        )
+        updated[...], first_out[...], second_out[...] = fresh
+        grad_out[...] = value
+        low_out[...] = fresh[0].astype(jnp.bfloat16)
+
+    @pl.when(pl.program_id(0) == 0)
+    def _():
+        local = small_inputs[0].shape[1]
+        units = small_inputs[3].shape[1]
+        early = early_ref
+        pieces = (
+            [early[4:5, :local], early[4:5, local : 2 * local]],
+            [early[4:5, 2 * local : 2 * local + units]],
+            [late_ref[0:1, :], early[0:1, :]],
+            [late_ref[1:2, :], early[2:3, :], early[1:2, :], early[3:4, :]],
+        )
+        for index in range(smalls):
+            master, first, second = small_inputs[3 * index : 3 * index + 3]
+            to = 5 * len(rates) + 4 * index
+            updated, first_out, second_out, grad_out = outputs[to : to + 4]
+            for row, value in enumerate(pieces[index]):
+                here = slice(row, row + 1)
+                fresh = adam_step(
+                    master[here, :], value, first[here, :], second[here, :], SMALL_RATE, 0.0, fixes
+                )
+                updated[here, :], first_out[here, :], second_out[here, :] = fresh
+                grad_out[here, :] = value
+
+
+ADAM_STEPS = 8
+
+
+def adam_call(matrices, smalls, late, early, fixes):
+    in_specs = [pl.BlockSpec(memory_space=pltpu.SMEM)] + [
+        pl.BlockSpec(rows.shape, lambda i: (0, 0)) for rows in (late, early)
+    ]
+    out_specs, out_shape, operands, rates = [], [], [fixes, late, early], []
+    for master, grad, first, second, rate in matrices:
+        lead = master.shape[:-2]
+        rows, columns = master.shape[-2] // ADAM_STEPS, master.shape[-1]
+        zeros = (0,) * len(lead)
+        whole = pl.BlockSpec(lead + (rows, columns), lambda i, z=zeros: z + (i, 0))
+        half = pl.BlockSpec(
+            (1,) + lead + (rows, columns),
+            lambda i, z=zeros: (i // (ADAM_STEPS // 2),) + z + (i % (ADAM_STEPS // 2), 0),
+        )
+        in_specs += [whole, half, whole, whole]
+        operands += [master, grad, first, second]
+        shape = jax.ShapeDtypeStruct(master.shape, jnp.float32)
+        out_specs += [whole] * 5
+        out_shape += [shape] * 4 + [jax.ShapeDtypeStruct(master.shape, jnp.bfloat16)]
+        rates.append(rate)
+    for group in smalls:
+        spec = pl.BlockSpec(group[0].shape, lambda i: (0, 0))
+        in_specs += [spec] * 3
+        operands += list(group)
+        out_specs += [spec] * 4
+        out_shape += [jax.ShapeDtypeStruct(group[0].shape, jnp.float32)] * 4
+    return pl.pallas_call(
+        functools.partial(adam_kernel, tuple(rates)),
+        grid=(ADAM_STEPS,),
+        in_specs=in_specs,
+        out_specs=out_specs,
+        out_shape=out_shape,
+        compiler_params=pltpu.CompilerParams(vmem_limit_bytes=VMEM_LIMIT),
+        name="adam",
+    )(*operands)
+
+
 def per_device(
     layer_input,
     cotangent,
@@ -1895,46 +2259,52 @@
     gains_second,
     shifts_second,
 ):
-    own_rows = layer_input.shape[0]
     parts = lax.axis_size("mp")
-    group_rows = own_rows * parts
-    slots_here = lengths.shape[0]
-    slot_len = group_rows // slots_here
     local_width = mix_weight.shape[2]
-    positions = jnp.arange(slot_len, dtype=jnp.int32)
-    live = (positions[None, :] >= offsets[:, None]) & (
-        positions[None, :] < (offsets + lengths)[:, None]
-    )
-    first_row = lax.axis_index("mp") * own_rows
-    own_live = own_slice(live.reshape(-1), first_row, own_rows)[:, None]
-    low = jnp.bfloat16
-    normed_one, mixed, mix_whole, out_whole = project_call(
+    bounds = jnp.concatenate([offsets, offsets + lengths])
+    (
+        normed_one,
+        mixed,
+        mix_whole,
+        out_whole,
+        up_low,
+        down_low,
+        own_branch,
+        bias_down_grad,
+    ) = project_call(
         layer_input,
         norm_gains[0:1],
         shifts[0:1],
-        mix_weight.astype(low),
-        out_weight.astype(low),
+        mix_weight,
+        out_weight,
         mix_bias,
+        up_weight,
+        down_weight,
+        cotangent,
+        bounds,
         parts // 2,
     )
-    out_grad = jnp.where(own_live, cotangent.astype(jnp.float32), 0.0)
-    bias_down_grad = jnp.sum(out_grad, axis=0)
-    seg_col = live.reshape(-1, 1).astype(jnp.float32)
-    seg_row = live.reshape(1, -1).astype(jnp.float32)
-    attended_flat, lse = attention_call(mixed, seg_col, seg_row)
-    resid_own, normed_mid, branch_grad, up_whole, down_whole = attend_out_call(
+    (
         attended_flat,
+        aux,
+        resid_own,
+        normed_mid,
+        branch_grad,
+        up_whole,
+        down_whole,
+    ) = attend_out_call(
+        mixed,
+        bounds,
         out_whole,
         layer_input,
-        out_grad.astype(low),
+        own_branch,
         norm_gains[1:2],
         shifts[2:3],
         shifts[1:2],
-        up_weight.astype(low),
-        down_weight.astype(low),
+        up_low,
+        down_low,
         parts // 2,
     )
-    own_branch = out_grad.astype(low)
     normed_two, active, hidden_grad, resid_grad, resid_low, row_sums, up_bias_grad = feed_call(
         normed_mid,
         branch_grad,
@@ -1947,23 +2317,24 @@
         parts // 2,
     )
     up_bias_grad = up_bias_grad[0]
-    attended_grad, down_pieces, out_pieces, layer_output = branch_back_call(
+    stacked, mix_bias_grad, down_pieces, out_grad, layer_output, _ = branch_back_call(
         resid_low,
         active,
         down_whole,
         attended_flat,
         out_whole,
+        shifts[3:4],
+        bounds,
+        mixed,
+        aux,
         resid_own,
-        shifts[3:4],
-        own_live.astype(jnp.float32),
         branch_grad,
         parts // 2,
     )
-    stacked, mix_bias_grad = attention_back_call(mixed, seg_col, seg_row, lse, attended_grad)
     early = jnp.concatenate(
         [
             row_sums,
-            bias_down_grad[None],
+            bias_down_grad,
             jnp.pad(
                 jnp.concatenate([mix_bias_grad.reshape(-1), up_bias_grad]),
                 (0, row_sums.shape[1] - 2 * local_width - up_bias_grad.shape[0]),
@@ -1971,7 +2342,7 @@
         ],
         axis=0,
     )
-    input_grad, late, early, mix_pieces, up_pieces = input_back_call(
+    input_grad, late, early, mix_pieces, up_pieces, out_pieces = input_back_call(
         stacked,
         mix_whole,
         layer_input,
@@ -1979,119 +2350,58 @@
         norm_gains[0:1],
         early,
         hidden_grad,
+        out_grad,
         normed_one,
         normed_two,
         parts // 2,
     )
-    mix_owned = mix_pieces.transpose(1, 0, 2, 3).reshape(mix_weight.shape)
-    up_owned = up_pieces.reshape(up_weight.shape)
-    down_owned = down_pieces.reshape(down_weight.shape)
-    out_owned = out_pieces.reshape(out_weight.shape)
-    mix_bias_total = early[4, : 2 * local_width].reshape(2, local_width)
-    up_bias_total = early[4, 2 * local_width : 2 * local_width + up_bias.shape[0]]
-    gain_total = jnp.stack([late[0], early[0]])
-    shift_total = jnp.stack([late[1], early[2], early[1], early[3]])
     step_count = step[0].astype(jnp.float32)
-    first_fix = 1.0 - BETA_FIRST**step_count
-    second_fix = 1.0 - BETA_SECOND**step_count
-    mix_new = adam_update(
-        mix_weight,
-        mix_owned,
-        mix_first,
-        mix_second,
-        D ** (-0.5),
-        MATRIX_DECAY,
-        first_fix,
-        second_fix,
-    )
-    out_new = adam_update(
-        out_weight,
-        out_owned,
-        out_first,
-        out_second,
-        OUT_FAN ** (-0.5),
-        MATRIX_DECAY,
-        first_fix,
-        second_fix,
-    )
-    up_new = adam_update(
-        up_weight, up_owned, up_first, up_second, D ** (-0.5), MATRIX_DECAY, first_fix, second_fix
-    )
-    down_new = adam_update(
-        down_weight,
-        down_owned,
-        down_first,
-        down_second,
-        FF ** (-0.5),
-        MATRIX_DECAY,
-        first_fix,
-        second_fix,
-    )
-    mix_bias_new = adam_update(
-        mix_bias,
-        mix_bias_total,
-        mix_bias_first,
-        mix_bias_second,
-        SMALL_RATE,
-        0.0,
-        first_fix,
-        second_fix,
-    )
-    up_bias_new = adam_update(
-        up_bias,
-        up_bias_total,
-        up_bias_first,
-        up_bias_second,
-        SMALL_RATE,
-        0.0,
-        first_fix,
-        second_fix,
-    )
-    gains_new = adam_update(
-        norm_gains, gain_total, gains_first, gains_second, SMALL_RATE, 0.0, first_fix, second_fix
-    )
-    shifts_new = adam_update(
-        shifts, shift_total, shifts_first, shifts_second, SMALL_RATE, 0.0, first_fix, second_fix
-    )
+    fixes = jnp.stack([1.0 - BETA_FIRST**step_count, 1.0 - BETA_SECOND**step_count])
+    news = adam_call(
+        [
+            (mix_weight, mix_pieces, mix_first, mix_second, D ** (-0.5)),
+            (out_weight, out_pieces, out_first, out_second, OUT_FAN ** (-0.5)),
+            (up_weight, up_pieces, up_first, up_second, D ** (-0.5)),
+            (down_weight, down_pieces, down_first, down_second, FF ** (-0.5)),
+        ],
+        [
+            (mix_bias, mix_bias_first, mix_bias_second),
+            (up_bias[None], up_bias_first[None], up_bias_second[None]),
+            (norm_gains, gains_first, gains_second),
+            (shifts, shifts_first, shifts_second),
+        ],
+        late,
+        early,
+        fixes,
+    )
+    mix, out, up, down = (news[5 * index : 5 * index + 5] for index in range(4))
+    biases, unit_biases, gains, moves = (
+        news[20 + 4 * index : 24 + 4 * index] for index in range(4)
+    )
+    unit_biases = [value[0] for value in unit_biases]
     return (
         layer_output,
         input_grad,
-        mix_new[0],
-        mix_new[1],
-        mix_new[2],
-        out_new[0],
-        out_new[1],
-        out_new[2],
-        up_new[0],
-        up_new[1],
-        up_new[2],
-        down_new[0],
-        down_new[1],
-        down_new[2],
-        mix_bias_new[0],
-        mix_bias_new[1],
-        mix_bias_new[2],
-        up_bias_new[0],
-        up_bias_new[1],
-        up_bias_new[2],
-        gains_new[0],
-        gains_new[1],
-        gains_new[2],
-        shifts_new[0],
-        shifts_new[1],
-        shifts_new[2],
-        mix_owned,
-        out_owned,
-        up_owned,
-        down_owned,
-        mix_bias_total,
-        up_bias_total,
-        gain_total,
-        shift_total,
-        mix_new[0].astype(jnp.bfloat16),
-        out_new[0].astype(jnp.bfloat16),
-        up_new[0].astype(jnp.bfloat16),
-        down_new[0].astype(jnp.bfloat16),
+        *mix[:3],
+        *out[:3],
+        *up[:3],
+        *down[:3],
+        *biases[:3],
+        *unit_biases[:3],
+        *gains[:3],
+        *moves[:3],
+        mix[3],
+        out[3],
+        up[3],
+        down[3],
+        biases[3],
+        unit_biases[3],
+        gains[3],
+        moves[3],
+        mix[4],
+        out[4],
+        up[4],
+        down[4],
     )
 
 

time: 701 us -> 578 us (0.82)
  Pallas kernels: 641 us -> 563 us
  other arithmetic: 32.2 us -> 1.83 us
  local copies, waits for them, and re-layouts: 16.5 us -> 5.54 us
    pallas_call x2 -> x1, Pallas kernels: 79.8 us -> 20.9 us  [adam_call(): pl.pallas_call(functools.partial(adam_kernel, tuple(rates)), grid=(ADAM_S...]
    convert_element_type x10 -> x0, other arithmetic: 26.4 us -> none  [the longest x1 7.5 us: per_device(): up_new[0].astype(jnp.bfloat16)]
    pallas_call x1, Pallas kernels: 136 us -> 123 us  [feed_call(): pl.pallas_call(functools.partial(feed_kernel, chips, parts), out_shape=(j...]
where the time goes in v4:
time: 578 us; the launch traced here: 573 us
  Pallas kernels  563 us (97%)
    pallas_call x1, Pallas kernels, feed_call(): pl.pallas_call(functools.partial(feed_kernel, chips, parts), out_shape=(j...  123 us
    pallas_call x1, Pallas kernels, branch_back_call(): pl.pallas_call(functools.partial(branch_back_kernel, chips, 2), out_shape...  121 us
    pallas_call x1, Pallas kernels, input_back_call(): pl.pallas_call(functools.partial(input_back_kernel, chips), out_shape=(ja...  107 us
    pallas_call x1, Pallas kernels, attend_out_call(): pl.pallas_call(functools.partial(attend_out_kernel, chips), out_shape=(ja...  104 us
    pallas_call x1, Pallas kernels, project_call(): pl.pallas_call(functools.partial(project_kernel, chips), out_shape=(jax.S...  86.5 us
    pallas_call x1, Pallas kernels, adam_call(): pl.pallas_call(functools.partial(adam_kernel, tuple(rates)), grid=(ADAM_S...  20.9 us

profile of v4, /device:TPU:0, one launch (start us, length us, event | category | flops | bytes accessed | tf_op | source)
XLA Modules:
  0.0 573.4 jit_solution(16879460651831267671)
XLA Ops:
  0.7 1.6 fusion
  3.5 0.6 pad_add_fusion.bounds_ref
  4.1 86.5 %project.1 = (bf16[2048,2048]{1,0:T(8,128)(2,1)}, bf16[3,2048,256]{2,1,0:T(8,128)(2,1)}, bf16[3,4,512,256]{3,2,1,0:T(8,128)(2,1)}, bf16[4,256,512]{2,1,0:T(8,128...) custom-call(bf16[256,2048]{1,0:T(8,128)(2,1)} %rows_hbm.3, ...), custom_call_target="tpu_custom_call" | custom-call | flops 45097156608 | tf_op jit(solution)/shard_map/project/pallas_call | solution.py:484
  90.7 104.2 %attend_out.1 = (bf16[2048,256]{1,0:T(8,128)(2,1)}, f32[2048,3]{1,0:T(8,128)}, f32[256,2048]{1,0:T(8,128)}, bf16[256,2048]{1,0:T(8,128)(2,1)}, bf16[2048,2048]{1...) custom-call(bf16[3,2048,256]{2,1,0:T(8,128)(2,1)} %get-tuple-element.107.mixed_hbm, ...), custom_call_target="tpu_custom_call" | custom-call | flops 99999997952 | tf_op jit(solution)/shard_map/attend_out/pallas_call | solution.py:1005
  194.9 122.8 %feed.1 = (bf16[2048,2048]{1,0:T(8,128)(2,1)}, bf16[2048,1024]{1,0:T(8,128)(2,1)}, bf16[2048,1024]{1,0:T(8,128)(2,1)}, f32[256,2048]{1,0:T(8,128)}, bf16[256,204...) custom-call(bf16[256,2048]{1,0:T(8,128)(2,1)} %get-tuple-element.112.normed_ref, ...), custom_call_target="tpu_custom_call" | custom-call | flops 99999997952 | tf_op jit(solution)/shard_map/feed/pallas_call | solution.py:1588
  317.6 0.0 copy-start.4
  317.7 0.0 copy-start.2
  317.7 0.0 copy-start.3
  317.7 121.5 %branch_back.1 = (bf16[3,2048,256]{2,1,0:T(8,128)(2,1)}, f32[2,256]{1,0:T(2,128)}, f32[2,512,512]{2,1,0:T(8,128)}, f32[256,2048]{1,0:T(8,128)}, bf16[256,2048]{1...) custom-call(bf16[256,2048]{1,0:T(8,128)(2,1)} %get-tuple-element.117.branch_ref, ...), custom_call_target="tpu_custom_call" | custom-call | flops 99999997952 | tf_op jit(solution)/shard_map/branch_back/pallas_call | solution.py:1857
  439.2 0.7 copy.67
  439.9 0.0 copy-done.4
  439.9 0.0 copy-done.2
  439.9 0.0 copy-done.3
  439.9 0.7 pad_maximum_fusion.early_ref
  440.6 107.1 %input_back.1 = (f32[256,2048]{1,0:T(8,128)}, f32[2,2048]{1,0:T(2,128)}, f32[5,2048]{1,0:T(8,128)}, f32[2,3,256,256]{3,2,1,0:T(8,128)}, f32[2,256,1024]{2,1,0:T(8,128)}, /*index=5*/f32[2,128,512]{2,1,0:T(8,128)}) custom-call(bf16[3,2048,256]{2,1,0:T(8,128)(2,1)} %get-tuple-element.122.stacked_hbm, bf16[3,4,512,256]{3,2,1,0:T(8,128)(2,1)} %get-tuple-element.123.mix_hbm, ...), custom_call_target="tpu_custom_call" | custom-call | flops 99999997952 | tf_op jit(solution)/shard_map/input_back/pallas_call | solution.py:1223
  548.4 0.6 pad_maximum_fusion.1.fix_ref
  549.0 0.0 copy-start.1
  549.0 20.9 %adam.1 = (f32[3,512,256]{2,1,0:T(8,128)}, f32[3,512,256]{2,1,0:T(8,128)}, f32[3,512,256]{2,1,0:T(8,128)}, f32[3,512,256]{2,1,0:T(8,128)}, bf16[3,512,256]{2,1,0...) custom-call(f32[2]{0:T(128)} %pad_maximum_fusion.1.fix_ref, ...), custom_call_target="tpu_custom_call" | custom-call | tf_op jit(solution)/shard_map/adam/pallas_call | solution.py:2220
  569.9 0.0 copy-start
  570.0 0.0 copy-done.1
  570.0 1.0 copy.73
  570.9 1.0 copy-done
  571.9 1.3 copy.74
  (1 shorter events, 0.0 us)
Async XLA Ops:
  317.6 122.2 %copy-start.4 = (f32[1,1024]{1,0:T(1,128)S(1)}, f32[1,1024]{1,0:T(1,128)}, u32[]{:S(2)}) copy-start(f32[1,1024]{1,0:T(1,128)} %get-tuple-element.128) | copy-start | bytes 12292
  317.7 122.2 %copy-start.2 = (f32[3,2048]{1,0:T(4,128)S(1)}, f32[3,2048]{1,0:T(4,128)}, u32[]{:S(2)}) copy-start(f32[3,2048]{1,0:T(4,128)} %get-tuple-element.125) | copy-start | bytes 73732
  317.7 122.2 %copy-start.3 = (f32[1,2048]{1,0:T(1,128)S(1)}, f32[1,2048]{1,0:T(1,128)}, u32[]{:S(2)}) copy-start(f32[1,2048]{1,0:T(1,128)} %get-tuple-element.126) | copy-start | bytes 24580
  549.0 21.0 %copy-start.1 = (bf16[256,2048]{1,0:T(8,128)(2,1)S(1)}, bf16[256,2048]{1,0:T(8,128)(2,1)}, u32[]{:S(2)}) copy-start(bf16[256,2048]{1,0:T(8,128)(2,1)} %get-tuple-element.222) | copy-start | bytes 3145732
  569.9 2.0 copy-start

commit v5 on v4

--- a/solution.py
+++ b/solution.py
@@ -204,12 +204,15 @@
             self.place.side,
         ).wait_recv()
 
+    def begin_part(self, part):
+        place = self.place
+        pl.when(place.has_up)(lambda: self.copy(0, place.chip, part, self.own).start())
+        pl.when(place.has_down)(lambda: self.copy(1, place.chip, part, self.own).start())
+        self.copy(2, place.chip, part, self.own).start()
+
     def begin(self):
-        place = self.place
         for part in range(self.parts):
-            pl.when(place.has_up)(lambda: self.copy(0, place.chip, part, self.own).start())
-            pl.when(place.has_down)(lambda: self.copy(1, place.chip, part, self.own).start())
-            self.copy(2, place.chip, part, self.own).start()
+            self.begin_part(part)
 
     def step(self, distance, part=0):
         place = self.place
@@ -306,15 +309,16 @@
 
 def project_kernel(
     chips,
+    parts,
     rows_ref,
     gain_ref,
     shift_ref,
-    mix_weight_ref,
-    out_weight_ref,
+    mix_weight_hbm,
+    out_weight_hbm,
     bias_ref,
-    up_weight_ref,
-    down_weight_ref,
-    cotangent_ref,
+    up_weight_hbm,
+    down_weight_hbm,
+    cotangent_hbm,
     bounds_ref,
     normed_ref,
     mixed_hbm,
@@ -324,6 +328,12 @@
     down_ref,
     branch_ref,
     branch_sum_ref,
+    mix_weight_ref,
+    out_weight_ref,
+    up_weight_ref,
+    down_weight_ref,
+    cotangent_ref,
+    fetch_sem,
     mix_ref,
     out_ref,
     mixed_ref,
@@ -341,7 +351,35 @@
 ):
     place = Place(chips)
     count = rows_ref.shape[0]
+    rows = count // parts
+    fetched = fetch(
+        [
+            (mix_weight_hbm, mix_weight_ref),
+            (out_weight_hbm, out_weight_ref),
+            (cotangent_hbm, cotangent_ref),
+            (up_weight_hbm, up_weight_ref),
+            (down_weight_hbm, down_weight_ref),
+        ],
+        fetch_sem,
+    )
+    line = LineGather(place, blocks, line_send, line_recv, parts)
+
+    def norm(part):
+        def one(span):
+            own = rows_ref[pl.ds(part * rows + span.start, 64), :].astype(jnp.float32)
+            normed = norm_rows(own, gain_ref[...], shift_ref[...])
+            blocks[2 * (place.chip * parts + part) + place.core, span, :] = normed.astype(
+                jnp.bfloat16
+            )
+
+        by_rows(rows, 64, one)
+
+    norm(0)
     place.greet(True)
+    line.begin_part(0)
+    for part in range(1, parts):
+        norm(part)
+        line.begin_part(part)
     mix = SquareGather(
         place,
         mix_ref,
@@ -365,26 +403,16 @@
 
         by_rows(source.shape[0], 64, one)
 
+    fetched[0].wait()
     for part in range(3):
         lower(mix_weight_ref.at[part], mix_ref.at[part])
-    lower(out_weight_ref, out_ref)
     mix.begin()
     own_mix = pltpu.make_async_copy(mix_ref, mix_whole.at[:, place.dp], own_sem.at[0])
+    own_mix.start()
+    fetched[1].wait()
+    lower(out_weight_ref, out_ref)
     own_out = pltpu.make_async_copy(out_ref, out_whole.at[place.dp], own_sem.at[1])
-    own_mix.start()
     own_out.start()
-    tile = 64
-
-    def norm(index, carry):
-        span = pl.ds(pl.multiple_of(index * tile, tile), tile)
-        rows = rows_ref[span, :].astype(jnp.float32)
-        normed = norm_rows(rows, gain_ref[...], shift_ref[...])
-        blocks[place.me, span, :] = normed.astype(jnp.bfloat16)
-        return carry
-
-    lax.fori_loop(0, count // tile, norm, 0)
-    line = LineGather(place, blocks, line_send, line_recv)
-    line.begin()
     branch_sum_ref[...] = jnp.zeros_like(branch_sum_ref)
 
     def branch(span):
@@ -393,82 +421,105 @@
         branch_ref[span, :] = grad.astype(jnp.bfloat16)
         branch_sum_ref[...] += jnp.sum(grad, axis=0, keepdims=True)
 
+    fetched[2].wait()
     by_rows(count, 64, branch)
+    fetched[3].wait()
     lower(up_weight_ref, up_ref)
+    fetched[4].wait()
     lower(down_weight_ref, down_ref)
-    mix.middle()
-    out.begin()
-
-    def keep(block):
-        span = pl.ds(pl.multiple_of(block * count, count), count)
-        return pltpu.make_async_copy(blocks.at[block], normed_ref.at[span], keep_sem.at[block])
-
-    def emit(block):
-        span = pl.ds(pl.multiple_of(block * count, count), count)
-        return pltpu.make_async_copy(
-            mixed_ref.at[:, span], mixed_hbm.at[:, span], emit_sem.at[block]
-        )
-
-    keep_mix = pltpu.make_async_copy(mix_whole, mix_hbm, emit_sem.at[2 * chips])
-
-    def project(block):
-        keep(block).start()
-        span = pl.ds(pl.multiple_of(block * count, count), count)
-        rows = blocks[block]
-        for part in range(3):
-            weight = mix_whole[part].reshape(-1, mix_whole.shape[3])
-            result = jnp.dot(rows, weight, preferred_element_type=jnp.float32)
-            if part == 0:
+
+    def span_of(chip, core, part):
+        start = (2 * chip + core) * count + part * rows
+        return pl.ds(pl.multiple_of(start, rows), rows)
+
+    def copies(chip, part):
+        piece = chip * parts + part
+        taken = []
+        for core in range(2):
+            span = span_of(chip, core, part)
+            taken.append(
+                pltpu.make_async_copy(
+                    blocks.at[2 * piece + core], normed_ref.at[span], keep_sem.at[piece, core]
+                )
+            )
+            taken.append(
+                pltpu.make_async_copy(
+                    mixed_ref.at[:, span], mixed_hbm.at[:, span], emit_sem.at[piece, core]
+                )
+            )
+        return taken
+
+    keep_mix = pltpu.make_async_copy(mix_whole, mix_hbm, own_sem.at[2])
+
+    def project(chip, part):
+        piece = chip * parts + part
+        line.arrive(chip, 1 - place.core, part)
+        pair = blocks[pl.ds(2 * piece, 2)].reshape(2 * rows, -1)
+        for kind in range(3):
+            weight = mix_whole[kind].reshape(-1, mix_whole.shape[3])
+            result = jnp.dot(pair, weight, preferred_element_type=jnp.float32)
+            if kind == 0:
                 result = result + bias_ref[0:1, :]
-            if part == 2:
+            if kind == 2:
                 result = result + bias_ref[1:2, :]
-            mixed_ref[part, span, :] = result.astype(jnp.bfloat16)
-        emit(block).start()
-
-    def step(distance, carry):
-        @pl.when((distance > 0) & (distance < chips))
+            low = result.astype(jnp.bfloat16)
+            for core in range(2):
+                mixed_ref[kind, span_of(chip, core, part), :] = low[
+                    core * rows : (core + 1) * rows
+                ]
+        for copy in copies(chip, part):
+            copy.start()
+
+    def turn(index, carry):
+        distance = index // parts
+        part = index % parts
+
+        @pl.when(distance > 0)
         def _():
-            line.step(distance)
-
-        @pl.when(distance == 1)
+            line.step(distance, part)
+
+        @pl.when(index == parts)
         def _():
+            mix.middle()
+            out.begin()
             mix.end()
             own_mix.wait()
             keep_mix.start()
             out.middle()
 
-        def one(index, inner):
-            near = distance - 1
-            side = index % 2
-            core = (place.core + index // 2) % 2
+        first = jnp.where(index == parts, 0, index)
+
+        def one(order, inner):
+            each = order // 2
+            side = order % 2
+            near = each // parts
             chip = place.chip + near * (2 * side - 1)
 
             @pl.when((chip >= 0) & (chip < chips) & ((near > 0) | (side == 0)))
             def _():
-                pl.when(index >= 2)(lambda: line.arrive(chip, core))
-                project(2 * chip + core)
+                project(chip, each % parts)
 
             return inner
 
-        @pl.when(distance > 0)
+        @pl.when(index >= parts)
         def _():
-            lax.fori_loop(0, 4, one, 0)
+            lax.fori_loop(2 * first, 2 * index + 2, one, 0)
 
         return carry
 
-    lax.fori_loop(0, chips + 1, step, 0)
+    lax.fori_loop(0, chips * parts, turn, 0)
     out.end()
     own_out.wait()
     line.finish()
     mix.finish()
     out.finish()
 
-    def kept(block, carry):
-        keep(block).wait()
-        emit(block).wait()
+    def kept(piece, carry):
+        for copy in copies(piece // parts, piece % parts):
+            copy.wait()
         return carry
 
-    lax.fori_loop(0, 2 * chips, kept, 0)
+    lax.fori_loop(0, parts * chips, kept, 0)
     keep_mix.wait()
 
 
@@ -478,11 +529,13 @@
     count, width = rows.shape
     total = 2 * chips * count
     local = mix_shard.shape[2]
+    parts = 2
     vmem = pl.BlockSpec(memory_space=pltpu.VMEM)
+    hbm = pl.BlockSpec(memory_space=pl.ANY)
     dma = pltpu.SemaphoreType.DMA
     flops = 2 * total * width * 3 * local
     return pl.pallas_call(
-        functools.partial(project_kernel, chips),
+        functools.partial(project_kernel, chips, parts),
         out_shape=(
             jax.ShapeDtypeStruct((total, width), jnp.bfloat16),
             jax.ShapeDtypeStruct((3, total, local), jnp.bfloat16),
@@ -493,23 +546,33 @@
             jax.ShapeDtypeStruct((count, width), jnp.bfloat16),
             jax.ShapeDtypeStruct((1, width), jnp.float32),
         ),
-        in_specs=[vmem] * 9 + [pl.BlockSpec(memory_space=pltpu.SMEM)],
-        out_specs=(pl.BlockSpec(memory_space=pl.ANY),) * 4 + (vmem,) * 4,
+        in_specs=[vmem] * 3
+        + [hbm] * 2
+        + [vmem]
+        + [hbm] * 3
+        + [pl.BlockSpec(memory_space=pltpu.SMEM)],
+        out_specs=(hbm,) * 4 + (vmem,) * 4,
         scratch_shapes=[
+            pltpu.VMEM(mix_shard.shape, jnp.float32),
+            pltpu.VMEM(out_shard.shape, jnp.float32),
+            pltpu.VMEM(up.shape, jnp.float32),
+            pltpu.VMEM(down.shape, jnp.float32),
+            pltpu.VMEM(cotangent.shape, jnp.bfloat16),
+            dma((5,)),
             pltpu.VMEM(mix_shard.shape, jnp.bfloat16),
             pltpu.VMEM(out_shard.shape, jnp.bfloat16),
             pltpu.VMEM((3, total, local), jnp.bfloat16),
             pltpu.VMEM((3, 4, mix_shard.shape[1], local), jnp.bfloat16),
-            dma((2 * chips + 1,)),
-            pltpu.VMEM((2 * chips, count, width), jnp.bfloat16),
-            dma((3, chips)),
-            dma((2 * chips,)),
+            dma((parts * chips, 2)),
+            pltpu.VMEM((2 * chips * parts, count // parts, width), jnp.bfloat16),
+            dma((3, chips * parts)),
+            dma((2 * chips * parts,)),
             dma((4,)),
             dma((4,)),
             dma((4,)),
             dma((4,)),
-            dma((2,)),
-            dma((2 * chips,)),
+            dma((3,)),
+            dma((parts * chips, 2)),
         ],
         compiler_params=pltpu.CompilerParams(
             collective_id=0, has_side_effects=True, vmem_limit_bytes=VMEM_LIMIT
@@ -607,10 +670,13 @@
     def begin(self):
         self.each(self.place.chips - 1, self.hand_over)
 
-    def step(self, index):
+    def step(self, index, early=False):
         distance = self.place.chips - 1 - index
-        pl.when(distance > 0)(lambda: self.each(distance - 1, self.hand_over))
+        ahead = (index > 0) if early else (index < 0)
+        pl.when(ahead & (distance > 0))(lambda: self.each(distance - 1, self.hand_over))
         self.each(distance, self.sum_up)
+        behind = (index == 0) if early else (index >= 0)
+        pl.when(behind & (distance > 0))(lambda: self.each(distance - 1, self.hand_over))
 
     def finish(self):
         place = self.place
@@ -907,17 +973,15 @@
 
     def prepare(chip):
         def one(index, carry):
-            for head in range(mixed_ref.shape[2] // HEAD_DIM):
-                attend_rows(
-                    head,
-                    chip * (2 * count // ATTEND_ROWS) + index,
-                    mixed_ref,
-                    seg_col_ref,
-                    seg_row_ref,
-                    attended_ref,
-                    lse_ref,
-                    score_ref,
-                )
+            attend_rows(
+                chip * (2 * count // ATTEND_ROWS) + index,
+                mixed_ref,
+                seg_col_ref,
+                seg_row_ref,
+                attended_ref,
+                lse_ref,
+                score_ref,
+            )
             return carry
 
         lax.fori_loop(0, 2 * count // ATTEND_ROWS, one, 0)
@@ -947,7 +1011,7 @@
         return pltpu.make_async_copy(source, branch_whole.at[span], keep_sem.at[block, part])
 
     def step(index, carry):
-        sums.step(index)
+        sums.step(index, True)
         pl.when(index < chips - 1)(lambda: line.step(index + 1))
 
         @pl.when(index == 1)
@@ -1022,7 +1086,7 @@
             dma((3,)),
             pltpu.VMEM((total, 1), jnp.float32),
             pltpu.VMEM((1, total), jnp.float32),
-            pltpu.VMEM((ATTEND_ROWS, total), jnp.float32),
+            pltpu.VMEM((local // HEAD_DIM, ATTEND_ROWS, total), jnp.float32),
             pltpu.VMEM((2 * chips, count, width), low),
             dma((3, chips)),
             dma((2 * chips,)),
@@ -1336,7 +1400,14 @@
 
     lax.fori_loop(0, parts, fill, 0)
     line = LineGather(place, blocks, line_send, line_recv, parts)
-    line.begin()
+    line.begin_part(0)
+    line.copy(2, place.chip, 1).start()
+    pl.when(place.has_up & jnp.logical_not(place.has_down))(
+        lambda: line.copy(0, place.chip, 1).start()
+    )
+    pl.when(place.has_down & jnp.logical_not(place.has_up))(
+        lambda: line.copy(1, place.chip, 1).start()
+    )
     bias_grad_ref[...] = jnp.zeros_like(bias_grad_ref)
 
     def piece_span(piece):
@@ -1400,14 +1471,13 @@
     width = 512
     tiles = up_ref.shape[2] // width
 
-    def compute(chip, part):
+    def compute(chip, part, side):
         piece = chip * parts + part
-        load(piece, 0).start()
         keep(piece, 0).start()
         keep(piece, 1).start()
         span = piece_span(piece)
         own_rows = blocks[pl.ds(2 * piece, 2)].reshape(pair, -1)
-        load(piece, 0).wait()
+        load(piece, side).wait()
 
         def tile(index, carry):
             units = pl.ds(pl.multiple_of(index * width, width), width)
@@ -1422,7 +1492,7 @@
             for owner in range(4):
                 columns = down_ref.shape[2]
                 product = lax.dot_general(
-                    branch_buf[0, :, owner * columns : (owner + 1) * columns],
+                    branch_buf[side, :, owner * columns : (owner + 1) * columns],
                     down_ref[owner, units, :],
                     TURNED,
                     preferred_element_type=jnp.float32,
@@ -1469,44 +1539,68 @@
 
             line_copy(way, chip, part, tile).start()
 
+    def coming(index, side):
+        count_beyond = jnp.where(side == 0, place.chip, last - place.chip)
+        early = index <= count_beyond
+        distance = jnp.where(early, index, 2 * count_beyond + 1 - index)
+        valid = (index == 0) | (index <= 2 * count_beyond)
+        chip = jnp.where(index == 0, place.chip, place.chip + distance * (2 * side - 1))
+        part = jnp.where(index == 0, side, jnp.where(early, 0, 1))
+        return valid, chip, part, count_beyond
+
     def turn(index, carry):
-        distance = index // parts
-        part = index % parts
-
-        @pl.when(distance < chips)
+        def ahead(side, inner):
+            valid, chip, part, _ = coming(index, side)
+            pl.when(valid)(lambda: load(chip * parts + part, side).start())
+            return inner
+
+        lax.fori_loop(0, 2, ahead, 0)
+
+        @pl.when(index > 0)
         def _():
-            pl.when(distance > 0)(lambda: line.step(distance, part))
-
-            def one(side, inner):
-                chip = place.chip + distance * (2 * side - 1)
-
-                @pl.when((chip >= 0) & (chip < chips) & ((distance > 0) | (side == 0)))
+            for side in range(2):
+                valid, chip, part, count_beyond = coming(index, side)
+                onward = (place.has_up, place.has_down)[side]
+
+                @pl.when(valid)
                 def _():
-                    line.arrive(chip, 1 - place.core, part)
-                    compute(chip, part)
-
-                return inner
-
-            lax.fori_loop(0, 2, one, 0)
-
-        upward = index - place.chip
-
-        @pl.when((upward >= 0) & (upward // parts > place.chip) & (upward // parts < chips))
-        def _():
-            pass_on(0, upward // parts, upward % parts)
-
-        downward = index - (last - place.chip)
-        target = last - downward // parts
-
-        @pl.when((downward >= 0) & (target >= 0) & (target < place.chip))
-        def _():
-            pass_on(1, target, downward % parts)
+                    line.arrive(chip, place.core, part)
+                    pl.when(onward)(lambda: line.copy(side, chip, part).start())
+                    pl.when(onward & (index == 2 * count_beyond))(
+                        lambda: line.copy(side, place.chip, 1).start()
+                    )
+                    line.copy(2, chip, part).start()
+
+        def one(side, inner):
+            valid, chip, part, _ = coming(index, side)
+
+            @pl.when(valid)
+            def _():
+                line.arrive(chip, 1 - place.core, part)
+                compute(chip, part, side)
+
+            return inner
+
+        lax.fori_loop(0, 2, one, 0)
+        mirrored = last - place.chip
+        for part in range(2):
+            reach = index - place.chip if part == 0 else 2 * last + 1 + place.chip - index
+
+            @pl.when((reach > place.chip) & (reach < chips))
+            def _():
+                pass_on(0, reach, part)
+
+            back = index - mirrored if part == 0 else 2 * last + 1 + mirrored - index
+
+            @pl.when((back > mirrored) & (back < chips))
+            def _():
+                pass_on(1, last - back, part)
 
         return carry
 
     fetched[0].wait()
     fetched[1].wait()
-    lax.fori_loop(0, parts * chips + last, turn, 0)
+    lax.fori_loop(0, 2 * last + 1, turn, 0)
     sums_ref[...] = jnp.zeros_like(sums_ref)
     fetched[2].wait()
     fetched[3].wait()
@@ -1608,7 +1702,7 @@
             dma((4,)),
             dma((pieces, 2)),
             pltpu.VMEM((2 * pieces, rows, width), low),
-            pltpu.VMEM((1, 2 * rows, width), low),
+            pltpu.VMEM((2, 2 * rows, width), low),
             pltpu.VMEM((2, rows, width), jnp.float32),
             pltpu.VMEM((pieces, rows, width), jnp.float32),
             pltpu.VMEM((pieces, rows, width), low),
@@ -1617,7 +1711,7 @@
             dma((3, pieces)),
             dma((2 * pieces,)),
             dma((pieces, 2)),
-            dma((1,)),
+            dma((2,)),
             dma((pieces,)),
             dma((pieces,)),
             dma((pieces, 4)),
@@ -1661,8 +1755,7 @@
     seg_row_ref,
     block_buf,
     columns_buf,
-    probs_ref,
-    flow_ref,
+    resid_buf,
     key_sum,
     value_sum,
     line_send,
@@ -1774,21 +1867,18 @@
                 attended_ref[span, :], here, CROSSED, preferred_element_type=jnp.float32
             )
         grad = result.astype(jnp.bfloat16)
-        for head in range(mixed_ref.shape[2] // HEAD_DIM):
-            attend_back_rows(
-                head,
-                block,
-                grad[:, head * HEAD_DIM : (head + 1) * HEAD_DIM],
-                mixed_ref,
-                aux_ref,
-                seg_row_ref,
-                stacked_ref,
-                probs_ref,
-                flow_ref,
-                key_sum,
-                value_sum,
-                bias_sum_ref,
-            )
+        attend_back_rows(
+            block,
+            grad,
+            attended_ref,
+            mixed_ref,
+            aux_ref,
+            seg_row_ref,
+            stacked_ref,
+            key_sum,
+            value_sum,
+            bias_sum_ref,
+        )
 
     for copy in fetched[2:]:
         copy.wait()
@@ -1813,7 +1903,7 @@
         return carry
 
     lax.fori_loop(0, chips, step, 0)
-    resid = pltpu.make_async_copy(resid_ref, probs_ref, columns_sem)
+    resid = pltpu.make_async_copy(resid_ref, resid_buf, columns_sem)
     resid.start()
     stacked_ref[1] = (key_sum[...] * HEAD_DIM ** (-0.5)).astype(jnp.bfloat16)
     value_grad = value_sum[...].astype(jnp.bfloat16)
@@ -1824,7 +1914,7 @@
     resid.wait()
 
     def emit(span):
-        result = probs_ref[span, :] + total[span, :] + shift_ref[...]
+        result = resid_buf[span, :] + total[span, :] + shift_ref[...]
         live = alive((64, 1), 0, place.me * count + span.start, bounds_ref)
         output_ref[span, :] = jnp.where(live > 0, result, 0.0).astype(jnp.bfloat16)
 
@@ -1877,8 +1967,7 @@
             pltpu.VMEM((1, total), jnp.float32),
             pltpu.VMEM((count, width), low),
             pltpu.VMEM((total, columns), low),
-            pltpu.VMEM((ATTEND_ROWS, total), jnp.float32),
-            pltpu.VMEM((ATTEND_ROWS, total), jnp.float32),
+            pltpu.VMEM((count, width), jnp.float32),
             pltpu.VMEM((total, local), jnp.float32),
             pltpu.VMEM((total, local), jnp.float32),
             dma((3, chips)),
@@ -1921,112 +2010,140 @@
     return causal & (seg_col_ref[row_span, 0:1] == seg_row_ref[:, key_span])
 
 
-def attend_rows(head, row_block, mixed_ref, seg_col_ref, seg_row_ref, attended_ref, lse_ref, score_ref):
+def attend_rows(
+    row_block, mixed_ref, seg_col_ref, seg_row_ref, attended_ref, lse_ref, score_ref
+):
     scale = HEAD_DIM ** (-0.5)
-    lanes = slice(head * HEAD_DIM, (head + 1) * HEAD_DIM)
+    heads = range(mixed_ref.shape[2] // HEAD_DIM)
+    lanes = [slice(head * HEAD_DIM, (head + 1) * HEAD_DIM) for head in heads]
     row_span = pl.ds(pl.multiple_of(row_block * ATTEND_ROWS, ATTEND_ROWS), ATTEND_ROWS)
     count = (row_block * ATTEND_ROWS) // ATTEND_KEYS + 1
-    query = mixed_ref[0, row_span, lanes]
-
-    def score(key_block, peak):
-        key_span = pl.ds(pl.multiple_of(key_block * ATTEND_KEYS, ATTEND_KEYS), ATTEND_KEYS)
-        scores = lax.dot_general(
-            query, mixed_ref[1, key_span, lanes], TURNED, preferred_element_type=jnp.float32
-        )
+    queries = [mixed_ref[0, row_span, lanes[head]] for head in heads]
+
+    def span_of(key_block):
+        return pl.ds(pl.multiple_of(key_block * ATTEND_KEYS, ATTEND_KEYS), ATTEND_KEYS)
+
+    def score(key_block, peaks):
+        key_span = span_of(key_block)
         mask = tile_mask(row_block, key_block, seg_col_ref, seg_row_ref)
-        scores = jnp.where(mask, scores * scale, MASK_FILL)
-        score_ref[:, key_span] = scores
-        for part in range(ATTEND_KEYS // 128):
-            peak = jnp.maximum(peak, scores[:, part * 128 : (part + 1) * 128])
-        return peak
-
-    peak = lax.fori_loop(0, count, score, jnp.full((ATTEND_ROWS, 128), MASK_FILL, jnp.float32))
-    peak = jnp.max(peak, axis=1, keepdims=True)
-
-    def weigh(key_block, mass):
-        key_span = pl.ds(pl.multiple_of(key_block * ATTEND_KEYS, ATTEND_KEYS), ATTEND_KEYS)
-        weights = jnp.exp(score_ref[:, key_span] - peak)
-        score_ref[:, key_span] = weights
-        for part in range(ATTEND_KEYS // 128):
-            mass = mass + weights[:, part * 128 : (part + 1) * 128]
-        return mass
-
-    mass = lax.fori_loop(0, count, weigh, jnp.zeros((ATTEND_ROWS, 128), jnp.float32))
-    mass = jnp.sum(mass, axis=1, keepdims=True)
-    inverse = 1.0 / mass
-    lse_ref[row_span, head + 1 : head + 2] = peak + jnp.log(mass)
-    if head == 0:
-        lse_ref[row_span, 0:1] = seg_col_ref[row_span, :]
-
-    def gather(key_block, total):
-        key_span = pl.ds(pl.multiple_of(key_block * ATTEND_KEYS, ATTEND_KEYS), ATTEND_KEYS)
-        probs = (score_ref[:, key_span] * inverse).astype(jnp.bfloat16)
-        return total + jnp.dot(
-            probs, mixed_ref[2, key_span, lanes], preferred_element_type=jnp.float32
-        )
-
-    total = lax.fori_loop(0, count, gather, jnp.zeros((ATTEND_ROWS, HEAD_DIM), jnp.float32))
-    attended_ref[row_span, lanes] = total.astype(jnp.bfloat16)
+        results = []
+        for head in heads:
+            scores = lax.dot_general(
+                queries[head],
+                mixed_ref[1, key_span, lanes[head]],
+                TURNED,
+                preferred_element_type=jnp.float32,
+            )
+            scores = jnp.where(mask, scores * scale, MASK_FILL)
+            score_ref[head, :, key_span] = scores
+            peak = peaks[head]
+            for part in range(ATTEND_KEYS // 128):
+                peak = jnp.maximum(peak, scores[:, part * 128 : (part + 1) * 128])
+            results.append(peak)
+        return tuple(results)
+
+    filled = jnp.full((ATTEND_ROWS, 128), MASK_FILL, jnp.float32)
+    peaks = lax.fori_loop(0, count, score, (filled,) * len(heads))
+    peaks = [jnp.max(peak, axis=1, keepdims=True) for peak in peaks]
+
+    def weigh(key_block, masses):
+        key_span = span_of(key_block)
+        results = []
+        for head in heads:
+            weights = jnp.exp(score_ref[head, :, key_span] - peaks[head])
+            score_ref[head, :, key_span] = weights
+            mass = masses[head]
+            for part in range(ATTEND_KEYS // 128):
+                mass = mass + weights[:, part * 128 : (part + 1) * 128]
+            results.append(mass)
+        return tuple(results)
+
+    nothing = jnp.zeros((ATTEND_ROWS, 128), jnp.float32)
+    masses = lax.fori_loop(0, count, weigh, (nothing,) * len(heads))
+    masses = [jnp.sum(mass, axis=1, keepdims=True) for mass in masses]
+    inverses = [1.0 / mass for mass in masses]
+    lse_ref[row_span, 0:1] = seg_col_ref[row_span, :]
+    for head in heads:
+        lse_ref[row_span, head + 1 : head + 2] = peaks[head] + jnp.log(masses[head])
+
+    def gather(key_block, totals):
+        key_span = span_of(key_block)
+        results = []
+        for head in heads:
+            probs = (score_ref[head, :, key_span] * inverses[head]).astype(jnp.bfloat16)
+            results.append(
+                totals[head]
+                + jnp.dot(
+                    probs,
+                    mixed_ref[2, key_span, lanes[head]],
+                    preferred_element_type=jnp.float32,
+                )
+            )
+        return tuple(results)
+
+    empty = jnp.zeros((ATTEND_ROWS, HEAD_DIM), jnp.float32)
+    totals = lax.fori_loop(0, count, gather, (empty,) * len(heads))
+    for head in heads:
+        attended_ref[row_span, lanes[head]] = totals[head].astype(jnp.bfloat16)
 
 
 def attend_back_rows(
-    head,
     row_block,
-    grad,
+    grads,
+    attended_ref,
     mixed_ref,
     aux_ref,
     seg_row_ref,
     stacked_ref,
-    probs_ref,
-    flow_ref,
     key_sum,
     value_sum,
     bias_sum,
 ):
     scale = HEAD_DIM ** (-0.5)
-    lanes = slice(head * HEAD_DIM, (head + 1) * HEAD_DIM)
     row_span = pl.ds(pl.multiple_of(row_block * ATTEND_ROWS, ATTEND_ROWS), ATTEND_ROWS)
     count = (row_block * ATTEND_ROWS) // ATTEND_KEYS + 1
-    query = mixed_ref[0, row_span, lanes]
-    lse = aux_ref[row_span, head + 1 : head + 2]
-
-    def first(key_block, delta):
+    row_live = seg_row_ref[:, row_span]
+    heads = []
+    for head in range(mixed_ref.shape[2] // HEAD_DIM):
+        lanes = slice(head * HEAD_DIM, (head + 1) * HEAD_DIM)
+        grad = grads[:, lanes]
+        product = grad.astype(jnp.float32) * attended_ref[row_span, lanes].astype(jnp.float32)
+        delta = jnp.sum(product, axis=1, keepdims=True).reshape(1, ATTEND_ROWS)
+        lse = aux_ref[row_span, head + 1 : head + 2].reshape(1, ATTEND_ROWS)
+        heads.append((lanes, mixed_ref[0, row_span, lanes], grad, lse, delta))
+
+    def one(key_block, totals):
         key_span = pl.ds(pl.multiple_of(key_block * ATTEND_KEYS, ATTEND_KEYS), ATTEND_KEYS)
-        scores = lax.dot_general(
-            query, mixed_ref[1, key_span, lanes], TURNED, preferred_element_type=jnp.float32
+        keys = lax.broadcasted_iota(jnp.int32, (ATTEND_KEYS, ATTEND_ROWS), 0)
+        rows = lax.broadcasted_iota(jnp.int32, (ATTEND_KEYS, ATTEND_ROWS), 1)
+        allowed = (keys - rows <= row_block * ATTEND_ROWS - key_block * ATTEND_KEYS) & (
+            aux_ref[key_span, 0:1] == row_live
         )
-        flow = lax.dot_general(
-            grad, mixed_ref[2, key_span, lanes], TURNED, preferred_element_type=jnp.float32
-        )
-        mask = tile_mask(row_block, key_block, aux_ref, seg_row_ref)
-        probs = jnp.exp(jnp.where(mask, scores * scale, MASK_FILL) - lse)
-        probs_ref[:, key_span] = probs
-        flow_ref[:, key_span] = flow
-        product = probs * flow
-        for part in range(ATTEND_KEYS // 128):
-            delta = delta + product[:, part * 128 : (part + 1) * 128]
-        value_sum[key_span, lanes] += lax.dot_general(
-            probs.astype(jnp.bfloat16), grad, CROSSED, preferred_element_type=jnp.float32
-        )
-        return delta
-
-    delta = lax.fori_loop(0, count, first, jnp.zeros((ATTEND_ROWS, 128), jnp.float32))
-    delta = jnp.sum(delta, axis=1, keepdims=True)
-
-    def second(key_block, total):
-        key_span = pl.ds(pl.multiple_of(key_block * ATTEND_KEYS, ATTEND_KEYS), ATTEND_KEYS)
-        low = (probs_ref[:, key_span] * (flow_ref[:, key_span] - delta)).astype(jnp.bfloat16)
-        key_sum[key_span, lanes] += lax.dot_general(
-            low, query, CROSSED, preferred_element_type=jnp.float32
-        )
-        return total + jnp.dot(
-            low, mixed_ref[1, key_span, lanes], preferred_element_type=jnp.float32
-        )
-
-    total = lax.fori_loop(0, count, second, jnp.zeros((ATTEND_ROWS, HEAD_DIM), jnp.float32))
-    query_grad = (total * scale).astype(jnp.bfloat16)
-    stacked_ref[0, row_span, lanes] = query_grad
-    bias_sum[0:1, lanes] += jnp.sum(query_grad.astype(jnp.float32), axis=0, keepdims=True)
+        results = []
+        for (lanes, query, grad, lse, delta), total in zip(heads, totals):
+            key = mixed_ref[1, key_span, lanes]
+            scores = lax.dot_general(key, query, TURNED, preferred_element_type=jnp.float32)
+            flow = lax.dot_general(
+                mixed_ref[2, key_span, lanes], grad, TURNED, preferred_element_type=jnp.float32
+            )
+            probs = jnp.exp(jnp.where(allowed, scores * scale, MASK_FILL) - lse)
+            value_sum[key_span, lanes] += jnp.dot(
+                probs.astype(jnp.bfloat16), grad, preferred_element_type=jnp.float32
+            )
+            low = (probs * (flow - delta)).astype(jnp.bfloat16)
+            key_sum[key_span, lanes] += jnp.dot(low, query, preferred_element_type=jnp.float32)
+            results.append(
+                total + lax.dot_general(low, key, CROSSED, preferred_element_type=jnp.float32)
+            )
+        return tuple(results)
+
+    totals = lax.fori_loop(
+        0, count, one, (jnp.zeros((ATTEND_ROWS, HEAD_DIM), jnp.float32),) * len(heads)
+    )
+    for (lanes, _, _, _, _), total in zip(heads, totals):
+        query_grad = (total * scale).astype(jnp.bfloat16)
+        stacked_ref[0, row_span, lanes] = query_grad
+        bias_sum[0:1, lanes] += jnp.sum(query_grad.astype(jnp.float32), axis=0, keepdims=True)
 
 
 def tile_scores(query_tile, keys, segment, row_block, col_block):
@@ -2188,7 +2305,7 @@
                 grad_out[here, :] = value
 
 
-ADAM_STEPS = 8
+ADAM_STEPS = 4
 
 
 def adam_call(matrices, smalls, late, early, fixes):

time: 578 us -> 537 us (0.929)
  Pallas kernels: 563 us -> 518 us
    pallas_call x1, Pallas kernels: 123 us -> 101 us  [feed_call(): pl.pallas_call(functools.partial(feed_kernel, chips, parts), out_shape=(j...]
    pallas_call x1, Pallas kernels: 121 us -> 103 us  [branch_back_call(): pl.pallas_call(functools.partial(branch_back_kernel, chips, 2), out_shape...]
where the time goes in v5:
time: 537 us; the launch traced here: 528 us
  Pallas kernels  518 us (96%)
  local copies, waits for them, and re-layouts  5.54 us (1%)
    pallas_call x1, Pallas kernels, attend_out_call(): pl.pallas_call(functools.partial(attend_out_kernel, chips), out_shape=(ja...  107 us
    pallas_call x1, Pallas kernels, input_back_call(): pl.pallas_call(functools.partial(input_back_kernel, chips), out_shape=(ja...  106 us
    pallas_call x1, Pallas kernels, branch_back_call(): pl.pallas_call(functools.partial(branch_back_kernel, chips, 2), out_shape...  103 us
    pallas_call x1, Pallas kernels, feed_call(): pl.pallas_call(functools.partial(feed_kernel, chips, parts), out_shape=(j...  101 us
    pallas_call x1, Pallas kernels, project_call(): pl.pallas_call(functools.partial(project_kernel, chips, parts), out_shape...  82.8 us
    pallas_call x1, Pallas kernels, adam_call(): pl.pallas_call(functools.partial(adam_kernel, tuple(rates)), grid=(ADAM_S...  18.6 us

profile of v5, /device:TPU:0, one launch (start us, length us, event | category | flops | bytes accessed | tf_op | source)
XLA Modules:
  0.0 528.5 jit_solution(10626612159570496163)
XLA Ops:
  0.7 1.6 fusion
  3.5 0.6 pad_add_fusion.bounds_ref
  4.1 82.8 %project.1 = (bf16[2048,2048]{1,0:T(8,128)(2,1)}, bf16[3,2048,256]{2,1,0:T(8,128)(2,1)}, bf16[3,4,512,256]{3,2,1,0:T(8,128)(2,1)}, bf16[4,256,512]{2,1,0:T(8,128...) custom-call(bf16[256,2048]{1,0:T(8,128)(2,1)} %rows_hbm.3, ...), custom_call_target="tpu_custom_call" | custom-call | flops 45097156608 | tf_op jit(solution)/shard_map/project/pallas_call | solution.py:537
  86.9 106.8 %attend_out.1 = (bf16[2048,256]{1,0:T(8,128)(2,1)}, f32[2048,3]{1,0:T(8,128)}, f32[256,2048]{1,0:T(8,128)}, bf16[256,2048]{1,0:T(8,128)(2,1)}, bf16[2048,2048]{1...) custom-call(bf16[3,2048,256]{2,1,0:T(8,128)(2,1)} %get-tuple-element.107.mixed_hbm, ...), custom_call_target="tpu_custom_call" | custom-call | flops 99999997952 | tf_op jit(solution)/shard_map/attend_out/pallas_call | solution.py:1069
  193.7 100.8 %feed.1 = (bf16[2048,2048]{1,0:T(8,128)(2,1)}, bf16[2048,1024]{1,0:T(8,128)(2,1)}, bf16[2048,1024]{1,0:T(8,128)(2,1)}, f32[256,2048]{1,0:T(8,128)}, bf16[256,204...) custom-call(bf16[256,2048]{1,0:T(8,128)(2,1)} %get-tuple-element.112.normed_ref, ...), custom_call_target="tpu_custom_call" | custom-call | flops 99999997952 | tf_op jit(solution)/shard_map/feed/pallas_call | solution.py:1682
  294.5 0.0 copy-start.4
  294.5 0.0 copy-start.2
  294.5 0.0 copy-start.3
  294.6 103.4 %branch_back.1 = (bf16[3,2048,256]{2,1,0:T(8,128)(2,1)}, f32[2,256]{1,0:T(2,128)}, f32[2,512,512]{2,1,0:T(8,128)}, f32[256,2048]{1,0:T(8,128)}, bf16[256,2048]{1...) custom-call(bf16[256,2048]{1,0:T(8,128)(2,1)} %get-tuple-element.117.branch_ref, ...), custom_call_target="tpu_custom_call" | custom-call | flops 99999997952 | tf_op jit(solution)/shard_map/branch_back/pallas_call | solution.py:1947
  398.0 0.7 copy.67
  398.7 0.0 copy-done.4
  398.7 0.0 copy-done.2
  398.7 0.0 copy-done.3
  398.7 0.7 pad_maximum_fusion.early_ref
  399.3 105.7 %input_back.1 = (f32[256,2048]{1,0:T(8,128)}, f32[2,2048]{1,0:T(2,128)}, f32[5,2048]{1,0:T(8,128)}, f32[2,3,256,256]{3,2,1,0:T(8,128)}, f32[2,256,1024]{2,1,0:T(8,128)}, /*index=5*/f32[2,128,512]{2,1,0:T(8,128)}) custom-call(bf16[3,2048,256]{2,1,0:T(8,128)(2,1)} %get-tuple-element.122.stacked_hbm, bf16[3,4,512,256]{3,2,1,0:T(8,128)(2,1)} %get-tuple-element.123.mix_hbm, ...), custom_call_target="tpu_custom_call" | custom-call | flops 99999997952 | tf_op jit(solution)/shard_map/input_back/pallas_call | solution.py:1287
  505.8 0.6 pad_maximum_fusion.1.fix_ref
  506.4 0.0 copy-start.1
  506.4 18.6 %adam.1 = (f32[3,512,256]{2,1,0:T(8,128)}, f32[3,512,256]{2,1,0:T(8,128)}, f32[3,512,256]{2,1,0:T(8,128)}, f32[3,512,256]{2,1,0:T(8,128)}, bf16[3,512,256]{2,1,0...) custom-call(f32[2]{0:T(128)} %pad_maximum_fusion.1.fix_ref, ...), custom_call_target="tpu_custom_call" | custom-call | tf_op jit(solution)/shard_map/adam/pallas_call | solution.py:2337
  525.0 0.0 copy-start
  525.0 0.0 copy-done.1
  525.0 1.0 copy.73
  526.0 1.0 copy-done
  526.9 1.3 copy.74
  (1 shorter events, 0.0 us)
Async XLA Ops:
  294.5 104.1 %copy-start.4 = (f32[1,1024]{1,0:T(1,128)S(1)}, f32[1,1024]{1,0:T(1,128)}, u32[]{:S(2)}) copy-start(f32[1,1024]{1,0:T(1,128)} %get-tuple-element.128) | copy-start | bytes 12292
  294.5 104.1 %copy-start.2 = (f32[3,2048]{1,0:T(4,128)S(1)}, f32[3,2048]{1,0:T(4,128)}, u32[]{:S(2)}) copy-start(f32[3,2048]{1,0:T(4,128)} %get-tuple-element.125) | copy-start | bytes 73732
  294.5 104.1 %copy-start.3 = (f32[1,2048]{1,0:T(1,128)S(1)}, f32[1,2048]{1,0:T(1,128)}, u32[]{:S(2)}) copy-start(f32[1,2048]{1,0:T(1,128)} %get-tuple-element.126) | copy-start | bytes 24580
  506.4 18.6 %copy-start.1 = (bf16[256,2048]{1,0:T(8,128)(2,1)S(1)}, bf16[256,2048]{1,0:T(8,128)(2,1)}, u32[]{:S(2)}) copy-start(bf16[256,2048]{1,0:T(8,128)(2,1)} %get-tuple-element.222) | copy-start | bytes 3145732
  525.0 2.0 copy-start

commit v6 on v5

--- a/solution.py
+++ b/solution.py
@@ -319,7 +319,8 @@
     up_weight_hbm,
     down_weight_hbm,
     cotangent_hbm,
-    bounds_ref,
+    offsets_ref,
+    lengths_ref,
     normed_ref,
     mixed_hbm,
     mix_hbm,
@@ -350,6 +351,7 @@
     keep_sem,
 ):
     place = Place(chips)
+    bounds = (offsets_ref[0], offsets_ref[0] + lengths_ref[0])
     count = rows_ref.shape[0]
     rows = count // parts
     fetched = fetch(
@@ -416,7 +418,7 @@
     branch_sum_ref[...] = jnp.zeros_like(branch_sum_ref)
 
     def branch(span):
-        live = alive((64, 1), 0, place.me * count + span.start, bounds_ref)
+        live = alive((64, 1), 0, place.me * count + span.start, bounds)
         grad = jnp.where(live > 0, cotangent_ref[span, :].astype(jnp.float32), 0.0)
         branch_ref[span, :] = grad.astype(jnp.bfloat16)
         branch_sum_ref[...] += jnp.sum(grad, axis=0, keepdims=True)
@@ -524,7 +526,7 @@
 
 
 def project_call(
-    rows, gain, shift, mix_shard, out_shard, bias, up, down, cotangent, bounds, chips
+    rows, gain, shift, mix_shard, out_shard, bias, up, down, cotangent, offsets, lengths, chips
 ):
     count, width = rows.shape
     total = 2 * chips * count
@@ -550,7 +552,7 @@
         + [hbm] * 2
         + [vmem]
         + [hbm] * 3
-        + [pl.BlockSpec(memory_space=pltpu.SMEM)],
+        + [pl.BlockSpec(memory_space=pltpu.SMEM)] * 2,
         out_specs=(hbm,) * 4 + (vmem,) * 4,
         scratch_shapes=[
             pltpu.VMEM(mix_shard.shape, jnp.float32),
@@ -579,7 +581,7 @@
         ),
         cost_estimate=pl.CostEstimate(flops=flops * 7, bytes_accessed=0, transcendentals=0),
         name="project",
-    )(rows, gain, shift, mix_shard, out_shard, bias, up, down, cotangent, bounds)
+    )(rows, gain, shift, mix_shard, out_shard, bias, up, down, cotangent, offsets, lengths)
 
 
 class LineScatter:
@@ -889,9 +891,9 @@
     ]
 
 
-def alive(shape, axis, start, bounds_ref):
+def alive(shape, axis, start, bounds):
     place = lax.broadcasted_iota(jnp.int32, shape, axis) + start
-    return jnp.where((place >= bounds_ref[0]) & (place < bounds_ref[1]), 1.0, 0.0)
+    return jnp.where((place >= bounds[0]) & (place < bounds[1]), 1.0, 0.0)
 
 
 def by_rows(count, tile, action):
@@ -905,7 +907,8 @@
 def attend_out_kernel(
     chips,
     mixed_hbm,
-    bounds_ref,
+    offsets_ref,
+    lengths_ref,
     out_hbm,
     rows_hbm,
     branch_ref,
@@ -940,6 +943,7 @@
     *scatter,
 ):
     place = Place(chips)
+    bounds = (offsets_ref[0], offsets_ref[0] + lengths_ref[0])
     count = rows_ref.shape[0]
     fetched = fetch(
         [(mixed_hbm, mixed_ref), (out_hbm, out_ref), (rows_hbm, rows_ref)], fetch_sem
@@ -992,10 +996,10 @@
     by_rows(count, 64, copy_in)
     line = LineGather(place, blocks, line_send, line_recv)
     line.begin()
-    seg_row_ref[...] = alive(seg_row_ref.shape, 1, 0, bounds_ref)
+    seg_row_ref[...] = alive(seg_row_ref.shape, 1, 0, bounds)
 
     def column(span):
-        seg_col_ref[span, :] = alive((64, 1), 0, span.start, bounds_ref)
+        seg_col_ref[span, :] = alive((64, 1), 0, span.start, bounds)
 
     by_rows(seg_col_ref.shape[0], 64, column)
     for copy in fetched:
@@ -1057,7 +1061,7 @@
 
 
 def attend_out_call(
-    mixed, bounds, out_whole, rows, branch, gain, shift, bias, up, down, chips
+    mixed, offsets, lengths, out_whole, rows, branch, gain, shift, bias, up, down, chips
 ):
     count, width = rows.shape
     local = mixed.shape[2]
@@ -1077,7 +1081,7 @@
             jax.ShapeDtypeStruct((4,) + up.shape, low),
             jax.ShapeDtypeStruct((4,) + down.shape, low),
         ),
-        in_specs=[hbm, pl.BlockSpec(memory_space=pltpu.SMEM), hbm, hbm] + [vmem] * 6,
+        in_specs=[hbm] + [pl.BlockSpec(memory_space=pltpu.SMEM)] * 2 + [hbm] * 2 + [vmem] * 6,
         out_specs=(vmem, vmem, vmem, vmem, hbm, hbm, hbm),
         scratch_shapes=[
             pltpu.VMEM(mixed.shape, low),
@@ -1103,7 +1107,7 @@
         ),
         cost_estimate=pl.CostEstimate(flops=10**11, bytes_accessed=0, transcendentals=0),
         name="attend_out",
-    )(mixed, bounds, out_whole, rows, branch, gain, shift, bias, up, down)
+    )(mixed, offsets, lengths, out_whole, rows, branch, gain, shift, bias, up, down)
 
 
 def input_back_kernel(
@@ -1113,7 +1117,10 @@
     rows_hbm,
     resid_grad_hbm,
     gain_ref,
-    early_ref,
+    row_sums_ref,
+    bias_down_ref,
+    mix_bias_ref,
+    up_bias_ref,
     hidden_hbm,
     out_grad_hbm,
     normed_one_ref,
@@ -1121,9 +1128,15 @@
     grad_ref,
     late_out_ref,
     early_out_ref,
+    mix_grad_hbm,
+    up_grad_hbm,
+    out_owned_hbm,
     mix_grad_ref,
     up_grad_ref,
     out_owned_ref,
+    hat_buf,
+    inverse_buf,
+    emit_sem,
     stacked_ref,
     mix_ref,
     rows_ref,
@@ -1151,7 +1164,14 @@
     place.greet(True, True)
     fetched[0].wait()
     fetched[1].wait()
-    early_out_ref[...] = early_ref[...]
+    local = mix_bias_ref.shape[1]
+    units = up_bias_ref.shape[1]
+    early_out_ref[0:3, :] = row_sums_ref[...]
+    early_out_ref[3:4, :] = bias_down_ref[...]
+    early_out_ref[4:5, :] = jnp.zeros((1, early_out_ref.shape[1]), jnp.float32)
+    early_out_ref[4:5, 0:local] = mix_bias_ref[0:1, :]
+    early_out_ref[4:5, local : 2 * local] = mix_bias_ref[1:2, :]
+    early_out_ref[4:5, 2 * local : 2 * local + units] = up_bias_ref[...]
     early = SmallSum(place, early_out_ref, 4, scatter[16:19], scatter[19:21])
     late = SmallSum(place, late_out_ref, late_out_ref.shape[0], scatter[21:24], scatter[24:26])
 
@@ -1230,8 +1250,30 @@
     for copy in fetched[2:]:
         copy.wait()
 
+    leaving = [
+        pltpu.make_async_copy(source, target, emit_sem.at[index])
+        for index, (source, target) in enumerate(
+            [
+                (up_grad_ref, up_grad_hbm),
+                (mix_grad_ref, mix_grad_hbm),
+                (out_owned_ref, out_owned_hbm),
+            ]
+        )
+    ]
+
+    def hats(span):
+        _, hat, inverse = layer_norm_parts(
+            rows_ref[span, :].astype(jnp.float32), gain_ref[...], 0.0
+        )
+        hat_buf[span, :] = hat
+        inverse_buf[span, :] = inverse
+
     def step(index, carry):
-        pl.when(index == 3)(lambda: stage(3))
+        @pl.when(index == 3)
+        def _():
+            stage(3)
+            by_rows(count, 64, hats)
+
         sums.step(index)
         for kind in range(3):
 
@@ -1251,32 +1293,34 @@
 
     def columns(span):
         one_grad = total[span, :]
-        _, hat, _ = layer_norm_parts(rows_ref[span, :].astype(jnp.float32), gain_ref[...], 0.0)
-        late_out_ref[0:1, :] += jnp.sum(one_grad * hat, axis=0, keepdims=True)
+        late_out_ref[0:1, :] += jnp.sum(one_grad * hat_buf[span, :], axis=0, keepdims=True)
         late_out_ref[1:2, :] += jnp.sum(one_grad, axis=0, keepdims=True)
 
     def back(span):
-        rows = rows_ref[span, :].astype(jnp.float32)
-        _, hat, inverse = layer_norm_parts(rows, gain_ref[...], 0.0)
         grad_ref[span, :] = resid_grad_ref[span, :] + layer_norm_back(
-            total[span, :], hat, inverse, gain_ref[...]
+            total[span, :], hat_buf[span, :], inverse_buf[span, :], gain_ref[...]
         )
 
     by_rows(count, 64, columns)
     late.begin()
     up.end()
+    leaving[0].start()
     late.middle()
+    mix.end()
+    leaving[1].start()
     by_rows(count, 64, back)
     late.late()
+    out.end()
+    leaving[2].start()
     early.end()
-    mix.end()
-    out.end()
     sums.finish()
     late.end()
+    for copy in leaving:
+        copy.wait()
 
 
 def input_back_call(
-    stacked, mix_whole, rows, resid_grad, gain, early, hidden, out_grad, normed_one, normed_two, chips
+    stacked, mix_whole, rows, resid_grad, gain, smalls, hidden, out_grad, normed_one, normed_two, chips
 ):
     count, width = rows.shape
     total, units = hidden.shape
@@ -1289,14 +1333,20 @@
         out_shape=(
             jax.ShapeDtypeStruct((count, width), jnp.float32),
             jax.ShapeDtypeStruct((2, width), jnp.float32),
-            jax.ShapeDtypeStruct(early.shape, jnp.float32),
+            jax.ShapeDtypeStruct((5, width), jnp.float32),
             jax.ShapeDtypeStruct((2, 3, half, local), jnp.float32),
             jax.ShapeDtypeStruct((2, half, units), jnp.float32),
             jax.ShapeDtypeStruct((2, local // 2, width // 4), jnp.float32),
         ),
-        in_specs=[hbm] * 4 + [vmem] * 2 + [hbm] * 4,
-        out_specs=(vmem,) * 6,
+        in_specs=[hbm] * 4 + [vmem] * 5 + [hbm] * 4,
+        out_specs=(vmem,) * 3 + (hbm,) * 3,
         scratch_shapes=[
+            pltpu.VMEM((2, 3, half, local), jnp.float32),
+            pltpu.VMEM((2, half, units), jnp.float32),
+            pltpu.VMEM((2, local // 2, width // 4), jnp.float32),
+            pltpu.VMEM((count, width), jnp.float32),
+            pltpu.VMEM((count, 1), jnp.float32),
+            pltpu.SemaphoreType.DMA((3,)),
             pltpu.VMEM(stacked.shape, jnp.bfloat16),
             pltpu.VMEM(mix_whole.shape, jnp.bfloat16),
             pltpu.VMEM(rows.shape, jnp.bfloat16),
@@ -1310,7 +1360,7 @@
         + scatter_scratch(chips, count, width)
         + square_scratch((3, half, local))
         + square_scratch((half, units))
-        + small_scratch(chips, early.shape[0], width)
+        + small_scratch(chips, 5, width)
         + small_scratch(chips, 2, width)
         + square_scratch((local // 2, width // 4)),
         compiler_params=pltpu.CompilerParams(
@@ -1318,7 +1368,7 @@
         ),
         cost_estimate=pl.CostEstimate(flops=10**11, bytes_accessed=0, transcendentals=0),
         name="input_back",
-    )(stacked, mix_whole, rows, resid_grad, gain, early, hidden, out_grad, normed_one, normed_two)
+    )(stacked, mix_whole, rows, resid_grad, gain, *smalls, hidden, out_grad, normed_one, normed_two)
 
 
 GELU_SLOPE = 0.7978845608028654
@@ -1734,17 +1784,22 @@
     attended_hbm,
     out_hbm,
     shift_ref,
-    bounds_ref,
+    offsets_ref,
+    lengths_ref,
     mixed_hbm,
     aux_hbm,
     resid_ref,
     cotangent_ref,
+    stacked_hbm,
+    bias_sum_ref,
+    down_grad_hbm,
+    out_grad_hbm,
+    output_ref,
+    blocks,
     stacked_ref,
-    bias_sum_ref,
     down_grad_ref,
     out_grad_ref,
-    output_ref,
-    blocks,
+    emit_sem,
     active_ref,
     down_ref,
     attended_ref,
@@ -1765,6 +1820,7 @@
     *scatter,
 ):
     place = Place(chips)
+    bounds = (offsets_ref[0], offsets_ref[0] + lengths_ref[0])
     count = branch_ref.shape[0]
     rows = count // parts
     fetched = fetch(
@@ -1775,6 +1831,7 @@
             (out_hbm, out_ref),
             (mixed_hbm, mixed_ref),
             (aux_hbm, aux_ref),
+            (resid_ref, resid_buf),
         ],
         fetch_sem,
     )
@@ -1796,7 +1853,7 @@
     fetched[1].wait()
     sums = LineScatter(place, term, 4, scatter[:4], scatter[4:8])
     sums.begin()
-    seg_row_ref[...] = alive(seg_row_ref.shape, 1, 0, bounds_ref)
+    seg_row_ref[...] = alive(seg_row_ref.shape, 1, 0, bounds)
     out_grad_ref[...] = jnp.zeros_like(out_grad_ref)
     key_sum[...] = jnp.zeros_like(key_sum)
     value_sum[...] = jnp.zeros_like(value_sum)
@@ -1880,8 +1937,28 @@
             bias_sum_ref,
         )
 
-    for copy in fetched[2:]:
+    for copy in fetched[2:-1]:
         copy.wait()
+    leaving = [
+        pltpu.make_async_copy(source, target, emit_sem.at[index])
+        for index, (source, target) in enumerate(
+            [
+                (stacked_ref, stacked_hbm),
+                (out_grad_ref, out_grad_hbm),
+                (down_grad_ref, down_grad_hbm),
+            ]
+        )
+    ]
+
+    def settle():
+        stacked_ref[1] = (key_sum[...] * HEAD_DIM ** (-0.5)).astype(jnp.bfloat16)
+        value_grad = value_sum[...].astype(jnp.bfloat16)
+        stacked_ref[2] = value_grad
+        leaving[0].start()
+        leaving[1].start()
+        bias_sum_ref[1:2, :] = jnp.sum(value_grad.astype(jnp.float32), axis=0, keepdims=True)
+        down.end()
+        leaving[2].start()
 
     def step(index, carry):
         def one(side, inner):
@@ -1899,28 +1976,24 @@
         for kind in range(4):
             pl.when(index == kind)(lambda: down_stage(kind))
         pl.when(index < chips - 1)(lambda: line.step(index + 1))
+        pl.when(index == chips - 1)(settle)
         sums.step(index)
         return carry
 
     lax.fori_loop(0, chips, step, 0)
-    resid = pltpu.make_async_copy(resid_ref, resid_buf, columns_sem)
-    resid.start()
-    stacked_ref[1] = (key_sum[...] * HEAD_DIM ** (-0.5)).astype(jnp.bfloat16)
-    value_grad = value_sum[...].astype(jnp.bfloat16)
-    stacked_ref[2] = value_grad
-    bias_sum_ref[1:2, :] = jnp.sum(value_grad.astype(jnp.float32), axis=0, keepdims=True)
-    down.end()
     total = scatter[0]
-    resid.wait()
+    fetched[-1].wait()
 
     def emit(span):
         result = resid_buf[span, :] + total[span, :] + shift_ref[...]
-        live = alive((64, 1), 0, place.me * count + span.start, bounds_ref)
+        live = alive((64, 1), 0, place.me * count + span.start, bounds)
         output_ref[span, :] = jnp.where(live > 0, result, 0.0).astype(jnp.bfloat16)
 
     by_rows(count, 64, emit)
     sums.finish()
     line.finish()
+    for copy in leaving:
+        copy.wait()
 
 
 def branch_back_call(
@@ -1930,7 +2003,8 @@
     attended,
     out_whole,
     shift,
-    bounds,
+    offsets,
+    lengths,
     mixed,
     aux,
     resid,
@@ -1954,16 +2028,20 @@
             jax.ShapeDtypeStruct((count, width), low),
             jax.ShapeDtypeStruct((2 * chips, count, width), low),
         ),
-        in_specs=[hbm] * 5 + [vmem, pl.BlockSpec(memory_space=pltpu.SMEM)] + [hbm] * 4,
-        out_specs=(vmem,) * 5 + (hbm,),
+        in_specs=[hbm] * 5 + [vmem] + [pl.BlockSpec(memory_space=pltpu.SMEM)] * 2 + [hbm] * 4,
+        out_specs=(hbm, vmem, hbm, hbm, vmem, hbm),
         scratch_shapes=[
+            pltpu.VMEM((3, total, local), low),
+            pltpu.VMEM((2, units // 2, columns), jnp.float32),
+            pltpu.VMEM((local, width), jnp.float32),
+            dma((3,)),
             pltpu.VMEM(active.shape, low),
             pltpu.VMEM(down_whole.shape, low),
             pltpu.VMEM(attended.shape, low),
             pltpu.VMEM(out_whole.shape, low),
             pltpu.VMEM(mixed.shape, low),
             pltpu.VMEM(aux.shape, jnp.float32),
-            dma((6,)),
+            dma((7,)),
             pltpu.VMEM((1, total), jnp.float32),
             pltpu.VMEM((count, width), low),
             pltpu.VMEM((total, columns), low),
@@ -1989,7 +2067,8 @@
         attended,
         out_whole,
         shift,
-        bounds,
+        offsets,
+        lengths,
         mixed,
         aux,
         resid,
@@ -2265,8 +2344,15 @@
     return master - rate * change, first_next, second_next
 
 
-def adam_kernel(rates, fix_ref, late_ref, early_ref, *refs):
-    fixes = (fix_ref[0], fix_ref[1])
+def adam_kernel(rates, step_ref, late_ref, early_ref, rows_ref, wide_ref, *refs):
+    one = jnp.float32(1.0)
+    fixes = tuple(
+        one - lax.fori_loop(0, step_ref[0], lambda index, value: value * jnp.float32(beta), one)
+        for beta in (BETA_FIRST, BETA_SECOND)
+    )
+    refs, (rows_out, wide_out) = refs[:-2], refs[-2:]
+    rows_out[...] = rows_ref[...]
+    wide_out[...] = wide_ref[...]
     smalls = 4
     matrix_inputs, small_inputs = refs[: 4 * len(rates)], refs[4 * len(rates) :][: 3 * smalls]
     outputs = refs[4 * len(rates) + 3 * smalls :]
@@ -2308,11 +2394,16 @@
 ADAM_STEPS = 4
 
 
-def adam_call(matrices, smalls, late, early, fixes):
+def adam_call(matrices, smalls, late, early, passing, step):
     in_specs = [pl.BlockSpec(memory_space=pltpu.SMEM)] + [
         pl.BlockSpec(rows.shape, lambda i: (0, 0)) for rows in (late, early)
     ]
-    out_specs, out_shape, operands, rates = [], [], [fixes, late, early], []
+    handed = [
+        pl.BlockSpec((rows.shape[0] // ADAM_STEPS, rows.shape[1]), lambda i: (i, 0))
+        for rows in passing
+    ]
+    in_specs += handed
+    out_specs, out_shape, operands, rates = [], [], [step, late, early, *passing], []
     for master, grad, first, second, rate in matrices:
         lead = master.shape[:-2]
         rows, columns = master.shape[-2] // ADAM_STEPS, master.shape[-1]
@@ -2334,6 +2425,8 @@
         operands += list(group)
         out_specs += [spec] * 4
         out_shape += [jax.ShapeDtypeStruct(group[0].shape, jnp.float32)] * 4
+    out_specs += handed
+    out_shape += [jax.ShapeDtypeStruct(rows.shape, rows.dtype) for rows in passing]
     return pl.pallas_call(
         functools.partial(adam_kernel, tuple(rates)),
         grid=(ADAM_STEPS,),
@@ -2378,7 +2471,6 @@
 ):
     parts = lax.axis_size("mp")
     local_width = mix_weight.shape[2]
-    bounds = jnp.concatenate([offsets, offsets + lengths])
     (
         normed_one,
         mixed,
@@ -2398,7 +2490,8 @@
         up_weight,
         down_weight,
         cotangent,
-        bounds,
+        offsets,
+        lengths,
         parts // 2,
     )
     (
@@ -2411,7 +2504,8 @@
         down_whole,
     ) = attend_out_call(
         mixed,
-        bounds,
+        offsets,
+        lengths,
         out_whole,
         layer_input,
         own_branch,
@@ -2433,7 +2527,6 @@
         norm_gains[1:2],
         parts // 2,
     )
-    up_bias_grad = up_bias_grad[0]
     stacked, mix_bias_grad, down_pieces, out_grad, layer_output, _ = branch_back_call(
         resid_low,
         active,
@@ -2441,23 +2534,13 @@
         attended_flat,
         out_whole,
         shifts[3:4],
-        bounds,
+        offsets,
+        lengths,
         mixed,
         aux,
         resid_own,
         branch_grad,
         parts // 2,
-    )
-    early = jnp.concatenate(
-        [
-            row_sums,
-            bias_down_grad,
-            jnp.pad(
-                jnp.concatenate([mix_bias_grad.reshape(-1), up_bias_grad]),
-                (0, row_sums.shape[1] - 2 * local_width - up_bias_grad.shape[0]),
-            )[None]
-        ],
-        axis=0,
     )
     input_grad, late, early, mix_pieces, up_pieces, out_pieces = input_back_call(
         stacked,
@@ -2465,15 +2548,13 @@
         layer_input,
         resid_grad,
         norm_gains[0:1],
-        early,
+        (row_sums, bias_down_grad, mix_bias_grad, up_bias_grad),
         hidden_grad,
         out_grad,
         normed_one,
         normed_two,
         parts // 2,
     )
-    step_count = step[0].astype(jnp.float32)
-    fixes = jnp.stack([1.0 - BETA_FIRST**step_count, 1.0 - BETA_SECOND**step_count])
     news = adam_call(
         [
             (mix_weight, mix_pieces, mix_first, mix_second, D ** (-0.5)),
@@ -2489,8 +2570,10 @@
         ],
         late,
         early,
-        fixes,
-    )
+        (layer_output, input_grad),
+        step,
+    )
+    layer_output, input_grad = news[-2:]
     mix, out, up, down = (news[5 * index : 5 * index + 5] for index in range(4))
     biases, unit_biases, gains, moves = (
         news[20 + 4 * index : 24 + 4 * index] for index in range(4)

time: 537 us -> 527 us (0.981)
  no operation moved by 1% of the time
where the time goes in v6:
time: 527 us; the launch traced here: 518 us
  Pallas kernels  513 us (97%)
    pallas_call x1, Pallas kernels, attend_out_call(): pl.pallas_call(functools.partial(attend_out_kernel, chips), out_shape=(ja...  107 us
    pallas_call x1, Pallas kernels, input_back_call(): pl.pallas_call(functools.partial(input_back_kernel, chips), out_shape=(ja...  104 us
    pallas_call x1, Pallas kernels, feed_call(): pl.pallas_call(functools.partial(feed_kernel, chips, parts), out_shape=(j...  101 us
    pallas_call x1, Pallas kernels, branch_back_call(): pl.pallas_call(functools.partial(branch_back_kernel, chips, 2), out_shape...  99.7 us
    pallas_call x1, Pallas kernels, project_call(): pl.pallas_call(functools.partial(project_kernel, chips, parts), out_shape...  82.8 us
    pallas_call x1, Pallas kernels, adam_call(): pl.pallas_call(functools.partial(adam_kernel, tuple(rates)), grid=(ADAM_S...  19.8 us

profile of v6, /device:TPU:0, one launch (start us, length us, event | category | flops | bytes accessed | tf_op | source)
XLA Modules:
  0.0 517.8 jit_solution(272285805089396927)
XLA Ops:
  0.7 1.6 fusion
  3.5 82.8 %project.1 = (bf16[2048,2048]{1,0:T(8,128)(2,1)}, bf16[3,2048,256]{2,1,0:T(8,128)(2,1)}, bf16[3,4,512,256]{3,2,1,0:T(8,128)(2,1)}, bf16[4,256,512]{2,1,0:T(8,128...) custom-call(bf16[256,2048]{1,0:T(8,128)(2,1)} %rows_hbm.3, ...), custom_call_target="tpu_custom_call" | custom-call | flops 45097156608 | tf_op jit(solution)/shard_map/project/pallas_call | solution.py:539
  86.4 106.7 %attend_out.1 = (bf16[2048,256]{1,0:T(8,128)(2,1)}, f32[2048,3]{1,0:T(8,128)}, f32[256,2048]{1,0:T(8,128)}, bf16[256,2048]{1,0:T(8,128)(2,1)}, bf16[2048,2048]{1...) custom-call(bf16[3,2048,256]{2,1,0:T(8,128)(2,1)} %get-tuple-element.109.mixed_hbm, ...), custom_call_target="tpu_custom_call" | custom-call | flops 99999997952 | tf_op jit(solution)/shard_map/attend_out/pallas_call | solution.py:1073
  193.0 100.7 %feed.1 = (bf16[2048,2048]{1,0:T(8,128)(2,1)}, bf16[2048,1024]{1,0:T(8,128)(2,1)}, bf16[2048,1024]{1,0:T(8,128)(2,1)}, f32[256,2048]{1,0:T(8,128)}, bf16[256,204...) custom-call(bf16[256,2048]{1,0:T(8,128)(2,1)} %get-tuple-element.114.normed_ref, ...), custom_call_target="tpu_custom_call" | custom-call | flops 99999997952 | tf_op jit(solution)/shard_map/feed/pallas_call | solution.py:1732
  293.7 99.7 %branch_back.1 = (bf16[3,2048,256]{2,1,0:T(8,128)(2,1)}, f32[2,256]{1,0:T(2,128)}, f32[2,512,512]{2,1,0:T(8,128)}, f32[256,2048]{1,0:T(8,128)}, bf16[256,2048]{1...) custom-call(bf16[256,2048]{1,0:T(8,128)(2,1)} %get-tuple-element.119.branch_ref, ...), custom_call_target="tpu_custom_call" | custom-call | flops 99999997952 | tf_op jit(solution)/shard_map/branch_back/pallas_call | solution.py:2021
  393.4 103.7 %input_back.1 = (f32[256,2048]{1,0:T(8,128)}, f32[2,2048]{1,0:T(2,128)}, f32[5,2048]{1,0:T(8,128)}, f32[2,3,256,256]{3,2,1,0:T(8,128)}, f32[2,256,1024]{2,1,0:T(8,128)}, /*index=5*/f32[2,128,512]{2,1,0:T(8,128)}) custom-call(bf16[3,2048,256]{2,1,0:T(8,128)(2,1)} %get-tuple-element.123.stacked_hbm, bf16[3,4,512,256]{3,2,1,0:T(8,128)(2,1)} %get-tuple-element.124.mix_hbm, ...), custom_call_target="tpu_custom_call" | custom-call | flops 99999997952 | tf_op jit(solution)/shard_map/input_back/pallas_call | solution.py:1331
  497.8 19.8 %adam.1 = (f32[3,512,256]{2,1,0:T(8,128)}, f32[3,512,256]{2,1,0:T(8,128)}, f32[3,512,256]{2,1,0:T(8,128)}, f32[3,512,256]{2,1,0:T(8,128)}, bf16[3,512,256]{2,1,0...) custom-call(s32[1]{0:T(128)S(6)} %copy.69.step_ref, ...), custom_call_target="tpu_custom_call" | custom-call | tf_op jit(solution)/shard_map/adam/pallas_call | solution.py:2430

commit v7 on v6

--- a/solution.py
+++ b/solution.py
@@ -124,6 +124,9 @@
         self.across = 3 - self.dp
         self.x_way = (self.x_peer, self.me)
         self.y_way = (self.y_peer, self.me)
+
+    def toward(self, way):
+        return (self.dp, jnp.where(way == 0, self.up[1], self.down[1]))
 
     def greet(self, square, everyone=False):
         barrier = pltpu.get_barrier_semaphore()
@@ -480,16 +483,19 @@
         def _():
             line.step(distance, part)
 
-        @pl.when(index == parts)
+        @pl.when(index == 2)
         def _():
             mix.middle()
             out.begin()
+
+        @pl.when(index == 3)
+        def _():
             mix.end()
             own_mix.wait()
             keep_mix.start()
-            out.middle()
-
-        first = jnp.where(index == parts, 0, index)
+
+        first = jnp.where(index < 6, 2 * (index - 3), index)
+        after = jnp.where(index < 6, 2 * (index - 2), index + 1)
 
         def one(order, inner):
             each = order // 2
@@ -503,10 +509,11 @@
 
             return inner
 
-        @pl.when(index >= parts)
+        @pl.when(index >= 3)
         def _():
-            lax.fori_loop(2 * first, 2 * index + 2, one, 0)
-
+            lax.fori_loop(2 * first, 2 * after, one, 0)
+
+        pl.when(index == 4)(out.middle)
         return carry
 
     lax.fori_loop(0, chips * parts, turn, 0)
@@ -641,8 +648,14 @@
     def hand_over(self, chip):
         self.prepare(chip)
         block = 2 * chip + 1 - self.place.core
-        for tile in range(self.tiles):
-            self.side_out[chip, :, self.span(tile)] = self.term(block, tile).astype(jnp.bfloat16)
+        width = self.total.shape[1] // self.tiles
+
+        def one(tile, carry):
+            span = pl.ds(pl.multiple_of(tile * width, width), width)
+            self.side_out[chip, :, span] = self.term(block, tile).astype(jnp.bfloat16)
+            return carry
+
+        lax.fori_loop(0, self.tiles, one, 0)
         self.side_copy(chip).start()
 
     def sum_up(self, chip):
@@ -674,11 +687,11 @@
 
     def step(self, index, early=False):
         distance = self.place.chips - 1 - index
-        ahead = (index > 0) if early else (index < 0)
-        pl.when(ahead & (distance > 0))(lambda: self.each(distance - 1, self.hand_over))
+        if early:
+            pl.when((index > 0) & (distance > 0))(lambda: self.each(distance - 1, self.hand_over))
         self.each(distance, self.sum_up)
-        behind = (index == 0) if early else (index >= 0)
-        pl.when(behind & (distance > 0))(lambda: self.each(distance - 1, self.hand_over))
+        behind = (index == 0) if early else (distance > 0)
+        pl.when(behind)(lambda: self.each(distance - 1, self.hand_over))
 
     def finish(self):
         place = self.place
@@ -964,6 +977,7 @@
     up = square(up_ref, up_whole, up_send, up_recv)
     down = square(down_ref, down_whole, down_send, down_recv)
     up.begin()
+    down.begin()
     own = [
         pltpu.make_async_copy(up_ref, up_whole.at[place.dp], own_sem.at[0]),
         pltpu.make_async_copy(down_ref, down_whole.at[place.dp], own_sem.at[1]),
@@ -1021,9 +1035,8 @@
         @pl.when(index == 1)
         def _():
             up.middle()
-            down.begin()
-
-        pl.when(index == 2)(down.middle)
+            down.middle()
+
         return carry
 
     lax.fori_loop(0, chips, step, 0)
@@ -1495,7 +1508,7 @@
             line_in.at[slot, :, span],
             out_send.at[piece, tile],
             out_recv.at[slot, tile],
-            (place.up, place.down)[way],
+            place.toward(way),
         )
 
     def line_landed(way, chip, part, tile):
@@ -1507,7 +1520,7 @@
             line_in.at[slot, :, span],
             out_send.at[piece, tile],
             out_recv.at[slot, tile],
-            (place.up, place.down)[way],
+            place.toward(way),
         ).wait_recv()
         return slot
 
@@ -1571,7 +1584,7 @@
     def pass_on(way, chip, part):
         piece = chip * parts + part
         side_copy(piece).wait_recv()
-        behind = (place.has_down, place.has_up)[way]
+        behind = ((way == 0) & place.has_down) | ((way == 1) & place.has_up)
         for tile in range(4):
             span = slice(tile * chunk, (tile + 1) * chunk)
             total = hold[piece, :, span] + side_in[piece, :, span].astype(jnp.float32)
@@ -1632,20 +1645,19 @@
             return inner
 
         lax.fori_loop(0, 2, one, 0)
-        mirrored = last - place.chip
-        for part in range(2):
-            reach = index - place.chip if part == 0 else 2 * last + 1 + place.chip - index
-
-            @pl.when((reach > place.chip) & (reach < chips))
+        def onward(order, inner):
+            way = order // 2
+            part = order % 2
+            here = place.chip + way * (last - 2 * place.chip)
+            reach = jnp.where(part == 0, index - here, 2 * last + 1 + here - index)
+
+            @pl.when((reach > here) & (reach < chips))
             def _():
-                pass_on(0, reach, part)
-
-            back = index - mirrored if part == 0 else 2 * last + 1 + mirrored - index
-
-            @pl.when((back > mirrored) & (back < chips))
-            def _():
-                pass_on(1, last - back, part)
-
+                pass_on(way, reach + way * (last - 2 * reach), part)
+
+            return inner
+
+        lax.fori_loop(0, 4, onward, 0)
         return carry
 
     fetched[0].wait()

time: 527 us -> 509 us (0.966); the launches traced: 518 us -> 509 us
  Pallas kernels: 513 us -> 504 us
    pallas_call x1, Pallas kernels: 104 us -> 93 us  [input_back_call(): pl.pallas_call(functools.partial(input_back_kernel, chips), out_shape=(ja...]
where the time goes in v7:
time: 509 us
  Pallas kernels  504 us (99%)
    pallas_call x1, Pallas kernels, attend_out_call(): pl.pallas_call(functools.partial(attend_out_kernel, chips), out_shape=(ja...  108 us
    pallas_call x1, Pallas kernels, feed_call(): pl.pallas_call(functools.partial(feed_kernel, chips, parts), out_shape=(j...  103 us
    pallas_call x1, Pallas kernels, branch_back_call(): pl.pallas_call(functools.partial(branch_back_kernel, chips, 2), out_shape...  101 us
    pallas_call x1, Pallas kernels, input_back_call(): pl.pallas_call(functools.partial(input_back_kernel, chips), out_shape=(ja...  93 us
    pallas_call x1, Pallas kernels, project_call(): pl.pallas_call(functools.partial(project_kernel, chips, parts), out_shape...  79 us
    pallas_call x1, Pallas kernels, adam_call(): pl.pallas_call(functools.partial(adam_kernel, tuple(rates)), grid=(ADAM_S...  20 us

profile of v7, /device:TPU:0, one launch (start us, length us, event | category | flops | bytes accessed | tf_op | source)
XLA Modules:
  0.0 508.5 jit_solution(12413090264125158400)
XLA Ops:
  0.7 1.6 fusion
  3.5 79.0 %project.1 = (bf16[2048,2048]{1,0:T(8,128)(2,1)}, bf16[3,2048,256]{2,1,0:T(8,128)(2,1)}, bf16[3,4,512,256]{3,2,1,0:T(8,128)(2,1)}, bf16[4,256,512]{2,1,0:T(8,128...) custom-call(bf16[256,2048]{1,0:T(8,128)(2,1)} %rows_hbm.3, ...), custom_call_target="tpu_custom_call" | custom-call | flops 45097156608 | tf_op jit(solution)/shard_map/project/pallas_call | solution.py:546
  82.5 108.3 %attend_out.1 = (bf16[2048,256]{1,0:T(8,128)(2,1)}, f32[2048,3]{1,0:T(8,128)}, f32[256,2048]{1,0:T(8,128)}, bf16[256,2048]{1,0:T(8,128)(2,1)}, bf16[2048,2048]{1...) custom-call(bf16[3,2048,256]{2,1,0:T(8,128)(2,1)} %get-tuple-element.109.mixed_hbm, ...), custom_call_target="tpu_custom_call" | custom-call | flops 99999997952 | tf_op jit(solution)/shard_map/attend_out/pallas_call | solution.py:1086
  190.9 102.7 %feed.1 = (bf16[2048,2048]{1,0:T(8,128)(2,1)}, bf16[2048,1024]{1,0:T(8,128)(2,1)}, bf16[2048,1024]{1,0:T(8,128)(2,1)}, f32[256,2048]{1,0:T(8,128)}, bf16[256,204...) custom-call(bf16[256,2048]{1,0:T(8,128)(2,1)} %get-tuple-element.114.normed_ref, ...), custom_call_target="tpu_custom_call" | custom-call | flops 99999997952 | tf_op jit(solution)/shard_map/feed/pallas_call | solution.py:1744
  293.5 101.2 %branch_back.1 = (bf16[3,2048,256]{2,1,0:T(8,128)(2,1)}, f32[2,256]{1,0:T(2,128)}, f32[2,512,512]{2,1,0:T(8,128)}, f32[256,2048]{1,0:T(8,128)}, bf16[256,2048]{1...) custom-call(bf16[256,2048]{1,0:T(8,128)(2,1)} %get-tuple-element.119.branch_ref, ...), custom_call_target="tpu_custom_call" | custom-call | flops 99999997952 | tf_op jit(solution)/shard_map/branch_back/pallas_call | solution.py:2033
  394.7 93.0 %input_back.1 = (f32[256,2048]{1,0:T(8,128)}, f32[2,2048]{1,0:T(2,128)}, f32[5,2048]{1,0:T(8,128)}, f32[2,3,256,256]{3,2,1,0:T(8,128)}, f32[2,256,1024]{2,1,0:T(8,128)}, /*index=5*/f32[2,128,512]{2,1,0:T(8,128)}) custom-call(bf16[3,2048,256]{2,1,0:T(8,128)(2,1)} %get-tuple-element.123.stacked_hbm, bf16[3,4,512,256]{3,2,1,0:T(8,128)(2,1)} %get-tuple-element.124.mix_hbm, ...), custom_call_target="tpu_custom_call" | custom-call | flops 99999997952 | tf_op jit(solution)/shard_map/input_back/pallas_call | solution.py:1344
  488.4 20.0 %adam.1 = (f32[3,512,256]{2,1,0:T(8,128)}, f32[3,512,256]{2,1,0:T(8,128)}, f32[3,512,256]{2,1,0:T(8,128)}, f32[3,512,256]{2,1,0:T(8,128)}, bf16[3,512,256]{2,1,0...) custom-call(s32[1]{0:T(128)S(6)} %copy.69.step_ref, ...), custom_call_target="tpu_custom_call" | custom-call | tf_op jit(solution)/shard_map/adam/pallas_call | solution.py:2442

commit v8 on v7

--- a/solution.py
+++ b/solution.py
@@ -1282,17 +1282,15 @@
         inverse_buf[span, :] = inverse
 
     def step(index, carry):
-        @pl.when(index == 3)
-        def _():
-            stage(3)
-            by_rows(count, 64, hats)
+        pl.when(index == 3)(lambda: by_rows(count, 64, hats))
 
         sums.step(index)
+        pl.when(index == 0)(lambda: stage(0))
         for kind in range(3):
 
             @pl.when(index == kind)
             def _():
-                stage(kind)
+                stage(kind + 1)
                 if kind == 1:
                     early.middle()
                 if kind == 2:

time: 509 us -> 509 us (level)
  no operation moved by 1% of the time
where the time goes in v8:
time: 509 us; the launch traced here: 508 us
  Pallas kernels  504 us (99%)
    pallas_call x1, Pallas kernels, attend_out_call(): pl.pallas_call(functools.partial(attend_out_kernel, chips), out_shape=(ja...  108 us
    pallas_call x1, Pallas kernels, feed_call(): pl.pallas_call(functools.partial(feed_kernel, chips, parts), out_shape=(j...  103 us
    pallas_call x1, Pallas kernels, branch_back_call(): pl.pallas_call(functools.partial(branch_back_kernel, chips, 2), out_shape...  101 us
    pallas_call x1, Pallas kernels, input_back_call(): pl.pallas_call(functools.partial(input_back_kernel, chips), out_shape=(ja...  92.7 us
    pallas_call x1, Pallas kernels, project_call(): pl.pallas_call(functools.partial(project_kernel, chips, parts), out_shape...  79 us
    pallas_call x1, Pallas kernels, adam_call(): pl.pallas_call(functools.partial(adam_kernel, tuple(rates)), grid=(ADAM_S...  19.8 us

profile of v8, /device:TPU:0, one launch (start us, length us, event | category | flops | bytes accessed | tf_op | source)
XLA Modules:
  0.0 508.0 jit_solution(2560183715261517877)
XLA Ops:
  0.7 1.6 fusion
  3.5 79.0 %project.1 = (bf16[2048,2048]{1,0:T(8,128)(2,1)}, bf16[3,2048,256]{2,1,0:T(8,128)(2,1)}, bf16[3,4,512,256]{3,2,1,0:T(8,128)(2,1)}, bf16[4,256,512]{2,1,0:T(8,128...) custom-call(bf16[256,2048]{1,0:T(8,128)(2,1)} %rows_hbm.3, ...), custom_call_target="tpu_custom_call" | custom-call | flops 45097156608 | tf_op jit(solution)/shard_map/project/pallas_call | solution.py:546
  82.5 108.3 %attend_out.1 = (bf16[2048,256]{1,0:T(8,128)(2,1)}, f32[2048,3]{1,0:T(8,128)}, f32[256,2048]{1,0:T(8,128)}, bf16[256,2048]{1,0:T(8,128)(2,1)}, bf16[2048,2048]{1...) custom-call(bf16[3,2048,256]{2,1,0:T(8,128)(2,1)} %get-tuple-element.109.mixed_hbm, ...), custom_call_target="tpu_custom_call" | custom-call | flops 99999997952 | tf_op jit(solution)/shard_map/attend_out/pallas_call | solution.py:1086
  190.9 102.7 %feed.1 = (bf16[2048,2048]{1,0:T(8,128)(2,1)}, bf16[2048,1024]{1,0:T(8,128)(2,1)}, bf16[2048,1024]{1,0:T(8,128)(2,1)}, f32[256,2048]{1,0:T(8,128)}, bf16[256,204...) custom-call(bf16[256,2048]{1,0:T(8,128)(2,1)} %get-tuple-element.114.normed_ref, ...), custom_call_target="tpu_custom_call" | custom-call | flops 99999997952 | tf_op jit(solution)/shard_map/feed/pallas_call | solution.py:1742
  293.5 101.2 %branch_back.1 = (bf16[3,2048,256]{2,1,0:T(8,128)(2,1)}, f32[2,256]{1,0:T(2,128)}, f32[2,512,512]{2,1,0:T(8,128)}, f32[256,2048]{1,0:T(8,128)}, bf16[256,2048]{1...) custom-call(bf16[256,2048]{1,0:T(8,128)(2,1)} %get-tuple-element.119.branch_ref, ...), custom_call_target="tpu_custom_call" | custom-call | flops 99999997952 | tf_op jit(solution)/shard_map/branch_back/pallas_call | solution.py:2031
  394.7 92.7 %input_back.1 = (f32[256,2048]{1,0:T(8,128)}, f32[2,2048]{1,0:T(2,128)}, f32[5,2048]{1,0:T(8,128)}, f32[2,3,256,256]{3,2,1,0:T(8,128)}, f32[2,256,1024]{2,1,0:T(8,128)}, /*index=5*/f32[2,128,512]{2,1,0:T(8,128)}) custom-call(bf16[3,2048,256]{2,1,0:T(8,128)(2,1)} %get-tuple-element.123.stacked_hbm, bf16[3,4,512,256]{3,2,1,0:T(8,128)(2,1)} %get-tuple-element.124.mix_hbm, ...), custom_call_target="tpu_custom_call" | custom-call | flops 99999997952 | tf_op jit(solution)/shard_map/input_back/pallas_call | solution.py:1342
  488.1 19.8 %adam.1 = (f32[3,512,256]{2,1,0:T(8,128)}, f32[3,512,256]{2,1,0:T(8,128)}, f32[3,512,256]{2,1,0:T(8,128)}, f32[3,512,256]{2,1,0:T(8,128)}, bf16[3,512,256]{2,1,0...) custom-call(s32[1]{0:T(128)S(6)} %copy.69.step_ref, ...), custom_call_target="tpu_custom_call" | custom-call | tf_op jit(solution)/shard_map/adam/pallas_call | solution.py:2440
